TPU v7x, 128 devices: a whole 4x4x4 slice. The times are simulated.
128 devices in a mesh: sta: 16 (over x, y_hi, core), freq: 8 (over y_lo, z).
Axes of the slice: x: 4, y: 4 (y_hi: 2, y_lo: 2; y = y_hi * 2 + y_lo), z: 4, core: 2. Of those that a mesh axis runs over, the one named last changes fastest.
Arguments:
- records: bfloat16 [2048, 256, 512], P('sta', 'freq'), may hold values from -6 to 6
- available: int32 [2048, 256], P('sta', 'freq'), may hold values 0 or 1
Outputs:
- cross_gram: bfloat16 [2, 128, 2048, 2048], P(None, 'freq', 'sta')
All inputs are finite; a program needn't handle non-finite values. No bound on the sum of `available` on one device may be relied on, other than what follows from the above.
Results may differ from a plain program's by a relative error of at most 0.0056.
Values may be sent and summed in bfloat16 or wider, within the bound.
No kernel may reach another device: no remote copies, remote signals or barrier semaphores. Data moves between devices by JAX's collectives and lax.ppermute only.
A program may use at most 192 MiB of HBM per device.

v0:
```python
import jax
import jax.numpy as jnp
from jax import lax
from jax.sharding import PartitionSpec as P

FFT_LEN = 512
BINS = 128
BAND_LO = 16


def spectra_table():
    sample_idx = jnp.arange(FFT_LEN, dtype=jnp.int32)[:, None]
    bin_idx = BAND_LO + jnp.arange(BINS, dtype=jnp.int32)[None, :]
    phase = (sample_idx * bin_idx % FFT_LEN).astype(jnp.float32) * (2.0 * jnp.pi / FFT_LEN)
    return jnp.concatenate([jnp.cos(phase), -jnp.sin(phase)], axis=1)


def gram_block(mine, other):
    count = mine.shape[3]
    both_real = jnp.einsum(
        "fas,fbs->fab", mine[:, 0], other[:, 0], preferred_element_type=jnp.float32
    )
    both_imag = jnp.einsum(
        "fas,fbs->fab", mine[:, 1], other[:, 1], preferred_element_type=jnp.float32
    )
    imag_real = jnp.einsum(
        "fas,fbs->fab", mine[:, 1], other[:, 0], preferred_element_type=jnp.float32
    )
    real_imag = jnp.einsum(
        "fas,fbs->fab", mine[:, 0], other[:, 1], preferred_element_type=jnp.float32
    )
    return jnp.stack([(both_real + both_imag) / count, (imag_real - real_imag) / count]).astype(
        jnp.bfloat16
    )


def shards(records, available):
    stations, segments, samples = records.shape
    sample_pos = jnp.arange(samples, dtype=jnp.float32)
    window_taper = 0.5 - 0.5 * jnp.cos(2.0 * jnp.pi * sample_pos / samples)
    tapered = records.astype(jnp.float32) * window_taper
    spectra = jnp.dot(
        tapered.reshape(stations * segments, samples),
        spectra_table(),
        precision=lax.Precision.HIGHEST,
        preferred_element_type=jnp.float32,
    )
    spectra = spectra.reshape(stations, segments, 2 * BINS)
    real_part = spectra[..., :BINS]
    imag_part = spectra[..., BINS:]
    power = jnp.mean(real_part * real_part + imag_part * imag_part, axis=-1, keepdims=True)
    weight = available.astype(jnp.float32)[..., None] / jnp.sqrt(power + 1e-05)
    whitened = jnp.stack([real_part * weight, imag_part * weight]).astype(jnp.bfloat16)
    whitened = jnp.transpose(whitened, (3, 0, 1, 2))
    panel = lax.all_to_all(whitened, "freq", split_axis=0, concat_axis=3, tiled=True)
    return gram_block(panel, lax.all_gather(panel, "sta", axis=2, tiled=True))


def solution(mesh):
    in_specs = (P("sta", "freq", None), P("sta", "freq"))
    out_specs = P(None, "freq", "sta", None)
    return jax.shard_map(shards, mesh=mesh, in_specs=in_specs, out_specs=out_specs, check_vma=False)
```

profile of v0, /device:TPU:1, one launch (start us, length us, event | category | flops | bytes accessed | tf_op | source)
XLA Modules:
  0.0 333.4 jit_solution(14007002556690948768)
XLA Ops:
  6.5 0.0 all-gather.2.cloned.1.call-start
  6.6 1.1 fusion.18
  7.6 3.4 %convert_multiply_fusion = f32[128,32,512]{2,1,0:T(8,128)S(1)} fusion(bf16[128,32,512]{2,1,0:T(8,128)(2,1)} %param.2, f32[512]{0:T(512)S(1)} %multiply_subtract_fusion), kind=kLoop, calls=%fused_computation.13 | loop fusion | flops 4194304 | bytes 12584960 | tf_op jit(solution)/shard_map/mul | solution.py:41
  11.1 0.0 copy-start.2
  11.1 11.3 %fusion.6 = f32[128,32,256]{2,0,1:T(8,128)S(1)} fusion(f32[128,32,512]{2,1,0:T(8,128)S(1)} %convert_multiply_fusion, f32[512,128]{1,0:T(8,128)S(1)} %get-tuple-element.8, f32[512,128]{1,0:T(8,128)S(1)} %get-tuple-element.7), kind=kOutput, calls=%fused_computation.11 | convolution fusion | flops 6442582016 | bytes 13107200 | tf_op jit(solution)/shard_map/dot_general | solution.py:42
  22.4 0.6 add_reduce_fusion
  23.0 0.0 copy-done.2
  23.0 0.8 fusion.8
  23.9 0.2 maximum_bitcast_fusion
  24.1 2.9 copy.12
  27.0 32.6 %all_to_all.18 = bf16[128,2,128,32]{2,3,1,0:T(8,128)(2,1)S(1)} all-to-all(bf16[128,2,128,32]{2,3,1,0:T(8,128)(2,1)} %copy.12), channel_id=1, replica_groups=mesh['sta'=16,'freq'=8] {'freq'}, dimensions={0} | all-to-all | bytes 4194304 | tf_op jit(solution)/shard_map/all_to_all | solution.py:55
  59.5 0.5 copy.13
  60.0 2.6 copy.14
  62.6 0.0 all-gather.2.cloned.1.call-update
  62.6 0.0 copy-start.1
  62.7 188.9 %all-gather.2.cloned.1.call-done = bf16[16,2,2048,256]{3,2,0,1:T(8,128)(2,1)} async-done(((bf16[16,2,128,256]{3,2,0,1:T(8,128)(2,1)}), bf16[16,2,2048,256]{3,2,0,1:T(8,128)(2,1)}) %all-gather.2.cloned.1.call-update) | async-done | bytes 33554448 | tf_op jit(solution)/shard_map/all_gather | solution.py:56
  251.6 12.8 %fusion = f32[16,128,2048]{2,1,0:T(8,128)} fusion(bf16[16,2,2048,256]{3,2,0,1:T(8,128)(2,1)} %all-gather.2.cloned.1.call-done, bf16[16,2,128,256]{3,2,0,1:T(8,128)(2,1)} %copy.14), kind=kOutput, calls=%fused_computation.5 | convolution fusion | flops 2147483648 | bytes 34603008 | tf_op jit(solution)/shard_map/fas,fbs->fab/dot_general | solution.py:26
  264.4 0.0 copy-done.1
  264.4 12.3 %fusion.1 = f32[16,128,2048]{2,1,0:T(8,128)} fusion(bf16[16,2,2048,256]{3,2,0,1:T(8,128)(2,1)} %all-gather.2.cloned.1.call-done, bf16[16,2,128,256]{3,2,0,1:T(8,128)(2,1)S(1)} %copy-done.1), kind=kOutput, calls=%fused_computation.6 | convolution fusion | flops 2147483648 | bytes 34603008 | tf_op jit(solution)/shard_map/fas,fbs->fab/dot_general | solution.py:20
  276.6 0.0 copy-start
  276.6 15.5 %fusion.5 = bf16[1,16,128,2048]{3,2,1,0:T(8,128)(2,1)} fusion(f32[16,128,2048]{2,1,0:T(8,128)} %fusion, bf16[16,2,2048,256]{3,2,0,1:T(8,128)(2,1)} %all-gather.2.cloned.1.call-done, bf16[16,2,128,256]{3,2,0,1:T(8,128)(2,1)S(1)} %copy-done.1), kind=kOutput, calls=%fused_computation.10 | convolution fusion | flops 2160066560 | bytes 42991616 | tf_op jit(solution)/shard_map/fas,fbs->fab/dot_general | solution.py:29
  292.1 2.9 copy-done
  295.1 17.7 %fusion.4 = bf16[1,16,128,2048]{3,2,1,0:T(8,128)(2,1)} fusion(f32[16,128,2048]{2,1,0:T(8,128)S(1)} %copy-done, bf16[16,2,2048,256]{3,2,0,1:T(8,128)(2,1)} %all-gather.2.cloned.1.call-done, bf16[16,2,128,256]{3,2,0,1:T(8,128)(2,1)S(1)} %copy-done.1), kind=kOutput, calls=%fused_computation.9 | convolution fusion | flops 2160066560 | bytes 42991616 | tf_op jit(solution)/shard_map/fas,fbs->fab/dot_general | solution.py:23
  312.8 13.8 %pad_maximum_fusion = bf16[2,16,128,2048]{3,2,1,0:T(8,128)(2,1)} fusion(bf16[1,16,128,2048]{3,2,1,0:T(8,128)(2,1)} %fusion.5, bf16[1,16,128,2048]{3,2,1,0:T(8,128)(2,1)} %fusion.4), kind=kLoop, calls=%fused_computation.2 | loop fusion | flops 8388608 | bytes 33554432 | tf_op jit(solution)/shard_map/stack | solution.py:32
  (3 shorter events, 0.1 us)
Async XLA Ops:
  6.5 245.0 %all-gather.2.cloned.1.call-start = ((), (), s32[]{:S(2)}) async-start(), calls=%async_computation.1 | async-start | bytes 35651584 | tf_op jit(solution)/shard_map/all_gather | solution.py:56
  11.1 11.9 %copy-start.2 = (s32[128,32]{0,1:T(8,128)S(1)}, s32[128,32]{0,1:T(8,128)}, u32[]{:S(2)}) copy-start(s32[128,32]{0,1:T(8,128)} %param.3) | copy-start | bytes 49156
  62.6 201.7 %copy-start.1 = (bf16[16,2,128,256]{3,2,0,1:T(8,128)(2,1)S(1)}, bf16[16,2,128,256]{3,2,0,1:T(8,128)(2,1)}, u32[]{:S(2)}) copy-start(bf16[16,2,128,256]{3,2,0,1:T(8,128)(2,1)} %copy.14) | copy-start | bytes 6291460
  276.6 18.4 %copy-start = (f32[16,128,2048]{2,1,0:T(8,128)S(1)}, f32[16,128,2048]{2,1,0:T(8,128)}, u32[]{:S(2)}) copy-start(f32[16,128,2048]{2,1,0:T(8,128)} %fusion.1) | copy-start | bytes 50331652
Sparse Core Ops, SparseCore 0:
  62.8 188.7 all-gather.1
where the time goes:
time: 334 us; the launch traced here: 333 us
  waiting for transfers between devices  189 us (57%)
  matrix products  69.5 us (21%)
  blocking collectives  32.6 us (10%)
  other arithmetic  20 us (6%)
  between operations  13.5 us (4%)
  local copies, waits for them, and re-layouts  8.93 us (3%)
    all_gather x1, waiting for transfers between devices, shards(): return gram_block(panel, lax.all_gather(panel, 'sta', axis=2, tiled=True))  189 us
    all_to_all x1, blocking collectives, shards(): lax.all_to_all(whitened, 'freq', split_axis=0, concat_axis=3, tiled=True)  32.6 us
    dot_general x1, matrix products, gram_block(): jnp.einsum('fas,fbs->fab', mine[:, 1], other[:, 1], preferred_element_typ...  17.7 us
    dot_general x1, matrix products, gram_block(): jnp.einsum('fas,fbs->fab', mine[:, 0], other[:, 1], preferred_element_typ...  15.5 us
    another operation x1, other arithmetic, gram_block(): jnp.stack([(both_real + both_imag) / count, (imag_real - real_imag) / cou...  13.8 us
    dot_general x1, matrix products, gram_block(): jnp.einsum('fas,fbs->fab', mine[:, 1], other[:, 0], preferred_element_typ...  12.8 us
    dot_general x1, matrix products, gram_block(): jnp.einsum('fas,fbs->fab', mine[:, 0], other[:, 0], preferred_element_typ...  12.3 us
    dot_general x1, matrix products, shards(): jnp.dot(tapered.reshape(stations * segments, samples), spectra_table(), p...  11.3 us
  transfers between devices with their start and end apart: 1, of which 1 were waited for; matrix products, arithmetic and copies ran while one was open for 0% of the time, Pallas kernels for 0%

commit v1 on v0

v1 whole, which is shorter than its diff:
```python
import functools

import jax
import jax.numpy as jnp
import numpy as np
from jax import lax
from jax.experimental import pallas as pl
from jax.experimental.pallas import tpu as pltpu
from jax.sharding import Mesh, PartitionSpec as P

FFT_LEN = 512
BINS = 128
BAND_LO = 16
SUBS = 2


def spectra_table():
    sample = np.arange(FFT_LEN)
    phase = (sample[:, None] * (BAND_LO + np.arange(BINS))[None, :] % FFT_LEN) * (2.0 * np.pi / FFT_LEN)
    taper = 0.5 - 0.5 * np.cos(2.0 * np.pi * sample / FFT_LEN)
    table = np.concatenate([np.cos(phase), -np.sin(phase)], axis=1) * taper[:, None]
    high = table.astype(jnp.bfloat16)
    low = (table - high.astype(np.float64)).astype(jnp.bfloat16)
    return np.concatenate([high, low], axis=1)


def gram_kernel(scale, where, mine_ref, own_ref, other_ref, *outs):
    out_ref = outs[-1]
    panel = jnp.concatenate([own_ref[0], other_ref[0]], axis=1)
    gram = jnp.dot(mine_ref[0], panel, preferred_element_type=jnp.float32) * scale
    gram = gram.astype(jnp.bfloat16)
    rows = gram.shape[0] // 2
    cols = gram.shape[1] // 2
    own = pl.ds(pl.multiple_of(where[1] * cols, cols), cols)
    other = pl.ds(pl.multiple_of((1 - where[1]) * cols, cols), cols)
    out_ref[0, 0, :, own] = gram[:rows, :cols]
    out_ref[1, 0, :, own] = gram[rows:, :cols]
    out_ref[0, 0, :, other] = gram[:rows, cols:]
    out_ref[1, 0, :, other] = gram[rows:, cols:]


def gram(first, chip, core, mine, own, other, shape, out):
    bins, depth, cols = own.shape
    rows = mine.shape[1] // 2
    where = jnp.stack([chip, core]).astype(jnp.int32)
    held = [] if out is None else [out]
    return pl.pallas_call(
        functools.partial(gram_kernel, 2.0 / depth),
        grid_spec=pltpu.PrefetchScalarGridSpec(
            num_scalar_prefetch=1,
            grid=(bins,),
            in_specs=[
                pl.BlockSpec((1, 2 * rows, depth), lambda f, w: (first + f, 0, 0)),
                pl.BlockSpec((1, depth, cols), lambda f, w: (f, 0, 0)),
                pl.BlockSpec((1, depth, cols), lambda f, w: (f, 0, 0)),
            ] + [pl.BlockSpec(memory_space=pl.ANY)] * len(held),
            out_specs=pl.BlockSpec((2, 1, rows, 2 * cols), lambda f, w: (0, first + f, 0, w[0])),
        ),
        out_shape=jax.ShapeDtypeStruct(shape, jnp.bfloat16),
        input_output_aliases={4: 0} if held else {},
        cost_estimate=pl.CostEstimate(
            flops=8 * bins * rows * depth * cols,
            bytes_accessed=2 * bins * (2 * rows * depth + 2 * depth * cols + 4 * rows * cols),
            transcendentals=0,
        ),
        name="gram",
    )(where, mine, own, other, *held)


def ring(size, step):
    return [(i, (i + step) % size) for i in range(size)]


def shards(records, available):
    stations, segments, samples = records.shape
    x, yh, core = lax.axis_index("x"), lax.axis_index("yh"), lax.axis_index("core")
    spectra = jnp.dot(
        records.reshape(stations * segments, samples),
        jnp.asarray(spectra_table()),
        preferred_element_type=jnp.float32,
    )
    spectra = spectra[:, : 2 * BINS] + spectra[:, 2 * BINS :]
    spectra = spectra.reshape(stations, segments, 2 * BINS)
    power = jnp.sum(spectra * spectra, axis=-1, keepdims=True) / BINS
    weight = available.astype(jnp.float32)[..., None] / jnp.sqrt(power + 1e-05)
    whitened = (spectra * weight).astype(jnp.bfloat16).reshape(stations, segments, 2, BINS)
    whitened = jnp.transpose(whitened, (3, 2, 1, 0))
    panel = lax.all_to_all(whitened, ("yl", "z"), split_axis=0, concat_axis=2, tiled=True)
    bins, _, depth, _ = panel.shape
    turned = jnp.transpose(panel, (0, 1, 3, 2))
    real, imag = turned[:, 0], turned[:, 1]
    mine = jnp.concatenate(
        [jnp.concatenate([real, imag], axis=2), jnp.concatenate([imag, -real], axis=2)], axis=1
    )
    panel = panel.reshape(bins, 2 * depth, stations)

    out, shape = None, (2, bins, stations, 16 * stations)
    sub = bins // SUBS
    blocks = []
    for part in range(SUBS):
        step = 1 if part % 2 == 0 else -1
        along = lambda v, s: lax.ppermute(v, "x", ring(4, s))
        across = lambda v: lax.ppermute(v, "yh", ring(2, 1))
        own = panel[part * sub : (part + 1) * sub]
        near = along(own, step)
        back = along(own, -step)
        over = across(own)
        far = along(near, step)
        near_over = across(near)
        back_over = along(over, -step)
        far_over = along(near_over, step)
        got = [
            (0, 0, own), (step, 0, near), (-step, 0, back), (0, 1, over),
            (2 * step, 0, far), (step, 1, near_over), (-step, 1, back_over), (2 * step, 1, far_over),
        ]
        blocks.append([(dx, dy, v, lax.ppermute(v, "core", ring(2, 1))) for dx, dy, v in got])
    for group in zip(*blocks):
        for part, (dx, dy, own, other) in enumerate(group):
            chip = (x - dx) % 4 * 2 + (yh + dy) % 2
            out = gram(part * sub, chip, core, mine, own, other, shape, out)
    return out


def solution(mesh):
    fine = Mesh(mesh.devices.reshape(4, 2, 2, 2, 4), ("x", "yh", "core", "yl", "z"))
    sta, freq = ("x", "yh", "core"), ("yl", "z")
    return jax.shard_map(
        shards,
        mesh=fine,
        in_specs=(P(sta, freq, None), P(sta, freq)),
        out_specs=P(None, freq, sta, None),
        check_vma=False,
    )
```

time: 334 us -> 324 us (0.970)
  Pallas kernels: 0 us -> 117 us
  waiting for transfers between devices: 189 us -> 89.6 us
  matrix products: 69.5 us -> 4.76 us
  starting transfers between devices: 0.01 us -> 36.1 us
  local copies, waits for them, and re-layouts: 8.93 us -> 23.3 us
  between operations: 13.5 us -> 0.2 us
    all_gather x1 -> x0, waiting for transfers between devices: 189 us -> none  [shards(): return gram_block(panel, lax.all_gather(panel, 'sta', axis=2, tiled=True))]
    pallas_call x0 -> x16, Pallas kernels: none -> 117 us  [gram(): pl.pallas_call(functools.partial(gram_kernel, 2.0 / depth), grid_spec=plt...]
    ppermute x0 -> x30, waiting for transfers between devices: none -> 89.6 us  [the longest x10 68.5 us: shards(): along = lambda v, s: lax.ppermute(v, 'x', ring(4, s))]
    dot_general x5 -> x1, matrix products: 69.5 us -> 4.76 us  [shards(): jnp.dot(records.reshape(stations * segments, samples), jnp.asarray(spectr...]
    ppermute x0 -> x30, starting transfers between devices: none -> 36.1 us  [the longest x16 16.6 us: shards(): lax.ppermute(v, 'core', ring(2, 1))]
    another operation x2 -> x9, other arithmetic: 14.6 us -> 5.68 us  [gram(): where = jnp.stack([chip, core]).astype(jnp.int32)]
    transpose x1, other arithmetic: 0.19 us -> 7.37 us  [shards(): whitened = jnp.transpose(whitened, (3, 2, 1, 0))]
    reshape x0 -> x1, local copies, waits for them, and re-layouts: none -> 5.76 us  [shards(): spectra = spectra.reshape(stations, segments, 2 * BINS)]
  transfers between devices with their start and end apart: 1 -> 30, of which waited for: 1 -> 6; matrix products, arithmetic and copies ran while one was open for 0% -> 4% of each run, Pallas kernels for 0% -> 34%
where the time goes in v1:
time: 324 us; the launch traced here: 322 us
  Pallas kernels  117 us (36%)
  waiting for transfers between devices  89.6 us (28%)
  starting transfers between devices  36.1 us (11%)
  blocking collectives  32.6 us (10%)
  local copies, waits for them, and re-layouts  23.3 us (7%)
  other arithmetic  18 us (6%)
  matrix products  4.76 us (1%)
    pallas_call x16, Pallas kernels, gram(): pl.pallas_call(functools.partial(gram_kernel, 2.0 / depth), grid_spec=plt...  117 us
    ppermute x10, waiting for transfers between devices, shards(): along = lambda v, s: lax.ppermute(v, 'x', ring(4, s))  68.5 us
    all_to_all x1, blocking collectives, shards(): lax.all_to_all(whitened, ('yl', 'z'), split_axis=0, concat_axis=2, tiled=...  32.6 us
    ppermute x4, waiting for transfers between devices, shards(): across = lambda v: lax.ppermute(v, 'yh', ring(2, 1))  21.1 us
    ppermute x16, starting transfers between devices, shards(): lax.ppermute(v, 'core', ring(2, 1))  16.6 us
    ppermute x10, starting transfers between devices, shards(): along = lambda v, s: lax.ppermute(v, 'x', ring(4, s))  11 us
    ppermute x4, starting transfers between devices, shards(): across = lambda v: lax.ppermute(v, 'yh', ring(2, 1))  8.54 us
    transpose x1, other arithmetic, shards(): whitened = jnp.transpose(whitened, (3, 2, 1, 0))  7.37 us
  transfers between devices with their start and end apart: 30, of which 6 were waited for; matrix products, arithmetic and copies ran while one was open for 4% of the time, Pallas kernels for 34%

profile of v1, /device:TPU:1, one launch (start us, length us, event | category | flops | bytes accessed | tf_op | source)
XLA Modules:
  0.0 321.5 jit_solution(276723294919037165)
XLA Ops:
  0.0 4.8 %convolution_bitcast_fusion = f32[4096,512]{0,1:T(8,128)S(1)} fusion(bf16[512,512]{1,0:T(8,128)(2,1)} %constant.126.clone, bf16[4096,512]{1,0:T(8,128)(2,1)} %bitcast.36), kind=kOutput, calls=%fused_computation | convolution fusion | flops 2147483648 | bytes 13107200 | tf_op jit(solution)/shard_map/dot_general | solution.py:77
  4.8 2.7 multiply_reduce_fusion
  7.5 5.6 %copy.36 = f32[4096,256]{1,0:T(8,128)} copy(f32[4096,256]{0,1:T(8,128)} %get-tuple-element.6) | data formatting | bytes 8388608 | tf_op jit(solution)/shard_map/add | solution.py:82
  13.1 5.8 %reshape.24 = f32[128,32,2,128]{3,2,1,0:T(2,128)} reshape(f32[4096,256]{1,0:T(8,128)} %copy.36) | data formatting | bytes 8388608 | tf_op jit(solution)/shard_map/reshape | solution.py:83
  19.1 7.4 %fusion = bf16[128,2,32,128]{0,1,2,3:T(2,128)(2,1)S(1)} fusion(f32[128,32,2,128]{3,2,1,0:T(2,128)} %reshape.24, f32[128,32]{1,0:T(8,128)S(1)} %convert_multiply_fusion), kind=kLoop, calls=%fused_computation.5 | loop fusion | flops 2097152 | bytes 6307840 | tf_op jit(solution)/shard_map/transpose | solution.py:87
  26.4 3.8 %copy.38 = bf16[128,2,32,128]{3,2,1,0:T(8,128)(2,1)} copy(bf16[128,2,32,128]{0,1,2,3:T(2,128)(2,1)S(1)} %fusion) | data formatting | bytes 4194304 | tf_op jit(solution)/shard_map/transpose | solution.py:87
  30.3 32.6 %all_to_all.18 = bf16[128,2,32,128]{3,2,1,0:T(8,128)(2,1)S(1)} all-to-all(bf16[128,2,32,128]{3,2,1,0:T(8,128)(2,1)} %copy.38), channel_id=1, replica_groups=mesh['x'=4,'yh'=2,'core'=2,'yl'=2,'z'=4] {'yl','z'}, dimensions={0} | all-to-all | bytes 4194304 | tf_op jit(solution)/shard_map/all_to_all | solution.py:88
  62.8 0.5 fusion.2
  63.4 2.5 collective-permute-start.29
  66.2 1.3 collective-permute-start.4
  67.4 1.5 collective-permute-start
  68.9 1.3 collective-permute-start.24
  70.4 2.6 collective-permute-start.11
  73.0 18.8 %collective-permute-done.4.own_ref = bf16[8,512,128]{2,1,0:T(8,128)(2,1)} collective-permute-done((bf16[8,512,128]{2,1,0:T(8,128)(2,1)S(1)}, bf16[8,512,128]{2,1,0:T(8,128)(2,1)}, u32[]{:S(2)}, u32[]{:S(2)}) %collective-permute-start.4) | collective-permute-done | bytes 1048608 | tf_op jit(solution)/shard_map/ppermute | solution.py:102
  91.9 2.6 collective-permute-start.8
  94.5 2.4 collective-permute-start.27
  96.9 17.1 %collective-permute-done.24.own_ref = bf16[8,512,128]{2,1,0:T(8,128)(2,1)S(1)} collective-permute-done((bf16[8,512,128]{2,1,0:T(8,128)(2,1)S(1)}, bf16[8,512,128]{2,1,0:T(8,128)(2,1)S(1)}, u32[]{:S(2)}, u32[]{:S(2)}) %collective-permute-start.24) | collective-permute-done | bytes 1048608 | tf_op jit(solution)/shard_map/ppermute | solution.py:102
  114.0 1.5 collective-permute-start.26
  116.0 2.0 collective-permute-done.8.own_ref
  118.0 2.1 collective-permute-start.21
  120.2 0.6 collective-permute-start.18
  120.8 2.2 collective-permute-start.16
  123.0 2.7 collective-permute-start.5
  125.7 0.6 collective-permute-start.1
  126.7 1.3 collective-permute-start.12
  128.0 18.1 %collective-permute-done.18.own_ref = bf16[8,512,128]{2,1,0:T(8,128)(2,1)S(1)} collective-permute-done((bf16[8,512,128]{2,1,0:T(8,128)(2,1)}, bf16[8,512,128]{2,1,0:T(8,128)(2,1)S(1)}, u32[]{:S(2)}, u32[]{:S(2)}) %collective-permute-start.18) | collective-permute-done | bytes 1048608 | tf_op jit(solution)/shard_map/ppermute | solution.py:102
  146.1 1.0 copy-done.12
  147.1 0.6 pad_add_fusion.9.where
  147.7 0.7 pad_add_fusion.7.where
  148.4 1.1 collective-permute-start.19
  149.5 2.4 collective-permute-start.17
  152.0 19.1 %collective-permute-done.1.own_ref = bf16[8,512,128]{2,1,0:T(8,128)(2,1)} collective-permute-done((bf16[8,512,128]{2,1,0:T(8,128)(2,1)}, bf16[8,512,128]{2,1,0:T(8,128)(2,1)}, u32[]{:S(2)}, u32[]{:S(2)}) %collective-permute-start.1) | collective-permute-done | bytes 1048608 | tf_op jit(solution)/shard_map/ppermute | solution.py:103
  171.1 1.9 collective-permute-start.15
  172.9 0.7 pad_add_fusion.8.where
  173.6 0.6 pad_add_fusion.6.where
  174.3 2.7 collective-permute-start.2
  176.9 0.6 pad_add_fusion.5.where
  177.6 0.7 pad_add_fusion.4.where
  178.2 0.6 pad_add_fusion.2.where
  178.8 0.6 pad_add_fusion.3.where
  179.4 0.6 pad_add_fusion
  180.0 1.8 copy.39
  181.9 2.9 copy.40
  185.0 0.6 collective-permute-start.14
  186.2 14.4 %collective-permute-done.6.own_ref = bf16[8,512,128]{2,1,0:T(8,128)(2,1)} collective-permute-done((bf16[8,512,128]{2,1,0:T(8,128)(2,1)}, bf16[8,512,128]{2,1,0:T(8,128)(2,1)}, u32[]{:S(2)}, u32[]{:S(2)}) %collective-permute-start.6) | collective-permute-done | bytes 1048608 | tf_op jit(solution)/shard_map/ppermute | solution.py:102
  200.6 0.8 collective-permute-start.7
  201.4 2.1 maximum_maximum_fusion.mine_ref
  203.5 7.3 %gram.16.outs_0_ = bf16[2,16,128,2048]{3,2,1,0:T(8,128)(2,1)} custom-call(s32[2]{0:T(128)} %pad_add_fusion.9.where, bf16[16,256,512]{2,1,0:T(8,128)(2,1)} %maximum_maximum_fusion.mine_ref, bf16[8,512,128]{2,1,0:T(8,128)(2,1)} %bitcast.41, bf16[8,512,128]{2,1,0:T(8,128)(2,1)} %copy-done.2), custom_call_target="tpu_custom_call" | custom-call | flops 536870912 | bytes 5242880 | tf_op jit(solution)/shard_map/gram/pallas_call | solution.py:47
  210.8 7.3 %gram.17.outs_0_ = bf16[2,16,128,2048]{3,2,1,0:T(8,128)(2,1)} custom-call(s32[2]{0:T(128)} %pad_add_fusion.9.where, bf16[16,256,512]{2,1,0:T(8,128)(2,1)} %maximum_maximum_fusion.mine_ref, bf16[8,512,128]{2,1,0:T(8,128)(2,1)} %bitcast.46, bf16[8,512,128]{2,1,0:T(8,128)(2,1)} %copy-done.3, ...), custom_call_target="tpu_custom_call", output_to_operand_aliasing={{}: (4, {})} | custom-call | flops 536870912 | bytes 5242880 | tf_op jit(solution)/shard_map/gram/pallas_call | solution.py:47
  218.1 7.3 %gram.18.outs_0_ = bf16[2,16,128,2048]{3,2,1,0:T(8,128)(2,1)} custom-call(s32[2]{0:T(128)} %pad_add_fusion.7.where, bf16[16,256,512]{2,1,0:T(8,128)(2,1)} %maximum_maximum_fusion.mine_ref, bf16[8,512,128]{2,1,0:T(8,128)(2,1)} %collective-permute-done.4.own_ref, bf16[8,512,128]{2,1,0:T(8,128)(2,1)} %copy-done.6, ...), custom_call_target="tpu_custom_call", output_to_operand_aliasing={{}: (4, {})} | custom-call | flops 536870912 | bytes 5242880 | tf_op jit(solution)/shard_map/gram/pallas_call | solution.py:47
  225.4 7.3 %gram.19.outs_0_ = bf16[2,16,128,2048]{3,2,1,0:T(8,128)(2,1)} custom-call(s32[2]{0:T(128)} %pad_add_fusion.8.where, bf16[16,256,512]{2,1,0:T(8,128)(2,1)} %maximum_maximum_fusion.mine_ref, bf16[8,512,128]{2,1,0:T(8,128)(2,1)} %collective-permute-done.own_ref, bf16[8,512,128]{2,1,0:T(8,128)(2,1)} %copy-done.7, ...), custom_call_target="tpu_custom_call", output_to_operand_aliasing={{}: (4, {})} | custom-call | flops 536870912 | bytes 5242880 | tf_op jit(solution)/shard_map/gram/pallas_call | solution.py:47
  232.8 7.3 %gram.20.outs_0_ = bf16[2,16,128,2048]{3,2,1,0:T(8,128)(2,1)} custom-call(s32[2]{0:T(128)} %pad_add_fusion.8.where, bf16[16,256,512]{2,1,0:T(8,128)(2,1)} %maximum_maximum_fusion.mine_ref, bf16[8,512,128]{2,1,0:T(8,128)(2,1)} %copy-done.4, bf16[8,512,128]{2,1,0:T(8,128)(2,1)} %copy-done.8, ...), custom_call_target="tpu_custom_call", output_to_operand_aliasing={{}: (4, {})} | custom-call | flops 536870912 | bytes 5242880 | tf_op jit(solution)/shard_map/gram/pallas_call | solution.py:47
  240.1 7.3 %gram.21.outs_0_ = bf16[2,16,128,2048]{3,2,1,0:T(8,128)(2,1)} custom-call(s32[2]{0:T(128)} %pad_add_fusion.7.where, bf16[16,256,512]{2,1,0:T(8,128)(2,1)} %maximum_maximum_fusion.mine_ref, bf16[8,512,128]{2,1,0:T(8,128)(2,1)} %copy-done.5, bf16[8,512,128]{2,1,0:T(8,128)(2,1)} %copy-done.9, ...), custom_call_target="tpu_custom_call", output_to_operand_aliasing={{}: (4, {})} | custom-call | flops 536870912 | bytes 5242880 | tf_op jit(solution)/shard_map/gram/pallas_call | solution.py:47
  247.4 7.3 %gram.22.outs_0_ = bf16[2,16,128,2048]{3,2,1,0:T(8,128)(2,1)} custom-call(s32[2]{0:T(128)} %pad_add_fusion.6.where, bf16[16,256,512]{2,1,0:T(8,128)(2,1)} %maximum_maximum_fusion.mine_ref, bf16[8,512,128]{2,1,0:T(8,128)(2,1)} %collective-permute-done.11.own_ref, bf16[8,512,128]{2,1,0:T(8,128)(2,1)} %copy-done.10, ...), custom_call_target="tpu_custom_call", output_to_operand_aliasing={{}: (4, {})} | custom-call | flops 536870912 | bytes 5242880 | tf_op jit(solution)/shard_map/gram/pallas_call | solution.py:47
  254.7 7.3 %gram.23.outs_0_ = bf16[2,16,128,2048]{3,2,1,0:T(8,128)(2,1)} custom-call(s32[2]{0:T(128)} %pad_add_fusion.6.where, bf16[16,256,512]{2,1,0:T(8,128)(2,1)} %maximum_maximum_fusion.mine_ref, bf16[8,512,128]{2,1,0:T(8,128)(2,1)} %collective-permute-done.8.own_ref, bf16[8,512,128]{2,1,0:T(8,128)(2,1)} %copy-done.11, ...), custom_call_target="tpu_custom_call", output_to_operand_aliasing={{}: (4, {})} | custom-call | flops 536870912 | bytes 5242880 | tf_op jit(solution)/shard_map/gram/pallas_call | solution.py:47
  262.0 7.3 %gram.24.outs_0_ = bf16[2,16,128,2048]{3,2,1,0:T(8,128)(2,1)} custom-call(s32[2]{0:T(128)} %pad_add_fusion.5.where, bf16[16,256,512]{2,1,0:T(8,128)(2,1)} %maximum_maximum_fusion.mine_ref, bf16[8,512,128]{2,1,0:T(8,128)(2,1)} %copy-done.12, bf16[8,512,128]{2,1,0:T(8,128)(2,1)} %collective-permute-done.19.other_ref, ...), custom_call_target="tpu_custom_call", output_to_operand_aliasing={{}: (4, {})} | custom-call | flops 536870912 | bytes 5242880 | tf_op jit(solution)/shard_map/gram/pallas_call | solution.py:47
  269.3 7.3 %gram.25.outs_0_ = bf16[2,16,128,2048]{3,2,1,0:T(8,128)(2,1)} custom-call(s32[2]{0:T(128)} %pad_add_fusion.4.where, bf16[16,256,512]{2,1,0:T(8,128)(2,1)} %maximum_maximum_fusion.mine_ref, bf16[8,512,128]{2,1,0:T(8,128)(2,1)} %collective-permute-done.16.own_ref, ...), custom_call_target="tpu_custom_call", output_to_operand_aliasing={{}: (4, {})} | custom-call | flops 536870912 | bytes 5242880 | tf_op jit(solution)/shard_map/gram/pallas_call | solution.py:47
  276.6 7.3 %gram.26.outs_0_ = bf16[2,16,128,2048]{3,2,1,0:T(8,128)(2,1)} custom-call(s32[2]{0:T(128)} %pad_add_fusion.2.where, bf16[16,256,512]{2,1,0:T(8,128)(2,1)} %maximum_maximum_fusion.mine_ref, bf16[8,512,128]{2,1,0:T(8,128)(2,1)} %collective-permute-done.5.own_ref, ...), custom_call_target="tpu_custom_call", output_to_operand_aliasing={{}: (4, {})} | custom-call | flops 536870912 | bytes 5242880 | tf_op jit(solution)/shard_map/gram/pallas_call | solution.py:47
  283.9 7.3 %gram.27.outs_0_ = bf16[2,16,128,2048]{3,2,1,0:T(8,128)(2,1)} custom-call(s32[2]{0:T(128)} %pad_add_fusion.3.where, bf16[16,256,512]{2,1,0:T(8,128)(2,1)} %maximum_maximum_fusion.mine_ref, bf16[8,512,128]{2,1,0:T(8,128)(2,1)} %collective-permute-done.1.own_ref, ...), custom_call_target="tpu_custom_call", output_to_operand_aliasing={{}: (4, {})} | custom-call | flops 536870912 | bytes 5242880 | tf_op jit(solution)/shard_map/gram/pallas_call | solution.py:47
  291.3 7.3 %gram.28.outs_0_ = bf16[2,16,128,2048]{3,2,1,0:T(8,128)(2,1)} custom-call(s32[2]{0:T(128)} %pad_add_fusion.3.where, bf16[16,256,512]{2,1,0:T(8,128)(2,1)} %maximum_maximum_fusion.mine_ref, bf16[8,512,128]{2,1,0:T(8,128)(2,1)} %collective-permute-done.12.own_ref, ...), custom_call_target="tpu_custom_call", output_to_operand_aliasing={{}: (4, {})} | custom-call | flops 536870912 | bytes 5242880 | tf_op jit(solution)/shard_map/gram/pallas_call | solution.py:47
  298.6 1.0 copy-done.13
  299.6 7.3 %gram.29.outs_0_ = bf16[2,16,128,2048]{3,2,1,0:T(8,128)(2,1)} custom-call(s32[2]{0:T(128)} %pad_add_fusion.2.where, bf16[16,256,512]{2,1,0:T(8,128)(2,1)} %maximum_maximum_fusion.mine_ref, bf16[8,512,128]{2,1,0:T(8,128)(2,1)} %collective-permute-done.9.own_ref, bf16[8,512,128]{2,1,0:T(8,128)(2,1)} %copy-done.13, ...), custom_call_target="tpu_custom_call", output_to_operand_aliasing={{}: (4, {})} | custom-call | flops 536870912 | bytes 5242880 | tf_op jit(solution)/shard_map/gram/pallas_call | solution.py:47
  306.9 7.3 %gram.30.outs_0_ = bf16[2,16,128,2048]{3,2,1,0:T(8,128)(2,1)} custom-call(s32[2]{0:T(128)} %get-tuple-element.12.where, bf16[16,256,512]{2,1,0:T(8,128)(2,1)} %maximum_maximum_fusion.mine_ref, bf16[8,512,128]{2,1,0:T(8,128)(2,1)} %collective-permute-done.6.own_ref, ...), custom_call_target="tpu_custom_call", output_to_operand_aliasing={{}: (4, {})} | custom-call | flops 536870912 | bytes 5242880 | tf_op jit(solution)/shard_map/gram/pallas_call | solution.py:47
  314.2 7.3 %gram.31 = bf16[2,16,128,2048]{3,2,1,0:T(8,128)(2,1)} custom-call(s32[2]{0:T(128)} %get-tuple-element.11.where, bf16[16,256,512]{2,1,0:T(8,128)(2,1)} %maximum_maximum_fusion.mine_ref, bf16[8,512,128]{2,1,0:T(8,128)(2,1)} %collective-permute-done.2.own_ref, bf16[8,512,128]{2,1,0:T(8,128)(2,1)} %collective-permute-done.3.other_ref, ...), custom_call_target="tpu_custom_call", output_to_operand_aliasing={{}: (4, {})} | custom-call | flops 536870912 | bytes 5242880 | tf_op jit(solution)/shard_map/gram/pallas_call | solution.py:47
  (70 shorter events, 2.6 us)
Async XLA Ops:
  13.1 5.8 %copy-start.14 = (s32[128,32]{0,1:T(8,128)S(1)}, s32[128,32]{0,1:T(8,128)}, u32[]{:S(2)}) copy-start(s32[128,32]{0,1:T(8,128)} %param.4) | copy-start | bytes 49156
  63.4 121.3 %copy-start = (bf16[8,2,8,32,128]{4,3,2,1,0:T(8,128)(2,1)}, bf16[8,2,8,32,128]{4,3,2,1,0:T(8,128)(2,1)S(1)}, u32[]{:S(2)}) copy-start(bf16[8,2,8,32,128]{4,3,2,1,0:T(8,128)(2,1)S(1)} %copy.42) | copy-start | bytes 3145732
  63.4 6.8 %collective-permute-start.29 = (bf16[8,512,128]{2,1,0:T(8,128)(2,1)S(1)}, bf16[8,512,128]{2,1,0:T(8,128)(2,1)S(1)}, u32[]{:S(2)}, u32[]{:S(2)}) collective-permute-start(bf16[8,512,128]{2,1,0:T(8,128)(2,1)S(1)} %bitcast.37), channel_id=1, source_target_pairs={{0,8},{8,0},{1,9},{9,1},{2,10},{10,2},{3,11},{11,3},{4,12},{12,4},... | collective-permute-start | bytes 3145736 | tf_op jit(solution)/shard_map/ppermute | solution.py:116
  66.1 49.5 %copy-start.1 = (bf16[8,2,8,32,128]{4,3,2,1,0:T(8,128)(2,1)}, bf16[8,2,8,32,128]{4,3,2,1,0:T(8,128)(2,1)S(1)}, u32[]{:S(2)}) copy-start(bf16[8,2,8,32,128]{4,3,2,1,0:T(8,128)(2,1)S(1)} %copy.41) | copy-start | bytes 3145732
  66.1 4.3 %collective-permute-start.28 = (bf16[8,512,128]{2,1,0:T(8,128)(2,1)S(1)}, bf16[8,512,128]{2,1,0:T(8,128)(2,1)S(1)}, u32[]{:S(2)}, u32[]{:S(2)}) collective-permute-start(bf16[8,512,128]{2,1,0:T(8,128)(2,1)S(1)} %bitcast.42), channel_id=1, source_target_pairs={{0,8},{8,0},{1,9},{9,1},{2,10},{10,2},{3,11},{11,3},{4,12},{12,4},... | collective-permute-start | bytes 3145736 | tf_op jit(solution)/shard_map/ppermute | solution.py:116
  66.2 25.7 %collective-permute-start.4 = (bf16[8,512,128]{2,1,0:T(8,128)(2,1)S(1)}, bf16[8,512,128]{2,1,0:T(8,128)(2,1)}, u32[]{:S(2)}, u32[]{:S(2)}) collective-permute-start(bf16[8,512,128]{2,1,0:T(8,128)(2,1)S(1)} %bitcast.38), channel_id=1, source_target_pairs={{0,32},{32,64},{64,96},{96,0},{1,33},{33,65},{65,97},{97,1},{2,34}... | collective-permute-start | bytes 3145736 | tf_op jit(solution)/shard_map/ppermute | solution.py:102
  67.4 27.0 %collective-permute-start = (bf16[8,512,128]{2,1,0:T(8,128)(2,1)S(1)}, bf16[8,512,128]{2,1,0:T(8,128)(2,1)}, u32[]{:S(2)}, u32[]{:S(2)}) collective-permute-start(bf16[8,512,128]{2,1,0:T(8,128)(2,1)S(1)} %bitcast.43), channel_id=1, source_target_pairs={{0,96},{32,0},{64,32},{96,64},{1,97},{33,1},{65,33},{97,65},{2,98}... | collective-permute-start | bytes 3145736 | tf_op jit(solution)/shard_map/ppermute | solution.py:102
  68.9 45.1 %collective-permute-start.24 = (bf16[8,512,128]{2,1,0:T(8,128)(2,1)S(1)}, bf16[8,512,128]{2,1,0:T(8,128)(2,1)S(1)}, u32[]{:S(2)}, u32[]{:S(2)}) collective-permute-start(bf16[8,512,128]{2,1,0:T(8,128)(2,1)S(1)} %bitcast.39), channel_id=1, source_target_pairs={{0,96},{32,0},{64,32},{96,64},{1,97},{33,1},{65,33},{97,65},{2,98}... | collective-permute-start | bytes 3145736 | tf_op jit(solution)/shard_map/ppermute | solution.py:102
  70.2 47.8 %copy-start.2 = (bf16[8,512,128]{2,1,0:T(8,128)(2,1)}, bf16[8,512,128]{2,1,0:T(8,128)(2,1)S(1)}, u32[]{:S(2)}) copy-start(bf16[8,512,128]{2,1,0:T(8,128)(2,1)S(1)} %collective-permute-done.29.other_ref) | copy-start | bytes 3145732
  70.2 45.3 %collective-permute-start.22 = (bf16[8,512,128]{2,1,0:T(8,128)(2,1)S(1)}, bf16[8,512,128]{2,1,0:T(8,128)(2,1)S(1)}, u32[]{:S(2)}, u32[]{:S(2)}) collective-permute-start(bf16[8,512,128]{2,1,0:T(8,128)(2,1)S(1)} %bitcast.44), channel_id=1, source_target_pairs={{0,32},{32,64},{64,96},{96,0},{1,33},{33,65},{65,97},{97,1},{2,34}... | collective-permute-start | bytes 3145736 | tf_op jit(solution)/shard_map/ppermute | solution.py:102
  70.4 49.7 %copy-start.3 = (bf16[8,512,128]{2,1,0:T(8,128)(2,1)}, bf16[8,512,128]{2,1,0:T(8,128)(2,1)S(1)}, u32[]{:S(2)}) copy-start(bf16[8,512,128]{2,1,0:T(8,128)(2,1)S(1)} %collective-permute-done.28.other_ref) | copy-start | bytes 3145732
  70.4 45.2 %collective-permute-start.11 = (bf16[8,512,128]{2,1,0:T(8,128)(2,1)S(1)}, bf16[8,512,128]{2,1,0:T(8,128)(2,1)}, u32[]{:S(2)}, u32[]{:S(2)}) collective-permute-start(bf16[8,512,128]{2,1,0:T(8,128)(2,1)S(1)} %bitcast.40), channel_id=1, source_target_pairs={{0,16},{16,0},{1,17},{17,1},{2,18},{18,2},{3,19},{19,3},{4,20},{20... | collective-permute-start | bytes 3145736 | tf_op jit(solution)/shard_map/ppermute | solution.py:103
  91.9 26.1 %collective-permute-start.8 = (bf16[8,512,128]{2,1,0:T(8,128)(2,1)S(1)}, bf16[8,512,128]{2,1,0:T(8,128)(2,1)}, u32[]{:S(2)}, u32[]{:S(2)}) collective-permute-start(bf16[8,512,128]{2,1,0:T(8,128)(2,1)S(1)} %bitcast.45), channel_id=1, source_target_pairs={{0,16},{16,0},{1,17},{17,1},{2,18},{18,2},{3,19},{19,3},{4,20},{20... | collective-permute-start | bytes 3145736 | tf_op jit(solution)/shard_map/ppermute | solution.py:103
  94.5 25.6 %collective-permute-start.27 = (bf16[8,512,128]{2,1,0:T(8,128)(2,1)}, bf16[8,512,128]{2,1,0:T(8,128)(2,1)S(1)}, u32[]{:S(2)}, u32[]{:S(2)}) collective-permute-start(bf16[8,512,128]{2,1,0:T(8,128)(2,1)} %collective-permute-done.4.own_ref), channel_id=1, source_target_pairs={{0,8},{8,0},{1,9},{9,1},{2,10},{10,2},{3,11},{11,3},{4,12},{12,4},... | collective-permute-start | bytes 3145736 | tf_op jit(solution)/shard_map/ppermute | solution.py:116
  114.0 6.0 %copy-start.4 = (bf16[8,512,128]{2,1,0:T(8,128)(2,1)}, bf16[8,512,128]{2,1,0:T(8,128)(2,1)S(1)}, u32[]{:S(2)}) copy-start(bf16[8,512,128]{2,1,0:T(8,128)(2,1)S(1)} %collective-permute-done.24.own_ref) | copy-start | bytes 3145732
  114.0 6.2 %collective-permute-start.26 = (bf16[8,512,128]{2,1,0:T(8,128)(2,1)}, bf16[8,512,128]{2,1,0:T(8,128)(2,1)S(1)}, u32[]{:S(2)}, u32[]{:S(2)}) collective-permute-start(bf16[8,512,128]{2,1,0:T(8,128)(2,1)} %collective-permute-done.own_ref), channel_id=1, source_target_pairs={{0,8},{8,0},{1,9},{9,1},{2,10},{10,2},{3,11},{11,3},{4,12},{12,4},... | collective-permute-start | bytes 3145736 | tf_op jit(solution)/shard_map/ppermute | solution.py:116
  115.5 5.3 %copy-start.5 = (bf16[8,512,128]{2,1,0:T(8,128)(2,1)}, bf16[8,512,128]{2,1,0:T(8,128)(2,1)S(1)}, u32[]{:S(2)}) copy-start(bf16[8,512,128]{2,1,0:T(8,128)(2,1)S(1)} %collective-permute-done.22.own_ref) | copy-start | bytes 3145732
  115.5 5.3 %collective-permute-start.25 = (bf16[8,512,128]{2,1,0:T(8,128)(2,1)S(1)}, bf16[8,512,128]{2,1,0:T(8,128)(2,1)S(1)}, u32[]{:S(2)}, u32[]{:S(2)}) collective-permute-start(bf16[8,512,128]{2,1,0:T(8,128)(2,1)S(1)} %collective-permute-done.24.own_ref), channel_id=1, source_target_pairs={{0,8},{8,0},{1,9},{9,1},{2,10},{10,2},{3,11},{11,3},{4,12},{12,4},... | collective-permute-start | bytes 3145736 | tf_op jit(solution)/shard_map/ppermute | solution.py:116
  115.6 7.4 %collective-permute-start.23 = (bf16[8,512,128]{2,1,0:T(8,128)(2,1)S(1)}, bf16[8,512,128]{2,1,0:T(8,128)(2,1)S(1)}, u32[]{:S(2)}, u32[]{:S(2)}) collective-permute-start(bf16[8,512,128]{2,1,0:T(8,128)(2,1)S(1)} %collective-permute-done.22.own_ref), channel_id=1, source_target_pairs={{0,8},{8,0},{1,9},{9,1},{2,10},{10,2},{3,11},{11,3},{4,12},{12,4},... | collective-permute-start | bytes 3145736 | tf_op jit(solution)/shard_map/ppermute | solution.py:116
  118.0 7.7 %collective-permute-start.21 = (bf16[8,512,128]{2,1,0:T(8,128)(2,1)}, bf16[8,512,128]{2,1,0:T(8,128)(2,1)S(1)}, u32[]{:S(2)}, u32[]{:S(2)}) collective-permute-start(bf16[8,512,128]{2,1,0:T(8,128)(2,1)} %collective-permute-done.11.own_ref), channel_id=1, source_target_pairs={{0,8},{8,0},{1,9},{9,1},{2,10},{10,2},{3,11},{11,3},{4,12},{12,4},... | collective-permute-start | bytes 3145736 | tf_op jit(solution)/shard_map/ppermute | solution.py:116
  120.1 2.9 copy-start.6
  120.1 6.3 %collective-permute-start.20 = (bf16[8,512,128]{2,1,0:T(8,128)(2,1)}, bf16[8,512,128]{2,1,0:T(8,128)(2,1)S(1)}, u32[]{:S(2)}, u32[]{:S(2)}) collective-permute-start(bf16[8,512,128]{2,1,0:T(8,128)(2,1)} %collective-permute-done.8.own_ref), channel_id=1, source_target_pairs={{0,8},{8,0},{1,9},{9,1},{2,10},{10,2},{3,11},{11,3},{4,12},{12,4},... | collective-permute-start | bytes 3145736 | tf_op jit(solution)/shard_map/ppermute | solution.py:116
  120.2 5.5 %copy-start.7 = (bf16[8,512,128]{2,1,0:T(8,128)(2,1)}, bf16[8,512,128]{2,1,0:T(8,128)(2,1)S(1)}, u32[]{:S(2)}) copy-start(bf16[8,512,128]{2,1,0:T(8,128)(2,1)S(1)} %collective-permute-done.26.other_ref) | copy-start | bytes 3145732
  120.2 25.9 %collective-permute-start.18 = (bf16[8,512,128]{2,1,0:T(8,128)(2,1)}, bf16[8,512,128]{2,1,0:T(8,128)(2,1)S(1)}, u32[]{:S(2)}, u32[]{:S(2)}) collective-permute-start(bf16[8,512,128]{2,1,0:T(8,128)(2,1)} %collective-permute-done.4.own_ref), channel_id=1, source_target_pairs={{0,32},{32,64},{64,96},{96,0},{1,33},{33,65},{65,97},{97,1},{2,34}... | collective-permute-start | bytes 3145736 | tf_op jit(solution)/shard_map/ppermute | solution.py:102
  120.8 4.9 %copy-start.8 = (bf16[8,512,128]{2,1,0:T(8,128)(2,1)}, bf16[8,512,128]{2,1,0:T(8,128)(2,1)S(1)}, u32[]{:S(2)}) copy-start(bf16[8,512,128]{2,1,0:T(8,128)(2,1)S(1)} %collective-permute-done.25.other_ref) | copy-start | bytes 3145732
  120.8 27.6 %collective-permute-start.16 = (bf16[8,512,128]{2,1,0:T(8,128)(2,1)}, bf16[8,512,128]{2,1,0:T(8,128)(2,1)}, u32[]{:S(2)}, u32[]{:S(2)}) collective-permute-start(bf16[8,512,128]{2,1,0:T(8,128)(2,1)} %collective-permute-done.own_ref), channel_id=1, source_target_pairs={{0,96},{32,0},{64,32},{96,64},{1,97},{33,1},{65,33},{97,65},{2,98}... | collective-permute-start | bytes 3145736 | tf_op jit(solution)/shard_map/ppermute | solution.py:102
  123.0 3.3 %copy-start.9 = (bf16[8,512,128]{2,1,0:T(8,128)(2,1)}, bf16[8,512,128]{2,1,0:T(8,128)(2,1)S(1)}, u32[]{:S(2)}) copy-start(bf16[8,512,128]{2,1,0:T(8,128)(2,1)S(1)} %collective-permute-done.23.other_ref) | copy-start | bytes 3145732
  123.0 26.5 %collective-permute-start.5 = (bf16[8,512,128]{2,1,0:T(8,128)(2,1)}, bf16[8,512,128]{2,1,0:T(8,128)(2,1)}, u32[]{:S(2)}, u32[]{:S(2)}) collective-permute-start(bf16[8,512,128]{2,1,0:T(8,128)(2,1)} %collective-permute-done.4.own_ref), channel_id=1, source_target_pairs={{0,16},{16,0},{1,17},{17,1},{2,18},{18,2},{3,19},{19,3},{4,20},{20... | collective-permute-start | bytes 3145736 | tf_op jit(solution)/shard_map/ppermute | solution.py:103
  125.7 1.0 copy-start.10
  125.7 45.3 %collective-permute-start.1 = (bf16[8,512,128]{2,1,0:T(8,128)(2,1)}, bf16[8,512,128]{2,1,0:T(8,128)(2,1)}, u32[]{:S(2)}, u32[]{:S(2)}) collective-permute-start(bf16[8,512,128]{2,1,0:T(8,128)(2,1)} %collective-permute-done.own_ref), channel_id=1, source_target_pairs={{0,16},{16,0},{1,17},{17,1},{2,18},{18,2},{3,19},{19,3},{4,20},{20... | collective-permute-start | bytes 3145736 | tf_op jit(solution)/shard_map/ppermute | solution.py:103
  126.7 1.3 copy-start.11
  126.7 47.6 %collective-permute-start.12 = (bf16[8,512,128]{2,1,0:T(8,128)(2,1)}, bf16[8,512,128]{2,1,0:T(8,128)(2,1)}, u32[]{:S(2)}, u32[]{:S(2)}) collective-permute-start(bf16[8,512,128]{2,1,0:T(8,128)(2,1)} %collective-permute-done.11.own_ref), channel_id=1, source_target_pairs={{0,96},{32,0},{64,32},{96,64},{1,97},{33,1},{65,33},{97,65},{2,98}... | collective-permute-start | bytes 3145736 | tf_op jit(solution)/shard_map/ppermute | solution.py:102
  146.1 1.0 copy-start.12
  147.1 27.2 %collective-permute-start.9 = (bf16[8,512,128]{2,1,0:T(8,128)(2,1)}, bf16[8,512,128]{2,1,0:T(8,128)(2,1)}, u32[]{:S(2)}, u32[]{:S(2)}) collective-permute-start(bf16[8,512,128]{2,1,0:T(8,128)(2,1)} %collective-permute-done.8.own_ref), channel_id=1, source_target_pairs={{0,32},{32,64},{64,96},{96,0},{1,33},{33,65},{65,97},{97,1},{2,34}... | collective-permute-start | bytes 3145736 | tf_op jit(solution)/shard_map/ppermute | solution.py:102
  148.4 36.6 %collective-permute-start.19 = (bf16[8,512,128]{2,1,0:T(8,128)(2,1)}, bf16[8,512,128]{2,1,0:T(8,128)(2,1)}, u32[]{:S(2)}, u32[]{:S(2)}) collective-permute-start(bf16[8,512,128]{2,1,0:T(8,128)(2,1)} %copy-done.12), channel_id=1, source_target_pairs={{0,8},{8,0},{1,9},{9,1},{2,10},{10,2},{3,11},{11,3},{4,12},{12,4},... | collective-permute-start | bytes 3145736 | tf_op jit(solution)/shard_map/ppermute | solution.py:116
  149.5 36.1 %collective-permute-start.17 = (bf16[8,512,128]{2,1,0:T(8,128)(2,1)}, bf16[8,512,128]{2,1,0:T(8,128)(2,1)}, u32[]{:S(2)}, u32[]{:S(2)}) collective-permute-start(bf16[8,512,128]{2,1,0:T(8,128)(2,1)} %collective-permute-done.16.own_ref), channel_id=1, source_target_pairs={{0,8},{8,0},{1,9},{9,1},{2,10},{10,2},{3,11},{11,3},{4,12},{12,4},... | collective-permute-start | bytes 3145736 | tf_op jit(solution)/shard_map/ppermute | solution.py:116
  171.1 14.7 %collective-permute-start.15 = (bf16[8,512,128]{2,1,0:T(8,128)(2,1)}, bf16[8,512,128]{2,1,0:T(8,128)(2,1)}, u32[]{:S(2)}, u32[]{:S(2)}) collective-permute-start(bf16[8,512,128]{2,1,0:T(8,128)(2,1)} %collective-permute-done.5.own_ref), channel_id=1, source_target_pairs={{0,8},{8,0},{1,9},{9,1},{2,10},{10,2},{3,11},{11,3},{4,12},{12,4},... | collective-permute-start | bytes 3145736 | tf_op jit(solution)/shard_map/ppermute | solution.py:116
  174.3 26.3 %collective-permute-start.6 = (bf16[8,512,128]{2,1,0:T(8,128)(2,1)}, bf16[8,512,128]{2,1,0:T(8,128)(2,1)}, u32[]{:S(2)}, u32[]{:S(2)}) collective-permute-start(bf16[8,512,128]{2,1,0:T(8,128)(2,1)} %collective-permute-done.5.own_ref), channel_id=1, source_target_pairs={{0,32},{32,64},{64,96},{96,0},{1,33},{33,65},{65,97},{97,1},{2,34}... | collective-permute-start | bytes 3145736 | tf_op jit(solution)/shard_map/ppermute | solution.py:102
  174.3 27.1 %collective-permute-start.2 = (bf16[8,512,128]{2,1,0:T(8,128)(2,1)}, bf16[8,512,128]{2,1,0:T(8,128)(2,1)}, u32[]{:S(2)}, u32[]{:S(2)}) collective-permute-start(bf16[8,512,128]{2,1,0:T(8,128)(2,1)} %collective-permute-done.1.own_ref), channel_id=1, source_target_pairs={{0,96},{32,0},{64,32},{96,64},{1,97},{33,1},{65,33},{97,65},{2,98}... | collective-permute-start | bytes 3145736 | tf_op jit(solution)/shard_map/ppermute | solution.py:102
  185.0 99.0 %collective-permute-start.14 = (bf16[8,512,128]{2,1,0:T(8,128)(2,1)}, bf16[8,512,128]{2,1,0:T(8,128)(2,1)}, u32[]{:S(2)}, u32[]{:S(2)}) collective-permute-start(bf16[8,512,128]{2,1,0:T(8,128)(2,1)} %collective-permute-done.1.own_ref), channel_id=1, source_target_pairs={{0,8},{8,0},{1,9},{9,1},{2,10},{10,2},{3,11},{11,3},{4,12},{12,4},... | collective-permute-start | bytes 3145736 | tf_op jit(solution)/shard_map/ppermute | solution.py:116
  185.6 105.7 %collective-permute-start.13 = (bf16[8,512,128]{2,1,0:T(8,128)(2,1)}, bf16[8,512,128]{2,1,0:T(8,128)(2,1)}, u32[]{:S(2)}, u32[]{:S(2)}) collective-permute-start(bf16[8,512,128]{2,1,0:T(8,128)(2,1)} %collective-permute-done.12.own_ref), channel_id=1, source_target_pairs={{0,8},{8,0},{1,9},{9,1},{2,10},{10,2},{3,11},{11,3},{4,12},{12,4},... | collective-permute-start | bytes 3145736 | tf_op jit(solution)/shard_map/ppermute | solution.py:116
  185.7 112.9 %collective-permute-start.10 = (bf16[8,512,128]{2,1,0:T(8,128)(2,1)}, bf16[8,512,128]{2,1,0:T(8,128)(2,1)S(1)}, u32[]{:S(2)}, u32[]{:S(2)}) collective-permute-start(bf16[8,512,128]{2,1,0:T(8,128)(2,1)} %collective-permute-done.9.own_ref), channel_id=1, source_target_pairs={{0,8},{8,0},{1,9},{9,1},{2,10},{10,2},{3,11},{11,3},{4,12},{12,4},... | collective-permute-start | bytes 3145736 | tf_op jit(solution)/shard_map/ppermute | solution.py:116
  200.6 106.3 %collective-permute-start.7 = (bf16[8,512,128]{2,1,0:T(8,128)(2,1)}, bf16[8,512,128]{2,1,0:T(8,128)(2,1)}, u32[]{:S(2)}, u32[]{:S(2)}) collective-permute-start(bf16[8,512,128]{2,1,0:T(8,128)(2,1)} %collective-permute-done.6.own_ref), channel_id=1, source_target_pairs={{0,8},{8,0},{1,9},{9,1},{2,10},{10,2},{3,11},{11,3},{4,12},{12,4},... | collective-permute-start | bytes 3145736 | tf_op jit(solution)/shard_map/ppermute | solution.py:116
  201.4 112.9 %collective-permute-start.3 = (bf16[8,512,128]{2,1,0:T(8,128)(2,1)}, bf16[8,512,128]{2,1,0:T(8,128)(2,1)}, u32[]{:S(2)}, u32[]{:S(2)}) collective-permute-start(bf16[8,512,128]{2,1,0:T(8,128)(2,1)} %collective-permute-done.2.own_ref), channel_id=1, source_target_pairs={{0,8},{8,0},{1,9},{9,1},{2,10},{10,2},{3,11},{11,3},{4,12},{12,4},... | collective-permute-start | bytes 3145736 | tf_op jit(solution)/shard_map/ppermute | solution.py:116
  298.6 1.0 copy-start.13

commit v2 on v1

v2 whole, which is shorter than its diff:
```python
import functools

import jax
import jax.numpy as jnp
import numpy as np
from jax import lax
from jax.experimental import pallas as pl
from jax.experimental.pallas import tpu as pltpu
from jax.sharding import Mesh, PartitionSpec as P

FFT_LEN = 512
BINS = 128
BAND_LO = 16
OWNERS = 8
HALF = 8
SEG_STEP = 8
MIB = 1024 * 1024


def spectra_table():
    sample = np.arange(FFT_LEN)
    bins = (BAND_LO + np.arange(BINS)).reshape(OWNERS, 2, HALF).transpose(1, 0, 2).reshape(-1)
    phase = (sample[:, None] * bins[None, :] % FFT_LEN) * (2.0 * np.pi / FFT_LEN)
    taper = 0.5 - 0.5 * np.cos(2.0 * np.pi * sample / FFT_LEN)
    table = np.stack([np.cos(phase), -np.sin(phase)], axis=2).reshape(FFT_LEN, 2 * BINS) * taper[:, None]
    high = table.astype(jnp.bfloat16)
    low = (table - high.astype(np.float64)).astype(jnp.bfloat16)
    return high, low


def whiten_kernel(records_ref, available_ref, high_ref, low_ref, first_ref, second_ref, rows_ref, turned_ref):
    stations, segs, samples = records_ref.shape
    flat = records_ref[...].reshape(stations * segs, samples)
    spectra = jnp.dot(flat, high_ref[...], preferred_element_type=jnp.float32)
    spectra += jnp.dot(flat, low_ref[...], preferred_element_type=jnp.float32)
    wide = spectra.shape[1]
    for part in range(2):
        rows_ref[part] = spectra[:, part * BINS : (part + 1) * BINS]
    for seg in range(segs):
        turned = jnp.concatenate(
            [rows_ref[part, pl.ds(seg, stations, stride=segs), :].T for part in range(2)], axis=0
        )
        power = jnp.sum(turned * turned, axis=0, keepdims=True) / BINS
        weight = available_ref[seg : seg + 1, :].astype(jnp.float32) / jnp.sqrt(power + 1e-05)
        turned_ref[pl.ds(seg, wide, stride=segs), :] = turned * weight
    whitened = turned_ref[...].reshape(2, OWNERS, HALF, 2, segs, stations).astype(jnp.bfloat16)
    first_ref[...] = whitened[0]
    second_ref[...] = whitened[1]


def whiten(records, available):
    stations, segments, samples = records.shape
    high, low = spectra_table()
    half = jax.ShapeDtypeStruct((OWNERS, HALF, 2, segments, stations), jnp.bfloat16)
    half_spec = pl.BlockSpec((OWNERS, HALF, 2, SEG_STEP, stations), lambda i: (0, 0, 0, i, 0))
    return pl.pallas_call(
        whiten_kernel,
        grid=(segments // SEG_STEP,),
        in_specs=[
            pl.BlockSpec((stations, SEG_STEP, samples), lambda i: (0, i, 0)),
            pl.BlockSpec((SEG_STEP, stations), lambda i: (i, 0)),
            pl.BlockSpec((samples, 2 * BINS), lambda i: (0, 0)),
            pl.BlockSpec((samples, 2 * BINS), lambda i: (0, 0)),
        ],
        out_specs=[half_spec, half_spec],
        out_shape=[half, half],
        scratch_shapes=[
            pltpu.VMEM((2, stations * SEG_STEP, BINS), jnp.float32),
            pltpu.VMEM((2 * BINS * SEG_STEP, stations), jnp.float32),
        ],
        compiler_params=pltpu.CompilerParams(vmem_limit_bytes=32 * MIB),
        name="whiten",
    )(records, available.T, jnp.asarray(high), jnp.asarray(low))


def rows_kernel(panel_ref, mine_ref):
    bins, depth, rows = panel_ref.shape
    half = depth // 2
    for f in range(bins):
        real = panel_ref[f, :half, :].T
        imag = panel_ref[f, half:, :].T
        mine_ref[f, :rows, :half] = real
        mine_ref[f, :rows, half:] = imag
        mine_ref[f, rows:, :half] = imag
        mine_ref[f, rows:, half:] = -real


def rows_of(panel):
    bins, depth, rows = panel.shape
    step = 2
    return pl.pallas_call(
        rows_kernel,
        grid=(bins // step,),
        in_specs=[pl.BlockSpec((step, depth, rows), lambda f: (f, 0, 0))],
        out_specs=pl.BlockSpec((step, 2 * rows, depth), lambda f: (f, 0, 0)),
        out_shape=jax.ShapeDtypeStruct((bins, 2 * rows, depth), panel.dtype),
        compiler_params=pltpu.CompilerParams(vmem_limit_bytes=16 * MIB),
        name="rows",
    )(panel)


def gram_kernel(scale, first, count, where, mine_ref, *refs):
    panels, (out_ref, slots, sems) = refs[: 2 * count], refs[-3:]
    step, steps = pl.program_id(0), pl.num_programs(0)
    bins = mine_ref.shape[0]
    rows, cols = mine_ref.shape[1] // 2, panels[0].shape[2]
    slot = lax.rem(step, 2)

    def write(at, block, held):
        spot = pl.ds(pl.multiple_of(where[block] * 2 * cols, 2 * cols), 2 * cols)
        return pltpu.make_async_copy(
            slots.at[held, block],
            out_ref.at[:, pl.ds(first + at * bins, bins), :, spot],
            sems.at[held, block],
        )

    @pl.when(step >= 2)
    def _():
        for block in range(count):
            write(step - 2, block, slot).wait()

    own = pl.ds(pl.multiple_of(where[count] * cols, cols), cols)
    other = pl.ds(pl.multiple_of((1 - where[count]) * cols, cols), cols)
    for block in range(count):
        for f in range(bins):
            panel = jnp.concatenate([panels[2 * block][f], panels[2 * block + 1][f]], axis=1)
            gram = jnp.dot(mine_ref[f], panel, preferred_element_type=jnp.float32) * scale
            gram = gram.astype(jnp.bfloat16)
            slots[slot, block, 0, f, :, own] = gram[:rows, :cols]
            slots[slot, block, 1, f, :, own] = gram[rows:, :cols]
            slots[slot, block, 0, f, :, other] = gram[:rows, cols:]
            slots[slot, block, 1, f, :, other] = gram[rows:, cols:]
        write(step, block, slot).start()

    @pl.when(step == steps - 1)
    def _():
        for block in range(count):
            write(step - 1, block, 1 - slot).wait()
            write(step, block, slot).wait()


def gram(first, core, mine, blocks, shape, out):
    bins, depth, cols = blocks[0][1].shape
    rows = mine.shape[1] // 2
    count, step = len(blocks), 2
    where = jnp.stack([chip for chip, _, _ in blocks] + [core]).astype(jnp.int32)
    held = [] if out is None else [out]
    panels = [v for _, own, other in blocks for v in (own, other)]
    return pl.pallas_call(
        functools.partial(gram_kernel, 2.0 / depth, first, count),
        grid_spec=pltpu.PrefetchScalarGridSpec(
            num_scalar_prefetch=1,
            grid=(bins // step,),
            in_specs=[pl.BlockSpec((step, 2 * rows, depth), lambda f, w: (f, 0, 0))]
            + [pl.BlockSpec((step, depth, cols), lambda f, w: (f, 0, 0))] * (2 * count)
            + [pl.BlockSpec(memory_space=pl.ANY)] * len(held),
            out_specs=pl.BlockSpec(memory_space=pl.ANY),
            scratch_shapes=[
                pltpu.VMEM((2, count, 2, step, rows, 2 * cols), jnp.bfloat16),
                pltpu.SemaphoreType.DMA((2, count)),
            ],
        ),
        out_shape=jax.ShapeDtypeStruct(shape, jnp.bfloat16),
        input_output_aliases={2 + 2 * count: 0} if held else {},
        cost_estimate=pl.CostEstimate(
            flops=16 * count * bins * rows * depth * cols,
            bytes_accessed=2 * bins * (2 * rows * depth + count * (2 * depth * cols + 4 * rows * cols)),
            transcendentals=0,
        ),
        compiler_params=pltpu.CompilerParams(vmem_limit_bytes=16 * MIB),
        name="gram",
    )(where, mine, *panels, *held)


def after(value, *others):
    return lax.optimization_barrier((value, *others))[0]


def ring(size, step):
    return [(i, (i + step) % size) for i in range(size)]


def shards(records, available):
    stations = records.shape[0]
    x, yh, core = lax.axis_index("x"), lax.axis_index("yh"), lax.axis_index("core")
    right = lambda v: lax.ppermute(v, "x", ring(4, 1))
    left = lambda v: lax.ppermute(v, "x", ring(4, -1))
    over = lambda v: lax.ppermute(v, "yh", ring(2, 1))
    swap = lambda v: lax.ppermute(v, "core", ring(2, 1))

    def owned(half):
        got = lax.all_to_all(half, ("yl", "z"), split_axis=0, concat_axis=0, tiled=True)
        got = jnp.transpose(got, (1, 2, 0, 3, 4))
        return got.reshape(HALF, -1, stations)

    def entry(dx, dy, own):
        chip = (x - dx) % 4 * 2 + (yh + dy) % 2
        return chip, own, swap(own)

    first, second = whiten(records, available)
    shape = (2, 2 * HALF, stations, 16 * stations)
    p0 = owned(first)
    a0, b0, c0 = right(p0), left(p0), over(p0)
    m0 = rows_of(p0)
    p1 = owned(after(second, p0))
    e_p0 = entry(0, 0, p0)
    b1, a1, c1 = right(after(p1, a0)), left(after(p1, b0)), over(after(p1, c0))
    m1 = rows_of(p1)
    e_p1 = entry(0, 0, p1)
    out = gram(0, core, m0, [e_p0], shape, None)
    out = gram(HALF, core, m1, [e_p1], shape, out)
    e0 = [entry(1, 0, a0), entry(-1, 0, b0), entry(0, 1, c0)]
    d0, g0, f0 = right(after(a0, b1)), left(after(c0, a1)), over(after(a0, c1))
    out = gram(0, core, m0, e0, shape, out)
    e1 = [entry(-1, 0, a1), entry(1, 0, b1), entry(0, 1, c1)]
    g1, d1, f1 = right(after(c1, d0, out)), left(after(a1, g0, out)), over(after(a1, f0, out))
    out = gram(HALF, core, m1, e1, shape, out)
    e0 = [entry(2, 0, d0), entry(-1, 1, g0), entry(1, 1, f0)]
    h0, h1 = right(after(f0, g1, out)), left(after(f1, d1, out))
    out = gram(0, core, m0, e0, shape, out)
    e1 = [entry(-2, 0, d1), entry(1, 1, g1), entry(-1, 1, f1)]
    out = gram(HALF, core, m1, e1, shape, out)
    out = gram(0, core, m0, [entry(2, 1, after(h0, out))], shape, out)
    out = gram(HALF, core, m1, [entry(-2, 1, h1)], shape, out)
    return out


def solution(mesh):
    fine = Mesh(mesh.devices.reshape(4, 2, 2, 2, 4), ("x", "yh", "core", "yl", "z"))
    sta, freq = ("x", "yh", "core"), ("yl", "z")
    return jax.shard_map(
        shards,
        mesh=fine,
        in_specs=(P(sta, freq, None), P(sta, freq)),
        out_specs=P(None, freq, sta, None),
        check_vma=False,
    )
```

time: 324 us -> 201 us (0.62)
  Pallas kernels: 117 us -> 49.2 us
  waiting for transfers between devices: 89.6 us -> 51.3 us
  starting transfers between devices: 36.1 us -> 54.8 us
  other arithmetic: 18 us -> 0.45 us
  blocking collectives: 32.6 us -> 21 us
  matrix products: 4.76 us -> 0 us
    pallas_call x16 -> x11, Pallas kernels: 117 us -> 49.2 us  [the longest x8 41.4 us: gram(): pl.pallas_call(functools.partial(gram_kernel, 2.0 / depth, first, count),...]
    ppermute x30, waiting for transfers between devices: 89.6 us -> 47.6 us  [the longest x4 23.8 us: shards(): over = lambda v: lax.ppermute(v, 'yh', ring(2, 1))]
    unnamed x31 -> x54, local copies, waits for them, and re-layouts: 2.45 us -> 22.3 us
    ppermute x30, starting transfers between devices: 36.1 us -> 51.3 us  [the longest x16 33.7 us: shards(): swap = lambda v: lax.ppermute(v, 'core', ring(2, 1))]
    all_to_all x1, blocking collectives: 32.6 us -> 21 us  [owned(): lax.all_to_all(half, ('yl', 'z'), split_axis=0, concat_axis=0, tiled=True)]
    transpose x1 -> x0, other arithmetic: 7.37 us -> none  [shards(): whitened = jnp.transpose(whitened, (3, 2, 1, 0))]
    reshape x1 -> x0, local copies, waits for them, and re-layouts: 5.76 us -> none  [shards(): spectra = spectra.reshape(stations, segments, 2 * BINS)]
    add x1 -> x0, local copies, waits for them, and re-layouts: 5.61 us -> none  [shards(): spectra = spectra[:, :2 * BINS] + spectra[:, 2 * BINS:]]
  transfers between devices with their start and end apart: 30 -> 31, of which waited for: 6 -> 9; matrix products, arithmetic and copies ran while one was open for 4% -> 0% of each run, Pallas kernels for 34% -> 19%
where the time goes in v2:
time: 201 us; the launch traced here: 200 us
  starting transfers between devices  54.8 us (27%)
  waiting for transfers between devices  51.3 us (26%)
  Pallas kernels  49.2 us (24%)
  local copies, waits for them, and re-layouts  22.5 us (11%)
  blocking collectives  21 us (10%)
    pallas_call x8, Pallas kernels, gram(): pl.pallas_call(functools.partial(gram_kernel, 2.0 / depth, first, count),...  41.4 us
    ppermute x16, starting transfers between devices, shards(): swap = lambda v: lax.ppermute(v, 'core', ring(2, 1))  33.7 us
    ppermute x4, waiting for transfers between devices, shards(): over = lambda v: lax.ppermute(v, 'yh', ring(2, 1))  23.8 us
    unnamed x54, local copies, waits for them, and re-layouts  22.3 us
    all_to_all x1, blocking collectives, owned(): lax.all_to_all(half, ('yl', 'z'), split_axis=0, concat_axis=0, tiled=True)  21 us
    ppermute x5, waiting for transfers between devices, shards(): right = lambda v: lax.ppermute(v, 'x', ring(4, 1))  18.6 us
    ppermute x5, starting transfers between devices, shards(): left = lambda v: lax.ppermute(v, 'x', ring(4, -1))  9.33 us
    pallas_call x1, Pallas kernels, whiten(): pl.pallas_call(whiten_kernel, grid=(segments // SEG_STEP,), in_specs=[pl....  6.77 us
  transfers between devices with their start and end apart: 31, of which 9 were waited for; matrix products, arithmetic and copies ran while one was open for 0% of the time, Pallas kernels for 19%

profile of v2, /device:TPU:1, one launch (start us, length us, event | category | flops | bytes accessed | tf_op | source)
XLA Modules:
  0.0 199.6 jit_solution(10456024300865809735)
XLA Ops:
  0.0 2.2 %copy-done.5 = bf16[128,32,512]{2,1,0:T(8,128)(2,1)S(1)} copy-done((bf16[128,32,512]{2,1,0:T(8,128)(2,1)S(1)}, bf16[128,32,512]{2,1,0:T(8,128)(2,1)}, u32[]{:S(2)}) %copy-start.5) | copy-done | bytes 4194328
  2.2 0.9 copy-done.24
  3.1 0.9 copy-done.25
  4.1 0.7 copy-done.26
  4.8 6.8 %whiten.1 = (bf16[8,8,2,32,128]{4,3,2,1,0:T(8,128)(2,1)S(1)}, bf16[8,8,2,32,128]{4,3,2,1,0:T(8,128)(2,1)}) custom-call(bf16[128,32,512]{2,1,0:T(8,128)(2,1)S(1)} %copy-done.5, s32[32,128]{1,0:T(8,128)S(1)} %bitcast.28, bf16[512,256]{1,0:T(8,128)(2,1)S(1)} %copy-done.24, bf16[512,256]{1,0:T(8,128)(2,1)S(1)} %copy-done.25), custom_call_target="tpu_custom_call" | custom-call | tf_op jit(solution)/shard_map/whiten/pallas_call | solution.py:56
  11.6 21.0 %all_to_all.10 = bf16[8,8,2,32,128]{4,3,2,1,0:T(8,128)(2,1)S(1)} all-to-all(bf16[8,8,2,32,128]{4,3,2,1,0:T(8,128)(2,1)S(1)} %get-tuple-element.21), channel_id=1, replica_groups=mesh['x'=4,'yh'=2,'core'=2,'yl'=2,'z'=4] {'yl','z'}, dimensions={0} | all-to-all | bytes 2097152 | tf_op jit(solution)/shard_map/all_to_all | solution.py:192
  32.6 1.3 collective-permute-start.2
  33.9 3.6 %all-to-all-start.1 = ((bf16[8,8,2,32,128]{4,3,2,1,0:T(8,128)(2,1)}), bf16[8,8,2,32,128]{4,3,2,1,0:T(8,128)(2,1)S(1)}, u32[]{:S(2)}, u32[]{:S(2)}) async-start(bf16[8,8,2,32,128]{4,3,2,1,0:T(8,128)(2,1)} %get-tuple-element.22), calls=%async_computation.1 | async-start | bytes 2097152 | tf_op jit(solution)/shard_map/all_to_all | solution.py:192
  37.5 1.5 collective-permute-start
  39.0 2.6 %collective-permute-start.3 = (bf16[8,512,128]{2,1,0:T(8,128)(2,1)S(1)}, bf16[8,512,128]{2,1,0:T(8,128)(2,1)}, u32[]{:S(2)}, u32[]{:S(2)}) collective-permute-start(bf16[8,512,128]{2,1,0:T(8,128)(2,1)S(1)} %bitcast.18), channel_id=1, source_target_pairs={{0,16},{16,0},{1,17},{17,1},{2,18},{18,2},{3,19},{19,3},{4,20},{20... | collective-permute-start | bytes 3145736 | tf_op jit(solution)/shard_map/ppermute | solution.py:188
  41.7 3.3 %collective-permute-start.10 = (bf16[8,512,128]{2,1,0:T(8,128)(2,1)S(1)}, bf16[8,512,128]{2,1,0:T(8,128)(2,1)S(1)}, u32[]{:S(2)}, u32[]{:S(2)}) collective-permute-start(bf16[8,512,128]{2,1,0:T(8,128)(2,1)S(1)} %bitcast.19), channel_id=1, source_target_pairs={{0,8},{8,0},{1,9},{9,1},{2,10},{10,2},{3,11},{11,3},{4,12},{12,4},... | collective-permute-start | bytes 3145736 | tf_op jit(solution)/shard_map/ppermute | solution.py:189
  44.9 3.7 %all-to-all-done.1 = bf16[8,8,2,32,128]{4,3,2,1,0:T(8,128)(2,1)S(1)} async-done(((bf16[8,8,2,32,128]{4,3,2,1,0:T(8,128)(2,1)}), bf16[8,8,2,32,128]{4,3,2,1,0:T(8,128)(2,1)S(1)}, u32[]{:S(2)}, u32[]{:S(2)}) %all-to-all-start.1) | async-done | bytes 1048608 | tf_op jit(solution)/shard_map/all_to_all | solution.py:192
  48.7 6.7 %collective-permute-start.9 = (bf16[8,512,128]{2,1,0:T(8,128)(2,1)S(1)}, bf16[8,512,128]{2,1,0:T(8,128)(2,1)S(1)}, u32[]{:S(2)}, u32[]{:S(2)}) collective-permute-start(bf16[8,512,128]{2,1,0:T(8,128)(2,1)S(1)} %bitcast.22), channel_id=1, source_target_pairs={{0,8},{8,0},{1,9},{9,1},{2,10},{10,2},{3,11},{11,3},{4,12},{12,4},... | collective-permute-start | bytes 3145736 | tf_op jit(solution)/shard_map/ppermute | solution.py:189
  55.4 0.9 collective-permute-done.2.refs_0_
  56.2 0.3 collective-permute-start.15
  56.6 3.0 %collective-permute-done.refs_2_ = bf16[8,512,128]{2,1,0:T(8,128)(2,1)} collective-permute-done((bf16[8,512,128]{2,1,0:T(8,128)(2,1)S(1)}, bf16[8,512,128]{2,1,0:T(8,128)(2,1)}, u32[]{:S(2)}, u32[]{:S(2)}) %collective-permute-start) | collective-permute-done | bytes 1048608 | tf_op jit(solution)/shard_map/ppermute | solution.py:187
  59.6 2.7 %collective-permute-start.1 = (bf16[8,512,128]{2,1,0:T(8,128)(2,1)S(1)}, bf16[8,512,128]{2,1,0:T(8,128)(2,1)S(1)}, u32[]{:S(2)}, u32[]{:S(2)}) collective-permute-start(bf16[8,512,128]{2,1,0:T(8,128)(2,1)S(1)} %bitcast.24), channel_id=1, source_target_pairs={{0,96},{32,0},{64,32},{96,64},{1,97},{33,1},{65,33},{97,65},{2,98}... | collective-permute-start | bytes 3145736 | tf_op jit(solution)/shard_map/ppermute | solution.py:187
  62.3 10.2 %collective-permute-done.3.refs_4_ = bf16[8,512,128]{2,1,0:T(8,128)(2,1)} collective-permute-done((bf16[8,512,128]{2,1,0:T(8,128)(2,1)S(1)}, bf16[8,512,128]{2,1,0:T(8,128)(2,1)}, u32[]{:S(2)}, u32[]{:S(2)}) %collective-permute-start.3) | collective-permute-done | bytes 1048608 | tf_op jit(solution)/shard_map/ppermute | solution.py:188
  72.5 0.3 collective-permute-start.4
  72.9 1.0 copy-done.3
  73.8 1.0 copy-done.12
  74.8 3.6 %collective-permute-start.6 = (bf16[8,512,128]{2,1,0:T(8,128)(2,1)}, bf16[8,512,128]{2,1,0:T(8,128)(2,1)}, u32[]{:S(2)}, u32[]{:S(2)}) collective-permute-start(bf16[8,512,128]{2,1,0:T(8,128)(2,1)} %collective-permute-done.2.refs_0_), channel_id=1, source_target_pairs={{0,8},{8,0},{1,9},{9,1},{2,10},{10,2},{3,11},{11,3},{4,12},{12,4},... | collective-permute-start | bytes 3145736 | tf_op jit(solution)/shard_map/ppermute | solution.py:189
  78.4 1.0 copy-done.14
  79.4 3.6 %collective-permute-start.7 = (bf16[8,512,128]{2,1,0:T(8,128)(2,1)}, bf16[8,512,128]{2,1,0:T(8,128)(2,1)}, u32[]{:S(2)}, u32[]{:S(2)}) collective-permute-start(bf16[8,512,128]{2,1,0:T(8,128)(2,1)} %collective-permute-done.refs_2_), channel_id=1, source_target_pairs={{0,8},{8,0},{1,9},{9,1},{2,10},{10,2},{3,11},{11,3},{4,12},{12,4},... | collective-permute-start | bytes 3145736 | tf_op jit(solution)/shard_map/ppermute | solution.py:189
  83.0 12.3 %collective-permute-done.4.refs_4_ = bf16[8,512,128]{2,1,0:T(8,128)(2,1)S(1)} collective-permute-done((bf16[8,512,128]{2,1,0:T(8,128)(2,1)S(1)}, bf16[8,512,128]{2,1,0:T(8,128)(2,1)S(1)}, u32[]{:S(2)}, u32[]{:S(2)}) %collective-permute-start.4) | collective-permute-done | bytes 1048608 | tf_op jit(solution)/shard_map/ppermute | solution.py:188
  95.4 1.5 collective-permute-start.12
  97.0 0.5 rows.3.mine_ref
  97.5 1.2 copy-done.4
  98.8 0.5 rows.2.mine_ref
  99.3 0.4 collective-permute-start.5
  99.7 4.8 %collective-permute-start.14 = (bf16[8,512,128]{2,1,0:T(8,128)(2,1)}, bf16[8,512,128]{2,1,0:T(8,128)(2,1)S(1)}, u32[]{:S(2)}, u32[]{:S(2)}) collective-permute-start(bf16[8,512,128]{2,1,0:T(8,128)(2,1)} %copy-done.8), channel_id=1, source_target_pairs={{0,8},{8,0},{1,9},{9,1},{2,10},{10,2},{3,11},{11,3},{4,12},{12,4},... | collective-permute-start | bytes 3145736 | tf_op jit(solution)/shard_map/ppermute | solution.py:189
  104.6 1.2 copy-done.13
  105.8 3.0 %gram.8.refs_2_ = bf16[2,16,128,2048]{3,2,1,0:T(8,128)(2,1)} custom-call(s32[2]{0:T(128)S(1)} %pad_add_fusion.1.where, bf16[8,256,512]{2,1,0:T(8,128)(2,1)S(1)} %rows.3.mine_ref, bf16[8,512,128]{2,1,0:T(8,128)(2,1)S(1)} %bitcast.21, bf16[8,512,128]{2,1,0:T(8,128)(2,1)S(1)} %copy-done.13), custom_call_target="tpu_custom_call" | custom-call | flops 1073741824 | bytes 5242880 | tf_op jit(solution)/shard_map/gram/pallas_call | solution.py:149
  108.8 3.0 %gram.9.refs_6_ = bf16[2,16,128,2048]{3,2,1,0:T(8,128)(2,1)} custom-call(s32[2]{0:T(128)S(1)} %pad_add_fusion.1.where, bf16[8,256,512]{2,1,0:T(8,128)(2,1)S(1)} %rows.2.mine_ref, bf16[8,512,128]{2,1,0:T(8,128)(2,1)S(1)} %bitcast.27, bf16[8,512,128]{2,1,0:T(8,128)(2,1)S(1)} %copy-done.15, ...), custom_call_target="tpu_custom_call", output_to_operand_aliasing={{}: (4, {})} | custom-call | flops 1073741824 | bytes 5242880 | tf_op jit(solution)/shard_map/gram/pallas_call | solution.py:149
  111.9 0.5 collective-permute-start.17
  112.4 7.2 %gram.10.refs_6_ = bf16[2,16,128,2048]{3,2,1,0:T(8,128)(2,1)} custom-call(s32[4]{0:T(128)S(1)} %add_add_fusion.where, bf16[8,256,512]{2,1,0:T(8,128)(2,1)S(1)} %rows.3.mine_ref, bf16[8,512,128]{2,1,0:T(8,128)(2,1)} %collective-permute-done.2.refs_0_, bf16[8,512,128]{2,1,0:T(8,128)(2,1)} %collective-permute-done.6.refs_1_, ...), custom_call_target="tpu_custom_call", output_to_operand_aliasing={{}: (8, {})} | custom-call | flops 3221225472 | bytes 11534336 | tf_op jit(solution)/shard_map/gram/pallas_call | solution.py:149
  119.6 0.5 collective-permute-start.21
  120.1 1.2 collective-permute-done.5.refs_4_
  121.4 1.2 collective-permute-start.13
  122.6 2.4 %collective-permute-start.11 = (bf16[8,512,128]{2,1,0:T(8,128)(2,1)S(1)}, bf16[8,512,128]{2,1,0:T(8,128)(2,1)}, u32[]{:S(2)}, u32[]{:S(2)}) collective-permute-start(bf16[8,512,128]{2,1,0:T(8,128)(2,1)S(1)} %copy-done.9), channel_id=1, source_target_pairs={{0,16},{16,0},{1,17},{17,1},{2,18},{18,2},{3,19},{19,3},{4,20},{20... | collective-permute-start | bytes 3145736 | tf_op jit(solution)/shard_map/ppermute | solution.py:188
  125.0 3.9 %collective-permute-start.28 = (bf16[8,512,128]{2,1,0:T(8,128)(2,1)}, bf16[8,512,128]{2,1,0:T(8,128)(2,1)S(1)}, u32[]{:S(2)}, u32[]{:S(2)}) collective-permute-start(bf16[8,512,128]{2,1,0:T(8,128)(2,1)} %collective-permute-done.5.refs_4_), channel_id=1, source_target_pairs={{0,8},{8,0},{1,9},{9,1},{2,10},{10,2},{3,11},{11,3},{4,12},{12,4},... | collective-permute-start | bytes 3145736 | tf_op jit(solution)/shard_map/ppermute | solution.py:189
  129.0 15.0 %collective-permute-done.21.refs_2_ = bf16[8,512,128]{2,1,0:T(8,128)(2,1)} collective-permute-done((bf16[8,512,128]{2,1,0:T(8,128)(2,1)S(1)}, bf16[8,512,128]{2,1,0:T(8,128)(2,1)}, u32[]{:S(2)}, u32[]{:S(2)}) %collective-permute-start.21) | collective-permute-done | bytes 1048608 | tf_op jit(solution)/shard_map/ppermute | solution.py:186
  144.1 2.5 %collective-permute-start.27 = (bf16[8,512,128]{2,1,0:T(8,128)(2,1)}, bf16[8,512,128]{2,1,0:T(8,128)(2,1)S(1)}, u32[]{:S(2)}, u32[]{:S(2)}) collective-permute-start(bf16[8,512,128]{2,1,0:T(8,128)(2,1)} %collective-permute-done.12.refs_2_), channel_id=1, source_target_pairs={{0,8},{8,0},{1,9},{9,1},{2,10},{10,2},{3,11},{11,3},{4,12},{12,4},... | collective-permute-start | bytes 3145736 | tf_op jit(solution)/shard_map/ppermute | solution.py:189
  146.7 0.4 collective-permute-start.23
  147.0 2.7 %collective-permute-start.25 = (bf16[8,512,128]{2,1,0:T(8,128)(2,1)}, bf16[8,512,128]{2,1,0:T(8,128)(2,1)}, u32[]{:S(2)}, u32[]{:S(2)}) collective-permute-start(bf16[8,512,128]{2,1,0:T(8,128)(2,1)} %collective-permute-done.11.refs_4_), channel_id=1, source_target_pairs={{0,8},{8,0},{1,9},{9,1},{2,10},{10,2},{3,11},{11,3},{4,12},{12,4},... | collective-permute-start | bytes 3145736 | tf_op jit(solution)/shard_map/ppermute | solution.py:189
  149.8 1.0 copy-done.16
  150.8 5.5 %gram.11.refs_6_ = bf16[2,16,128,2048]{3,2,1,0:T(8,128)(2,1)} custom-call(s32[4]{0:T(128)S(1)} %add_add_fusion.1.where, bf16[8,256,512]{2,1,0:T(8,128)(2,1)S(1)} %rows.2.mine_ref, bf16[8,512,128]{2,1,0:T(8,128)(2,1)S(1)} %copy-done.9, bf16[8,512,128]{2,1,0:T(8,128)(2,1)S(1)} %collective-permute-done.14.refs_1_, ...), custom_call_target="tpu_custom_call", output_to_operand_aliasing={{}: (8, {})} | custom-call | flops 3221225472 | bytes 11534336 | tf_op jit(solution)/shard_map/gram/pallas_call | solution.py:149
  156.3 1.0 copy-done.18
  157.5 1.0 copy-done.20
  158.5 2.4 %collective-permute-start.18 = (bf16[8,512,128]{2,1,0:T(8,128)(2,1)}, bf16[8,512,128]{2,1,0:T(8,128)(2,1)}, u32[]{:S(2)}, u32[]{:S(2)}) collective-permute-start(bf16[8,512,128]{2,1,0:T(8,128)(2,1)} %collective-permute-done.11.refs_4_), channel_id=1, source_target_pairs={{0,96},{32,0},{64,32},{96,64},{1,97},{33,1},{65,33},{97,65},{2,98}... | collective-permute-start | bytes 3145736 | tf_op jit(solution)/shard_map/ppermute | solution.py:187
  161.1 1.6 copy-done.1
  162.7 1.2 copy-done.17
  163.9 1.2 copy-done.19
  165.1 1.2 copy-done.21
  166.3 6.7 %gram.12.refs_6_ = bf16[2,16,128,2048]{3,2,1,0:T(8,128)(2,1)} custom-call(s32[4]{0:T(128)S(1)} %add_add_fusion.3.where, bf16[8,256,512]{2,1,0:T(8,128)(2,1)S(1)} %copy-done.1, bf16[8,512,128]{2,1,0:T(8,128)(2,1)} %collective-permute-done.20.refs_0_, bf16[8,512,128]{2,1,0:T(8,128)(2,1)S(1)} %copy-done.19, ...), custom_call_target="tpu_custom_call", output_to_operand_aliasing={{}: (8, {})} | custom-call | flops 3221225472 | bytes 11534336 | tf_op jit(solution)/shard_map/gram/pallas_call | solution.py:149
  173.1 7.2 %gram.13.refs_2_ = bf16[2,16,128,2048]{3,2,1,0:T(8,128)(2,1)} custom-call(s32[4]{0:T(128)S(1)} %add_add_fusion.2.where, bf16[8,256,512]{2,1,0:T(8,128)(2,1)S(1)} %rows.2.mine_ref, bf16[8,512,128]{2,1,0:T(8,128)(2,1)} %collective-permute-done.13.refs_0_, bf16[8,512,128]{2,1,0:T(8,128)(2,1)} %collective-permute-done.23.refs_1_, ...), custom_call_target="tpu_custom_call", output_to_operand_aliasing={{}: (8, {})} | custom-call | flops 3221225472 | bytes 11534336 | tf_op jit(solution)/shard_map/gram/pallas_call | solution.py:149
  180.3 2.7 %collective-permute-done.22.refs_0_ = bf16[8,512,128]{2,1,0:T(8,128)(2,1)} collective-permute-done((bf16[8,512,128]{2,1,0:T(8,128)(2,1)}, bf16[8,512,128]{2,1,0:T(8,128)(2,1)}, u32[]{:S(2)}, u32[]{:S(2)}) %collective-permute-start.22) | collective-permute-done | bytes 1048608 | tf_op jit(solution)/shard_map/ppermute | solution.py:186
  183.0 1.4 collective-permute-start.29
  184.7 2.2 %collective-permute-done.29.refs_1_ = bf16[8,512,128]{2,1,0:T(8,128)(2,1)S(1)} collective-permute-done((bf16[8,512,128]{2,1,0:T(8,128)(2,1)}, bf16[8,512,128]{2,1,0:T(8,128)(2,1)S(1)}, u32[]{:S(2)}, u32[]{:S(2)}) %collective-permute-start.29) | collective-permute-done | bytes 1048608 | tf_op jit(solution)/shard_map/ppermute | solution.py:189
  186.9 1.0 copy-done.22
  187.8 1.6 copy-done.2
  189.4 1.2 copy-done.23
  190.7 4.3 %gram.14.refs_2_ = bf16[2,16,128,2048]{3,2,1,0:T(8,128)(2,1)} custom-call(s32[2]{0:T(128)S(1)} %get-tuple-element.36.where, bf16[8,256,512]{2,1,0:T(8,128)(2,1)S(1)} %copy-done.2, bf16[8,512,128]{2,1,0:T(8,128)(2,1)} %collective-permute-done.22.refs_0_, bf16[8,512,128]{2,1,0:T(8,128)(2,1)S(1)} %copy-done.23, ...), custom_call_target="tpu_custom_call", output_to_operand_aliasing={{}: (4, {})} | custom-call | flops 1073741824 | bytes 5242880 | tf_op jit(solution)/shard_map/gram/pallas_call | solution.py:149
  195.0 4.5 %gram.15 = bf16[2,16,128,2048]{3,2,1,0:T(8,128)(2,1)} custom-call(s32[2]{0:T(128)S(1)} %get-tuple-element.35.where, bf16[8,256,512]{2,1,0:T(8,128)(2,1)S(1)} %rows.2.mine_ref, bf16[8,512,128]{2,1,0:T(8,128)(2,1)} %collective-permute-done.18.refs_0_, bf16[8,512,128]{2,1,0:T(8,128)(2,1)} %collective-permute-done.19.refs_1_, ...), custom_call_target="tpu_custom_call", output_to_operand_aliasing={{}: (4, {})} | custom-call | flops 1073741824 | bytes 5242880 | tf_op jit(solution)/shard_map/gram/pallas_call | solution.py:149
  (72 shorter events, 1.5 us)
Async XLA Ops:
  0.0 2.2 %copy-start.5 = (bf16[128,32,512]{2,1,0:T(8,128)(2,1)S(1)}, bf16[128,32,512]{2,1,0:T(8,128)(2,1)}, u32[]{:S(2)}) copy-start(bf16[128,32,512]{2,1,0:T(8,128)(2,1)} %records_ref.1) | copy-start | bytes 12582916
  2.2 0.9 copy-start.24
  3.1 0.9 copy-start.25
  4.1 0.7 copy-start.26
  32.6 23.6 %collective-permute-start.2 = (bf16[8,512,128]{2,1,0:T(8,128)(2,1)S(1)}, bf16[8,512,128]{2,1,0:T(8,128)(2,1)}, u32[]{:S(2)}, u32[]{:S(2)}) collective-permute-start(bf16[8,512,128]{2,1,0:T(8,128)(2,1)S(1)} %bitcast.16), channel_id=1, source_target_pairs={{0,32},{32,64},{64,96},{96,0},{1,33},{33,65},{65,97},{97,1},{2,34}... | collective-permute-start | bytes 3145736 | tf_op jit(solution)/shard_map/ppermute | solution.py:186
  33.9 14.7 %all-to-all-start.1 = ((bf16[8,8,2,32,128]{4,3,2,1,0:T(8,128)(2,1)}), bf16[8,8,2,32,128]{4,3,2,1,0:T(8,128)(2,1)S(1)}, u32[]{:S(2)}, u32[]{:S(2)}) async-start(bf16[8,8,2,32,128]{4,3,2,1,0:T(8,128)(2,1)} %get-tuple-element.22), calls=%async_computation.1 | async-start | bytes 2097152 | tf_op jit(solution)/shard_map/all_to_all | solution.py:192
  37.5 22.1 %collective-permute-start = (bf16[8,512,128]{2,1,0:T(8,128)(2,1)S(1)}, bf16[8,512,128]{2,1,0:T(8,128)(2,1)}, u32[]{:S(2)}, u32[]{:S(2)}) collective-permute-start(bf16[8,512,128]{2,1,0:T(8,128)(2,1)S(1)} %bitcast.17), channel_id=1, source_target_pairs={{0,96},{32,0},{64,32},{96,64},{1,97},{33,1},{65,33},{97,65},{2,98}... | collective-permute-start | bytes 3145736 | tf_op jit(solution)/shard_map/ppermute | solution.py:187
  39.0 33.5 %collective-permute-start.3 = (bf16[8,512,128]{2,1,0:T(8,128)(2,1)S(1)}, bf16[8,512,128]{2,1,0:T(8,128)(2,1)}, u32[]{:S(2)}, u32[]{:S(2)}) collective-permute-start(bf16[8,512,128]{2,1,0:T(8,128)(2,1)S(1)} %bitcast.18), channel_id=1, source_target_pairs={{0,16},{16,0},{1,17},{17,1},{2,18},{18,2},{3,19},{19,3},{4,20},{20... | collective-permute-start | bytes 3145736 | tf_op jit(solution)/shard_map/ppermute | solution.py:188
  41.7 32.2 %collective-permute-start.10 = (bf16[8,512,128]{2,1,0:T(8,128)(2,1)S(1)}, bf16[8,512,128]{2,1,0:T(8,128)(2,1)S(1)}, u32[]{:S(2)}, u32[]{:S(2)}) collective-permute-start(bf16[8,512,128]{2,1,0:T(8,128)(2,1)S(1)} %bitcast.19), channel_id=1, source_target_pairs={{0,8},{8,0},{1,9},{9,1},{2,10},{10,2},{3,11},{11,3},{4,12},{12,4},... | collective-permute-start | bytes 3145736 | tf_op jit(solution)/shard_map/ppermute | solution.py:189
  48.7 29.7 %collective-permute-start.9 = (bf16[8,512,128]{2,1,0:T(8,128)(2,1)S(1)}, bf16[8,512,128]{2,1,0:T(8,128)(2,1)S(1)}, u32[]{:S(2)}, u32[]{:S(2)}) collective-permute-start(bf16[8,512,128]{2,1,0:T(8,128)(2,1)S(1)} %bitcast.22), channel_id=1, source_target_pairs={{0,8},{8,0},{1,9},{9,1},{2,10},{10,2},{3,11},{11,3},{4,12},{12,4},... | collective-permute-start | bytes 3145736 | tf_op jit(solution)/shard_map/ppermute | solution.py:189
  56.2 23.2 %collective-permute-start.15 = (bf16[8,512,128]{2,1,0:T(8,128)(2,1)S(1)}, bf16[8,512,128]{2,1,0:T(8,128)(2,1)S(1)}, u32[]{:S(2)}, u32[]{:S(2)}) collective-permute-start(bf16[8,512,128]{2,1,0:T(8,128)(2,1)S(1)} %bitcast.23), channel_id=1, source_target_pairs={{0,32},{32,64},{64,96},{96,0},{1,33},{33,65},{65,97},{97,1},{2,34}... | collective-permute-start | bytes 3145736 | tf_op jit(solution)/shard_map/ppermute | solution.py:186
  59.6 23.4 %collective-permute-start.1 = (bf16[8,512,128]{2,1,0:T(8,128)(2,1)S(1)}, bf16[8,512,128]{2,1,0:T(8,128)(2,1)S(1)}, u32[]{:S(2)}, u32[]{:S(2)}) collective-permute-start(bf16[8,512,128]{2,1,0:T(8,128)(2,1)S(1)} %bitcast.24), channel_id=1, source_target_pairs={{0,96},{32,0},{64,32},{96,64},{1,97},{33,1},{65,33},{97,65},{2,98}... | collective-permute-start | bytes 3145736 | tf_op jit(solution)/shard_map/ppermute | solution.py:187
  72.5 22.9 %collective-permute-start.4 = (bf16[8,512,128]{2,1,0:T(8,128)(2,1)S(1)}, bf16[8,512,128]{2,1,0:T(8,128)(2,1)S(1)}, u32[]{:S(2)}, u32[]{:S(2)}) collective-permute-start(bf16[8,512,128]{2,1,0:T(8,128)(2,1)S(1)} %bitcast.25), channel_id=1, source_target_pairs={{0,16},{16,0},{1,17},{17,1},{2,18},{18,2},{3,19},{19,3},{4,20},{20... | collective-permute-start | bytes 3145736 | tf_op jit(solution)/shard_map/ppermute | solution.py:188
  72.9 1.0 copy-start.3
  73.8 1.0 copy-start.12
  74.8 24.5 %collective-permute-start.6 = (bf16[8,512,128]{2,1,0:T(8,128)(2,1)}, bf16[8,512,128]{2,1,0:T(8,128)(2,1)}, u32[]{:S(2)}, u32[]{:S(2)}) collective-permute-start(bf16[8,512,128]{2,1,0:T(8,128)(2,1)} %collective-permute-done.2.refs_0_), channel_id=1, source_target_pairs={{0,8},{8,0},{1,9},{9,1},{2,10},{10,2},{3,11},{11,3},{4,12},{12,4},... | collective-permute-start | bytes 3145736 | tf_op jit(solution)/shard_map/ppermute | solution.py:189
  78.4 1.0 copy-start.14
  79.4 20.3 %collective-permute-start.8 = (bf16[8,512,128]{2,1,0:T(8,128)(2,1)}, bf16[8,512,128]{2,1,0:T(8,128)(2,1)}, u32[]{:S(2)}, u32[]{:S(2)}) collective-permute-start(bf16[8,512,128]{2,1,0:T(8,128)(2,1)} %collective-permute-done.3.refs_4_), channel_id=1, source_target_pairs={{0,8},{8,0},{1,9},{9,1},{2,10},{10,2},{3,11},{11,3},{4,12},{12,4},... | collective-permute-start | bytes 3145736 | tf_op jit(solution)/shard_map/ppermute | solution.py:189
  79.4 16.0 %copy-start.6 = (bf16[8,512,128]{2,1,0:T(8,128)(2,1)}, bf16[8,512,128]{2,1,0:T(8,128)(2,1)S(1)}, u32[]{:S(2)}) copy-start(bf16[8,512,128]{2,1,0:T(8,128)(2,1)S(1)} %collective-permute-done.15.refs_2_) | copy-start | bytes 3145732
  79.4 25.1 %collective-permute-start.7 = (bf16[8,512,128]{2,1,0:T(8,128)(2,1)}, bf16[8,512,128]{2,1,0:T(8,128)(2,1)}, u32[]{:S(2)}, u32[]{:S(2)}) collective-permute-start(bf16[8,512,128]{2,1,0:T(8,128)(2,1)} %collective-permute-done.refs_2_), channel_id=1, source_target_pairs={{0,8},{8,0},{1,9},{9,1},{2,10},{10,2},{3,11},{11,3},{4,12},{12,4},... | collective-permute-start | bytes 3145736 | tf_op jit(solution)/shard_map/ppermute | solution.py:189
  83.0 13.8 %copy-start.8 = (bf16[8,512,128]{2,1,0:T(8,128)(2,1)}, bf16[8,512,128]{2,1,0:T(8,128)(2,1)S(1)}, u32[]{:S(2)}) copy-start(bf16[8,512,128]{2,1,0:T(8,128)(2,1)S(1)} %collective-permute-done.1.refs_0_) | copy-start | bytes 3145732
  83.0 28.8 %collective-permute-start.20 = (bf16[8,512,128]{2,1,0:T(8,128)(2,1)}, bf16[8,512,128]{2,1,0:T(8,128)(2,1)}, u32[]{:S(2)}, u32[]{:S(2)}) collective-permute-start(bf16[8,512,128]{2,1,0:T(8,128)(2,1)} %collective-permute-done.2.refs_0_), channel_id=1, source_target_pairs={{0,32},{32,64},{64,96},{96,0},{1,33},{33,65},{65,97},{97,1},{2,34}... | collective-permute-start | bytes 3145736 | tf_op jit(solution)/shard_map/ppermute | solution.py:186
  95.4 1.5 copy-start.10
  95.4 24.2 %collective-permute-start.12 = (bf16[8,512,128]{2,1,0:T(8,128)(2,1)}, bf16[8,512,128]{2,1,0:T(8,128)(2,1)}, u32[]{:S(2)}, u32[]{:S(2)}) collective-permute-start(bf16[8,512,128]{2,1,0:T(8,128)(2,1)} %collective-permute-done.3.refs_4_), channel_id=1, source_target_pairs={{0,96},{32,0},{64,32},{96,64},{1,97},{33,1},{65,33},{97,65},{2,98}... | collective-permute-start | bytes 3145736 | tf_op jit(solution)/shard_map/ppermute | solution.py:187
  96.9 11.9 %copy-start.15 = (bf16[8,512,128]{2,1,0:T(8,128)(2,1)S(1)}, bf16[8,512,128]{2,1,0:T(8,128)(2,1)}, u32[]{:S(2)}) copy-start(bf16[8,512,128]{2,1,0:T(8,128)(2,1)} %copy-done.14) | copy-start | bytes 3145732
  97.5 1.2 copy-start.4
  98.8 13.6 %copy-start = (bf16[8,256,512]{2,1,0:T(8,128)(2,1)}, bf16[8,256,512]{2,1,0:T(8,128)(2,1)S(1)}, u32[]{:S(2)}) copy-start(bf16[8,256,512]{2,1,0:T(8,128)(2,1)S(1)} %rows.3.mine_ref) | copy-start | bytes 6291460
  99.3 22.1 %collective-permute-start.5 = (bf16[8,512,128]{2,1,0:T(8,128)(2,1)}, bf16[8,512,128]{2,1,0:T(8,128)(2,1)}, u32[]{:S(2)}, u32[]{:S(2)}) collective-permute-start(bf16[8,512,128]{2,1,0:T(8,128)(2,1)} %collective-permute-done.2.refs_0_), channel_id=1, source_target_pairs={{0,16},{16,0},{1,17},{17,1},{2,18},{18,2},{3,19},{19,3},{4,20},{20... | collective-permute-start | bytes 3145736 | tf_op jit(solution)/shard_map/ppermute | solution.py:188
  99.7 22.9 %collective-permute-start.14 = (bf16[8,512,128]{2,1,0:T(8,128)(2,1)}, bf16[8,512,128]{2,1,0:T(8,128)(2,1)S(1)}, u32[]{:S(2)}, u32[]{:S(2)}) collective-permute-start(bf16[8,512,128]{2,1,0:T(8,128)(2,1)} %copy-done.8), channel_id=1, source_target_pairs={{0,8},{8,0},{1,9},{9,1},{2,10},{10,2},{3,11},{11,3},{4,12},{12,4},... | collective-permute-start | bytes 3145736 | tf_op jit(solution)/shard_map/ppermute | solution.py:189
  104.5 20.5 %collective-permute-start.16 = (bf16[8,512,128]{2,1,0:T(8,128)(2,1)}, bf16[8,512,128]{2,1,0:T(8,128)(2,1)S(1)}, u32[]{:S(2)}, u32[]{:S(2)}) collective-permute-start(bf16[8,512,128]{2,1,0:T(8,128)(2,1)} %copy-done.6), channel_id=1, source_target_pairs={{0,8},{8,0},{1,9},{9,1},{2,10},{10,2},{3,11},{11,3},{4,12},{12,4},... | collective-permute-start | bytes 3145736 | tf_op jit(solution)/shard_map/ppermute | solution.py:189
  104.6 1.2 copy-start.13
  108.8 3.0 %copy-start.11 = (bf16[8,512,128]{2,1,0:T(8,128)(2,1)S(1)}, bf16[8,512,128]{2,1,0:T(8,128)(2,1)}, u32[]{:S(2)}) copy-start(bf16[8,512,128]{2,1,0:T(8,128)(2,1)} %copy-done.10) | copy-start | bytes 3145732
  111.8 9.5 %copy-start.9 = (bf16[8,512,128]{2,1,0:T(8,128)(2,1)S(1)}, bf16[8,512,128]{2,1,0:T(8,128)(2,1)}, u32[]{:S(2)}) copy-start(bf16[8,512,128]{2,1,0:T(8,128)(2,1)} %copy-done.8) | copy-start | bytes 3145732
  111.8 38.9 %copy-start.7 = (bf16[8,512,128]{2,1,0:T(8,128)(2,1)S(1)}, bf16[8,512,128]{2,1,0:T(8,128)(2,1)}, u32[]{:S(2)}) copy-start(bf16[8,512,128]{2,1,0:T(8,128)(2,1)} %copy-done.6) | copy-start | bytes 3145732
  111.9 17.1 %collective-permute-start.17 = (bf16[8,512,128]{2,1,0:T(8,128)(2,1)S(1)}, bf16[8,512,128]{2,1,0:T(8,128)(2,1)S(1)}, u32[]{:S(2)}, u32[]{:S(2)}) collective-permute-start(bf16[8,512,128]{2,1,0:T(8,128)(2,1)S(1)} %copy-done.11), channel_id=1, source_target_pairs={{0,8},{8,0},{1,9},{9,1},{2,10},{10,2},{3,11},{11,3},{4,12},{12,4},... | collective-permute-start | bytes 3145736 | tf_op jit(solution)/shard_map/ppermute | solution.py:189
  119.6 24.4 %collective-permute-start.21 = (bf16[8,512,128]{2,1,0:T(8,128)(2,1)S(1)}, bf16[8,512,128]{2,1,0:T(8,128)(2,1)}, u32[]{:S(2)}, u32[]{:S(2)}) collective-permute-start(bf16[8,512,128]{2,1,0:T(8,128)(2,1)S(1)} %copy-done.11), channel_id=1, source_target_pairs={{0,32},{32,64},{64,96},{96,0},{1,33},{33,65},{65,97},{97,1},{2,34}... | collective-permute-start | bytes 3145736 | tf_op jit(solution)/shard_map/ppermute | solution.py:186
  121.4 25.3 %collective-permute-start.13 = (bf16[8,512,128]{2,1,0:T(8,128)(2,1)S(1)}, bf16[8,512,128]{2,1,0:T(8,128)(2,1)}, u32[]{:S(2)}, u32[]{:S(2)}) collective-permute-start(bf16[8,512,128]{2,1,0:T(8,128)(2,1)S(1)} %copy-done.9), channel_id=1, source_target_pairs={{0,96},{32,0},{64,32},{96,64},{1,97},{33,1},{65,33},{97,65},{2,98}... | collective-permute-start | bytes 3145736 | tf_op jit(solution)/shard_map/ppermute | solution.py:187
  122.6 24.5 %collective-permute-start.11 = (bf16[8,512,128]{2,1,0:T(8,128)(2,1)S(1)}, bf16[8,512,128]{2,1,0:T(8,128)(2,1)}, u32[]{:S(2)}, u32[]{:S(2)}) collective-permute-start(bf16[8,512,128]{2,1,0:T(8,128)(2,1)S(1)} %copy-done.9), channel_id=1, source_target_pairs={{0,16},{16,0},{1,17},{17,1},{2,18},{18,2},{3,19},{19,3},{4,20},{20... | collective-permute-start | bytes 3145736 | tf_op jit(solution)/shard_map/ppermute | solution.py:188
  125.0 24.8 %collective-permute-start.28 = (bf16[8,512,128]{2,1,0:T(8,128)(2,1)}, bf16[8,512,128]{2,1,0:T(8,128)(2,1)S(1)}, u32[]{:S(2)}, u32[]{:S(2)}) collective-permute-start(bf16[8,512,128]{2,1,0:T(8,128)(2,1)} %collective-permute-done.5.refs_4_), channel_id=1, source_target_pairs={{0,8},{8,0},{1,9},{9,1},{2,10},{10,2},{3,11},{11,3},{4,12},{12,4},... | collective-permute-start | bytes 3145736 | tf_op jit(solution)/shard_map/ppermute | solution.py:189
  129.0 27.3 %collective-permute-start.26 = (bf16[8,512,128]{2,1,0:T(8,128)(2,1)}, bf16[8,512,128]{2,1,0:T(8,128)(2,1)S(1)}, u32[]{:S(2)}, u32[]{:S(2)}) collective-permute-start(bf16[8,512,128]{2,1,0:T(8,128)(2,1)} %collective-permute-done.20.refs_0_), channel_id=1, source_target_pairs={{0,8},{8,0},{1,9},{9,1},{2,10},{10,2},{3,11},{11,3},{4,12},{12,4},... | collective-permute-start | bytes 3145736 | tf_op jit(solution)/shard_map/ppermute | solution.py:189
  144.1 13.4 %collective-permute-start.27 = (bf16[8,512,128]{2,1,0:T(8,128)(2,1)}, bf16[8,512,128]{2,1,0:T(8,128)(2,1)S(1)}, u32[]{:S(2)}, u32[]{:S(2)}) collective-permute-start(bf16[8,512,128]{2,1,0:T(8,128)(2,1)} %collective-permute-done.12.refs_2_), channel_id=1, source_target_pairs={{0,8},{8,0},{1,9},{9,1},{2,10},{10,2},{3,11},{11,3},{4,12},{12,4},... | collective-permute-start | bytes 3145736 | tf_op jit(solution)/shard_map/ppermute | solution.py:189
  146.7 26.4 %collective-permute-start.23 = (bf16[8,512,128]{2,1,0:T(8,128)(2,1)}, bf16[8,512,128]{2,1,0:T(8,128)(2,1)}, u32[]{:S(2)}, u32[]{:S(2)}) collective-permute-start(bf16[8,512,128]{2,1,0:T(8,128)(2,1)} %collective-permute-done.13.refs_0_), channel_id=1, source_target_pairs={{0,8},{8,0},{1,9},{9,1},{2,10},{10,2},{3,11},{11,3},{4,12},{12,4},... | collective-permute-start | bytes 3145736 | tf_op jit(solution)/shard_map/ppermute | solution.py:189
  147.0 26.0 %collective-permute-start.25 = (bf16[8,512,128]{2,1,0:T(8,128)(2,1)}, bf16[8,512,128]{2,1,0:T(8,128)(2,1)}, u32[]{:S(2)}, u32[]{:S(2)}) collective-permute-start(bf16[8,512,128]{2,1,0:T(8,128)(2,1)} %collective-permute-done.11.refs_4_), channel_id=1, source_target_pairs={{0,8},{8,0},{1,9},{9,1},{2,10},{10,2},{3,11},{11,3},{4,12},{12,4},... | collective-permute-start | bytes 3145736 | tf_op jit(solution)/shard_map/ppermute | solution.py:189
  149.8 1.0 copy-start.16
  150.8 22.3 %collective-permute-start.24 = (bf16[8,512,128]{2,1,0:T(8,128)(2,1)}, bf16[8,512,128]{2,1,0:T(8,128)(2,1)}, u32[]{:S(2)}, u32[]{:S(2)}) collective-permute-start(bf16[8,512,128]{2,1,0:T(8,128)(2,1)} %collective-permute-done.21.refs_2_), channel_id=1, source_target_pairs={{0,8},{8,0},{1,9},{9,1},{2,10},{10,2},{3,11},{11,3},{4,12},{12,4},... | collective-permute-start | bytes 3145736 | tf_op jit(solution)/shard_map/ppermute | solution.py:189
  156.3 1.0 copy-start.18
  157.3 25.7 %collective-permute-start.22 = (bf16[8,512,128]{2,1,0:T(8,128)(2,1)}, bf16[8,512,128]{2,1,0:T(8,128)(2,1)}, u32[]{:S(2)}, u32[]{:S(2)}) collective-permute-start(bf16[8,512,128]{2,1,0:T(8,128)(2,1)} %collective-permute-done.5.refs_4_), channel_id=1, source_target_pairs={{0,32},{32,64},{64,96},{96,0},{1,33},{33,65},{65,97},{97,1},{2,34}... | collective-permute-start | bytes 3145736 | tf_op jit(solution)/shard_map/ppermute | solution.py:186
  157.5 1.0 copy-start.20
  158.5 25.9 %collective-permute-start.18 = (bf16[8,512,128]{2,1,0:T(8,128)(2,1)}, bf16[8,512,128]{2,1,0:T(8,128)(2,1)}, u32[]{:S(2)}, u32[]{:S(2)}) collective-permute-start(bf16[8,512,128]{2,1,0:T(8,128)(2,1)} %collective-permute-done.11.refs_4_), channel_id=1, source_target_pairs={{0,96},{32,0},{64,32},{96,64},{1,97},{33,1},{65,33},{97,65},{2,98}... | collective-permute-start | bytes 3145736 | tf_op jit(solution)/shard_map/ppermute | solution.py:187
  161.1 1.6 copy-start.1
  162.7 1.2 copy-start.17
  163.9 1.2 copy-start.19
  165.1 1.2 copy-start.21
  183.0 3.9 %collective-permute-start.29 = (bf16[8,512,128]{2,1,0:T(8,128)(2,1)}, bf16[8,512,128]{2,1,0:T(8,128)(2,1)S(1)}, u32[]{:S(2)}, u32[]{:S(2)}) collective-permute-start(bf16[8,512,128]{2,1,0:T(8,128)(2,1)} %collective-permute-done.22.refs_0_), channel_id=1, source_target_pairs={{0,8},{8,0},{1,9},{9,1},{2,10},{10,2},{3,11},{11,3},{4,12},{12,4},... | collective-permute-start | bytes 3145736 | tf_op jit(solution)/shard_map/ppermute | solution.py:189
  184.4 10.6 %collective-permute-start.19 = (bf16[8,512,128]{2,1,0:T(8,128)(2,1)}, bf16[8,512,128]{2,1,0:T(8,128)(2,1)}, u32[]{:S(2)}, u32[]{:S(2)}) collective-permute-start(bf16[8,512,128]{2,1,0:T(8,128)(2,1)} %collective-permute-done.18.refs_0_), channel_id=1, source_target_pairs={{0,8},{8,0},{1,9},{9,1},{2,10},{10,2},{3,11},{11,3},{4,12},{12,4},... | collective-permute-start | bytes 3145736 | tf_op jit(solution)/shard_map/ppermute | solution.py:189
  186.9 1.0 copy-start.22
  187.8 1.6 copy-start.2
  189.4 1.2 copy-start.23

commit v3 on v2

--- a/solution.py
+++ b/solution.py
@@ -68,7 +68,7 @@
             pltpu.VMEM((2, stations * SEG_STEP, BINS), jnp.float32),
             pltpu.VMEM((2 * BINS * SEG_STEP, stations), jnp.float32),
         ],
-        compiler_params=pltpu.CompilerParams(vmem_limit_bytes=32 * MIB),
+        compiler_params=pltpu.CompilerParams(vmem_limit_bytes=60 * MIB),
         name="whiten",
     )(records, available.T, jnp.asarray(high), jnp.asarray(low))
 
@@ -94,23 +94,24 @@
         in_specs=[pl.BlockSpec((step, depth, rows), lambda f: (f, 0, 0))],
         out_specs=pl.BlockSpec((step, 2 * rows, depth), lambda f: (f, 0, 0)),
         out_shape=jax.ShapeDtypeStruct((bins, 2 * rows, depth), panel.dtype),
-        compiler_params=pltpu.CompilerParams(vmem_limit_bytes=16 * MIB),
+        compiler_params=pltpu.CompilerParams(vmem_limit_bytes=60 * MIB),
         name="rows",
     )(panel)
 
 
-def gram_kernel(scale, first, count, where, mine_ref, *refs):
-    panels, (out_ref, slots, sems) = refs[: 2 * count], refs[-3:]
+def gram_kernel(scale, halves, where, mine0_ref, mine1_ref, *refs):
+    count = len(halves)
+    panels, (out_ref, slots, sems) = [v.at[0] if len(v.shape) == 4 else v for v in refs[: 2 * count]], refs[-3:]
     step, steps = pl.program_id(0), pl.num_programs(0)
-    bins = mine_ref.shape[0]
-    rows, cols = mine_ref.shape[1] // 2, panels[0].shape[2]
+    bins = mine0_ref.shape[0]
+    rows, cols = mine0_ref.shape[1] // 2, panels[0].shape[2]
     slot = lax.rem(step, 2)
 
     def write(at, block, held):
         spot = pl.ds(pl.multiple_of(where[block] * 2 * cols, 2 * cols), 2 * cols)
         return pltpu.make_async_copy(
             slots.at[held, block],
-            out_ref.at[:, pl.ds(first + at * bins, bins), :, spot],
+            out_ref.at[:, pl.ds(halves[block] * HALF + at * bins, bins), :, spot],
             sems.at[held, block],
         )
 
@@ -122,6 +123,7 @@
     own = pl.ds(pl.multiple_of(where[count] * cols, cols), cols)
     other = pl.ds(pl.multiple_of((1 - where[count]) * cols, cols), cols)
     for block in range(count):
+        mine_ref = mine1_ref if halves[block] else mine0_ref
         for f in range(bins):
             panel = jnp.concatenate([panels[2 * block][f], panels[2 * block + 1][f]], axis=1)
             gram = jnp.dot(mine_ref[f], panel, preferred_element_type=jnp.float32) * scale
@@ -139,20 +141,30 @@
             write(step, block, slot).wait()
 
 
-def gram(first, core, mine, blocks, shape, out):
-    bins, depth, cols = blocks[0][1].shape
-    rows = mine.shape[1] // 2
+def gram(core, mine, blocks, shape, out):
+    bins, depth, cols = blocks[0][2].shape
+    rows = shape[2]
     count, step = len(blocks), 2
-    where = jnp.stack([chip for chip, _, _ in blocks] + [core]).astype(jnp.int32)
+    halves = [half for half, _, _, _ in blocks]
+    where = jnp.stack([chip for _, chip, _, _ in blocks] + [core]).astype(jnp.int32)
     held = [] if out is None else [out]
-    panels = [v for _, own, other in blocks for v in (own, other)]
+    panels = [v for _, _, own, other in blocks for v in (own, other)]
+    used = [
+        pl.BlockSpec((step, 2 * rows, depth), (lambda f, w: (f, 0, 0)) if half in halves else (lambda f, w: (0, 0, 0)))
+        for half in range(2)
+    ]
     return pl.pallas_call(
-        functools.partial(gram_kernel, 2.0 / depth, first, count),
+        functools.partial(gram_kernel, 2.0 / depth, halves),
         grid_spec=pltpu.PrefetchScalarGridSpec(
             num_scalar_prefetch=1,
             grid=(bins // step,),
-            in_specs=[pl.BlockSpec((step, 2 * rows, depth), lambda f, w: (f, 0, 0))]
-            + [pl.BlockSpec((step, depth, cols), lambda f, w: (f, 0, 0))] * (2 * count)
+            in_specs=used
+            + [
+                pl.BlockSpec((step, depth, cols), lambda f, w: (f, 0, 0))
+                if v.ndim == 3
+                else pl.BlockSpec((1, step, depth, cols), lambda f, w: (1 - w[count], f, 0, 0))
+                for v in panels
+            ]
             + [pl.BlockSpec(memory_space=pl.ANY)] * len(held),
             out_specs=pl.BlockSpec(memory_space=pl.ANY),
             scratch_shapes=[
@@ -161,15 +173,15 @@
             ],
         ),
         out_shape=jax.ShapeDtypeStruct(shape, jnp.bfloat16),
-        input_output_aliases={2 + 2 * count: 0} if held else {},
+        input_output_aliases={3 + 2 * count: 0} if held else {},
         cost_estimate=pl.CostEstimate(
             flops=16 * count * bins * rows * depth * cols,
             bytes_accessed=2 * bins * (2 * rows * depth + count * (2 * depth * cols + 4 * rows * cols)),
             transcendentals=0,
         ),
-        compiler_params=pltpu.CompilerParams(vmem_limit_bytes=16 * MIB),
+        compiler_params=pltpu.CompilerParams(vmem_limit_bytes=60 * MIB),
         name="gram",
-    )(where, mine, *panels, *held)
+    )(where, *mine, *panels, *held)
 
 
 def after(value, *others):
@@ -187,42 +199,50 @@
     left = lambda v: lax.ppermute(v, "x", ring(4, -1))
     over = lambda v: lax.ppermute(v, "yh", ring(2, 1))
     swap = lambda v: lax.ppermute(v, "core", ring(2, 1))
+    both = lambda v: lax.all_gather(v, "core")
 
     def owned(half):
         got = lax.all_to_all(half, ("yl", "z"), split_axis=0, concat_axis=0, tiled=True)
         got = jnp.transpose(got, (1, 2, 0, 3, 4))
         return got.reshape(HALF, -1, stations)
 
-    def entry(dx, dy, own):
-        chip = (x - dx) % 4 * 2 + (yh + dy) % 2
-        return chip, own, swap(own)
-
+    def entry(half, dx, dy, own, other):
+        return half, (x - dx) % 4 * 2 + (yh + dy) % 2, own, other
+
+    gate = lambda *values: lax.optimization_barrier(values)
+    shape = (2, 2 * HALF, stations, 16 * stations)
     first, second = whiten(records, available)
-    shape = (2, 2 * HALF, stations, 16 * stations)
     p0 = owned(first)
-    a0, b0, c0 = right(p0), left(p0), over(p0)
-    m0 = rows_of(p0)
-    p1 = owned(after(second, p0))
-    e_p0 = entry(0, 0, p0)
-    b1, a1, c1 = right(after(p1, a0)), left(after(p1, b0)), over(after(p1, c0))
+    p0, second = gate(p0, second)
+
+    a0, b0, p1, sp0, m0 = right(p0), left(p0), owned(second), swap(p0), rows_of(p0)
+    p0, p1, a0, b0, sp0, m0 = gate(p0, p1, a0, b0, sp0, m0)
+
+    b1, a1, c0, sa0, sb0, sp1 = right(p1), left(p1), over(p0), swap(a0), swap(b0), both(p1)
     m1 = rows_of(p1)
-    e_p1 = entry(0, 0, p1)
-    out = gram(0, core, m0, [e_p0], shape, None)
-    out = gram(HALF, core, m1, [e_p1], shape, out)
-    e0 = [entry(1, 0, a0), entry(-1, 0, b0), entry(0, 1, c0)]
-    d0, g0, f0 = right(after(a0, b1)), left(after(c0, a1)), over(after(a0, c1))
-    out = gram(0, core, m0, e0, shape, out)
-    e1 = [entry(-1, 0, a1), entry(1, 0, b1), entry(0, 1, c1)]
-    g1, d1, f1 = right(after(c1, d0, out)), left(after(a1, g0, out)), over(after(a1, f0, out))
-    out = gram(HALF, core, m1, e1, shape, out)
-    e0 = [entry(2, 0, d0), entry(-1, 1, g0), entry(1, 1, f0)]
-    h0, h1 = right(after(f0, g1, out)), left(after(f1, d1, out))
-    out = gram(0, core, m0, e0, shape, out)
-    e1 = [entry(-2, 0, d1), entry(1, 1, g1), entry(-1, 1, f1)]
-    out = gram(HALF, core, m1, e1, shape, out)
-    out = gram(0, core, m0, [entry(2, 1, after(h0, out))], shape, out)
-    out = gram(HALF, core, m1, [entry(-2, 1, h1)], shape, out)
-    return out
+    out = gram(core, (m0, m0), [entry(0, 0, 0, p0, sp0)], shape, None)
+    p1, a0, b0, a1, b1, c0, sa0, sb0, sp1, m1, out = gate(p1, a0, b0, a1, b1, c0, sa0, sb0, sp1, m1, out)
+    mine = m0, m1
+
+    d0, d1, c1, sa1, sb1, sc0 = right(a0), left(a1), over(p1), swap(a1), swap(b1), both(c0)
+    blocks = [entry(1, 0, 0, p1, sp1), entry(0, 1, 0, a0, sa0), entry(0, -1, 0, b0, sb0)]
+    out = gram(core, mine, blocks, shape, out)
+    a0, a1, b1, c0, c1, d0, d1, sa1, sb1, sc0, out = gate(a0, a1, b1, c0, c1, d0, d1, sa1, sb1, sc0, out)
+
+    g1, g0, f0, sd0, sd1, sc1 = right(c1), left(c0), over(a0), swap(d0), swap(d1), both(c1)
+    blocks = [entry(1, -1, 0, a1, sa1), entry(1, 1, 0, b1, sb1), entry(0, 0, 1, c0, sc0)]
+    out = gram(core, mine, blocks, shape, out)
+    c1, d0, d1, g0, g1, f0, sd0, sd1, sc1, out = gate(c1, d0, d1, g0, g1, f0, sd0, sd1, sc1, out)
+
+    h0, e1, f1, sg0, sg1, sf0 = right(f0), left(c1), over(d1), swap(g0), swap(g1), both(f0)
+    blocks = [entry(0, 2, 0, d0, sd0), entry(1, -2, 0, d1, sd1), entry(1, 0, 1, c1, sc1)]
+    out = gram(core, mine, blocks, shape, out)
+    blocks = [entry(0, -1, 1, g0, sg0), entry(1, 1, 1, g1, sg1), entry(0, 1, 1, f0, sf0)]
+    out = gram(core, mine, blocks, shape, out)
+    h0, e1, f1, out = gate(h0, e1, f1, out)
+
+    blocks = [entry(0, 2, 1, h0, swap(h0)), entry(1, -1, 1, e1, swap(e1)), entry(1, -2, 1, f1, swap(f1))]
+    return gram(core, mine, blocks, shape, out)
 
 
 def solution(mesh):

time: 201 us -> 204 us (1.015)
  local copies, waits for them, and re-layouts: 22.5 us -> 3.15 us
  Pallas kernels: 49.2 us -> 63.1 us
  starting transfers between devices: 54.8 us -> 41.9 us
  between operations: 0.44 us -> 13.3 us
  waiting for transfers between devices: 51.3 us -> 57.4 us
  other arithmetic: 0.45 us -> 3.58 us
    unnamed x54 -> x22, local copies, waits for them, and re-layouts: 22.3 us -> 1.95 us
    ppermute x16 -> x12, starting transfers between devices: 33.7 us -> 18.6 us  [shards(): swap = lambda v: lax.ppermute(v, 'core', ring(2, 1))]
    ppermute x5, waiting for transfers between devices: 3.02 us -> 16.8 us  [shards(): left = lambda v: lax.ppermute(v, 'x', ring(4, -1))]
    ppermute x5, waiting for transfers between devices: 18.6 us -> 8.28 us  [shards(): right = lambda v: lax.ppermute(v, 'x', ring(4, 1))]
    all_to_all x1, waiting for transfers between devices: 3.67 us -> 11.2 us  [owned(): lax.all_to_all(half, ('yl', 'z'), split_axis=0, concat_axis=0, tiled=True)]
    ppermute x4, waiting for transfers between devices: 23.8 us -> 16.4 us  [shards(): over = lambda v: lax.ppermute(v, 'yh', ring(2, 1))]
    pallas_call x2, Pallas kernels: 1.02 us -> 7.54 us  [rows_of(): pl.pallas_call(rows_kernel, grid=(bins // step,), in_specs=[pl.BlockSpec(...]
    pallas_call x8 -> x6, Pallas kernels: 41.4 us -> 47.8 us  [gram(): pl.pallas_call(functools.partial(gram_kernel, 2.0 / depth, halves), grid_...]
  transfers between devices with their start and end apart: 31 -> 31, of which waited for: 9 -> 15; matrix products, arithmetic and copies ran while one was open for 0% -> 2% of each run, Pallas kernels for 19% -> 23%
where the time goes in v3:
time: 204 us
  Pallas kernels  63.1 us (31%)
  waiting for transfers between devices  57.4 us (28%)
  starting transfers between devices  41.9 us (21%)
  blocking collectives  21.2 us (10%)
  between operations  13.3 us (7%)
  other arithmetic  3.58 us (2%)
  local copies, waits for them, and re-layouts  3.15 us (2%)
    pallas_call x6, Pallas kernels, gram(): pl.pallas_call(functools.partial(gram_kernel, 2.0 / depth, halves), grid_...  47.8 us
    all_to_all x1, blocking collectives, owned(): lax.all_to_all(half, ('yl', 'z'), split_axis=0, concat_axis=0, tiled=True)  21.2 us
    ppermute x12, starting transfers between devices, shards(): swap = lambda v: lax.ppermute(v, 'core', ring(2, 1))  18.6 us
    ppermute x5, waiting for transfers between devices, shards(): left = lambda v: lax.ppermute(v, 'x', ring(4, -1))  16.8 us
    ppermute x4, waiting for transfers between devices, shards(): over = lambda v: lax.ppermute(v, 'yh', ring(2, 1))  16.4 us
    all_to_all x1, waiting for transfers between devices, owned(): lax.all_to_all(half, ('yl', 'z'), split_axis=0, concat_axis=0, tiled=True)  11.2 us
    ppermute x5, starting transfers between devices, shards(): left = lambda v: lax.ppermute(v, 'x', ring(4, -1))  9.87 us
    ppermute x5, waiting for transfers between devices, shards(): right = lambda v: lax.ppermute(v, 'x', ring(4, 1))  8.28 us
  transfers between devices with their start and end apart: 31, of which 15 were waited for; matrix products, arithmetic and copies ran while one was open for 2% of the time, Pallas kernels for 23%

profile of v3, /device:TPU:1, one launch (start us, length us, event | category | flops | bytes accessed | tf_op | source)
XLA Modules:
  0.0 203.6 jit_solution(12324116613767679604)
XLA Ops:
  6.5 7.8 %whiten.1 = (bf16[8,8,2,32,128]{4,3,2,1,0:T(8,128)(2,1)}, bf16[8,8,2,32,128]{4,3,2,1,0:T(8,128)(2,1)}) custom-call(bf16[128,32,512]{2,1,0:T(8,128)(2,1)} %records_ref.1, s32[32,128]{1,0:T(8,128)} %bitcast.38, bf16[512,256]{1,0:T(8,128)(2,1)} %constant.121.clone.high_ref, bf16[512,256]{1,0:T(8,128)(2,1)} %constant.122.clone.low_ref), custom_call_target="tpu_custom_call" | custom-call | tf_op jit(solution)/shard_map/whiten/pallas_call | solution.py:56
  14.3 21.2 %all_to_all.10 = bf16[8,8,2,32,128]{4,3,2,1,0:T(8,128)(2,1)S(1)} all-to-all(bf16[8,8,2,32,128]{4,3,2,1,0:T(8,128)(2,1)} %get-tuple-element.51), channel_id=1, replica_groups=mesh['x'=4,'yh'=2,'core'=2,'yl'=2,'z'=4] {'yl','z'}, dimensions={0} | all-to-all | bytes 2097152 | tf_op jit(solution)/shard_map/all_to_all | solution.py:205
  35.5 0.1 copy.12
  35.6 1.3 collective-permute-start
  36.9 1.5 collective-permute-start.1
  38.4 3.0 %collective-permute-start.2 = (bf16[8,512,128]{2,1,0:T(8,128)(2,1)S(1)}, bf16[8,512,128]{2,1,0:T(8,128)(2,1)}, u32[]{:S(2)}, u32[]{:S(2)}) collective-permute-start(bf16[8,512,128]{2,1,0:T(8,128)(2,1)S(1)} %bitcast.28), channel_id=1, source_target_pairs={{0,8},{8,0},{1,9},{9,1},{2,10},{10,2},{3,11},{11,3},{4,12},{12,4},... | collective-permute-start | bytes 3145736 | tf_op jit(solution)/shard_map/ppermute | solution.py:201
  41.4 3.6 %all-to-all-start.1 = ((bf16[8,8,2,32,128]{4,3,2,1,0:T(8,128)(2,1)}), bf16[8,8,2,32,128]{4,3,2,1,0:T(8,128)(2,1)S(1)}, u32[]{:S(2)}, u32[]{:S(2)}) async-start(bf16[8,8,2,32,128]{4,3,2,1,0:T(8,128)(2,1)} %get-tuple-element.54), calls=%async_computation.1 | async-start | bytes 2097152 | tf_op jit(solution)/shard_map/all_to_all | solution.py:205
  44.9 0.0 all-gather.9.cloned.1.call-start
  45.0 3.8 %rows.2.mine0_ref.mine1_ref = bf16[8,256,512]{2,1,0:T(8,128)(2,1)} custom-call(bf16[8,512,128]{2,1,0:T(8,128)(2,1)} %bitcast.29), custom_call_target="tpu_custom_call" | custom-call | tf_op jit(solution)/shard_map/rows/pallas_call | solution.py:91
  48.8 11.2 %all-to-all-done.1 = bf16[8,8,2,32,128]{4,3,2,1,0:T(8,128)(2,1)S(1)} async-done(((bf16[8,8,2,32,128]{4,3,2,1,0:T(8,128)(2,1)}), bf16[8,8,2,32,128]{4,3,2,1,0:T(8,128)(2,1)S(1)}, u32[]{:S(2)}, u32[]{:S(2)}) %all-to-all-start.1) | async-done | bytes 1048608 | tf_op jit(solution)/shard_map/all_to_all | solution.py:205
  60.0 1.1 copy.13
  61.1 0.0 all-gather.11.cloned.1.call-start
  61.2 1.2 collective-permute-start.3
  62.4 0.3 collective-permute-start.4
  62.7 2.6 %collective-permute-start.5 = (bf16[8,512,128]{2,1,0:T(8,128)(2,1)}, bf16[8,512,128]{2,1,0:T(8,128)(2,1)S(1)}, u32[]{:S(2)}, u32[]{:S(2)}) collective-permute-start(bf16[8,512,128]{2,1,0:T(8,128)(2,1)} %bitcast.30), channel_id=1, source_target_pairs={{0,16},{16,0},{1,17},{17,1},{2,18},{18,2},{3,19},{19,3},{4,20},{20... | collective-permute-start | bytes 3145736 | tf_op jit(solution)/shard_map/ppermute | solution.py:200
  65.3 3.1 %collective-permute-start.6 = (bf16[8,512,128]{2,1,0:T(8,128)(2,1)}, bf16[8,512,128]{2,1,0:T(8,128)(2,1)}, u32[]{:S(2)}, u32[]{:S(2)}) collective-permute-start(bf16[8,512,128]{2,1,0:T(8,128)(2,1)} %collective-permute-done.refs_2_), channel_id=1, source_target_pairs={{0,8},{8,0},{1,9},{9,1},{2,10},{10,2},{3,11},{11,3},{4,12},{12,4},... | collective-permute-start | bytes 3145736 | tf_op jit(solution)/shard_map/ppermute | solution.py:201
  68.5 0.6 pad_add_fusion.where
  69.1 3.8 %rows.3.mine1_ref = bf16[8,256,512]{2,1,0:T(8,128)(2,1)} custom-call(bf16[8,512,128]{2,1,0:T(8,128)(2,1)} %bitcast.23), custom_call_target="tpu_custom_call" | custom-call | tf_op jit(solution)/shard_map/rows/pallas_call | solution.py:91
  72.9 5.6 %gram.6.refs_6_ = bf16[2,16,128,2048]{3,2,1,0:T(8,128)(2,1)} custom-call(s32[2]{0:T(128)} %pad_add_fusion.where, bf16[8,256,512]{2,1,0:T(8,128)(2,1)} %rows.2.mine0_ref.mine1_ref, bf16[8,256,512]{2,1,0:T(8,128)(2,1)} %rows.2.mine0_ref.mine1_ref, bf16[8,512,128]{2,1,0:T(8,128)(2,1)} %bitcast.31, bf16[8,512,128]{2,1,0:T(8,128)(2,1)} %collective-permute-done.2.refs_1_), custom_call_target="tpu_custom_call" | custom-call | flops 1073741824 | bytes 5242880 | tf_op jit(solution)/shard_map/gram/pallas_call | solution.py:156
  78.5 6.3 %collective-permute-done.3.refs_0_ = bf16[8,512,128]{2,1,0:T(8,128)(2,1)} collective-permute-done((bf16[8,512,128]{2,1,0:T(8,128)(2,1)}, bf16[8,512,128]{2,1,0:T(8,128)(2,1)}, u32[]{:S(2)}, u32[]{:S(2)}) %collective-permute-start.3) | collective-permute-done | bytes 1048608 | tf_op jit(solution)/shard_map/ppermute | solution.py:199
  84.7 0.7 collective-permute-done.4.refs_2_
  85.4 0.8 collective-permute-done.5.refs_4_
  86.2 0.0 all-gather.9.cloned.1.call-done
  86.3 0.9 copy-done.4
  87.2 0.0 all-gather.13.cloned.1.call-start
  87.2 1.9 collective-permute-start.10
  89.1 4.7 %collective-permute-start.11 = (bf16[8,512,128]{2,1,0:T(8,128)(2,1)}, bf16[8,512,128]{2,1,0:T(8,128)(2,1)}, u32[]{:S(2)}, u32[]{:S(2)}) collective-permute-start(bf16[8,512,128]{2,1,0:T(8,128)(2,1)} %collective-permute-done.3.refs_0_), channel_id=1, source_target_pairs={{0,8},{8,0},{1,9},{9,1},{2,10},{10,2},{3,11},{11,3},{4,12},{12,4},... | collective-permute-start | bytes 3145736 | tf_op jit(solution)/shard_map/ppermute | solution.py:201
  93.8 2.6 %collective-permute-start.8 = (bf16[8,512,128]{2,1,0:T(8,128)(2,1)S(1)}, bf16[8,512,128]{2,1,0:T(8,128)(2,1)S(1)}, u32[]{:S(2)}, u32[]{:S(2)}) collective-permute-start(bf16[8,512,128]{2,1,0:T(8,128)(2,1)S(1)} %bitcast.25), channel_id=1, source_target_pairs={{0,16},{16,0},{1,17},{17,1},{2,18},{18,2},{3,19},{19,3},{4,20},{20... | collective-permute-start | bytes 3145736 | tf_op jit(solution)/shard_map/ppermute | solution.py:200
  96.4 0.6 add_add_fusion.1.where
  96.9 8.8 %gram.7.refs_6_ = bf16[2,16,128,2048]{3,2,1,0:T(8,128)(2,1)} custom-call(s32[4]{0:T(128)} %add_add_fusion.1.where, bf16[8,256,512]{2,1,0:T(8,128)(2,1)} %rows.2.mine0_ref.mine1_ref, bf16[8,256,512]{2,1,0:T(8,128)(2,1)} %rows.3.mine1_ref, bf16[8,512,128]{2,1,0:T(8,128)(2,1)} %bitcast.24, ...), custom_call_target="tpu_custom_call", output_to_operand_aliasing={{}: (9, {})} | custom-call | flops 3221225472 | bytes 11534336 | tf_op jit(solution)/shard_map/gram/pallas_call | solution.py:156
  105.7 2.7 %collective-permute-done.10.refs_2_ = bf16[8,512,128]{2,1,0:T(8,128)(2,1)} collective-permute-done((bf16[8,512,128]{2,1,0:T(8,128)(2,1)}, bf16[8,512,128]{2,1,0:T(8,128)(2,1)}, u32[]{:S(2)}, u32[]{:S(2)}) %collective-permute-start.10) | collective-permute-done | bytes 1048608 | tf_op jit(solution)/shard_map/ppermute | solution.py:199
  108.5 11.0 %collective-permute-done.8.refs_4_ = bf16[8,512,128]{2,1,0:T(8,128)(2,1)S(1)} collective-permute-done((bf16[8,512,128]{2,1,0:T(8,128)(2,1)S(1)}, bf16[8,512,128]{2,1,0:T(8,128)(2,1)S(1)}, u32[]{:S(2)}, u32[]{:S(2)}) %collective-permute-start.8) | collective-permute-done | bytes 1048608 | tf_op jit(solution)/shard_map/ppermute | solution.py:200
  119.5 2.3 %collective-permute-done.9.refs_0_ = bf16[8,512,128]{2,1,0:T(8,128)(2,1)} collective-permute-done((bf16[8,512,128]{2,1,0:T(8,128)(2,1)}, bf16[8,512,128]{2,1,0:T(8,128)(2,1)}, u32[]{:S(2)}, u32[]{:S(2)}) %collective-permute-start.9) | collective-permute-done | bytes 1048608 | tf_op jit(solution)/shard_map/ppermute | solution.py:198
  121.8 0.0 all-gather.13.cloned.1.call-update
  121.8 0.0 all-gather.15.cloned.1.call-start
  121.9 0.1 collective-permute-start.14
  122.0 2.7 %collective-permute-start.13 = (bf16[8,512,128]{2,1,0:T(8,128)(2,1)S(1)}, bf16[8,512,128]{2,1,0:T(8,128)(2,1)}, u32[]{:S(2)}, u32[]{:S(2)}) collective-permute-start(bf16[8,512,128]{2,1,0:T(8,128)(2,1)S(1)} %copy-done.5), channel_id=1, source_target_pairs={{0,96},{32,0},{64,32},{96,64},{1,97},{33,1},{65,33},{97,65},{2,98}... | collective-permute-start | bytes 3145736 | tf_op jit(solution)/shard_map/ppermute | solution.py:199
  124.6 1.4 collective-permute-start.15
  126.0 2.1 %collective-permute-start.16 = (bf16[8,512,128]{2,1,0:T(8,128)(2,1)}, bf16[8,512,128]{2,1,0:T(8,128)(2,1)}, u32[]{:S(2)}, u32[]{:S(2)}) collective-permute-start(bf16[8,512,128]{2,1,0:T(8,128)(2,1)} %collective-permute-done.9.refs_0_), channel_id=1, source_target_pairs={{0,8},{8,0},{1,9},{9,1},{2,10},{10,2},{3,11},{11,3},{4,12},{12,4},... | collective-permute-start | bytes 3145736 | tf_op jit(solution)/shard_map/ppermute | solution.py:201
  128.1 0.6 add_add_fusion.2.where
  128.7 8.7 %gram.8.refs_6_ = bf16[2,16,128,2048]{3,2,1,0:T(8,128)(2,1)} custom-call(s32[4]{0:T(128)} %add_add_fusion.2.where, bf16[8,256,512]{2,1,0:T(8,128)(2,1)} %rows.2.mine0_ref.mine1_ref, bf16[8,256,512]{2,1,0:T(8,128)(2,1)} %rows.3.mine1_ref, bf16[8,512,128]{2,1,0:T(8,128)(2,1)} %collective-permute-done.3.refs_0_, ...), custom_call_target="tpu_custom_call", output_to_operand_aliasing={{}: (9, {})} | custom-call | flops 3221225472 | bytes 11534336 | tf_op jit(solution)/shard_map/gram/pallas_call | solution.py:156
  137.4 7.7 %collective-permute-done.13.refs_0_ = bf16[8,512,128]{2,1,0:T(8,128)(2,1)} collective-permute-done((bf16[8,512,128]{2,1,0:T(8,128)(2,1)S(1)}, bf16[8,512,128]{2,1,0:T(8,128)(2,1)}, u32[]{:S(2)}, u32[]{:S(2)}) %collective-permute-start.13) | collective-permute-done | bytes 1048608 | tf_op jit(solution)/shard_map/ppermute | solution.py:199
  145.1 1.3 collective-permute-done.14.refs_2_
  146.5 2.3 %collective-permute-done.15.refs_4_ = bf16[8,512,128]{2,1,0:T(8,128)(2,1)S(1)} collective-permute-done((bf16[8,512,128]{2,1,0:T(8,128)(2,1)}, bf16[8,512,128]{2,1,0:T(8,128)(2,1)S(1)}, u32[]{:S(2)}, u32[]{:S(2)}) %collective-permute-start.15) | collective-permute-done | bytes 1048608 | tf_op jit(solution)/shard_map/ppermute | solution.py:200
  148.8 0.0 all-gather.13.cloned.1.call-done
  148.8 1.0 copy-done.6
  149.8 3.2 %collective-permute-start.21 = (bf16[8,512,128]{2,1,0:T(8,128)(2,1)}, bf16[8,512,128]{2,1,0:T(8,128)(2,1)}, u32[]{:S(2)}, u32[]{:S(2)}) collective-permute-start(bf16[8,512,128]{2,1,0:T(8,128)(2,1)} %collective-permute-done.13.refs_0_), channel_id=1, source_target_pairs={{0,8},{8,0},{1,9},{9,1},{2,10},{10,2},{3,11},{11,3},{4,12},{12,4},... | collective-permute-start | bytes 3145736 | tf_op jit(solution)/shard_map/ppermute | solution.py:201
  153.1 0.1 collective-permute-start.22
  153.2 2.7 %collective-permute-start.19 = (bf16[8,512,128]{2,1,0:T(8,128)(2,1)S(1)}, bf16[8,512,128]{2,1,0:T(8,128)(2,1)S(1)}, u32[]{:S(2)}, u32[]{:S(2)}) collective-permute-start(bf16[8,512,128]{2,1,0:T(8,128)(2,1)S(1)} %copy-done.3), channel_id=1, source_target_pairs={{0,96},{32,0},{64,32},{96,64},{1,97},{33,1},{65,33},{97,65},{2,98}... | collective-permute-start | bytes 3145736 | tf_op jit(solution)/shard_map/ppermute | solution.py:199
  155.8 1.4 collective-permute-start.20
  157.2 0.6 add_add_fusion.4.where
  157.9 0.6 add_add_fusion.3.where
  158.4 8.4 %gram.9.refs_6_ = bf16[2,16,128,2048]{3,2,1,0:T(8,128)(2,1)} custom-call(s32[4]{0:T(128)} %add_add_fusion.4.where, bf16[8,256,512]{2,1,0:T(8,128)(2,1)} %rows.2.mine0_ref.mine1_ref, bf16[8,256,512]{2,1,0:T(8,128)(2,1)} %rows.3.mine1_ref, bf16[8,512,128]{2,1,0:T(8,128)(2,1)} %collective-permute-done.9.refs_0_, ...), custom_call_target="tpu_custom_call", output_to_operand_aliasing={{}: (9, {})} | custom-call | flops 3221225472 | bytes 11534336 | tf_op jit(solution)/shard_map/gram/pallas_call | solution.py:156
  166.9 0.0 all-gather.15.cloned.1.call-done
  166.9 8.2 %gram.10.refs_6_ = bf16[2,16,128,2048]{3,2,1,0:T(8,128)(2,1)} custom-call(s32[4]{0:T(128)} %add_add_fusion.3.where, bf16[8,256,512]{2,1,0:T(8,128)(2,1)} %rows.2.mine0_ref.mine1_ref, bf16[8,256,512]{2,1,0:T(8,128)(2,1)} %rows.3.mine1_ref, bf16[8,512,128]{2,1,0:T(8,128)(2,1)} %collective-permute-done.13.refs_0_, ...), custom_call_target="tpu_custom_call", output_to_operand_aliasing={{}: (9, {})} | custom-call | flops 3221225472 | bytes 11534336 | tf_op jit(solution)/shard_map/gram/pallas_call | solution.py:156
  175.1 4.0 %collective-permute-done.18.refs_0_ = bf16[8,512,128]{2,1,0:T(8,128)(2,1)S(1)} collective-permute-done((bf16[8,512,128]{2,1,0:T(8,128)(2,1)}, bf16[8,512,128]{2,1,0:T(8,128)(2,1)S(1)}, u32[]{:S(2)}, u32[]{:S(2)}) %collective-permute-start.18) | collective-permute-done | bytes 1048608 | tf_op jit(solution)/shard_map/ppermute | solution.py:198
  179.0 2.3 %collective-permute-done.20.refs_4_ = bf16[8,512,128]{2,1,0:T(8,128)(2,1)} collective-permute-done((bf16[8,512,128]{2,1,0:T(8,128)(2,1)}, bf16[8,512,128]{2,1,0:T(8,128)(2,1)}, u32[]{:S(2)}, u32[]{:S(2)}) %collective-permute-start.20) | collective-permute-done | bytes 1048608 | tf_op jit(solution)/shard_map/ppermute | solution.py:200
  181.3 1.9 collective-permute-start.23
  183.2 0.5 collective-permute-start.25
  183.7 0.6 add_add_fusion.where
  184.3 2.6 %collective-permute-done.23.refs_1_ = bf16[8,512,128]{2,1,0:T(8,128)(2,1)S(1)} collective-permute-done((bf16[8,512,128]{2,1,0:T(8,128)(2,1)S(1)}, bf16[8,512,128]{2,1,0:T(8,128)(2,1)S(1)}, u32[]{:S(2)}, u32[]{:S(2)}) %collective-permute-start.23) | collective-permute-done | bytes 1048608 | tf_op jit(solution)/shard_map/ppermute | solution.py:201
  187.0 1.5 collective-permute-done.24.refs_3_
  188.5 0.3 collective-permute-done.25.refs_5_
  188.9 8.2 %gram.11 = bf16[2,16,128,2048]{3,2,1,0:T(8,128)(2,1)} custom-call(s32[4]{0:T(128)} %add_add_fusion.where, bf16[8,256,512]{2,1,0:T(8,128)(2,1)} %rows.2.mine0_ref.mine1_ref, bf16[8,256,512]{2,1,0:T(8,128)(2,1)} %rows.3.mine1_ref, bf16[8,512,128]{2,1,0:T(8,128)(2,1)} %copy-done.8, bf16[8,512,128]{2,1,0:T(8,128)(2,1)} %copy-done.10, ...), custom_call_target="tpu_custom_call", output_to_operand_aliasing={{}: (9, {})} | custom-call | flops 3221225472 | bytes 11534336 | tf_op jit(solution)/shard_map/gram/pallas_call | solution.py:156
  (42 shorter events, 0.1 us)
Async XLA Ops:
  35.6 9.4 %copy-start.1 = (bf16[8,2,8,32,128]{4,3,2,1,0:T(8,128)(2,1)}, bf16[8,2,8,32,128]{4,3,2,1,0:T(8,128)(2,1)S(1)}, u32[]{:S(2)}) copy-start(bf16[8,2,8,32,128]{4,3,2,1,0:T(8,128)(2,1)S(1)} %copy.12) | copy-start | bytes 3145732
  35.6 25.5 %collective-permute-start = (bf16[8,512,128]{2,1,0:T(8,128)(2,1)S(1)}, bf16[8,512,128]{2,1,0:T(8,128)(2,1)}, u32[]{:S(2)}, u32[]{:S(2)}) collective-permute-start(bf16[8,512,128]{2,1,0:T(8,128)(2,1)S(1)} %bitcast.26), channel_id=1, source_target_pairs={{0,32},{32,64},{64,96},{96,0},{1,33},{33,65},{65,97},{97,1},{2,34}... | collective-permute-start | bytes 3145736 | tf_op jit(solution)/shard_map/ppermute | solution.py:198
  36.9 24.2 %collective-permute-start.1 = (bf16[8,512,128]{2,1,0:T(8,128)(2,1)S(1)}, bf16[8,512,128]{2,1,0:T(8,128)(2,1)S(1)}, u32[]{:S(2)}, u32[]{:S(2)}) collective-permute-start(bf16[8,512,128]{2,1,0:T(8,128)(2,1)S(1)} %bitcast.27), channel_id=1, source_target_pairs={{0,96},{32,0},{64,32},{96,64},{1,97},{33,1},{65,33},{97,65},{2,98}... | collective-permute-start | bytes 3145736 | tf_op jit(solution)/shard_map/ppermute | solution.py:199
  38.4 22.7 %collective-permute-start.2 = (bf16[8,512,128]{2,1,0:T(8,128)(2,1)S(1)}, bf16[8,512,128]{2,1,0:T(8,128)(2,1)}, u32[]{:S(2)}, u32[]{:S(2)}) collective-permute-start(bf16[8,512,128]{2,1,0:T(8,128)(2,1)S(1)} %bitcast.28), channel_id=1, source_target_pairs={{0,8},{8,0},{1,9},{9,1},{2,10},{10,2},{3,11},{11,3},{4,12},{12,4},... | collective-permute-start | bytes 3145736 | tf_op jit(solution)/shard_map/ppermute | solution.py:201
  41.4 18.6 %all-to-all-start.1 = ((bf16[8,8,2,32,128]{4,3,2,1,0:T(8,128)(2,1)}), bf16[8,8,2,32,128]{4,3,2,1,0:T(8,128)(2,1)S(1)}, u32[]{:S(2)}, u32[]{:S(2)}) async-start(bf16[8,8,2,32,128]{4,3,2,1,0:T(8,128)(2,1)} %get-tuple-element.54), calls=%async_computation.1 | async-start | bytes 2097152 | tf_op jit(solution)/shard_map/all_to_all | solution.py:205
  44.9 41.3 %all-gather.9.cloned.1.call-start = ((), (), s32[]{:S(2)}) async-start(), calls=%async_computation.2 | async-start | bytes 3145728 | tf_op jit(solution)/shard_map/all_gather | solution.py:202
  61.1 17.4 %copy-start.7 = (bf16[8,512,128]{2,1,0:T(8,128)(2,1)}, bf16[8,512,128]{2,1,0:T(8,128)(2,1)S(1)}, u32[]{:S(2)}) copy-start(bf16[8,512,128]{2,1,0:T(8,128)(2,1)S(1)} %collective-permute-done.1.refs_4_) | copy-start | bytes 3145732
  61.1 60.7 %all-gather.11.cloned.1.call-start = ((), (), s32[]{:S(2)}) async-start(), calls=%async_computation.3 | async-start | bytes 3145728 | tf_op jit(solution)/shard_map/all_gather | solution.py:202
  61.2 23.6 %collective-permute-start.3 = (bf16[8,512,128]{2,1,0:T(8,128)(2,1)}, bf16[8,512,128]{2,1,0:T(8,128)(2,1)}, u32[]{:S(2)}, u32[]{:S(2)}) collective-permute-start(bf16[8,512,128]{2,1,0:T(8,128)(2,1)} %bitcast.21), channel_id=1, source_target_pairs={{0,96},{32,0},{64,32},{96,64},{1,97},{33,1},{65,33},{97,65},{2,98}... | collective-permute-start | bytes 3145736 | tf_op jit(solution)/shard_map/ppermute | solution.py:199
  62.4 23.0 %collective-permute-start.4 = (bf16[8,512,128]{2,1,0:T(8,128)(2,1)}, bf16[8,512,128]{2,1,0:T(8,128)(2,1)}, u32[]{:S(2)}, u32[]{:S(2)}) collective-permute-start(bf16[8,512,128]{2,1,0:T(8,128)(2,1)} %bitcast.22), channel_id=1, source_target_pairs={{0,32},{32,64},{64,96},{96,0},{1,33},{33,65},{65,97},{97,1},{2,34}... | collective-permute-start | bytes 3145736 | tf_op jit(solution)/shard_map/ppermute | solution.py:198
  62.7 23.5 %collective-permute-start.5 = (bf16[8,512,128]{2,1,0:T(8,128)(2,1)}, bf16[8,512,128]{2,1,0:T(8,128)(2,1)S(1)}, u32[]{:S(2)}, u32[]{:S(2)}) collective-permute-start(bf16[8,512,128]{2,1,0:T(8,128)(2,1)} %bitcast.30), channel_id=1, source_target_pairs={{0,16},{16,0},{1,17},{17,1},{2,18},{18,2},{3,19},{19,3},{4,20},{20... | collective-permute-start | bytes 3145736 | tf_op jit(solution)/shard_map/ppermute | solution.py:200
  65.3 20.9 %collective-permute-start.6 = (bf16[8,512,128]{2,1,0:T(8,128)(2,1)}, bf16[8,512,128]{2,1,0:T(8,128)(2,1)}, u32[]{:S(2)}, u32[]{:S(2)}) collective-permute-start(bf16[8,512,128]{2,1,0:T(8,128)(2,1)} %collective-permute-done.refs_2_), channel_id=1, source_target_pairs={{0,8},{8,0},{1,9},{9,1},{2,10},{10,2},{3,11},{11,3},{4,12},{12,4},... | collective-permute-start | bytes 3145736 | tf_op jit(solution)/shard_map/ppermute | solution.py:201
  68.5 17.7 %collective-permute-start.7 = (bf16[8,512,128]{2,1,0:T(8,128)(2,1)S(1)}, bf16[8,512,128]{2,1,0:T(8,128)(2,1)}, u32[]{:S(2)}, u32[]{:S(2)}) collective-permute-start(bf16[8,512,128]{2,1,0:T(8,128)(2,1)S(1)} %collective-permute-done.1.refs_4_), channel_id=1, source_target_pairs={{0,8},{8,0},{1,9},{9,1},{2,10},{10,2},{3,11},{11,3},{4,12},{12,4},... | collective-permute-start | bytes 3145736 | tf_op jit(solution)/shard_map/ppermute | solution.py:201
  72.9 20.9 %copy-start = (bf16[8,2,8,32,128]{4,3,2,1,0:T(8,128)(2,1)S(1)}, bf16[8,2,8,32,128]{4,3,2,1,0:T(8,128)(2,1)}, u32[]{:S(2)}) copy-start(bf16[8,2,8,32,128]{4,3,2,1,0:T(8,128)(2,1)} %copy.13) | copy-start | bytes 3145732
  86.2 1.0 copy-start.4
  87.2 61.6 %all-gather.13.cloned.1.call-start = ((), (), s32[]{:S(2)}) async-start(), calls=%async_computation.4 | async-start | bytes 3145728 | tf_op jit(solution)/shard_map/all_gather | solution.py:202
  87.2 21.2 %collective-permute-start.10 = (bf16[8,512,128]{2,1,0:T(8,128)(2,1)}, bf16[8,512,128]{2,1,0:T(8,128)(2,1)}, u32[]{:S(2)}, u32[]{:S(2)}) collective-permute-start(bf16[8,512,128]{2,1,0:T(8,128)(2,1)} %collective-permute-done.3.refs_0_), channel_id=1, source_target_pairs={{0,96},{32,0},{64,32},{96,64},{1,97},{33,1},{65,33},{97,65},{2,98}... | collective-permute-start | bytes 3145736 | tf_op jit(solution)/shard_map/ppermute | solution.py:199
  89.1 19.4 %collective-permute-start.11 = (bf16[8,512,128]{2,1,0:T(8,128)(2,1)}, bf16[8,512,128]{2,1,0:T(8,128)(2,1)}, u32[]{:S(2)}, u32[]{:S(2)}) collective-permute-start(bf16[8,512,128]{2,1,0:T(8,128)(2,1)} %collective-permute-done.3.refs_0_), channel_id=1, source_target_pairs={{0,8},{8,0},{1,9},{9,1},{2,10},{10,2},{3,11},{11,3},{4,12},{12,4},... | collective-permute-start | bytes 3145736 | tf_op jit(solution)/shard_map/ppermute | solution.py:201
  93.8 14.7 %collective-permute-start.12 = (bf16[8,512,128]{2,1,0:T(8,128)(2,1)}, bf16[8,512,128]{2,1,0:T(8,128)(2,1)}, u32[]{:S(2)}, u32[]{:S(2)}) collective-permute-start(bf16[8,512,128]{2,1,0:T(8,128)(2,1)} %collective-permute-done.4.refs_2_), channel_id=1, source_target_pairs={{0,8},{8,0},{1,9},{9,1},{2,10},{10,2},{3,11},{11,3},{4,12},{12,4},... | collective-permute-start | bytes 3145736 | tf_op jit(solution)/shard_map/ppermute | solution.py:201
  93.8 25.7 %collective-permute-start.8 = (bf16[8,512,128]{2,1,0:T(8,128)(2,1)S(1)}, bf16[8,512,128]{2,1,0:T(8,128)(2,1)S(1)}, u32[]{:S(2)}, u32[]{:S(2)}) collective-permute-start(bf16[8,512,128]{2,1,0:T(8,128)(2,1)S(1)} %bitcast.25), channel_id=1, source_target_pairs={{0,16},{16,0},{1,17},{17,1},{2,18},{18,2},{3,19},{19,3},{4,20},{20... | collective-permute-start | bytes 3145736 | tf_op jit(solution)/shard_map/ppermute | solution.py:200
  96.4 25.4 %collective-permute-start.9 = (bf16[8,512,128]{2,1,0:T(8,128)(2,1)}, bf16[8,512,128]{2,1,0:T(8,128)(2,1)}, u32[]{:S(2)}, u32[]{:S(2)}) collective-permute-start(bf16[8,512,128]{2,1,0:T(8,128)(2,1)} %collective-permute-done.refs_2_), channel_id=1, source_target_pairs={{0,32},{32,64},{64,96},{96,0},{1,33},{33,65},{65,97},{97,1},{2,34}... | collective-permute-start | bytes 3145736 | tf_op jit(solution)/shard_map/ppermute | solution.py:198
  96.9 25.0 %copy-start.5 = (bf16[8,512,128]{2,1,0:T(8,128)(2,1)S(1)}, bf16[8,512,128]{2,1,0:T(8,128)(2,1)}, u32[]{:S(2)}) copy-start(bf16[8,512,128]{2,1,0:T(8,128)(2,1)} %copy-done.4) | copy-start | bytes 3145732
  119.5 2.3 %copy-start.2 = (bf16[8,512,128]{2,1,0:T(8,128)(2,1)}, bf16[8,512,128]{2,1,0:T(8,128)(2,1)S(1)}, u32[]{:S(2)}) copy-start(bf16[8,512,128]{2,1,0:T(8,128)(2,1)S(1)} %collective-permute-done.8.refs_4_) | copy-start | bytes 3145732
  121.8 45.0 %all-gather.15.cloned.1.call-start = ((), (), s32[]{:S(2)}) async-start(), calls=%async_computation.5 | async-start | bytes 3145728 | tf_op jit(solution)/shard_map/all_gather | solution.py:202
  121.9 24.6 %collective-permute-start.14 = (bf16[8,512,128]{2,1,0:T(8,128)(2,1)}, bf16[8,512,128]{2,1,0:T(8,128)(2,1)}, u32[]{:S(2)}, u32[]{:S(2)}) collective-permute-start(bf16[8,512,128]{2,1,0:T(8,128)(2,1)} %copy-done.2), channel_id=1, source_target_pairs={{0,32},{32,64},{64,96},{96,0},{1,33},{33,65},{65,97},{97,1},{2,34}... | collective-permute-start | bytes 3145736 | tf_op jit(solution)/shard_map/ppermute | solution.py:198
  122.0 23.1 %collective-permute-start.13 = (bf16[8,512,128]{2,1,0:T(8,128)(2,1)S(1)}, bf16[8,512,128]{2,1,0:T(8,128)(2,1)}, u32[]{:S(2)}, u32[]{:S(2)}) collective-permute-start(bf16[8,512,128]{2,1,0:T(8,128)(2,1)S(1)} %copy-done.5), channel_id=1, source_target_pairs={{0,96},{32,0},{64,32},{96,64},{1,97},{33,1},{65,33},{97,65},{2,98}... | collective-permute-start | bytes 3145736 | tf_op jit(solution)/shard_map/ppermute | solution.py:199
  124.6 24.1 %collective-permute-start.15 = (bf16[8,512,128]{2,1,0:T(8,128)(2,1)}, bf16[8,512,128]{2,1,0:T(8,128)(2,1)S(1)}, u32[]{:S(2)}, u32[]{:S(2)}) collective-permute-start(bf16[8,512,128]{2,1,0:T(8,128)(2,1)} %collective-permute-done.refs_2_), channel_id=1, source_target_pairs={{0,16},{16,0},{1,17},{17,1},{2,18},{18,2},{3,19},{19,3},{4,20},{20... | collective-permute-start | bytes 3145736 | tf_op jit(solution)/shard_map/ppermute | solution.py:200
  126.0 22.8 %collective-permute-start.16 = (bf16[8,512,128]{2,1,0:T(8,128)(2,1)}, bf16[8,512,128]{2,1,0:T(8,128)(2,1)}, u32[]{:S(2)}, u32[]{:S(2)}) collective-permute-start(bf16[8,512,128]{2,1,0:T(8,128)(2,1)} %collective-permute-done.9.refs_0_), channel_id=1, source_target_pairs={{0,8},{8,0},{1,9},{9,1},{2,10},{10,2},{3,11},{11,3},{4,12},{12,4},... | collective-permute-start | bytes 3145736 | tf_op jit(solution)/shard_map/ppermute | solution.py:201
  128.1 20.7 %collective-permute-start.17 = (bf16[8,512,128]{2,1,0:T(8,128)(2,1)}, bf16[8,512,128]{2,1,0:T(8,128)(2,1)}, u32[]{:S(2)}, u32[]{:S(2)}) collective-permute-start(bf16[8,512,128]{2,1,0:T(8,128)(2,1)} %collective-permute-done.10.refs_2_), channel_id=1, source_target_pairs={{0,8},{8,0},{1,9},{9,1},{2,10},{10,2},{3,11},{11,3},{4,12},{12,4},... | collective-permute-start | bytes 3145736 | tf_op jit(solution)/shard_map/ppermute | solution.py:201
  128.7 24.4 %copy-start.3 = (bf16[8,512,128]{2,1,0:T(8,128)(2,1)S(1)}, bf16[8,512,128]{2,1,0:T(8,128)(2,1)}, u32[]{:S(2)}) copy-start(bf16[8,512,128]{2,1,0:T(8,128)(2,1)} %copy-done.2) | copy-start | bytes 3145732
  148.8 1.0 copy-start.6
  149.8 17.0 %collective-permute-start.21 = (bf16[8,512,128]{2,1,0:T(8,128)(2,1)}, bf16[8,512,128]{2,1,0:T(8,128)(2,1)}, u32[]{:S(2)}, u32[]{:S(2)}) collective-permute-start(bf16[8,512,128]{2,1,0:T(8,128)(2,1)} %collective-permute-done.13.refs_0_), channel_id=1, source_target_pairs={{0,8},{8,0},{1,9},{9,1},{2,10},{10,2},{3,11},{11,3},{4,12},{12,4},... | collective-permute-start | bytes 3145736 | tf_op jit(solution)/shard_map/ppermute | solution.py:201
  153.1 13.8 %collective-permute-start.22 = (bf16[8,512,128]{2,1,0:T(8,128)(2,1)}, bf16[8,512,128]{2,1,0:T(8,128)(2,1)}, u32[]{:S(2)}, u32[]{:S(2)}) collective-permute-start(bf16[8,512,128]{2,1,0:T(8,128)(2,1)} %collective-permute-done.14.refs_2_), channel_id=1, source_target_pairs={{0,8},{8,0},{1,9},{9,1},{2,10},{10,2},{3,11},{11,3},{4,12},{12,4},... | collective-permute-start | bytes 3145736 | tf_op jit(solution)/shard_map/ppermute | solution.py:201
  153.2 25.9 %collective-permute-start.18 = (bf16[8,512,128]{2,1,0:T(8,128)(2,1)}, bf16[8,512,128]{2,1,0:T(8,128)(2,1)S(1)}, u32[]{:S(2)}, u32[]{:S(2)}) collective-permute-start(bf16[8,512,128]{2,1,0:T(8,128)(2,1)} %copy-done.6), channel_id=1, source_target_pairs={{0,32},{32,64},{64,96},{96,0},{1,33},{33,65},{65,97},{97,1},{2,34}... | collective-permute-start | bytes 3145736 | tf_op jit(solution)/shard_map/ppermute | solution.py:198
  153.2 25.8 %collective-permute-start.19 = (bf16[8,512,128]{2,1,0:T(8,128)(2,1)S(1)}, bf16[8,512,128]{2,1,0:T(8,128)(2,1)S(1)}, u32[]{:S(2)}, u32[]{:S(2)}) collective-permute-start(bf16[8,512,128]{2,1,0:T(8,128)(2,1)S(1)} %copy-done.3), channel_id=1, source_target_pairs={{0,96},{32,0},{64,32},{96,64},{1,97},{33,1},{65,33},{97,65},{2,98}... | collective-permute-start | bytes 3145736 | tf_op jit(solution)/shard_map/ppermute | solution.py:199
  155.8 25.5 %collective-permute-start.20 = (bf16[8,512,128]{2,1,0:T(8,128)(2,1)}, bf16[8,512,128]{2,1,0:T(8,128)(2,1)}, u32[]{:S(2)}, u32[]{:S(2)}) collective-permute-start(bf16[8,512,128]{2,1,0:T(8,128)(2,1)} %collective-permute-done.10.refs_2_), channel_id=1, source_target_pairs={{0,16},{16,0},{1,17},{17,1},{2,18},{18,2},{3,19},{19,3},{4,20},{20... | collective-permute-start | bytes 3145736 | tf_op jit(solution)/shard_map/ppermute | solution.py:200
  179.0 9.9 %copy-start.8 = (bf16[8,512,128]{2,1,0:T(8,128)(2,1)}, bf16[8,512,128]{2,1,0:T(8,128)(2,1)S(1)}, u32[]{:S(2)}) copy-start(bf16[8,512,128]{2,1,0:T(8,128)(2,1)S(1)} %collective-permute-done.18.refs_0_) | copy-start | bytes 3145732
  179.0 9.9 %copy-start.9 = (bf16[8,512,128]{2,1,0:T(8,128)(2,1)}, bf16[8,512,128]{2,1,0:T(8,128)(2,1)S(1)}, u32[]{:S(2)}) copy-start(bf16[8,512,128]{2,1,0:T(8,128)(2,1)S(1)} %collective-permute-done.19.refs_2_) | copy-start | bytes 3145732
  181.3 5.6 %collective-permute-start.23 = (bf16[8,512,128]{2,1,0:T(8,128)(2,1)S(1)}, bf16[8,512,128]{2,1,0:T(8,128)(2,1)S(1)}, u32[]{:S(2)}, u32[]{:S(2)}) collective-permute-start(bf16[8,512,128]{2,1,0:T(8,128)(2,1)S(1)} %collective-permute-done.18.refs_0_), channel_id=1, source_target_pairs={{0,8},{8,0},{1,9},{9,1},{2,10},{10,2},{3,11},{11,3},{4,12},{12,4},... | collective-permute-start | bytes 3145736 | tf_op jit(solution)/shard_map/ppermute | solution.py:201
  183.2 5.3 %collective-permute-start.24 = (bf16[8,512,128]{2,1,0:T(8,128)(2,1)S(1)}, bf16[8,512,128]{2,1,0:T(8,128)(2,1)}, u32[]{:S(2)}, u32[]{:S(2)}) collective-permute-start(bf16[8,512,128]{2,1,0:T(8,128)(2,1)S(1)} %collective-permute-done.19.refs_2_), channel_id=1, source_target_pairs={{0,8},{8,0},{1,9},{9,1},{2,10},{10,2},{3,11},{11,3},{4,12},{12,4},... | collective-permute-start | bytes 3145736 | tf_op jit(solution)/shard_map/ppermute | solution.py:201
  183.2 5.6 %collective-permute-start.25 = (bf16[8,512,128]{2,1,0:T(8,128)(2,1)}, bf16[8,512,128]{2,1,0:T(8,128)(2,1)}, u32[]{:S(2)}, u32[]{:S(2)}) collective-permute-start(bf16[8,512,128]{2,1,0:T(8,128)(2,1)} %collective-permute-done.20.refs_4_), channel_id=1, source_target_pairs={{0,8},{8,0},{1,9},{9,1},{2,10},{10,2},{3,11},{11,3},{4,12},{12,4},... | collective-permute-start | bytes 3145736 | tf_op jit(solution)/shard_map/ppermute | solution.py:201
  187.0 1.9 copy-start.10
Sparse Core Ops, SparseCore 0:
  61.3 13.8 all-gather.8
  87.3 16.4 all-gather.10
  122.0 11.6 all-gather.12
  149.9 12.4 all-gather.14

commit v4 on v3

v4 whole, which is shorter than its diff:
```python
import functools

import jax
import jax.numpy as jnp
import numpy as np
from jax import lax
from jax.experimental import pallas as pl
from jax.experimental.pallas import tpu as pltpu
from jax.sharding import Mesh, PartitionSpec as P

FFT_LEN = 512
BINS = 128
BAND_LO = 16
OWNERS = 8
CHUNK = 4
SEG_STEP = 8
MIB = 1024 * 1024


def spectra_table():
    sample = np.arange(FFT_LEN)
    bins = (BAND_LO + np.arange(BINS)).reshape(OWNERS, 2, 2, CHUNK).transpose(2, 0, 1, 3).reshape(-1)
    phase = (sample[:, None] * bins[None, :] % FFT_LEN) * (2.0 * np.pi / FFT_LEN)
    taper = 0.5 - 0.5 * np.cos(2.0 * np.pi * sample / FFT_LEN)
    table = np.stack([np.cos(phase), -np.sin(phase)], axis=2).reshape(FFT_LEN, 2 * BINS) * taper[:, None]
    high = table.astype(jnp.bfloat16)
    low = (table - high.astype(np.float64)).astype(jnp.bfloat16)
    return high, low


def whiten_kernel(records_ref, available_ref, high_ref, low_ref, first_ref, second_ref, rows_ref, turned_ref):
    stations, segs, samples = records_ref.shape
    flat = records_ref[...].reshape(stations * segs, samples)
    spectra = jnp.dot(flat, high_ref[...], preferred_element_type=jnp.float32)
    spectra += jnp.dot(flat, low_ref[...], preferred_element_type=jnp.float32)
    wide = spectra.shape[1]
    for part in range(2):
        rows_ref[part] = spectra[:, part * BINS : (part + 1) * BINS]
    for seg in range(segs):
        turned = jnp.concatenate(
            [rows_ref[part, pl.ds(seg, stations, stride=segs), :].T for part in range(2)], axis=0
        )
        power = jnp.sum(turned * turned, axis=0, keepdims=True) / BINS
        weight = available_ref[seg : seg + 1, :].astype(jnp.float32) / jnp.sqrt(power + 1e-05)
        turned_ref[pl.ds(seg, wide, stride=segs), :] = turned * weight
    whitened = turned_ref[...].reshape(2, 2 * OWNERS, CHUNK, 2, segs, stations).astype(jnp.bfloat16)
    first_ref[...] = whitened[0]
    second_ref[...] = whitened[1]


def whiten(records, available):
    stations, segments, samples = records.shape
    high, low = spectra_table()
    half = jax.ShapeDtypeStruct((2 * OWNERS, CHUNK, 2, segments, stations), jnp.bfloat16)
    half_spec = pl.BlockSpec((2 * OWNERS, CHUNK, 2, SEG_STEP, stations), lambda i: (0, 0, 0, i, 0))
    return pl.pallas_call(
        whiten_kernel,
        grid=(segments // SEG_STEP,),
        in_specs=[
            pl.BlockSpec((stations, SEG_STEP, samples), lambda i: (0, i, 0)),
            pl.BlockSpec((SEG_STEP, stations), lambda i: (i, 0)),
            pl.BlockSpec((samples, 2 * BINS), lambda i: (0, 0)),
            pl.BlockSpec((samples, 2 * BINS), lambda i: (0, 0)),
        ],
        out_specs=[half_spec, half_spec],
        out_shape=[half, half],
        scratch_shapes=[
            pltpu.VMEM((2, stations * SEG_STEP, BINS), jnp.float32),
            pltpu.VMEM((2 * BINS * SEG_STEP, stations), jnp.float32),
        ],
        compiler_params=pltpu.CompilerParams(vmem_limit_bytes=60 * MIB),
        name="whiten",
    )(records, available.T, jnp.asarray(high), jnp.asarray(low))


def rows_kernel(panel_ref, mine_ref):
    bins, depth, width = panel_ref.shape
    half, rows = depth // 2, width // 2
    for f in range(bins):
        for core in range(2):
            real = panel_ref[f, :half, core * rows : (core + 1) * rows].T
            imag = panel_ref[f, half:, core * rows : (core + 1) * rows].T
            base = 2 * rows * core
            mine_ref[f, base : base + rows, :half] = real
            mine_ref[f, base : base + rows, half:] = imag
            mine_ref[f, base + rows : base + 2 * rows, :half] = imag
            mine_ref[f, base + rows : base + 2 * rows, half:] = -real


def rows_of(panel):
    bins, depth, width = panel.shape
    return pl.pallas_call(
        rows_kernel,
        grid=(bins,),
        in_specs=[pl.BlockSpec((1, depth, width), lambda f: (f, 0, 0))],
        out_specs=pl.BlockSpec((1, 2 * width, depth), lambda f: (f, 0, 0)),
        out_shape=jax.ShapeDtypeStruct((bins, 2 * width, depth), panel.dtype),
        compiler_params=pltpu.CompilerParams(vmem_limit_bytes=60 * MIB),
        name="rows",
    )(panel)


def placing(where, count, placed, sent_ref, out_ref, place_sem):
    core = where[count]
    for at, chunk in enumerate(placed):
        bins, cols = sent_ref.shape[2], sent_ref.shape[4]
        spot = pl.ds(pl.multiple_of(where[count + 1 + at] * cols, cols), cols)
        first = (1 - core) * 2 * CHUNK + chunk * CHUNK
        yield pltpu.make_async_copy(
            sent_ref.at[at], out_ref.at[:, pl.ds(first, bins), :, spot], place_sem.at[at]
        )


def gram_kernel(scale, chunks, placed, where, mine0_ref, mine1_ref, *refs):
    count = len(chunks)
    panels, rest = refs[:count], refs[count:]
    sent_ref = rest[0] if placed else None
    out_ref, send_ref, slots, sems, place_sem = rest[-5:]
    step, steps = pl.program_id(0), pl.num_programs(0)
    rows, cols = mine0_ref.shape[1] // 4, panels[0].shape[2]
    slot, core = lax.rem(step, 2), where[count]

    def writes(at, block, held):
        spot = pl.ds(pl.multiple_of(where[block] * cols, cols), cols)
        first = core * 2 * CHUNK + chunks[block] * CHUNK + at
        return (
            pltpu.make_async_copy(
                slots.at[held, block, core],
                out_ref.at[:, first, :, spot],
                sems.at[held, block, 0],
            ),
            pltpu.make_async_copy(
                slots.at[held, block, 1 - core],
                send_ref.at[block, :, at],
                sems.at[held, block, 1],
            ),
        )

    def place():
        return placing(where, count, placed, sent_ref, out_ref, place_sem)

    @pl.when(step == 0)
    def _():
        for copy in place():
            copy.start()

    @pl.when(step >= 2)
    def _():
        for block in range(count):
            for copy in writes(step - 2, block, slot):
                copy.wait()

    for block in range(count):
        mine_ref = mine1_ref if chunks[block] else mine0_ref
        gram = jnp.dot(mine_ref[0], panels[block][0], preferred_element_type=jnp.float32) * scale
        gram = gram.astype(jnp.bfloat16)
        for target in range(2):
            for part in range(2):
                base = (2 * target + part) * rows
                slots[slot, block, target, part] = gram[base : base + rows]
        for copy in writes(step, block, slot):
            copy.start()

    @pl.when(step == steps - 1)
    def _():
        for block in range(count):
            for copy in (*writes(step - 1, block, 1 - slot), *writes(step, block, slot)):
                copy.wait()
        for copy in place():
            copy.wait()


def gram(core, mine, blocks, shape, out, sent):
    bins, depth, cols = blocks[0][3].shape
    rows = shape[2]
    count = len(blocks)
    chunks = [block[0] for block in blocks]
    placed = [block[0] for block in sent[0]] if sent else []
    where = [block[1] for block in blocks] + [core] + ([block[2] for block in sent[0]] if sent else [])
    held = ([sent[1]] if sent else []) + ([] if out is None else [out])
    used = [
        pl.BlockSpec((1, 4 * rows, depth), (lambda f, w: (f, 0, 0)) if chunk in chunks else (lambda f, w: (0, 0, 0)))
        for chunk in range(2)
    ]
    send = jax.ShapeDtypeStruct((count, 2, bins, rows, cols), jnp.bfloat16)
    return pl.pallas_call(
        functools.partial(gram_kernel, 2.0 / depth, chunks, placed),
        grid_spec=pltpu.PrefetchScalarGridSpec(
            num_scalar_prefetch=1,
            grid=(bins,),
            in_specs=used
            + [pl.BlockSpec((1, depth, cols), lambda f, w: (f, 0, 0))] * count
            + [pl.BlockSpec(memory_space=pl.ANY)] * len(held),
            out_specs=[pl.BlockSpec(memory_space=pl.ANY)] * 2,
            scratch_shapes=[
                pltpu.VMEM((2, count, 2, 2, rows, cols), jnp.bfloat16),
                pltpu.SemaphoreType.DMA((2, count, 2)),
                pltpu.SemaphoreType.DMA((4,)),
            ],
        ),
        out_shape=[jax.ShapeDtypeStruct(shape, jnp.bfloat16), send],
        input_output_aliases={2 + count + len(held): 0} if out is not None else {},
        cost_estimate=pl.CostEstimate(
            flops=8 * count * bins * rows * depth * cols,
            bytes_accessed=2 * bins * (8 * rows * depth + count * (depth * cols + 4 * rows * cols)),
            transcendentals=0,
        ),
        compiler_params=pltpu.CompilerParams(vmem_limit_bytes=60 * MIB),
        name="gram",
    )(jnp.stack(where).astype(jnp.int32), *mine, *[block[3] for block in blocks], *held)


def place_kernel(placed, where, sent_ref, _, out_ref, place_sem):
    for copy in placing(where, 0, placed, sent_ref, out_ref, place_sem):
        copy.start()
    for copy in placing(where, 0, placed, sent_ref, out_ref, place_sem):
        copy.wait()


def place(core, sent, out):
    return pl.pallas_call(
        functools.partial(place_kernel, [block[0] for block in sent[0]]),
        grid_spec=pltpu.PrefetchScalarGridSpec(
            num_scalar_prefetch=1,
            grid=(1,),
            in_specs=[pl.BlockSpec(memory_space=pl.ANY)] * 2,
            out_specs=pl.BlockSpec(memory_space=pl.ANY),
            scratch_shapes=[pltpu.SemaphoreType.DMA((4,))],
        ),
        out_shape=jax.ShapeDtypeStruct(out.shape, out.dtype),
        input_output_aliases={2: 0},
        compiler_params=pltpu.CompilerParams(vmem_limit_bytes=60 * MIB),
        name="place",
    )(jnp.stack([core] + [block[2] for block in sent[0]]).astype(jnp.int32), sent[1], out)


def mirrored(step):
    return [
        (2 * x + core, (x + (1 - 2 * core) * step) % 4 * 2 + core) for x in range(4) for core in range(2)
    ]


def shards(records, available):
    stations = records.shape[0]
    x, yh, core = lax.axis_index("x"), lax.axis_index("yh"), lax.axis_index("core")
    fwd = lambda v: lax.ppermute(v, ("x", "core"), mirrored(1))
    bwd = lambda v: lax.ppermute(v, ("x", "core"), mirrored(-1))
    over = lambda v: lax.ppermute(v, "yh", [(0, 1), (1, 0)])
    swap = lambda v: lax.ppermute(v, "core", [(0, 1), (1, 0)])
    gate = lambda *values: lax.optimization_barrier(values)

    def owned(chunk):
        got = lax.all_to_all(chunk, ("yl", "z", "core"), split_axis=0, concat_axis=0, tiled=True)
        got = got.reshape(OWNERS, 2, *got.shape[1:])
        return jnp.transpose(got, (2, 3, 0, 4, 1, 5)).reshape(CHUNK, -1, 2 * stations)

    def entry(chunk, dx, dy, panel):
        sign = 1 - 2 * core
        chips = [(x - way * dx) % 4 * 2 + (yh + dy) % 2 for way in (sign, -sign)]
        return chunk, *chips, panel

    shape = (2, 4 * CHUNK, stations, 16 * stations)
    first, second = whiten(records, available)
    pa = owned(first)
    pa, second = gate(pa, second)

    na, ba, pb, ma = fwd(pa), bwd(pa), owned(second), rows_of(pa)
    pa, pb, na, ba, ma = gate(pa, pb, na, ba, ma)

    nb, bb, oa, mb = fwd(pb), bwd(pb), over(pa), rows_of(pb)
    blocks1 = [entry(0, 0, 0, pa), entry(0, 1, 0, na), entry(0, -1, 0, ba)]
    out, sent = gram(core, (ma, ma), blocks1, shape, None, None)
    na, nb, bb, oa, mb, pb, out, sent = gate(na, nb, bb, oa, mb, pb, out, sent)
    mine = ma, mb

    fa, fb, ob, sent1 = fwd(na), fwd(nb), over(pb), swap(sent)
    blocks2 = [entry(1, 0, 0, pb), entry(1, 1, 0, nb), entry(1, -1, 0, bb), entry(0, 0, 1, oa)]
    out, sent = gram(core, mine, blocks2, shape, out, None)
    na, oa, fa, fb, ob, sent1, out, sent = gate(na, oa, fa, fb, ob, sent1, out, sent)

    boa, bob, noa, sent2 = bwd(oa), bwd(ob), over(na), swap(sent)
    blocks3 = [entry(0, 2, 0, fa), entry(1, 2, 0, fb), entry(1, 0, 1, ob)]
    out, sent = gram(core, mine, blocks3, shape, out, (blocks1, sent1))
    ob, fb, boa, bob, noa, sent2, out, sent = gate(ob, fb, boa, bob, noa, sent2, out, sent)

    foa, nob, fob, sent3 = fwd(noa), fwd(ob), over(fb), swap(sent)
    blocks4 = [entry(0, -1, 1, boa), entry(1, -1, 1, bob), entry(0, 1, 1, noa)]
    out, sent = gram(core, mine, blocks4, shape, out, (blocks2, sent2))
    foa, nob, fob, sent3, out, sent = gate(foa, nob, fob, sent3, out, sent)

    sent4 = swap(sent)
    blocks5 = [entry(0, 2, 1, foa), entry(1, 1, 1, nob), entry(1, 2, 1, fob)]
    out, sent = gram(core, mine, blocks5, shape, out, (blocks3, sent3))
    sent5 = swap(sent)
    out = place(core, (blocks4, sent4), out)
    return place(core, (blocks5, sent5), out)


def solution(mesh):
    fine = Mesh(mesh.devices.reshape(4, 2, 2, 2, 4), ("x", "yh", "core", "yl", "z"))
    sta, freq = ("x", "yh", "core"), ("yl", "z")
    return jax.shard_map(
        shards,
        mesh=fine,
        in_specs=(P(sta, freq, None), P(sta, freq)),
        out_specs=P(None, freq, sta, None),
        check_vma=False,
    )
```

time: 204 us -> 403 us (1.98)
  Pallas kernels: 63.1 us -> 301 us
  waiting for transfers between devices: 57.4 us -> 37.1 us
  starting transfers between devices: 41.9 us -> 26.5 us
  between operations: 13.3 us -> 0.35 us
  local copies, waits for them, and re-layouts: 3.15 us -> 12.4 us
    pallas_call x8 -> x9, Pallas kernels: 55.3 us -> 294 us  [the longest x5 187 us: gram(): pl.pallas_call(functools.partial(gram_kernel, 2.0 / depth, chunks, placed...]
    ppermute x26 -> x19, waiting for transfers between devices: 46 us -> 24.9 us  [the longest x6 17 us: shards(): fwd = lambda v: lax.ppermute(v, ('x', 'core'), mirrored(1))]
    ppermute x26 -> x19, starting transfers between devices: 38.2 us -> 21.2 us  [the longest x4 8.21 us: shards(): over = lambda v: lax.ppermute(v, 'yh', [(0, 1), (1, 0)])]
    reshape x0 -> x4, local copies, waits for them, and re-layouts: none -> 5.2 us  [the longest x2 3.04 us: owned(): jnp.transpose(got, (2, 3, 0, 4, 1, 5)).reshape(CHUNK, -1, 2 * stations)]
  transfers between devices with their start and end apart: 31 -> 20, of which waited for: 15 -> 6; matrix products, arithmetic and copies ran while one was open for 2% -> 2% of each run, Pallas kernels for 23% -> 61%
where the time goes in v4:
time: 403 us; the launch traced here: 402 us
  Pallas kernels  301 us (75%)
  waiting for transfers between devices  37.1 us (9%)
  starting transfers between devices  26.5 us (7%)
  blocking collectives  23.3 us (6%)
  local copies, waits for them, and re-layouts  12.4 us (3%)
    pallas_call x5, Pallas kernels, gram(): pl.pallas_call(functools.partial(gram_kernel, 2.0 / depth, chunks, placed...  187 us
    pallas_call x2, Pallas kernels, place(): pl.pallas_call(functools.partial(place_kernel, [block[0] for block in sen...  98.9 us
    all_to_all x1, blocking collectives, owned(): lax.all_to_all(chunk, ('yl', 'z', 'core'), split_axis=0, concat_axis=0, t...  23.3 us
    ppermute x6, waiting for transfers between devices, shards(): fwd = lambda v: lax.ppermute(v, ('x', 'core'), mirrored(1))  17 us
    all_to_all x1, waiting for transfers between devices, owned(): lax.all_to_all(chunk, ('yl', 'z', 'core'), split_axis=0, concat_axis=0, t...  12.2 us
    ppermute x4, starting transfers between devices, shards(): over = lambda v: lax.ppermute(v, 'yh', [(0, 1), (1, 0)])  8.21 us
  transfers between devices with their start and end apart: 20, of which 6 were waited for; matrix products, arithmetic and copies ran while one was open for 2% of the time, Pallas kernels for 61%

profile of v4, /device:TPU:1, one launch (start us, length us, event | category | flops | bytes accessed | tf_op | source)
XLA Modules:
  0.0 402.0 jit_solution(10894001648781780958)
XLA Ops:
  0.0 7.8 %whiten.1 = (bf16[16,4,2,32,128]{4,3,2,1,0:T(8,128)(2,1)}, bf16[16,4,2,32,128]{4,3,2,1,0:T(8,128)(2,1)}) custom-call(bf16[128,32,512]{2,1,0:T(8,128)(2,1)} %records_ref.1, s32[32,128]{1,0:T(8,128)} %bitcast.28, bf16[512,256]{1,0:T(8,128)(2,1)} %constant.183.clone.high_ref, bf16[512,256]{1,0:T(8,128)(2,1)} %constant.184.clone.low_ref), custom_call_target="tpu_custom_call" | custom-call | tf_op jit(solution)/shard_map/whiten/pallas_call | solution.py:56
  7.8 23.3 %all_to_all.10 = bf16[16,4,2,32,128]{4,3,2,1,0:T(8,128)(2,1)S(1)} all-to-all(bf16[16,4,2,32,128]{4,3,2,1,0:T(8,128)(2,1)} %get-tuple-element.54), channel_id=1, replica_groups=mesh['x'=4,'yh'=2,'core'=2,'yl'=2,'z'=4] {'yl','z','core'}, dimensions={0} | all-to-all | bytes 2097152 | tf_op jit(solution)/shard_map/all_to_all | solution.py:253
  31.1 1.1 copy.16
  32.1 1.5 reshape.13.panel_ref.refs_0_
  33.7 2.5 collective-permute-start
  36.1 0.0 collective-permute-start.1
  36.1 5.4 %all-to-all-start.1 = ((bf16[16,4,2,32,128]{4,3,2,1,0:T(8,128)(2,1)}), bf16[16,4,2,32,128]{4,3,2,1,0:T(8,128)(2,1)S(1)}, u32[]{:S(2)}, u32[]{:S(2)}) async-start(bf16[16,4,2,32,128]{4,3,2,1,0:T(8,128)(2,1)} %get-tuple-element.57), calls=%async_computation.1 | async-start | bytes 2097152 | tf_op jit(solution)/shard_map/all_to_all | solution.py:253
  41.5 3.8 rows.2.mine0_ref.mine1_ref
  45.3 12.2 %all-to-all-done.1 = bf16[16,4,2,32,128]{4,3,2,1,0:T(8,128)(2,1)S(1)} async-done(((bf16[16,4,2,32,128]{4,3,2,1,0:T(8,128)(2,1)}), bf16[16,4,2,32,128]{4,3,2,1,0:T(8,128)(2,1)S(1)}, u32[]{:S(2)}, u32[]{:S(2)}) %all-to-all-start.1) | async-done | bytes 1048608 | tf_op jit(solution)/shard_map/all_to_all | solution.py:253
  57.4 1.1 copy.15
  58.5 1.5 reshape.15.panel_ref.refs_0_
  60.0 0.0 collective-permute-done.refs_1_
  60.0 1.7 collective-permute-done.1.refs_2_
  61.7 0.6 collective-permute-start.2
  62.3 0.9 collective-permute-start.3
  63.2 2.6 collective-permute-start.4
  65.8 0.6 pad_add_fusion.1.where
  66.4 3.8 rows.3.mine1_ref
  70.2 8.3 %gram.5 = (bf16[2,16,128,2048]{3,2,1,0:T(8,128)(2,1)}, bf16[3,2,4,128,256]{4,3,2,1,0:T(8,128)(2,1)}) custom-call(s32[4]{0:T(128)} %pad_add_fusion.1.where, bf16[4,512,512]{2,1,0:T(8,128)(2,1)} %rows.2.mine0_ref.mine1_ref, bf16[4,512,512]{2,1,0:T(8,128)(2,1)} %rows.2.mine0_ref.mine1_ref, bf16[4,512,256]{2,1,0:T(8,128)(2,1)} %reshape.13.panel_ref.refs_0_, ...), custom_call_target="tpu_custom_call" | custom-call | flops 1610612736 | bytes 10485760 | tf_op jit(solution)/shard_map/gram/pallas_call | solution.py:186
  78.4 6.6 %collective-permute-done.2.refs_1_ = bf16[4,512,256]{2,1,0:T(8,128)(2,1)S(1)} collective-permute-done((bf16[4,512,256]{2,1,0:T(8,128)(2,1)}, bf16[4,512,256]{2,1,0:T(8,128)(2,1)S(1)}, u32[]{:S(2)}, u32[]{:S(2)}) %collective-permute-start.2) | collective-permute-done | bytes 1048608 | tf_op jit(solution)/shard_map/ppermute | solution.py:246
  85.0 3.3 collective-permute-done.3.refs_2_
  88.3 0.0 collective-permute-done.4.refs_3_
  88.3 1.0 copy-done.6
  89.3 1.3 collective-permute-start.8
  90.6 1.7 collective-permute-start.5
  92.3 0.0 collective-permute-start.6
  92.4 2.6 collective-permute-start.7
  95.0 0.7 stack.103.where
  95.7 10.0 %gram.6 = (bf16[2,16,128,2048]{3,2,1,0:T(8,128)(2,1)}, bf16[4,2,4,128,256]{4,3,2,1,0:T(8,128)(2,1)}) custom-call(s32[5]{0:T(128)} %stack.103.where, bf16[4,512,512]{2,1,0:T(8,128)(2,1)} %rows.2.mine0_ref.mine1_ref, bf16[4,512,512]{2,1,0:T(8,128)(2,1)} %rows.3.mine1_ref, ...), custom_call_target="tpu_custom_call", output_to_operand_aliasing={{0}: (7, {})} | custom-call | flops 2147483648 | bytes 12582912 | tf_op jit(solution)/shard_map/gram/pallas_call | solution.py:186
  105.6 0.0 collective-permute-done.5.refs_0_
  105.7 10.4 %collective-permute-done.6.refs_1_ = bf16[4,512,256]{2,1,0:T(8,128)(2,1)} collective-permute-done((bf16[4,512,256]{2,1,0:T(8,128)(2,1)}, bf16[4,512,256]{2,1,0:T(8,128)(2,1)}, u32[]{:S(2)}, u32[]{:S(2)}) %collective-permute-start.6) | collective-permute-done | bytes 1048608 | tf_op jit(solution)/shard_map/ppermute | solution.py:246
  116.1 2.9 collective-permute-done.7.refs_2_
  119.0 0.0 collective-permute-done.8.refs_3_
  119.0 1.2 copy-done.3
  120.2 0.4 collective-permute-start.12
  120.6 1.8 collective-permute-start.10
  122.4 2.6 collective-permute-start.11
  125.1 0.0 collective-permute-start.9
  125.1 0.7 stack.107.where
  125.7 51.0 %gram.7 = (bf16[2,16,128,2048]{3,2,1,0:T(8,128)(2,1)}, bf16[3,2,4,128,256]{4,3,2,1,0:T(8,128)(2,1)}) custom-call(s32[7]{0:T(128)} %stack.107.where, bf16[4,512,512]{2,1,0:T(8,128)(2,1)} %rows.2.mine0_ref.mine1_ref, bf16[4,512,512]{2,1,0:T(8,128)(2,1)} %rows.3.mine1_ref, ...), custom_call_target="tpu_custom_call", output_to_operand_aliasing={{0}: (7, {})} | custom-call | flops 1610612736 | bytes 10485760 | tf_op jit(solution)/shard_map/gram/pallas_call | solution.py:186
  176.7 0.0 collective-permute-done.10.refs_1_
  176.7 0.0 collective-permute-done.11.refs_2_
  176.7 0.0 collective-permute-done.9.refs_0_
  176.8 0.0 collective-permute-done.12.refs_3_
  176.8 1.2 collective-permute-start.16
  178.0 1.7 collective-permute-start.13
  179.8 0.0 collective-permute-start.14
  179.8 0.3 collective-permute-start.15
  180.2 0.7 stack.109.where
  180.8 0.6 stack.98.where
  181.4 66.9 %gram.8 = (bf16[2,16,128,2048]{3,2,1,0:T(8,128)(2,1)}, bf16[3,2,4,128,256]{4,3,2,1,0:T(8,128)(2,1)}) custom-call(s32[8]{0:T(128)} %stack.109.where, bf16[4,512,512]{2,1,0:T(8,128)(2,1)} %rows.2.mine0_ref.mine1_ref, bf16[4,512,512]{2,1,0:T(8,128)(2,1)} %rows.3.mine1_ref, ...), custom_call_target="tpu_custom_call", output_to_operand_aliasing={{0}: (7, {})} | custom-call | flops 1610612736 | bytes 10485760 | tf_op jit(solution)/shard_map/gram/pallas_call | solution.py:186
  248.3 0.0 collective-permute-done.13.refs_0_
  248.3 0.0 collective-permute-done.14.refs_1_
  248.3 0.0 collective-permute-done.15.refs_2_
  248.3 0.0 collective-permute-done.16.refs_3_
  248.3 0.2 collective-permute-start.18
  248.5 51.0 %gram.9 = (bf16[2,16,128,2048]{3,2,1,0:T(8,128)(2,1)}, bf16[3,2,4,128,256]{4,3,2,1,0:T(8,128)(2,1)}) custom-call(s32[7]{0:T(128)} %stack.98.where, bf16[4,512,512]{2,1,0:T(8,128)(2,1)} %rows.2.mine0_ref.mine1_ref, bf16[4,512,512]{2,1,0:T(8,128)(2,1)} %rows.3.mine1_ref, ...), custom_call_target="tpu_custom_call", output_to_operand_aliasing={{0}: (7, {})} | custom-call | flops 1610612736 | bytes 10485760 | tf_op jit(solution)/shard_map/gram/pallas_call | solution.py:186
  299.5 0.5 collective-permute-start.17
  300.0 0.6 pad_add_fusion
  300.6 1.2 copy-done.1
  301.8 49.4 %place.2._ = bf16[2,16,128,2048]{3,2,1,0:T(8,128)(2,1)} custom-call(s32[4]{0:T(128)} %get-tuple-element.104.where, bf16[3,2,4,128,256]{4,3,2,1,0:T(8,128)(2,1)} %copy-done.1, bf16[2,16,128,2048]{3,2,1,0:T(8,128)(2,1)} %get-tuple-element.102._), custom_call_target="tpu_custom_call", output_to_operand_aliasing={{}: (2, {})} | custom-call | tf_op jit(solution)/shard_map/place/pallas_call | solution.py:221
  351.2 0.0 collective-permute-done.17.sent_ref
  351.3 1.2 copy-done.2
  352.4 49.4 %place.3 = bf16[2,16,128,2048]{3,2,1,0:T(8,128)(2,1)} custom-call(s32[4]{0:T(128)} %get-tuple-element.103.where, bf16[3,2,4,128,256]{4,3,2,1,0:T(8,128)(2,1)} %copy-done.2, bf16[2,16,128,2048]{3,2,1,0:T(8,128)(2,1)} %place.2._), custom_call_target="tpu_custom_call", output_to_operand_aliasing={{}: (2, {})} | custom-call | tf_op jit(solution)/shard_map/place/pallas_call | solution.py:221
  (15 shorter events, 0.0 us)
Async XLA Ops:
  33.7 26.4 %collective-permute-start = (bf16[4,512,256]{2,1,0:T(8,128)(2,1)}, bf16[4,512,256]{2,1,0:T(8,128)(2,1)S(1)}, u32[]{:S(2)}, u32[]{:S(2)}) collective-permute-start(bf16[4,512,256]{2,1,0:T(8,128)(2,1)} %reshape.13.panel_ref.refs_0_), channel_id=1, source_target_pairs={{0,32},{8,104},{32,64},{40,8},{64,96},{72,40},{96,0},{104,72},{1,3... | collective-permute-start | bytes 3145736 | tf_op jit(solution)/shard_map/ppermute | solution.py:246
  36.1 25.6 %collective-permute-start.1 = (bf16[4,512,256]{2,1,0:T(8,128)(2,1)}, bf16[4,512,256]{2,1,0:T(8,128)(2,1)}, u32[]{:S(2)}, u32[]{:S(2)}) collective-permute-start(bf16[4,512,256]{2,1,0:T(8,128)(2,1)} %reshape.13.panel_ref.refs_0_), channel_id=1, source_target_pairs={{0,96},{8,40},{32,0},{40,72},{64,32},{72,104},{96,64},{104,8},{1,9... | collective-permute-start | bytes 3145736 | tf_op jit(solution)/shard_map/ppermute | solution.py:247
  36.1 21.3 %all-to-all-start.1 = ((bf16[16,4,2,32,128]{4,3,2,1,0:T(8,128)(2,1)}), bf16[16,4,2,32,128]{4,3,2,1,0:T(8,128)(2,1)S(1)}, u32[]{:S(2)}, u32[]{:S(2)}) async-start(bf16[16,4,2,32,128]{4,3,2,1,0:T(8,128)(2,1)} %get-tuple-element.57), calls=%async_computation.1 | async-start | bytes 2097152 | tf_op jit(solution)/shard_map/all_to_all | solution.py:253
  60.0 1.7 copy-start.8
  61.7 23.3 %collective-permute-start.2 = (bf16[4,512,256]{2,1,0:T(8,128)(2,1)}, bf16[4,512,256]{2,1,0:T(8,128)(2,1)S(1)}, u32[]{:S(2)}, u32[]{:S(2)}) collective-permute-start(bf16[4,512,256]{2,1,0:T(8,128)(2,1)} %reshape.15.panel_ref.refs_0_), channel_id=1, source_target_pairs={{0,32},{8,104},{32,64},{40,8},{64,96},{72,40},{96,0},{104,72},{1,3... | collective-permute-start | bytes 3145736 | tf_op jit(solution)/shard_map/ppermute | solution.py:246
  62.3 26.0 %collective-permute-start.3 = (bf16[4,512,256]{2,1,0:T(8,128)(2,1)}, bf16[4,512,256]{2,1,0:T(8,128)(2,1)S(1)}, u32[]{:S(2)}, u32[]{:S(2)}) collective-permute-start(bf16[4,512,256]{2,1,0:T(8,128)(2,1)} %reshape.15.panel_ref.refs_0_), channel_id=1, source_target_pairs={{0,96},{8,40},{32,0},{40,72},{64,32},{72,104},{96,64},{104,8},{1,9... | collective-permute-start | bytes 3145736 | tf_op jit(solution)/shard_map/ppermute | solution.py:247
  63.2 25.2 %collective-permute-start.4 = (bf16[4,512,256]{2,1,0:T(8,128)(2,1)}, bf16[4,512,256]{2,1,0:T(8,128)(2,1)S(1)}, u32[]{:S(2)}, u32[]{:S(2)}) collective-permute-start(bf16[4,512,256]{2,1,0:T(8,128)(2,1)} %reshape.13.panel_ref.refs_0_), channel_id=1, source_target_pairs={{0,16},{16,0},{1,17},{17,1},{2,18},{18,2},{3,19},{19,3},{4,20},{20... | collective-permute-start | bytes 3145736 | tf_op jit(solution)/shard_map/ppermute | solution.py:248
  85.0 3.3 copy-start.5
  88.3 1.0 copy-start.6
  88.3 7.3 %copy-start.4 = (bf16[4,512,256]{2,1,0:T(8,128)(2,1)}, bf16[4,512,256]{2,1,0:T(8,128)(2,1)S(1)}, u32[]{:S(2)}) copy-start(bf16[4,512,256]{2,1,0:T(8,128)(2,1)S(1)} %collective-permute-done.4.refs_3_) | copy-start | bytes 3145732
  89.3 29.7 %collective-permute-start.8 = (bf16[3,2,4,128,256]{4,3,2,1,0:T(8,128)(2,1)}, bf16[3,2,4,128,256]{4,3,2,1,0:T(8,128)(2,1)S(1)}, u32[]{:S(2)}, u32[]{:S(2)}) collective-permute-start(bf16[3,2,4,128,256]{4,3,2,1,0:T(8,128)(2,1)} %get-tuple-element.70), channel_id=1, source_target_pairs={{0,8},{8,0},{1,9},{9,1},{2,10},{10,2},{3,11},{11,3},{4,12},{12,4},... | collective-permute-start | bytes 4718600 | tf_op jit(solution)/shard_map/ppermute | solution.py:249
  90.6 15.1 %collective-permute-start.5 = (bf16[4,512,256]{2,1,0:T(8,128)(2,1)}, bf16[4,512,256]{2,1,0:T(8,128)(2,1)}, u32[]{:S(2)}, u32[]{:S(2)}) collective-permute-start(bf16[4,512,256]{2,1,0:T(8,128)(2,1)} %copy-done.8), channel_id=1, source_target_pairs={{0,32},{8,104},{32,64},{40,8},{64,96},{72,40},{96,0},{104,72},{1,3... | collective-permute-start | bytes 3145736 | tf_op jit(solution)/shard_map/ppermute | solution.py:246
  92.3 23.7 %collective-permute-start.6 = (bf16[4,512,256]{2,1,0:T(8,128)(2,1)}, bf16[4,512,256]{2,1,0:T(8,128)(2,1)}, u32[]{:S(2)}, u32[]{:S(2)}) collective-permute-start(bf16[4,512,256]{2,1,0:T(8,128)(2,1)} %copy-done.5), channel_id=1, source_target_pairs={{0,32},{8,104},{32,64},{40,8},{64,96},{72,40},{96,0},{104,72},{1,3... | collective-permute-start | bytes 3145736 | tf_op jit(solution)/shard_map/ppermute | solution.py:246
  92.4 26.6 %collective-permute-start.7 = (bf16[4,512,256]{2,1,0:T(8,128)(2,1)}, bf16[4,512,256]{2,1,0:T(8,128)(2,1)}, u32[]{:S(2)}, u32[]{:S(2)}) collective-permute-start(bf16[4,512,256]{2,1,0:T(8,128)(2,1)} %reshape.15.panel_ref.refs_0_), channel_id=1, source_target_pairs={{0,16},{16,0},{1,17},{17,1},{2,18},{18,2},{3,19},{19,3},{4,20},{20... | collective-permute-start | bytes 3145736 | tf_op jit(solution)/shard_map/ppermute | solution.py:248
  119.0 1.2 copy-start.3
  120.2 56.6 %collective-permute-start.12 = (bf16[4,2,4,128,256]{4,3,2,1,0:T(8,128)(2,1)}, bf16[4,2,4,128,256]{4,3,2,1,0:T(8,128)(2,1)S(1)}, u32[]{:S(2)}, u32[]{:S(2)}) collective-permute-start(bf16[4,2,4,128,256]{4,3,2,1,0:T(8,128)(2,1)} %get-tuple-element.79), channel_id=1, source_target_pairs={{0,8},{8,0},{1,9},{9,1},{2,10},{10,2},{3,11},{11,3},{4,12},{12,4},... | collective-permute-start | bytes 6291464 | tf_op jit(solution)/shard_map/ppermute | solution.py:249
  120.6 56.1 %collective-permute-start.10 = (bf16[4,512,256]{2,1,0:T(8,128)(2,1)}, bf16[4,512,256]{2,1,0:T(8,128)(2,1)S(1)}, u32[]{:S(2)}, u32[]{:S(2)}) collective-permute-start(bf16[4,512,256]{2,1,0:T(8,128)(2,1)} %collective-permute-done.7.refs_2_), channel_id=1, source_target_pairs={{0,96},{8,40},{32,0},{40,72},{64,32},{72,104},{96,64},{104,8},{1,9... | collective-permute-start | bytes 3145736 | tf_op jit(solution)/shard_map/ppermute | solution.py:247
  122.4 54.3 %collective-permute-start.11 = (bf16[4,512,256]{2,1,0:T(8,128)(2,1)}, bf16[4,512,256]{2,1,0:T(8,128)(2,1)}, u32[]{:S(2)}, u32[]{:S(2)}) collective-permute-start(bf16[4,512,256]{2,1,0:T(8,128)(2,1)} %copy-done.8), channel_id=1, source_target_pairs={{0,16},{16,0},{1,17},{17,1},{2,18},{18,2},{3,19},{19,3},{4,20},{20... | collective-permute-start | bytes 3145736 | tf_op jit(solution)/shard_map/ppermute | solution.py:248
  125.1 51.7 %collective-permute-start.9 = (bf16[4,512,256]{2,1,0:T(8,128)(2,1)}, bf16[4,512,256]{2,1,0:T(8,128)(2,1)}, u32[]{:S(2)}, u32[]{:S(2)}) collective-permute-start(bf16[4,512,256]{2,1,0:T(8,128)(2,1)} %copy-done.4), channel_id=1, source_target_pairs={{0,96},{8,40},{32,0},{40,72},{64,32},{72,104},{96,64},{104,8},{1,9... | collective-permute-start | bytes 3145736 | tf_op jit(solution)/shard_map/ppermute | solution.py:247
  176.7 4.7 %copy-start.7 = (bf16[4,512,256]{2,1,0:T(8,128)(2,1)}, bf16[4,512,256]{2,1,0:T(8,128)(2,1)S(1)}, u32[]{:S(2)}) copy-start(bf16[4,512,256]{2,1,0:T(8,128)(2,1)S(1)} %collective-permute-done.10.refs_1_) | copy-start | bytes 3145732
  176.8 4.7 %copy-start = (bf16[4,2,4,128,256]{4,3,2,1,0:T(8,128)(2,1)}, bf16[4,2,4,128,256]{4,3,2,1,0:T(8,128)(2,1)S(1)}, u32[]{:S(2)}) copy-start(bf16[4,2,4,128,256]{4,3,2,1,0:T(8,128)(2,1)S(1)} %collective-permute-done.12.refs_3_) | copy-start | bytes 6291460
  176.8 71.6 %collective-permute-start.16 = (bf16[3,2,4,128,256]{4,3,2,1,0:T(8,128)(2,1)}, bf16[3,2,4,128,256]{4,3,2,1,0:T(8,128)(2,1)}, u32[]{:S(2)}, u32[]{:S(2)}) collective-permute-start(bf16[3,2,4,128,256]{4,3,2,1,0:T(8,128)(2,1)} %get-tuple-element.88), channel_id=1, source_target_pairs={{0,8},{8,0},{1,9},{9,1},{2,10},{10,2},{3,11},{11,3},{4,12},{12,4},... | collective-permute-start | bytes 4718600 | tf_op jit(solution)/shard_map/ppermute | solution.py:249
  178.0 70.3 %collective-permute-start.13 = (bf16[4,512,256]{2,1,0:T(8,128)(2,1)}, bf16[4,512,256]{2,1,0:T(8,128)(2,1)}, u32[]{:S(2)}, u32[]{:S(2)}) collective-permute-start(bf16[4,512,256]{2,1,0:T(8,128)(2,1)} %collective-permute-done.11.refs_2_), channel_id=1, source_target_pairs={{0,32},{8,104},{32,64},{40,8},{64,96},{72,40},{96,0},{104,72},{1,3... | collective-permute-start | bytes 3145736 | tf_op jit(solution)/shard_map/ppermute | solution.py:246
  179.8 68.5 %collective-permute-start.14 = (bf16[4,512,256]{2,1,0:T(8,128)(2,1)}, bf16[4,512,256]{2,1,0:T(8,128)(2,1)}, u32[]{:S(2)}, u32[]{:S(2)}) collective-permute-start(bf16[4,512,256]{2,1,0:T(8,128)(2,1)} %collective-permute-done.7.refs_2_), channel_id=1, source_target_pairs={{0,32},{8,104},{32,64},{40,8},{64,96},{72,40},{96,0},{104,72},{1,3... | collective-permute-start | bytes 3145736 | tf_op jit(solution)/shard_map/ppermute | solution.py:246
  179.8 68.5 %collective-permute-start.15 = (bf16[4,512,256]{2,1,0:T(8,128)(2,1)}, bf16[4,512,256]{2,1,0:T(8,128)(2,1)}, u32[]{:S(2)}, u32[]{:S(2)}) collective-permute-start(bf16[4,512,256]{2,1,0:T(8,128)(2,1)} %collective-permute-done.6.refs_1_), channel_id=1, source_target_pairs={{0,16},{16,0},{1,17},{17,1},{2,18},{18,2},{3,19},{19,3},{4,20},{20... | collective-permute-start | bytes 3145736 | tf_op jit(solution)/shard_map/ppermute | solution.py:248
  248.3 52.3 %collective-permute-start.18 = (bf16[3,2,4,128,256]{4,3,2,1,0:T(8,128)(2,1)}, bf16[3,2,4,128,256]{4,3,2,1,0:T(8,128)(2,1)S(1)}, u32[]{:S(2)}, u32[]{:S(2)}) collective-permute-start(bf16[3,2,4,128,256]{4,3,2,1,0:T(8,128)(2,1)} %get-tuple-element.101), channel_id=1, source_target_pairs={{0,8},{8,0},{1,9},{9,1},{2,10},{10,2},{3,11},{11,3},{4,12},{12,4},... | collective-permute-start | bytes 4718600 | tf_op jit(solution)/shard_map/ppermute | solution.py:249
  299.5 51.7 %collective-permute-start.17 = (bf16[3,2,4,128,256]{4,3,2,1,0:T(8,128)(2,1)}, bf16[3,2,4,128,256]{4,3,2,1,0:T(8,128)(2,1)S(1)}, u32[]{:S(2)}, u32[]{:S(2)}) collective-permute-start(bf16[3,2,4,128,256]{4,3,2,1,0:T(8,128)(2,1)} %get-tuple-element.100), channel_id=1, source_target_pairs={{0,8},{8,0},{1,9},{9,1},{2,10},{10,2},{3,11},{11,3},{4,12},{12,4},... | collective-permute-start | bytes 4718600 | tf_op jit(solution)/shard_map/ppermute | solution.py:249
  300.6 1.2 copy-start.1
  351.3 1.2 copy-start.2

commit v5 on v4

v5 whole, which is shorter than its diff:
```python
import functools

import jax
import jax.numpy as jnp
import numpy as np
from jax import lax
from jax.experimental import pallas as pl
from jax.experimental.pallas import tpu as pltpu
from jax.sharding import Mesh, PartitionSpec as P

FFT_LEN = 512
BINS = 128
BAND_LO = 16
OWNERS = 8
CHUNK = 4
SEG_STEP = 8
MIB = 1024 * 1024


def spectra_table():
    sample = np.arange(FFT_LEN)
    bins = (BAND_LO + np.arange(BINS)).reshape(OWNERS, 2, 2, CHUNK).transpose(2, 0, 1, 3).reshape(-1)
    phase = (sample[:, None] * bins[None, :] % FFT_LEN) * (2.0 * np.pi / FFT_LEN)
    taper = 0.5 - 0.5 * np.cos(2.0 * np.pi * sample / FFT_LEN)
    table = np.stack([np.cos(phase), -np.sin(phase)], axis=2).reshape(FFT_LEN, 2 * BINS) * taper[:, None]
    high = table.astype(jnp.bfloat16)
    low = (table - high.astype(np.float64)).astype(jnp.bfloat16)
    return high, low


def whiten_kernel(records_ref, available_ref, high_ref, low_ref, first_ref, second_ref, rows_ref, turned_ref):
    stations, segs, samples = records_ref.shape
    flat = records_ref[...].reshape(stations * segs, samples)
    spectra = jnp.dot(flat, high_ref[...], preferred_element_type=jnp.float32)
    spectra += jnp.dot(flat, low_ref[...], preferred_element_type=jnp.float32)
    wide = spectra.shape[1]
    for part in range(2):
        rows_ref[part] = spectra[:, part * BINS : (part + 1) * BINS]
    for seg in range(segs):
        turned = jnp.concatenate(
            [rows_ref[part, pl.ds(seg, stations, stride=segs), :].T for part in range(2)], axis=0
        )
        power = jnp.sum(turned * turned, axis=0, keepdims=True) / BINS
        weight = available_ref[seg : seg + 1, :].astype(jnp.float32) / jnp.sqrt(power + 1e-05)
        turned_ref[pl.ds(seg, wide, stride=segs), :] = turned * weight
    whitened = turned_ref[...].reshape(2, 2 * OWNERS, CHUNK, 2, segs, stations).astype(jnp.bfloat16)
    first_ref[...] = whitened[0]
    second_ref[...] = whitened[1]


def whiten(records, available):
    stations, segments, samples = records.shape
    high, low = spectra_table()
    half = jax.ShapeDtypeStruct((2 * OWNERS, CHUNK, 2, segments, stations), jnp.bfloat16)
    half_spec = pl.BlockSpec((2 * OWNERS, CHUNK, 2, SEG_STEP, stations), lambda i: (0, 0, 0, i, 0))
    return pl.pallas_call(
        whiten_kernel,
        grid=(segments // SEG_STEP,),
        in_specs=[
            pl.BlockSpec((stations, SEG_STEP, samples), lambda i: (0, i, 0)),
            pl.BlockSpec((SEG_STEP, stations), lambda i: (i, 0)),
            pl.BlockSpec((samples, 2 * BINS), lambda i: (0, 0)),
            pl.BlockSpec((samples, 2 * BINS), lambda i: (0, 0)),
        ],
        out_specs=[half_spec, half_spec],
        out_shape=[half, half],
        scratch_shapes=[
            pltpu.VMEM((2, stations * SEG_STEP, BINS), jnp.float32),
            pltpu.VMEM((2 * BINS * SEG_STEP, stations), jnp.float32),
        ],
        compiler_params=pltpu.CompilerParams(vmem_limit_bytes=60 * MIB),
        name="whiten",
    )(records, available.T, jnp.asarray(high), jnp.asarray(low))


def rows_kernel(panel_ref, mine_ref):
    bins, depth, width = panel_ref.shape
    half, rows = depth // 2, width // 2
    for f in range(bins):
        for core in range(2):
            real = panel_ref[f, :half, core * rows : (core + 1) * rows].T
            imag = panel_ref[f, half:, core * rows : (core + 1) * rows].T
            base = 2 * rows * core
            mine_ref[f, base : base + rows, :half] = real
            mine_ref[f, base : base + rows, half:] = imag
            mine_ref[f, base + rows : base + 2 * rows, :half] = imag
            mine_ref[f, base + rows : base + 2 * rows, half:] = -real


def rows_of(panel):
    bins, depth, width = panel.shape
    return pl.pallas_call(
        rows_kernel,
        grid=(bins,),
        in_specs=[pl.BlockSpec((1, depth, width), lambda f: (f, 0, 0))],
        out_specs=pl.BlockSpec((1, 2 * width, depth), lambda f: (f, 0, 0)),
        out_shape=jax.ShapeDtypeStruct((bins, 2 * width, depth), panel.dtype),
        compiler_params=pltpu.CompilerParams(vmem_limit_bytes=60 * MIB),
        name="rows",
    )(panel)


def spot_of(where, at, cols):
    return pl.ds(pl.multiple_of(where[at] * cols, cols), cols)


def gram_kernel(scale, chunks, placed, where, mine0_ref, mine1_ref, *refs):
    count, sets = len(chunks), len(placed)
    panels, sent, rest = refs[:count], refs[count : count + sets], refs[count + sets :]
    out_ref, send_ref, slots, place_slots, sems, place_sems = rest[-6:]
    step, steps = pl.program_id(0), pl.num_programs(0)
    bins = mine0_ref.shape[0]
    rows, cols = mine0_ref.shape[1] // 4, panels[0].shape[2]
    slot, core = lax.rem(step, 2), where[count]
    received = [(which, at, chunk) for which, some in enumerate(placed) for at, chunk in enumerate(some)]

    def first_bin(owner, chunk, at):
        return owner * 2 * CHUNK + chunk * CHUNK + at * bins

    def writes(at, held):
        for block, chunk in enumerate(chunks):
            spot = out_ref.at[:, pl.ds(first_bin(core, chunk, at), bins), :, spot_of(where, block, cols)]
            yield pltpu.make_async_copy(slots.at[held, block, core], spot, sems.at[held, block, 0])
            spot = send_ref.at[block, :, pl.ds(at * bins, bins)]
            yield pltpu.make_async_copy(slots.at[held, block, 1 - core], spot, sems.at[held, block, 1])

    def places(at, held):
        for k, (_, _, chunk) in enumerate(received):
            spot = spot_of(where, count + 1 + k, cols)
            spot = out_ref.at[:, pl.ds(first_bin(1 - core, chunk, at), bins), :, spot]
            yield pltpu.make_async_copy(place_slots.at[held, k], spot, place_sems.at[held, k])

    @pl.when(step >= 2)
    def _():
        for copy in (*writes(step - 2, slot), *places(step - 2, slot)):
            copy.wait()

    for k, (which, at, _) in enumerate(received):
        place_slots[slot, k] = sent[which][at]
    for copy in places(step, slot):
        copy.start()
    for block, chunk in enumerate(chunks):
        mine_ref = mine1_ref if chunk else mine0_ref
        for f in range(bins):
            gram = jnp.dot(mine_ref[f], panels[block][f], preferred_element_type=jnp.float32) * scale
            gram = gram.astype(jnp.bfloat16)
            for target in range(2):
                for part in range(2):
                    base = (2 * target + part) * rows
                    slots[slot, block, target, part, f] = gram[base : base + rows]
    for copy in writes(step, slot):
        copy.start()

    @pl.when(step == steps - 1)
    def _():
        for copy in (*writes(step - 1, 1 - slot), *places(step - 1, 1 - slot)):
            copy.wait()
        for copy in (*writes(step, slot), *places(step, slot)):
            copy.wait()


def sent_spec(results, step):
    block = (results.shape[0], 2, step, *results.shape[3:])
    return pl.BlockSpec(block, lambda f, w: (0, 0, f, 0, 0))


def gram(core, mine, blocks, shape, out, *sent):
    bins, depth, cols = blocks[0][3].shape
    rows, step = shape[2], 2
    count = len(blocks)
    chunks = [block[0] for block in blocks]
    received = [block for some, _ in sent for block in some]
    where = [block[1] for block in blocks] + [core] + [block[2] for block in received]
    held = [] if out is None else [out]
    used = [
        pl.BlockSpec((step, 4 * rows, depth), (lambda f, w: (f, 0, 0)) if chunk in chunks else (lambda f, w: (0, 0, 0)))
        for chunk in range(2)
    ]
    send = jax.ShapeDtypeStruct((count, 2, bins, rows, cols), jnp.bfloat16)
    spots = max(len(received), 1)
    return pl.pallas_call(
        functools.partial(gram_kernel, 2.0 / depth, chunks, [[block[0] for block in some] for some, _ in sent]),
        grid_spec=pltpu.PrefetchScalarGridSpec(
            num_scalar_prefetch=1,
            grid=(bins // step,),
            in_specs=used
            + [pl.BlockSpec((step, depth, cols), lambda f, w: (f, 0, 0))] * count
            + [sent_spec(results, step) for _, results in sent]
            + [pl.BlockSpec(memory_space=pl.ANY)] * len(held),
            out_specs=[pl.BlockSpec(memory_space=pl.ANY)] * 2,
            scratch_shapes=[
                pltpu.VMEM((2, count, 2, 2, step, rows, cols), jnp.bfloat16),
                pltpu.VMEM((2, spots, 2, step, rows, cols), jnp.bfloat16),
                pltpu.SemaphoreType.DMA((2, count, 2)),
                pltpu.SemaphoreType.DMA((2, spots)),
            ],
        ),
        out_shape=[jax.ShapeDtypeStruct(shape, jnp.bfloat16), send],
        input_output_aliases={3 + count + len(sent): 0} if held else {},
        cost_estimate=pl.CostEstimate(
            flops=8 * count * bins * rows * depth * cols,
            bytes_accessed=2 * bins * (8 * rows * depth + count * (depth * cols + 4 * rows * cols)),
            transcendentals=0,
        ),
        compiler_params=pltpu.CompilerParams(vmem_limit_bytes=60 * MIB),
        name="gram",
    )(jnp.stack(where).astype(jnp.int32), *mine, *[block[3] for block in blocks], *[r for _, r in sent], *held)


def place_kernel(chunks, where, sent_ref, _, out_ref, sems):
    bins, cols = sent_ref.shape[2], sent_ref.shape[4]
    step, core = pl.program_id(0), where[len(chunks)]
    copies = []
    for k, chunk in enumerate(chunks):
        first = (1 - core) * 2 * CHUNK + chunk * CHUNK + step * bins
        spot = out_ref.at[:, pl.ds(first, bins), :, spot_of(where, k, cols)]
        copies.append(pltpu.make_async_copy(sent_ref.at[k], spot, sems.at[k]))
    for copy in copies:
        copy.start()
    for copy in copies:
        copy.wait()


def place(core, sent, out):
    blocks, results = sent
    return pl.pallas_call(
        functools.partial(place_kernel, [block[0] for block in blocks]),
        grid_spec=pltpu.PrefetchScalarGridSpec(
            num_scalar_prefetch=1,
            grid=(results.shape[2] // 2,),
            in_specs=[sent_spec(results, 2), pl.BlockSpec(memory_space=pl.ANY)],
            out_specs=pl.BlockSpec(memory_space=pl.ANY),
            scratch_shapes=[pltpu.SemaphoreType.DMA((len(blocks),))],
        ),
        out_shape=jax.ShapeDtypeStruct(out.shape, out.dtype),
        input_output_aliases={2: 0},
        compiler_params=pltpu.CompilerParams(vmem_limit_bytes=60 * MIB),
        name="place",
    )(jnp.stack([block[2] for block in blocks] + [core]).astype(jnp.int32), results, out)


def mirrored(step):
    return [
        (2 * x + core, (x + (1 - 2 * core) * step) % 4 * 2 + core) for x in range(4) for core in range(2)
    ]


def shards(records, available):
    stations = records.shape[0]
    x, yh, core = lax.axis_index("x"), lax.axis_index("yh"), lax.axis_index("core")
    fwd = lambda v: lax.ppermute(v, ("x", "core"), mirrored(1))
    bwd = lambda v: lax.ppermute(v, ("x", "core"), mirrored(-1))
    over = lambda v: lax.ppermute(v, "yh", [(0, 1), (1, 0)])
    swap = lambda v: lax.ppermute(v, "core", [(0, 1), (1, 0)])
    after = lambda value, *others: lax.optimization_barrier((value, *others))[0]

    def owned(chunk):
        got = lax.all_to_all(chunk, ("yl", "z", "core"), split_axis=0, concat_axis=0, tiled=True)
        got = got.reshape(OWNERS, 2, *got.shape[1:])
        return jnp.transpose(got, (2, 3, 0, 4, 1, 5)).reshape(CHUNK, -1, 2 * stations)

    def entry(chunk, dx, dy, panel):
        sign = 1 - 2 * core
        chips = [(x - way * dx) % 4 * 2 + (yh + dy) % 2 for way in (sign, -sign)]
        return chunk, *chips, panel

    shape = (2, 4 * CHUNK, stations, 16 * stations)
    first, second = whiten(records, available)
    pa = owned(first)
    na, ba = fwd(pa), bwd(pa)
    pb = owned(after(second, pa))
    ma = rows_of(pa)

    nb, bb, oa = fwd(after(pb, na)), bwd(after(pb, ba)), over(after(pa, pb))
    blocks1 = [entry(0, 0, 0, pa), entry(0, 1, 0, na), entry(0, -1, 0, ba)]
    out, sent = gram(core, (ma, ma), blocks1, shape, None)
    mine = ma, rows_of(pb)

    fa, fb, ob = fwd(after(na, nb, out)), fwd(after(nb, bb)), over(after(pb, oa))
    sent1 = blocks1, swap(sent)
    blocks2 = [entry(1, 0, 0, pb), entry(1, 1, 0, nb), entry(1, -1, 0, bb), entry(0, 0, 1, oa)]
    out, sent = gram(core, mine, blocks2, shape, out)

    boa, bob, noa = bwd(after(oa, fa, out)), bwd(after(ob, fb)), over(after(na, ob))
    sent2 = blocks2, swap(sent)
    blocks3 = [entry(0, 2, 0, fa), entry(1, 2, 0, fb), entry(1, 0, 1, ob)]
    out, sent = gram(core, mine, blocks3, shape, out, sent1)

    foa, nob, fob = fwd(after(noa, boa, out)), fwd(after(ob, bob)), over(after(fb, noa))
    sent3 = blocks3, swap(sent)
    blocks4 = [entry(0, -1, 1, boa), entry(1, -1, 1, bob), entry(0, 1, 1, noa)]
    out, sent = gram(core, mine, blocks4, shape, out, sent2)

    sent4 = blocks4, swap(sent)
    blocks5 = [entry(0, 2, 1, foa), entry(1, 1, 1, nob), entry(1, 2, 1, fob)]
    out, sent = gram(core, mine, blocks5, shape, out, sent3)
    out = place(core, sent4, out)
    return place(core, (blocks5, swap(sent)), out)


def solution(mesh):
    fine = Mesh(mesh.devices.reshape(4, 2, 2, 2, 4), ("x", "yh", "core", "yl", "z"))
    sta, freq = ("x", "yh", "core"), ("yl", "z")
    return jax.shard_map(
        shards,
        mesh=fine,
        in_specs=(P(sta, freq, None), P(sta, freq)),
        out_specs=P(None, freq, sta, None),
        check_vma=False,
    )
```

time: 403 us -> 183 us (0.45)
  Pallas kernels: 301 us -> 56.9 us
  blocking collectives: 23.3 us -> 43.1 us
  starting transfers between devices: 26.5 us -> 38.4 us
  waiting for transfers between devices: 37.1 us -> 31.8 us
    pallas_call x7, Pallas kernels: 286 us -> 41.6 us  [the longest x5 34.4 us: gram(): pl.pallas_call(functools.partial(gram_kernel, 2.0 / depth, chunks, [[bloc...]
    all_to_all x1 -> x2, blocking collectives: 23.3 us -> 43.1 us  [owned(): lax.all_to_all(chunk, ('yl', 'z', 'core'), split_axis=0, concat_axis=0, t...]
    ppermute x5, starting transfers between devices: 3.59 us -> 19.8 us  [shards(): swap = lambda v: lax.ppermute(v, 'core', [(0, 1), (1, 0)])]
    ppermute x4, waiting for transfers between devices: 2.89 us -> 17.7 us  [shards(): over = lambda v: lax.ppermute(v, 'yh', [(0, 1), (1, 0)])]
    all_to_all x1 -> x0, waiting for transfers between devices: 12.2 us -> none  [owned(): lax.all_to_all(chunk, ('yl', 'z', 'core'), split_axis=0, concat_axis=0, t...]
    ppermute x6, waiting for transfers between devices: 17 us -> 9.67 us  [shards(): fwd = lambda v: lax.ppermute(v, ('x', 'core'), mirrored(1))]
    all_to_all x1 -> x0, starting transfers between devices: 5.36 us -> none  [owned(): lax.all_to_all(chunk, ('yl', 'z', 'core'), split_axis=0, concat_axis=0, t...]
  transfers between devices with their start and end apart: 20 -> 19, of which waited for: 6 -> 8; matrix products, arithmetic and copies ran while one was open for 2% -> 3% of each run, Pallas kernels for 61% -> 25%
where the time goes in v5:
time: 183 us; the launch traced here: 182 us
  Pallas kernels  56.9 us (31%)
  blocking collectives  43.1 us (24%)
  starting transfers between devices  38.4 us (21%)
  waiting for transfers between devices  31.8 us (17%)
  local copies, waits for them, and re-layouts  9.93 us (5%)
    all_to_all x2, blocking collectives, owned(): lax.all_to_all(chunk, ('yl', 'z', 'core'), split_axis=0, concat_axis=0, t...  43.1 us
    pallas_call x5, Pallas kernels, gram(): pl.pallas_call(functools.partial(gram_kernel, 2.0 / depth, chunks, [[bloc...  34.4 us
    ppermute x5, starting transfers between devices, shards(): swap = lambda v: lax.ppermute(v, 'core', [(0, 1), (1, 0)])  19.8 us
    ppermute x4, waiting for transfers between devices, shards(): over = lambda v: lax.ppermute(v, 'yh', [(0, 1), (1, 0)])  17.7 us
    ppermute x4, starting transfers between devices, shards(): over = lambda v: lax.ppermute(v, 'yh', [(0, 1), (1, 0)])  11.2 us
    ppermute x6, waiting for transfers between devices, shards(): fwd = lambda v: lax.ppermute(v, ('x', 'core'), mirrored(1))  9.67 us
    pallas_call x1, Pallas kernels, whiten(): pl.pallas_call(whiten_kernel, grid=(segments // SEG_STEP,), in_specs=[pl....  7.77 us
    pallas_call x2, Pallas kernels, rows_of(): pl.pallas_call(rows_kernel, grid=(bins,), in_specs=[pl.BlockSpec((1, dept...  7.5 us
  transfers between devices with their start and end apart: 19, of which 8 were waited for; matrix products, arithmetic and copies ran while one was open for 3% of the time, Pallas kernels for 25%

profile of v5, /device:TPU:1, one launch (start us, length us, event | category | flops | bytes accessed | tf_op | source)
XLA Modules:
  0.0 181.6 jit_solution(16527316403256835826)
XLA Ops:
  0.0 7.8 %whiten.1 = (bf16[16,4,2,32,128]{4,3,2,1,0:T(8,128)(2,1)}, bf16[16,4,2,32,128]{4,3,2,1,0:T(8,128)(2,1)}) custom-call(bf16[128,32,512]{2,1,0:T(8,128)(2,1)} %records_ref.1, s32[32,128]{1,0:T(8,128)} %bitcast.28, bf16[512,256]{1,0:T(8,128)(2,1)} %constant.183.clone.high_ref, bf16[512,256]{1,0:T(8,128)(2,1)} %constant.184.clone.low_ref), custom_call_target="tpu_custom_call" | custom-call | tf_op jit(solution)/shard_map/whiten/pallas_call | solution.py:56
  7.8 23.3 %all_to_all.10 = bf16[16,4,2,32,128]{4,3,2,1,0:T(8,128)(2,1)S(1)} all-to-all(bf16[16,4,2,32,128]{4,3,2,1,0:T(8,128)(2,1)} %get-tuple-element.30), channel_id=1, replica_groups=mesh['x'=4,'yh'=2,'core'=2,'yl'=2,'z'=4] {'yl','z','core'}, dimensions={0} | all-to-all | bytes 2097152 | tf_op jit(solution)/shard_map/all_to_all | solution.py:258
  31.0 1.1 copy.16
  32.1 0.7 reshape.13.panel_ref.refs_0_
  32.8 2.5 %collective-permute-start = (bf16[4,512,256]{2,1,0:T(8,128)(2,1)S(1)}, bf16[4,512,256]{2,1,0:T(8,128)(2,1)}, u32[]{:S(2)}, u32[]{:S(2)}) collective-permute-start(bf16[4,512,256]{2,1,0:T(8,128)(2,1)S(1)} %reshape.13.panel_ref.refs_0_), channel_id=1, source_target_pairs={{0,32},{8,104},{32,64},{40,8},{64,96},{72,40},{96,0},{104,72},{1,3... | collective-permute-start | bytes 3145736 | tf_op jit(solution)/shard_map/ppermute | solution.py:251
  35.4 0.0 collective-permute-start.5
  35.4 19.8 %all_to_all.11 = bf16[16,4,2,32,128]{4,3,2,1,0:T(8,128)(2,1)S(1)} all-to-all(bf16[16,4,2,32,128]{4,3,2,1,0:T(8,128)(2,1)S(1)} %copy-done.7), channel_id=1, replica_groups=mesh['x'=4,'yh'=2,'core'=2,'yl'=2,'z'=4] {'yl','z','core'}, dimensions={0} | all-to-all | bytes 2097152 | tf_op jit(solution)/shard_map/all_to_all | solution.py:258
  55.2 1.1 copy.15
  56.3 0.7 reshape.15.panel_ref.refs_0_
  57.0 0.0 copy-done.1
  57.1 2.7 %collective-permute-start.1 = (bf16[4,512,256]{2,1,0:T(8,128)(2,1)S(1)}, bf16[4,512,256]{2,1,0:T(8,128)(2,1)S(1)}, u32[]{:S(2)}, u32[]{:S(2)}) collective-permute-start(bf16[4,512,256]{2,1,0:T(8,128)(2,1)S(1)} %reshape.13.panel_ref.refs_0_), channel_id=1, source_target_pairs={{0,16},{16,0},{1,17},{17,1},{2,18},{18,2},{3,19},{19,3},{4,20},{20... | collective-permute-start | bytes 3145736 | tf_op jit(solution)/shard_map/ppermute | solution.py:253
  59.8 0.0 collective-permute-done.refs_1_
  59.8 1.6 collective-permute-start.4
  61.4 0.0 collective-permute-done.5.refs_2_
  61.4 0.0 collective-permute-start.7
  61.4 0.7 add_add_fusion.1.where
  62.0 3.7 %rows.2.mine0_ref.mine1_ref = bf16[4,512,512]{2,1,0:T(8,128)(2,1)} custom-call(bf16[4,512,256]{2,1,0:T(8,128)(2,1)} %copy-done.1), custom_call_target="tpu_custom_call" | custom-call | tf_op jit(solution)/shard_map/rows/pallas_call | solution.py:92
  65.8 6.7 %gram.5 = (bf16[2,16,128,2048]{3,2,1,0:T(8,128)(2,1)}, bf16[3,2,4,128,256]{4,3,2,1,0:T(8,128)(2,1)}) custom-call(s32[4]{0:T(128)} %add_add_fusion.1.where, bf16[4,512,512]{2,1,0:T(8,128)(2,1)} %rows.2.mine0_ref.mine1_ref, bf16[4,512,512]{2,1,0:T(8,128)(2,1)} %rows.2.mine0_ref.mine1_ref, bf16[4,512,256]{2,1,0:T(8,128)(2,1)} %copy-done.1, ...), custom_call_target="tpu_custom_call" | custom-call | flops 1610612736 | bytes 10485760 | tf_op jit(solution)/shard_map/gram/pallas_call | solution.py:181
  72.4 3.2 %collective-permute-start.10 = (bf16[3,2,4,128,256]{4,3,2,1,0:T(8,128)(2,1)}, bf16[3,2,4,128,256]{4,3,2,1,0:T(8,128)(2,1)}, u32[]{:S(2)}, u32[]{:S(2)}) collective-permute-start(bf16[3,2,4,128,256]{4,3,2,1,0:T(8,128)(2,1)} %get-tuple-element.43), channel_id=1, source_target_pairs={{0,8},{8,0},{1,9},{9,1},{2,10},{10,2},{3,11},{11,3},{4,12},{12,4},... | collective-permute-start | bytes 4718600 | tf_op jit(solution)/shard_map/ppermute | solution.py:254
  75.6 6.5 %collective-permute-done.1.refs_3_ = bf16[4,512,256]{2,1,0:T(8,128)(2,1)S(1)} collective-permute-done((bf16[4,512,256]{2,1,0:T(8,128)(2,1)S(1)}, bf16[4,512,256]{2,1,0:T(8,128)(2,1)S(1)}, u32[]{:S(2)}, u32[]{:S(2)}) %collective-permute-start.1) | collective-permute-done | bytes 1048608 | tf_op jit(solution)/shard_map/ppermute | solution.py:253
  82.1 2.7 %collective-permute-start.2 = (bf16[4,512,256]{2,1,0:T(8,128)(2,1)S(1)}, bf16[4,512,256]{2,1,0:T(8,128)(2,1)}, u32[]{:S(2)}, u32[]{:S(2)}) collective-permute-start(bf16[4,512,256]{2,1,0:T(8,128)(2,1)S(1)} %reshape.15.panel_ref.refs_0_), channel_id=1, source_target_pairs={{0,16},{16,0},{1,17},{17,1},{2,18},{18,2},{3,19},{19,3},{4,20},{20... | collective-permute-start | bytes 3145736 | tf_op jit(solution)/shard_map/ppermute | solution.py:253
  84.9 0.0 collective-permute-done.4.refs_1_
  84.9 1.6 collective-permute-start.6
  86.5 1.1 collective-permute-done.7.refs_2_
  87.6 0.0 collective-permute-start.9
  87.6 0.7 stack.103.where
  88.2 3.8 %rows.3.mine1_ref = bf16[4,512,512]{2,1,0:T(8,128)(2,1)} custom-call(bf16[4,512,256]{2,1,0:T(8,128)(2,1)} %copy-done), custom_call_target="tpu_custom_call" | custom-call | tf_op jit(solution)/shard_map/rows/pallas_call | solution.py:92
  92.0 6.9 %gram.6 = (bf16[2,16,128,2048]{3,2,1,0:T(8,128)(2,1)}, bf16[4,2,4,128,256]{4,3,2,1,0:T(8,128)(2,1)}) custom-call(s32[5]{0:T(128)} %stack.103.where, bf16[4,512,512]{2,1,0:T(8,128)(2,1)} %rows.2.mine0_ref.mine1_ref, bf16[4,512,512]{2,1,0:T(8,128)(2,1)} %rows.3.mine1_ref, bf16[4,512,256]{2,1,0:T(8,128)(2,1)} %copy-done, ...), custom_call_target="tpu_custom_call", output_to_operand_aliasing={{0}: (7, {})} | custom-call | flops 2147483648 | bytes 12582912 | tf_op jit(solution)/shard_map/gram/pallas_call | solution.py:181
  98.9 1.4 collective-permute-start.16
  100.3 6.0 %collective-permute-done.2.refs_2_ = bf16[4,512,256]{2,1,0:T(8,128)(2,1)} collective-permute-done((bf16[4,512,256]{2,1,0:T(8,128)(2,1)S(1)}, bf16[4,512,256]{2,1,0:T(8,128)(2,1)}, u32[]{:S(2)}, u32[]{:S(2)}) %collective-permute-start.2) | collective-permute-done | bytes 1048608 | tf_op jit(solution)/shard_map/ppermute | solution.py:253
  106.3 2.8 %collective-permute-start.3 = (bf16[4,512,256]{2,1,0:T(8,128)(2,1)}, bf16[4,512,256]{2,1,0:T(8,128)(2,1)}, u32[]{:S(2)}, u32[]{:S(2)}) collective-permute-start(bf16[4,512,256]{2,1,0:T(8,128)(2,1)} %collective-permute-done.refs_1_), channel_id=1, source_target_pairs={{0,16},{16,0},{1,17},{17,1},{2,18},{18,2},{3,19},{19,3},{4,20},{20... | collective-permute-start | bytes 3145736 | tf_op jit(solution)/shard_map/ppermute | solution.py:253
  109.1 0.0 collective-permute-done.6.refs_0_
  109.1 0.0 collective-permute-start.8
  109.2 1.2 collective-permute-done.9.refs_1_
  110.4 0.0 collective-permute-start.12
  110.4 0.6 stack.107.where
  110.9 0.0 collective-permute-done.10.refs_3_
  110.9 6.8 %gram.7 = (bf16[2,16,128,2048]{3,2,1,0:T(8,128)(2,1)}, bf16[3,2,4,128,256]{4,3,2,1,0:T(8,128)(2,1)}) custom-call(s32[7]{0:T(128)} %stack.107.where, bf16[4,512,512]{2,1,0:T(8,128)(2,1)} %rows.2.mine0_ref.mine1_ref, bf16[4,512,512]{2,1,0:T(8,128)(2,1)} %rows.3.mine1_ref, ...), custom_call_target="tpu_custom_call", output_to_operand_aliasing={{0}: (7, {})} | custom-call | flops 1610612736 | bytes 10485760 | tf_op jit(solution)/shard_map/gram/pallas_call | solution.py:181
  117.8 7.5 %collective-permute-start.15 = (bf16[3,2,4,128,256]{4,3,2,1,0:T(8,128)(2,1)}, bf16[3,2,4,128,256]{4,3,2,1,0:T(8,128)(2,1)}, u32[]{:S(2)}, u32[]{:S(2)}) collective-permute-start(bf16[3,2,4,128,256]{4,3,2,1,0:T(8,128)(2,1)} %get-tuple-element.49), channel_id=1, source_target_pairs={{0,8},{8,0},{1,9},{9,1},{2,10},{10,2},{3,11},{11,3},{4,12},{12,4},... | collective-permute-start | bytes 4718600 | tf_op jit(solution)/shard_map/ppermute | solution.py:254
  125.3 4.5 %collective-permute-done.3.refs_2_ = bf16[4,512,256]{2,1,0:T(8,128)(2,1)} collective-permute-done((bf16[4,512,256]{2,1,0:T(8,128)(2,1)}, bf16[4,512,256]{2,1,0:T(8,128)(2,1)}, u32[]{:S(2)}, u32[]{:S(2)}) %collective-permute-start.3) | collective-permute-done | bytes 1048608 | tf_op jit(solution)/shard_map/ppermute | solution.py:253
  129.8 2.9 %collective-permute-start.14 = (bf16[4,512,256]{2,1,0:T(8,128)(2,1)}, bf16[4,512,256]{2,1,0:T(8,128)(2,1)}, u32[]{:S(2)}, u32[]{:S(2)}) collective-permute-start(bf16[4,512,256]{2,1,0:T(8,128)(2,1)} %collective-permute-done.9.refs_1_), channel_id=1, source_target_pairs={{0,16},{16,0},{1,17},{17,1},{2,18},{18,2},{3,19},{19,3},{4,20},{20... | collective-permute-start | bytes 3145736 | tf_op jit(solution)/shard_map/ppermute | solution.py:253
  132.7 0.0 collective-permute-done.8.refs_0_
  132.7 1.6 collective-permute-start.11
  134.3 3.3 %collective-permute-done.12.refs_1_ = bf16[4,512,256]{2,1,0:T(8,128)(2,1)} collective-permute-done((bf16[4,512,256]{2,1,0:T(8,128)(2,1)}, bf16[4,512,256]{2,1,0:T(8,128)(2,1)}, u32[]{:S(2)}, u32[]{:S(2)}) %collective-permute-start.12) | collective-permute-done | bytes 1048608 | tf_op jit(solution)/shard_map/ppermute | solution.py:252
  137.6 0.0 collective-permute-start.13
  137.6 0.7 stack.109.where
  138.3 0.7 stack.98.where
  139.0 0.0 collective-permute-done.16.refs_3_
  139.0 1.4 copy-done.2
  140.4 7.2 %gram.8 = (bf16[2,16,128,2048]{3,2,1,0:T(8,128)(2,1)}, bf16[3,2,4,128,256]{4,3,2,1,0:T(8,128)(2,1)}) custom-call(s32[8]{0:T(128)} %stack.109.where, bf16[4,512,512]{2,1,0:T(8,128)(2,1)} %rows.2.mine0_ref.mine1_ref, bf16[4,512,512]{2,1,0:T(8,128)(2,1)} %rows.3.mine1_ref, bf16[4,512,256]{2,1,0:T(8,128)(2,1)} %copy-done.6, ...), custom_call_target="tpu_custom_call", output_to_operand_aliasing={{0}: (7, {})} | custom-call | flops 1610612736 | bytes 10485760 | tf_op jit(solution)/shard_map/gram/pallas_call | solution.py:181
  147.5 4.0 %collective-permute-start.18 = (bf16[3,2,4,128,256]{4,3,2,1,0:T(8,128)(2,1)}, bf16[3,2,4,128,256]{4,3,2,1,0:T(8,128)(2,1)S(1)}, u32[]{:S(2)}, u32[]{:S(2)}) collective-permute-start(bf16[3,2,4,128,256]{4,3,2,1,0:T(8,128)(2,1)} %get-tuple-element.53), channel_id=1, source_target_pairs={{0,8},{8,0},{1,9},{9,1},{2,10},{10,2},{3,11},{11,3},{4,12},{12,4},... | collective-permute-start | bytes 4718600 | tf_op jit(solution)/shard_map/ppermute | solution.py:254
  151.5 0.0 collective-permute-done.15.refs_3_
  151.6 0.8 collective-permute-done.14.refs_2_
  152.3 0.0 collective-permute-done.11.refs_0_
  152.3 8.4 %collective-permute-done.13.refs_1_ = bf16[4,512,256]{2,1,0:T(8,128)(2,1)} collective-permute-done((bf16[4,512,256]{2,1,0:T(8,128)(2,1)}, bf16[4,512,256]{2,1,0:T(8,128)(2,1)}, u32[]{:S(2)}, u32[]{:S(2)}) %collective-permute-start.13) | collective-permute-done | bytes 1048608 | tf_op jit(solution)/shard_map/ppermute | solution.py:251
  160.8 6.8 %gram.9 = (bf16[2,16,128,2048]{3,2,1,0:T(8,128)(2,1)}, bf16[3,2,4,128,256]{4,3,2,1,0:T(8,128)(2,1)}) custom-call(s32[7]{0:T(128)} %stack.98.where, bf16[4,512,512]{2,1,0:T(8,128)(2,1)} %rows.2.mine0_ref.mine1_ref, bf16[4,512,512]{2,1,0:T(8,128)(2,1)} %rows.3.mine1_ref, ...), custom_call_target="tpu_custom_call", output_to_operand_aliasing={{0}: (7, {})} | custom-call | flops 1610612736 | bytes 10485760 | tf_op jit(solution)/shard_map/gram/pallas_call | solution.py:181
  167.6 3.7 %collective-permute-start.17 = (bf16[3,2,4,128,256]{4,3,2,1,0:T(8,128)(2,1)}, bf16[3,2,4,128,256]{4,3,2,1,0:T(8,128)(2,1)S(1)}, u32[]{:S(2)}, u32[]{:S(2)}) collective-permute-start(bf16[3,2,4,128,256]{4,3,2,1,0:T(8,128)(2,1)} %get-tuple-element.52), channel_id=1, source_target_pairs={{0,8},{8,0},{1,9},{9,1},{2,10},{10,2},{3,11},{11,3},{4,12},{12,4},... | collective-permute-start | bytes 4718600 | tf_op jit(solution)/shard_map/ppermute | solution.py:254
  171.3 0.6 add_add_fusion
  171.9 0.0 collective-permute-done.18.sent_ref
  171.9 1.2 copy-done.3
  173.1 3.6 %place.2._ = bf16[2,16,128,2048]{3,2,1,0:T(8,128)(2,1)} custom-call(s32[4]{0:T(128)} %get-tuple-element.56.where, bf16[3,2,4,128,256]{4,3,2,1,0:T(8,128)(2,1)} %copy-done.3, bf16[2,16,128,2048]{3,2,1,0:T(8,128)(2,1)} %get-tuple-element.54._), custom_call_target="tpu_custom_call", output_to_operand_aliasing={{}: (2, {})} | custom-call | tf_op jit(solution)/shard_map/place/pallas_call | solution.py:226
  176.7 0.0 collective-permute-done.17.sent_ref
  176.7 1.2 copy-done.4
  177.9 3.6 %place.3 = bf16[2,16,128,2048]{3,2,1,0:T(8,128)(2,1)} custom-call(s32[4]{0:T(128)} %get-tuple-element.55.where, bf16[3,2,4,128,256]{4,3,2,1,0:T(8,128)(2,1)} %copy-done.4, bf16[2,16,128,2048]{3,2,1,0:T(8,128)(2,1)} %place.2._), custom_call_target="tpu_custom_call", output_to_operand_aliasing={{}: (2, {})} | custom-call | tf_op jit(solution)/shard_map/place/pallas_call | solution.py:226
  (12 shorter events, 0.0 us)
Async XLA Ops:
  31.0 4.4 %copy-start.7 = (bf16[16,4,2,32,128]{4,3,2,1,0:T(8,128)(2,1)S(1)}, bf16[16,4,2,32,128]{4,3,2,1,0:T(8,128)(2,1)}, u32[]{:S(2)}) copy-start(bf16[16,4,2,32,128]{4,3,2,1,0:T(8,128)(2,1)} %get-tuple-element.32) | copy-start | bytes 3145732
  32.8 24.2 %copy-start.1 = (bf16[4,512,256]{2,1,0:T(8,128)(2,1)}, bf16[4,512,256]{2,1,0:T(8,128)(2,1)S(1)}, u32[]{:S(2)}) copy-start(bf16[4,512,256]{2,1,0:T(8,128)(2,1)S(1)} %reshape.13.panel_ref.refs_0_) | copy-start | bytes 3145732
  32.8 26.9 %collective-permute-start = (bf16[4,512,256]{2,1,0:T(8,128)(2,1)S(1)}, bf16[4,512,256]{2,1,0:T(8,128)(2,1)}, u32[]{:S(2)}, u32[]{:S(2)}) collective-permute-start(bf16[4,512,256]{2,1,0:T(8,128)(2,1)S(1)} %reshape.13.panel_ref.refs_0_), channel_id=1, source_target_pairs={{0,32},{8,104},{32,64},{40,8},{64,96},{72,40},{96,0},{104,72},{1,3... | collective-permute-start | bytes 3145736 | tf_op jit(solution)/shard_map/ppermute | solution.py:251
  35.4 26.0 %collective-permute-start.5 = (bf16[4,512,256]{2,1,0:T(8,128)(2,1)S(1)}, bf16[4,512,256]{2,1,0:T(8,128)(2,1)}, u32[]{:S(2)}, u32[]{:S(2)}) collective-permute-start(bf16[4,512,256]{2,1,0:T(8,128)(2,1)S(1)} %reshape.13.panel_ref.refs_0_), channel_id=1, source_target_pairs={{0,96},{8,40},{32,0},{40,72},{64,32},{72,104},{96,64},{104,8},{1,9... | collective-permute-start | bytes 3145736 | tf_op jit(solution)/shard_map/ppermute | solution.py:252
  57.1 25.1 %copy-start = (bf16[4,512,256]{2,1,0:T(8,128)(2,1)}, bf16[4,512,256]{2,1,0:T(8,128)(2,1)S(1)}, u32[]{:S(2)}) copy-start(bf16[4,512,256]{2,1,0:T(8,128)(2,1)S(1)} %reshape.15.panel_ref.refs_0_) | copy-start | bytes 3145732
  57.1 25.1 %collective-permute-start.1 = (bf16[4,512,256]{2,1,0:T(8,128)(2,1)S(1)}, bf16[4,512,256]{2,1,0:T(8,128)(2,1)S(1)}, u32[]{:S(2)}, u32[]{:S(2)}) collective-permute-start(bf16[4,512,256]{2,1,0:T(8,128)(2,1)S(1)} %reshape.13.panel_ref.refs_0_), channel_id=1, source_target_pairs={{0,16},{16,0},{1,17},{17,1},{2,18},{18,2},{3,19},{19,3},{4,20},{20... | collective-permute-start | bytes 3145736 | tf_op jit(solution)/shard_map/ppermute | solution.py:253
  59.8 25.1 %collective-permute-start.4 = (bf16[4,512,256]{2,1,0:T(8,128)(2,1)S(1)}, bf16[4,512,256]{2,1,0:T(8,128)(2,1)}, u32[]{:S(2)}, u32[]{:S(2)}) collective-permute-start(bf16[4,512,256]{2,1,0:T(8,128)(2,1)S(1)} %reshape.15.panel_ref.refs_0_), channel_id=1, source_target_pairs={{0,32},{8,104},{32,64},{40,8},{64,96},{72,40},{96,0},{104,72},{1,3... | collective-permute-start | bytes 3145736 | tf_op jit(solution)/shard_map/ppermute | solution.py:251
  61.4 26.2 %collective-permute-start.7 = (bf16[4,512,256]{2,1,0:T(8,128)(2,1)S(1)}, bf16[4,512,256]{2,1,0:T(8,128)(2,1)}, u32[]{:S(2)}, u32[]{:S(2)}) collective-permute-start(bf16[4,512,256]{2,1,0:T(8,128)(2,1)S(1)} %reshape.15.panel_ref.refs_0_), channel_id=1, source_target_pairs={{0,96},{8,40},{32,0},{40,72},{64,32},{72,104},{96,64},{104,8},{1,9... | collective-permute-start | bytes 3145736 | tf_op jit(solution)/shard_map/ppermute | solution.py:252
  72.4 38.5 %collective-permute-start.10 = (bf16[3,2,4,128,256]{4,3,2,1,0:T(8,128)(2,1)}, bf16[3,2,4,128,256]{4,3,2,1,0:T(8,128)(2,1)}, u32[]{:S(2)}, u32[]{:S(2)}) collective-permute-start(bf16[3,2,4,128,256]{4,3,2,1,0:T(8,128)(2,1)} %get-tuple-element.43), channel_id=1, source_target_pairs={{0,8},{8,0},{1,9},{9,1},{2,10},{10,2},{3,11},{11,3},{4,12},{12,4},... | collective-permute-start | bytes 4718600 | tf_op jit(solution)/shard_map/ppermute | solution.py:254
  82.1 9.9 %copy-start.5 = (bf16[4,512,256]{2,1,0:T(8,128)(2,1)}, bf16[4,512,256]{2,1,0:T(8,128)(2,1)S(1)}, u32[]{:S(2)}) copy-start(bf16[4,512,256]{2,1,0:T(8,128)(2,1)S(1)} %collective-permute-done.1.refs_3_) | copy-start | bytes 3145732
  82.1 24.2 %collective-permute-start.2 = (bf16[4,512,256]{2,1,0:T(8,128)(2,1)S(1)}, bf16[4,512,256]{2,1,0:T(8,128)(2,1)}, u32[]{:S(2)}, u32[]{:S(2)}) collective-permute-start(bf16[4,512,256]{2,1,0:T(8,128)(2,1)S(1)} %reshape.15.panel_ref.refs_0_), channel_id=1, source_target_pairs={{0,16},{16,0},{1,17},{17,1},{2,18},{18,2},{3,19},{19,3},{4,20},{20... | collective-permute-start | bytes 3145736 | tf_op jit(solution)/shard_map/ppermute | solution.py:253
  84.9 24.3 %collective-permute-start.6 = (bf16[4,512,256]{2,1,0:T(8,128)(2,1)}, bf16[4,512,256]{2,1,0:T(8,128)(2,1)}, u32[]{:S(2)}, u32[]{:S(2)}) collective-permute-start(bf16[4,512,256]{2,1,0:T(8,128)(2,1)} %collective-permute-done.refs_1_), channel_id=1, source_target_pairs={{0,32},{8,104},{32,64},{40,8},{64,96},{72,40},{96,0},{104,72},{1,3... | collective-permute-start | bytes 3145736 | tf_op jit(solution)/shard_map/ppermute | solution.py:251
  87.6 22.8 %collective-permute-start.9 = (bf16[4,512,256]{2,1,0:T(8,128)(2,1)}, bf16[4,512,256]{2,1,0:T(8,128)(2,1)}, u32[]{:S(2)}, u32[]{:S(2)}) collective-permute-start(bf16[4,512,256]{2,1,0:T(8,128)(2,1)} %collective-permute-done.4.refs_1_), channel_id=1, source_target_pairs={{0,32},{8,104},{32,64},{40,8},{64,96},{72,40},{96,0},{104,72},{1,3... | collective-permute-start | bytes 3145736 | tf_op jit(solution)/shard_map/ppermute | solution.py:251
  98.9 40.1 %collective-permute-start.16 = (bf16[4,2,4,128,256]{4,3,2,1,0:T(8,128)(2,1)}, bf16[4,2,4,128,256]{4,3,2,1,0:T(8,128)(2,1)S(1)}, u32[]{:S(2)}, u32[]{:S(2)}) collective-permute-start(bf16[4,2,4,128,256]{4,3,2,1,0:T(8,128)(2,1)} %get-tuple-element.50), channel_id=1, source_target_pairs={{0,8},{8,0},{1,9},{9,1},{2,10},{10,2},{3,11},{11,3},{4,12},{12,4},... | collective-permute-start | bytes 6291464 | tf_op jit(solution)/shard_map/ppermute | solution.py:254
  106.3 23.5 %collective-permute-start.3 = (bf16[4,512,256]{2,1,0:T(8,128)(2,1)}, bf16[4,512,256]{2,1,0:T(8,128)(2,1)}, u32[]{:S(2)}, u32[]{:S(2)}) collective-permute-start(bf16[4,512,256]{2,1,0:T(8,128)(2,1)} %collective-permute-done.refs_1_), channel_id=1, source_target_pairs={{0,16},{16,0},{1,17},{17,1},{2,18},{18,2},{3,19},{19,3},{4,20},{20... | collective-permute-start | bytes 3145736 | tf_op jit(solution)/shard_map/ppermute | solution.py:253
  109.1 23.6 %collective-permute-start.8 = (bf16[4,512,256]{2,1,0:T(8,128)(2,1)}, bf16[4,512,256]{2,1,0:T(8,128)(2,1)S(1)}, u32[]{:S(2)}, u32[]{:S(2)}) collective-permute-start(bf16[4,512,256]{2,1,0:T(8,128)(2,1)} %copy-done.5), channel_id=1, source_target_pairs={{0,96},{8,40},{32,0},{40,72},{64,32},{72,104},{96,64},{104,8},{1,9... | collective-permute-start | bytes 3145736 | tf_op jit(solution)/shard_map/ppermute | solution.py:252
  110.4 27.2 %collective-permute-start.12 = (bf16[4,512,256]{2,1,0:T(8,128)(2,1)}, bf16[4,512,256]{2,1,0:T(8,128)(2,1)}, u32[]{:S(2)}, u32[]{:S(2)}) collective-permute-start(bf16[4,512,256]{2,1,0:T(8,128)(2,1)} %collective-permute-done.2.refs_2_), channel_id=1, source_target_pairs={{0,96},{8,40},{32,0},{40,72},{64,32},{72,104},{96,64},{104,8},{1,9... | collective-permute-start | bytes 3145736 | tf_op jit(solution)/shard_map/ppermute | solution.py:252
  117.8 33.7 %collective-permute-start.15 = (bf16[3,2,4,128,256]{4,3,2,1,0:T(8,128)(2,1)}, bf16[3,2,4,128,256]{4,3,2,1,0:T(8,128)(2,1)}, u32[]{:S(2)}, u32[]{:S(2)}) collective-permute-start(bf16[3,2,4,128,256]{4,3,2,1,0:T(8,128)(2,1)} %get-tuple-element.49), channel_id=1, source_target_pairs={{0,8},{8,0},{1,9},{9,1},{2,10},{10,2},{3,11},{11,3},{4,12},{12,4},... | collective-permute-start | bytes 4718600 | tf_op jit(solution)/shard_map/ppermute | solution.py:254
  129.8 22.5 %collective-permute-start.14 = (bf16[4,512,256]{2,1,0:T(8,128)(2,1)}, bf16[4,512,256]{2,1,0:T(8,128)(2,1)}, u32[]{:S(2)}, u32[]{:S(2)}) collective-permute-start(bf16[4,512,256]{2,1,0:T(8,128)(2,1)} %collective-permute-done.9.refs_1_), channel_id=1, source_target_pairs={{0,16},{16,0},{1,17},{17,1},{2,18},{18,2},{3,19},{19,3},{4,20},{20... | collective-permute-start | bytes 3145736 | tf_op jit(solution)/shard_map/ppermute | solution.py:253
  132.7 6.3 %copy-start.6 = (bf16[4,512,256]{2,1,0:T(8,128)(2,1)}, bf16[4,512,256]{2,1,0:T(8,128)(2,1)S(1)}, u32[]{:S(2)}) copy-start(bf16[4,512,256]{2,1,0:T(8,128)(2,1)S(1)} %collective-permute-done.8.refs_0_) | copy-start | bytes 3145732
  132.7 19.6 %collective-permute-start.11 = (bf16[4,512,256]{2,1,0:T(8,128)(2,1)}, bf16[4,512,256]{2,1,0:T(8,128)(2,1)}, u32[]{:S(2)}, u32[]{:S(2)}) collective-permute-start(bf16[4,512,256]{2,1,0:T(8,128)(2,1)} %collective-permute-done.3.refs_2_), channel_id=1, source_target_pairs={{0,32},{8,104},{32,64},{40,8},{64,96},{72,40},{96,0},{104,72},{1,3... | collective-permute-start | bytes 3145736 | tf_op jit(solution)/shard_map/ppermute | solution.py:251
  137.6 23.2 %collective-permute-start.13 = (bf16[4,512,256]{2,1,0:T(8,128)(2,1)}, bf16[4,512,256]{2,1,0:T(8,128)(2,1)}, u32[]{:S(2)}, u32[]{:S(2)}) collective-permute-start(bf16[4,512,256]{2,1,0:T(8,128)(2,1)} %collective-permute-done.2.refs_2_), channel_id=1, source_target_pairs={{0,32},{8,104},{32,64},{40,8},{64,96},{72,40},{96,0},{104,72},{1,3... | collective-permute-start | bytes 3145736 | tf_op jit(solution)/shard_map/ppermute | solution.py:251
  139.0 1.4 copy-start.2
  147.5 24.4 %collective-permute-start.18 = (bf16[3,2,4,128,256]{4,3,2,1,0:T(8,128)(2,1)}, bf16[3,2,4,128,256]{4,3,2,1,0:T(8,128)(2,1)S(1)}, u32[]{:S(2)}, u32[]{:S(2)}) collective-permute-start(bf16[3,2,4,128,256]{4,3,2,1,0:T(8,128)(2,1)} %get-tuple-element.53), channel_id=1, source_target_pairs={{0,8},{8,0},{1,9},{9,1},{2,10},{10,2},{3,11},{11,3},{4,12},{12,4},... | collective-permute-start | bytes 4718600 | tf_op jit(solution)/shard_map/ppermute | solution.py:254
  167.6 9.1 %collective-permute-start.17 = (bf16[3,2,4,128,256]{4,3,2,1,0:T(8,128)(2,1)}, bf16[3,2,4,128,256]{4,3,2,1,0:T(8,128)(2,1)S(1)}, u32[]{:S(2)}, u32[]{:S(2)}) collective-permute-start(bf16[3,2,4,128,256]{4,3,2,1,0:T(8,128)(2,1)} %get-tuple-element.52), channel_id=1, source_target_pairs={{0,8},{8,0},{1,9},{9,1},{2,10},{10,2},{3,11},{11,3},{4,12},{12,4},... | collective-permute-start | bytes 4718600 | tf_op jit(solution)/shard_map/ppermute | solution.py:254
  171.9 1.2 copy-start.3
  176.7 1.2 copy-start.4

commit v6 on v5

--- a/solution.py
+++ b/solution.py
@@ -95,7 +95,7 @@
         in_specs=[pl.BlockSpec((1, depth, width), lambda f: (f, 0, 0))],
         out_specs=pl.BlockSpec((1, 2 * width, depth), lambda f: (f, 0, 0)),
         out_shape=jax.ShapeDtypeStruct((bins, 2 * width, depth), panel.dtype),
-        compiler_params=pltpu.CompilerParams(vmem_limit_bytes=60 * MIB),
+        compiler_params=pltpu.CompilerParams(vmem_limit_bytes=24 * MIB),
         name="rows",
     )(panel)
 
@@ -104,10 +104,11 @@
     return pl.ds(pl.multiple_of(where[at] * cols, cols), cols)
 
 
-def gram_kernel(scale, chunks, placed, where, mine0_ref, mine1_ref, *refs):
+def gram_kernel(scale, chunks, placed, own, other, where, mine0_ref, mine1_ref, *refs):
     count, sets = len(chunks), len(placed)
     panels, sent, rest = refs[:count], refs[count : count + sets], refs[count + sets :]
-    out_ref, send_ref, slots, place_slots, sems, place_sems = rest[-6:]
+    slots, place_slots, sems, place_sems = rest[-4:]
+    out_ref, send_ref = rest[-5 - (own and other)], rest[-5]
     step, steps = pl.program_id(0), pl.num_programs(0)
     bins = mine0_ref.shape[0]
     rows, cols = mine0_ref.shape[1] // 4, panels[0].shape[2]
@@ -119,10 +120,14 @@
 
     def writes(at, held):
         for block, chunk in enumerate(chunks):
-            spot = out_ref.at[:, pl.ds(first_bin(core, chunk, at), bins), :, spot_of(where, block, cols)]
-            yield pltpu.make_async_copy(slots.at[held, block, core], spot, sems.at[held, block, 0])
-            spot = send_ref.at[block, :, pl.ds(at * bins, bins)]
-            yield pltpu.make_async_copy(slots.at[held, block, 1 - core], spot, sems.at[held, block, 1])
+            if own:
+                spot = out_ref.at[:, pl.ds(first_bin(core, chunk, at), bins), :, spot_of(where, block, cols)]
+                source = slots.at[held, block, core if other else 0]
+                yield pltpu.make_async_copy(source, spot, sems.at[held, block, 0])
+            if other:
+                spot = send_ref.at[block, :, pl.ds(at * bins, bins)]
+                source = slots.at[held, block, 1 - core if own else 0]
+                yield pltpu.make_async_copy(source, spot, sems.at[held, block, 1])
 
     def places(at, held):
         for k, (_, _, chunk) in enumerate(received):
@@ -142,9 +147,14 @@
     for block, chunk in enumerate(chunks):
         mine_ref = mine1_ref if chunk else mine0_ref
         for f in range(bins):
-            gram = jnp.dot(mine_ref[f], panels[block][f], preferred_element_type=jnp.float32) * scale
+            if own and other:
+                mine = mine_ref[f]
+            else:
+                target = core if own else 1 - core
+                mine = mine_ref[f, pl.ds(pl.multiple_of(target * 2 * rows, 2 * rows), 2 * rows), :]
+            gram = jnp.dot(mine, panels[block][f], preferred_element_type=jnp.float32) * scale
             gram = gram.astype(jnp.bfloat16)
-            for target in range(2):
+            for target in range(own + other):
                 for part in range(2):
                     base = (2 * target + part) * rows
                     slots[slot, block, target, part, f] = gram[base : base + rows]
@@ -164,7 +174,7 @@
     return pl.BlockSpec(block, lambda f, w: (0, 0, f, 0, 0))
 
 
-def gram(core, mine, blocks, shape, out, *sent):
+def gram(core, mine, blocks, shape, out, *sent, own=True, other=True):
     bins, depth, cols = blocks[0][3].shape
     rows, step = shape[2], 2
     count = len(blocks)
@@ -179,7 +189,9 @@
     send = jax.ShapeDtypeStruct((count, 2, bins, rows, cols), jnp.bfloat16)
     spots = max(len(received), 1)
     return pl.pallas_call(
-        functools.partial(gram_kernel, 2.0 / depth, chunks, [[block[0] for block in some] for some, _ in sent]),
+        functools.partial(
+            gram_kernel, 2.0 / depth, chunks, [[block[0] for block in some] for some, _ in sent], own, other
+        ),
         grid_spec=pltpu.PrefetchScalarGridSpec(
             num_scalar_prefetch=1,
             grid=(bins // step,),
@@ -187,22 +199,22 @@
             + [pl.BlockSpec((step, depth, cols), lambda f, w: (f, 0, 0))] * count
             + [sent_spec(results, step) for _, results in sent]
             + [pl.BlockSpec(memory_space=pl.ANY)] * len(held),
-            out_specs=[pl.BlockSpec(memory_space=pl.ANY)] * 2,
+            out_specs=[pl.BlockSpec(memory_space=pl.ANY)] * (own + other),
             scratch_shapes=[
-                pltpu.VMEM((2, count, 2, 2, step, rows, cols), jnp.bfloat16),
+                pltpu.VMEM((2, count, own + other, 2, step, rows, cols), jnp.bfloat16),
                 pltpu.VMEM((2, spots, 2, step, rows, cols), jnp.bfloat16),
                 pltpu.SemaphoreType.DMA((2, count, 2)),
                 pltpu.SemaphoreType.DMA((2, spots)),
             ],
         ),
-        out_shape=[jax.ShapeDtypeStruct(shape, jnp.bfloat16), send],
+        out_shape=[jax.ShapeDtypeStruct(shape, jnp.bfloat16)] * own + [send] * other,
         input_output_aliases={3 + count + len(sent): 0} if held else {},
         cost_estimate=pl.CostEstimate(
             flops=8 * count * bins * rows * depth * cols,
             bytes_accessed=2 * bins * (8 * rows * depth + count * (depth * cols + 4 * rows * cols)),
             transcendentals=0,
         ),
-        compiler_params=pltpu.CompilerParams(vmem_limit_bytes=60 * MIB),
+        compiler_params=pltpu.CompilerParams(vmem_limit_bytes=24 * MIB),
         name="gram",
     )(jnp.stack(where).astype(jnp.int32), *mine, *[block[3] for block in blocks], *[r for _, r in sent], *held)
 
@@ -234,7 +246,7 @@
         ),
         out_shape=jax.ShapeDtypeStruct(out.shape, out.dtype),
         input_output_aliases={2: 0},
-        compiler_params=pltpu.CompilerParams(vmem_limit_bytes=60 * MIB),
+        compiler_params=pltpu.CompilerParams(vmem_limit_bytes=24 * MIB),
         name="place",
     )(jnp.stack([block[2] for block in blocks] + [core]).astype(jnp.int32), results, out)
 
@@ -293,8 +305,8 @@
 
     sent4 = blocks4, swap(sent)
     blocks5 = [entry(0, 2, 1, foa), entry(1, 1, 1, nob), entry(1, 2, 1, fob)]
-    out, sent = gram(core, mine, blocks5, shape, out, sent3)
-    out = place(core, sent4, out)
+    (sent,) = gram(core, mine, blocks5, shape, None, own=False)
+    (out,) = gram(core, mine, blocks5, shape, out, sent3, sent4, other=False)
     return place(core, (blocks5, swap(sent)), out)
 
 

time: 183 us -> 183 us (level)
  waiting for transfers between devices: 31.8 us -> 51.2 us
  Pallas kernels: 56.9 us -> 45.4 us
  starting transfers between devices: 38.4 us -> 27.6 us
  local copies, waits for them, and re-layouts: 9.93 us -> 13.6 us
    ppermute x4, waiting for transfers between devices: 17.7 us -> 37.2 us  [shards(): over = lambda v: lax.ppermute(v, 'yh', [(0, 1), (1, 0)])]
    ppermute x5, starting transfers between devices: 19.8 us -> 9.54 us  [shards(): swap = lambda v: lax.ppermute(v, 'core', [(0, 1), (1, 0)])]
    pallas_call x2, Pallas kernels: 7.5 us -> 2.9 us  [rows_of(): pl.pallas_call(rows_kernel, grid=(bins,), in_specs=[pl.BlockSpec((1, dept...]
    pallas_call x2 -> x1, Pallas kernels: 7.16 us -> 3.46 us  [place(): pl.pallas_call(functools.partial(place_kernel, [block[0] for block in blo...]
    unnamed x16, local copies, waits for them, and re-layouts: 3.76 us -> 6.89 us
    pallas_call x5 -> x6, Pallas kernels: 34.4 us -> 31.3 us  [gram(): pl.pallas_call(functools.partial(gram_kernel, 2.0 / depth, chunks, [[bloc...]
    another operation x4, local copies, waits for them, and re-layouts: 2.59 us -> 0.34 us  [gram(): jnp.stack(where).astype(jnp.int32)]
  transfers between devices with their start and end apart: 19 -> 19, of which waited for: 8 -> 8; matrix products, arithmetic and copies ran while one was open for 3% -> 2% of each run, Pallas kernels for 25% -> 19%
where the time goes in v6:
time: 183 us; the launch traced here: 182 us
  waiting for transfers between devices  51.2 us (28%)
  Pallas kernels  45.4 us (25%)
  blocking collectives  43.1 us (24%)
  starting transfers between devices  27.6 us (15%)
  local copies, waits for them, and re-layouts  13.6 us (7%)
    all_to_all x2, blocking collectives, owned(): lax.all_to_all(chunk, ('yl', 'z', 'core'), split_axis=0, concat_axis=0, t...  43.1 us
    ppermute x4, waiting for transfers between devices, shards(): over = lambda v: lax.ppermute(v, 'yh', [(0, 1), (1, 0)])  37.2 us
    pallas_call x6, Pallas kernels, gram(): pl.pallas_call(functools.partial(gram_kernel, 2.0 / depth, chunks, [[bloc...  31.3 us
    ppermute x4, starting transfers between devices, shards(): over = lambda v: lax.ppermute(v, 'yh', [(0, 1), (1, 0)])  10.6 us
    ppermute x6, waiting for transfers between devices, shards(): fwd = lambda v: lax.ppermute(v, ('x', 'core'), mirrored(1))  9.77 us
    ppermute x5, starting transfers between devices, shards(): swap = lambda v: lax.ppermute(v, 'core', [(0, 1), (1, 0)])  9.54 us
    pallas_call x1, Pallas kernels, whiten(): pl.pallas_call(whiten_kernel, grid=(segments // SEG_STEP,), in_specs=[pl....  7.8 us
    ppermute x6, starting transfers between devices, shards(): fwd = lambda v: lax.ppermute(v, ('x', 'core'), mirrored(1))  7.47 us
  transfers between devices with their start and end apart: 19, of which 8 were waited for; matrix products, arithmetic and copies ran while one was open for 2% of the time, Pallas kernels for 19%

profile of v6, /device:TPU:1, one launch (start us, length us, event | category | flops | bytes accessed | tf_op | source)
XLA Modules:
  0.0 181.5 jit_solution(11180638803046799613)
XLA Ops:
  0.0 7.8 %whiten.1 = (bf16[16,4,2,32,128]{4,3,2,1,0:T(8,128)(2,1)}, bf16[16,4,2,32,128]{4,3,2,1,0:T(8,128)(2,1)}) custom-call(bf16[128,32,512]{2,1,0:T(8,128)(2,1)} %records_ref.1, s32[32,128]{1,0:T(8,128)} %bitcast.28, bf16[512,256]{1,0:T(8,128)(2,1)} %constant.183.clone.high_ref, bf16[512,256]{1,0:T(8,128)(2,1)} %constant.184.clone.low_ref), custom_call_target="tpu_custom_call" | custom-call | tf_op jit(solution)/shard_map/whiten/pallas_call | solution.py:56
  7.8 23.3 %all_to_all.10 = bf16[16,4,2,32,128]{4,3,2,1,0:T(8,128)(2,1)S(1)} all-to-all(bf16[16,4,2,32,128]{4,3,2,1,0:T(8,128)(2,1)} %get-tuple-element.28), channel_id=1, replica_groups=mesh['x'=4,'yh'=2,'core'=2,'yl'=2,'z'=4] {'yl','z','core'}, dimensions={0} | all-to-all | bytes 2097152 | tf_op jit(solution)/shard_map/all_to_all | solution.py:270
  31.1 1.1 copy.15
  32.1 1.5 reshape.13.panel_ref.refs_0_
  33.6 2.5 %collective-permute-start = (bf16[4,512,256]{2,1,0:T(8,128)(2,1)}, bf16[4,512,256]{2,1,0:T(8,128)(2,1)}, u32[]{:S(2)}, u32[]{:S(2)}) collective-permute-start(bf16[4,512,256]{2,1,0:T(8,128)(2,1)} %reshape.13.panel_ref.refs_0_), channel_id=1, source_target_pairs={{0,32},{8,104},{32,64},{40,8},{64,96},{72,40},{96,0},{104,72},{1,3... | collective-permute-start | bytes 3145736 | tf_op jit(solution)/shard_map/ppermute | solution.py:263
  36.1 0.0 collective-permute-start.5
  36.1 19.8 %all_to_all.11 = bf16[16,4,2,32,128]{4,3,2,1,0:T(8,128)(2,1)S(1)} all-to-all(bf16[16,4,2,32,128]{4,3,2,1,0:T(8,128)(2,1)S(1)} %copy-done.7), channel_id=1, replica_groups=mesh['x'=4,'yh'=2,'core'=2,'yl'=2,'z'=4] {'yl','z','core'}, dimensions={0} | all-to-all | bytes 2097152 | tf_op jit(solution)/shard_map/all_to_all | solution.py:270
  56.0 2.0 %copy.14 = bf16[8,2,4,2,32,128]{5,1,4,0,3,2:T(2,128)(2,1)} copy(bf16[8,2,4,2,32,128]{5,4,3,2,1,0:T(8,128)(2,1)S(1)} %bitcast.26) | data formatting | bytes 2097152 | tf_op jit(solution)/shard_map/reshape | solution.py:271
  58.0 1.7 reshape.15.panel_ref.refs_0_
  59.8 2.7 %collective-permute-start.1 = (bf16[4,512,256]{2,1,0:T(8,128)(2,1)}, bf16[4,512,256]{2,1,0:T(8,128)(2,1)}, u32[]{:S(2)}, u32[]{:S(2)}) collective-permute-start(bf16[4,512,256]{2,1,0:T(8,128)(2,1)} %reshape.13.panel_ref.refs_0_), channel_id=1, source_target_pairs={{0,16},{16,0},{1,17},{17,1},{2,18},{18,2},{3,19},{19,3},{4,20},{20... | collective-permute-start | bytes 3145736 | tf_op jit(solution)/shard_map/ppermute | solution.py:265
  62.5 0.0 collective-permute-done.refs_1_
  62.5 1.6 collective-permute-start.4
  64.1 0.0 collective-permute-done.5.refs_2_
  64.1 1.0 copy-done.4
  65.1 0.0 collective-permute-start.7
  65.1 0.1 add_add_fusion.2.where
  65.1 2.4 %rows.2.mine0_ref.mine1_ref = bf16[4,512,512]{2,1,0:T(8,128)(2,1)S(1)} custom-call(bf16[4,512,256]{2,1,0:T(8,128)(2,1)} %reshape.13.panel_ref.refs_0_), custom_call_target="tpu_custom_call" | custom-call | tf_op jit(solution)/shard_map/rows/pallas_call | solution.py:92
  67.5 5.1 %gram.6 = (bf16[2,16,128,2048]{3,2,1,0:T(8,128)(2,1)}, bf16[3,2,4,128,256]{4,3,2,1,0:T(8,128)(2,1)}) custom-call(s32[4]{0:T(128)S(1)} %add_add_fusion.2.where, bf16[4,512,512]{2,1,0:T(8,128)(2,1)S(1)} %rows.2.mine0_ref.mine1_ref, bf16[4,512,512]{2,1,0:T(8,128)(2,1)S(1)} %rows.2.mine0_ref.mine1_ref, bf16[4,512,256]{2,1,0:T(8,128)(2,1)} %reshape.13.panel_ref.refs_0_, ...), custom_call_target="tpu_custom_call" | custom-call | flops 1610612736 | bytes 10485760 | tf_op jit(solution)/shard_map/gram/pallas_call | solution.py:191
  72.6 12.5 %collective-permute-done.1.refs_3_ = bf16[4,512,256]{2,1,0:T(8,128)(2,1)} collective-permute-done((bf16[4,512,256]{2,1,0:T(8,128)(2,1)}, bf16[4,512,256]{2,1,0:T(8,128)(2,1)}, u32[]{:S(2)}, u32[]{:S(2)}) %collective-permute-start.1) | collective-permute-done | bytes 1048608 | tf_op jit(solution)/shard_map/ppermute | solution.py:265
  85.2 2.6 %collective-permute-start.2 = (bf16[4,512,256]{2,1,0:T(8,128)(2,1)S(1)}, bf16[4,512,256]{2,1,0:T(8,128)(2,1)}, u32[]{:S(2)}, u32[]{:S(2)}) collective-permute-start(bf16[4,512,256]{2,1,0:T(8,128)(2,1)S(1)} %reshape.15.panel_ref.refs_0_), channel_id=1, source_target_pairs={{0,16},{16,0},{1,17},{17,1},{2,18},{18,2},{3,19},{19,3},{4,20},{20... | collective-permute-start | bytes 3145736 | tf_op jit(solution)/shard_map/ppermute | solution.py:265
  87.8 0.0 collective-permute-done.4.refs_1_
  87.8 1.6 collective-permute-start.6
  89.4 1.2 collective-permute-done.7.refs_2_
  90.6 0.0 collective-permute-start.9
  90.6 1.3 collective-permute-start.10
  91.9 0.1 stack.105.where
  92.0 0.5 rows.3.mine1_ref
  92.5 6.1 %gram.7 = (bf16[2,16,128,2048]{3,2,1,0:T(8,128)(2,1)}, bf16[4,2,4,128,256]{4,3,2,1,0:T(8,128)(2,1)}) custom-call(s32[5]{0:T(128)S(1)} %stack.105.where, bf16[4,512,512]{2,1,0:T(8,128)(2,1)S(1)} %rows.2.mine0_ref.mine1_ref, bf16[4,512,512]{2,1,0:T(8,128)(2,1)S(1)} %rows.3.mine1_ref, ...), custom_call_target="tpu_custom_call", output_to_operand_aliasing={{0}: (7, {})} | custom-call | flops 2147483648 | bytes 12582912 | tf_op jit(solution)/shard_map/gram/pallas_call | solution.py:191
  98.7 0.1 collective-permute-start.17
  98.8 10.5 %collective-permute-done.2.refs_2_ = bf16[4,512,256]{2,1,0:T(8,128)(2,1)} collective-permute-done((bf16[4,512,256]{2,1,0:T(8,128)(2,1)S(1)}, bf16[4,512,256]{2,1,0:T(8,128)(2,1)}, u32[]{:S(2)}, u32[]{:S(2)}) %collective-permute-start.2) | collective-permute-done | bytes 1048608 | tf_op jit(solution)/shard_map/ppermute | solution.py:265
  109.3 2.6 %collective-permute-start.3 = (bf16[4,512,256]{2,1,0:T(8,128)(2,1)}, bf16[4,512,256]{2,1,0:T(8,128)(2,1)}, u32[]{:S(2)}, u32[]{:S(2)}) collective-permute-start(bf16[4,512,256]{2,1,0:T(8,128)(2,1)} %collective-permute-done.refs_1_), channel_id=1, source_target_pairs={{0,16},{16,0},{1,17},{17,1},{2,18},{18,2},{3,19},{19,3},{4,20},{20... | collective-permute-start | bytes 3145736 | tf_op jit(solution)/shard_map/ppermute | solution.py:265
  112.0 1.3 collective-permute-done.9.refs_1_
  113.3 0.0 collective-permute-start.12
  113.3 0.1 stack.109.where
  113.4 0.0 collective-permute-done.10.refs_3_
  113.4 1.6 copy-done.1
  115.0 5.4 %gram.8 = (bf16[2,16,128,2048]{3,2,1,0:T(8,128)(2,1)}, bf16[3,2,4,128,256]{4,3,2,1,0:T(8,128)(2,1)S(1)}) custom-call(s32[7]{0:T(128)S(1)} %stack.109.where, bf16[4,512,512]{2,1,0:T(8,128)(2,1)S(1)} %rows.2.mine0_ref.mine1_ref, bf16[4,512,512]{2,1,0:T(8,128)(2,1)S(1)} %copy-done.1, ...), custom_call_target="tpu_custom_call", output_to_operand_aliasing={{0}: (7, {})} | custom-call | flops 1610612736 | bytes 10485760 | tf_op jit(solution)/shard_map/gram/pallas_call | solution.py:191
  120.4 1.1 copy-done.6
  121.6 11.2 %collective-permute-done.3.refs_2_ = bf16[4,512,256]{2,1,0:T(8,128)(2,1)} collective-permute-done((bf16[4,512,256]{2,1,0:T(8,128)(2,1)}, bf16[4,512,256]{2,1,0:T(8,128)(2,1)}, u32[]{:S(2)}, u32[]{:S(2)}) %collective-permute-start.3) | collective-permute-done | bytes 1048608 | tf_op jit(solution)/shard_map/ppermute | solution.py:265
  132.8 2.6 %collective-permute-start.14 = (bf16[4,512,256]{2,1,0:T(8,128)(2,1)}, bf16[4,512,256]{2,1,0:T(8,128)(2,1)S(1)}, u32[]{:S(2)}, u32[]{:S(2)}) collective-permute-start(bf16[4,512,256]{2,1,0:T(8,128)(2,1)} %collective-permute-done.9.refs_1_), channel_id=1, source_target_pairs={{0,16},{16,0},{1,17},{17,1},{2,18},{18,2},{3,19},{19,3},{4,20},{20... | collective-permute-start | bytes 3145736 | tf_op jit(solution)/shard_map/ppermute | solution.py:265
  135.4 1.6 collective-permute-start.11
  137.0 3.0 %collective-permute-done.12.refs_1_ = bf16[4,512,256]{2,1,0:T(8,128)(2,1)} collective-permute-done((bf16[4,512,256]{2,1,0:T(8,128)(2,1)}, bf16[4,512,256]{2,1,0:T(8,128)(2,1)}, u32[]{:S(2)}, u32[]{:S(2)}) %collective-permute-start.12) | collective-permute-done | bytes 1048608 | tf_op jit(solution)/shard_map/ppermute | solution.py:264
  140.0 0.2 collective-permute-start.13
  140.2 0.1 stack.114.where
  140.3 0.1 add_add_fusion.1.where
  140.3 4.4 %collective-permute-start.16 = (bf16[3,2,4,128,256]{4,3,2,1,0:T(8,128)(2,1)}, bf16[3,2,4,128,256]{4,3,2,1,0:T(8,128)(2,1)}, u32[]{:S(2)}, u32[]{:S(2)}) collective-permute-start(bf16[3,2,4,128,256]{4,3,2,1,0:T(8,128)(2,1)} %copy-done.6), channel_id=1, source_target_pairs={{0,8},{8,0},{1,9},{9,1},{2,10},{10,2},{3,11},{11,3},{4,12},{12,4},... | collective-permute-start | bytes 4718600 | tf_op jit(solution)/shard_map/ppermute | solution.py:266
  144.8 0.0 collective-permute-done.17.refs_3_
  144.8 1.6 copy-done.2
  146.3 5.8 %gram.10 = (bf16[2,16,128,2048]{3,2,1,0:T(8,128)(2,1)}, bf16[3,2,4,128,256]{4,3,2,1,0:T(8,128)(2,1)}) custom-call(s32[8]{0:T(128)S(1)} %stack.114.where, bf16[4,512,512]{2,1,0:T(8,128)(2,1)S(1)} %rows.2.mine0_ref.mine1_ref, bf16[4,512,512]{2,1,0:T(8,128)(2,1)S(1)} %copy-done.2, ...), custom_call_target="tpu_custom_call", output_to_operand_aliasing={{0}: (7, {})} | custom-call | flops 1610612736 | bytes 10485760 | tf_op jit(solution)/shard_map/gram/pallas_call | solution.py:191
  152.2 0.1 collective-permute-start.18
  152.3 2.9 %collective-permute-done.14.refs_2_ = bf16[4,512,256]{2,1,0:T(8,128)(2,1)S(1)} collective-permute-done((bf16[4,512,256]{2,1,0:T(8,128)(2,1)}, bf16[4,512,256]{2,1,0:T(8,128)(2,1)S(1)}, u32[]{:S(2)}, u32[]{:S(2)}) %collective-permute-start.14) | collective-permute-done | bytes 1048608 | tf_op jit(solution)/shard_map/ppermute | solution.py:265
  155.2 0.0 collective-permute-done.11.refs_0_
  155.2 8.4 %collective-permute-done.13.refs_1_ = bf16[4,512,256]{2,1,0:T(8,128)(2,1)} collective-permute-done((bf16[4,512,256]{2,1,0:T(8,128)(2,1)}, bf16[4,512,256]{2,1,0:T(8,128)(2,1)}, u32[]{:S(2)}, u32[]{:S(2)}) %collective-permute-start.13) | collective-permute-done | bytes 1048608 | tf_op jit(solution)/shard_map/ppermute | solution.py:263
  163.7 4.0 %gram.9 = bf16[3,2,4,128,256]{4,3,2,1,0:T(8,128)(2,1)} custom-call(s32[4]{0:T(128)S(1)} %add_add_fusion.1.where, bf16[4,512,512]{2,1,0:T(8,128)(2,1)S(1)} %rows.2.mine0_ref.mine1_ref, bf16[4,512,512]{2,1,0:T(8,128)(2,1)S(1)} %copy-done.2, bf16[4,512,256]{2,1,0:T(8,128)(2,1)} %collective-permute-done.11.refs_0_, ...), custom_call_target="tpu_custom_call" | custom-call | flops 1610612736 | bytes 10485760 | tf_op jit(solution)/shard_map/gram/pallas_call | solution.py:191
  167.6 3.6 %collective-permute-start.15 = (bf16[3,2,4,128,256]{4,3,2,1,0:T(8,128)(2,1)}, bf16[3,2,4,128,256]{4,3,2,1,0:T(8,128)(2,1)}, u32[]{:S(2)}, u32[]{:S(2)}) collective-permute-start(bf16[3,2,4,128,256]{4,3,2,1,0:T(8,128)(2,1)} %gram.9), channel_id=1, source_target_pairs={{0,8},{8,0},{1,9},{9,1},{2,10},{10,2},{3,11},{11,3},{4,12},{12,4},... | collective-permute-start | bytes 4718600 | tf_op jit(solution)/shard_map/ppermute | solution.py:266
  171.2 0.1 stack.112.where
  171.3 0.1 add_add_fusion.where
  171.4 0.0 collective-permute-done.16.refs_3_
  171.4 0.0 collective-permute-done.18.refs_4_
  171.4 0.0 copy-start.3
  171.4 1.6 copy-done.3
  173.0 4.8 %gram.11._ = bf16[2,16,128,2048]{3,2,1,0:T(8,128)(2,1)} custom-call(s32[10]{0:T(128)S(1)} %stack.112.where, bf16[4,512,512]{2,1,0:T(8,128)(2,1)S(1)} %rows.2.mine0_ref.mine1_ref, bf16[4,512,512]{2,1,0:T(8,128)(2,1)S(1)} %copy-done.3, bf16[4,512,256]{2,1,0:T(8,128)(2,1)} %collective-permute-done.11.refs_0_, ...), custom_call_target="tpu_custom_call", output_to_operand_aliasing={{}: (8, {})} | custom-call | flops 1610612736 | bytes 10485760 | tf_op jit(solution)/shard_map/gram/pallas_call | solution.py:191
  177.9 0.0 collective-permute-done.15.sent_ref
  177.9 3.5 %place.1 = bf16[2,16,128,2048]{3,2,1,0:T(8,128)(2,1)} custom-call(s32[4]{0:T(128)S(1)} %add_add_fusion.where, bf16[3,2,4,128,256]{4,3,2,1,0:T(8,128)(2,1)} %collective-permute-done.15.sent_ref, bf16[2,16,128,2048]{3,2,1,0:T(8,128)(2,1)} %gram.11._), custom_call_target="tpu_custom_call", output_to_operand_aliasing={{}: (2, {})} | custom-call | tf_op jit(solution)/shard_map/place/pallas_call | solution.py:238
  (13 shorter events, 0.0 us)
Async XLA Ops:
  31.1 5.1 %copy-start.7 = (bf16[16,4,2,32,128]{4,3,2,1,0:T(8,128)(2,1)S(1)}, bf16[16,4,2,32,128]{4,3,2,1,0:T(8,128)(2,1)}, u32[]{:S(2)}) copy-start(bf16[16,4,2,32,128]{4,3,2,1,0:T(8,128)(2,1)} %get-tuple-element.30) | copy-start | bytes 3145732
  33.6 28.8 %collective-permute-start = (bf16[4,512,256]{2,1,0:T(8,128)(2,1)}, bf16[4,512,256]{2,1,0:T(8,128)(2,1)}, u32[]{:S(2)}, u32[]{:S(2)}) collective-permute-start(bf16[4,512,256]{2,1,0:T(8,128)(2,1)} %reshape.13.panel_ref.refs_0_), channel_id=1, source_target_pairs={{0,32},{8,104},{32,64},{40,8},{64,96},{72,40},{96,0},{104,72},{1,3... | collective-permute-start | bytes 3145736 | tf_op jit(solution)/shard_map/ppermute | solution.py:263
  36.1 28.0 %collective-permute-start.5 = (bf16[4,512,256]{2,1,0:T(8,128)(2,1)}, bf16[4,512,256]{2,1,0:T(8,128)(2,1)S(1)}, u32[]{:S(2)}, u32[]{:S(2)}) collective-permute-start(bf16[4,512,256]{2,1,0:T(8,128)(2,1)} %reshape.13.panel_ref.refs_0_), channel_id=1, source_target_pairs={{0,96},{8,40},{32,0},{40,72},{64,32},{72,104},{96,64},{104,8},{1,9... | collective-permute-start | bytes 3145736 | tf_op jit(solution)/shard_map/ppermute | solution.py:264
  59.8 25.4 %collective-permute-start.1 = (bf16[4,512,256]{2,1,0:T(8,128)(2,1)}, bf16[4,512,256]{2,1,0:T(8,128)(2,1)}, u32[]{:S(2)}, u32[]{:S(2)}) collective-permute-start(bf16[4,512,256]{2,1,0:T(8,128)(2,1)} %reshape.13.panel_ref.refs_0_), channel_id=1, source_target_pairs={{0,16},{16,0},{1,17},{17,1},{2,18},{18,2},{3,19},{19,3},{4,20},{20... | collective-permute-start | bytes 3145736 | tf_op jit(solution)/shard_map/ppermute | solution.py:265
  62.5 25.3 %collective-permute-start.4 = (bf16[4,512,256]{2,1,0:T(8,128)(2,1)S(1)}, bf16[4,512,256]{2,1,0:T(8,128)(2,1)}, u32[]{:S(2)}, u32[]{:S(2)}) collective-permute-start(bf16[4,512,256]{2,1,0:T(8,128)(2,1)S(1)} %reshape.15.panel_ref.refs_0_), channel_id=1, source_target_pairs={{0,32},{8,104},{32,64},{40,8},{64,96},{72,40},{96,0},{104,72},{1,3... | collective-permute-start | bytes 3145736 | tf_op jit(solution)/shard_map/ppermute | solution.py:263
  64.1 1.0 copy-start.4
  65.1 25.5 %collective-permute-start.7 = (bf16[4,512,256]{2,1,0:T(8,128)(2,1)S(1)}, bf16[4,512,256]{2,1,0:T(8,128)(2,1)}, u32[]{:S(2)}, u32[]{:S(2)}) collective-permute-start(bf16[4,512,256]{2,1,0:T(8,128)(2,1)S(1)} %reshape.15.panel_ref.refs_0_), channel_id=1, source_target_pairs={{0,96},{8,40},{32,0},{40,72},{64,32},{72,104},{96,64},{104,8},{1,9... | collective-permute-start | bytes 3145736 | tf_op jit(solution)/shard_map/ppermute | solution.py:264
  65.1 2.5 %copy-start.5 = (bf16[4,512,256]{2,1,0:T(8,128)(2,1)S(1)}, bf16[4,512,256]{2,1,0:T(8,128)(2,1)}, u32[]{:S(2)}) copy-start(bf16[4,512,256]{2,1,0:T(8,128)(2,1)} %copy-done.4) | copy-start | bytes 3145732
  85.2 24.2 %collective-permute-start.2 = (bf16[4,512,256]{2,1,0:T(8,128)(2,1)S(1)}, bf16[4,512,256]{2,1,0:T(8,128)(2,1)}, u32[]{:S(2)}, u32[]{:S(2)}) collective-permute-start(bf16[4,512,256]{2,1,0:T(8,128)(2,1)S(1)} %reshape.15.panel_ref.refs_0_), channel_id=1, source_target_pairs={{0,16},{16,0},{1,17},{17,1},{2,18},{18,2},{3,19},{19,3},{4,20},{20... | collective-permute-start | bytes 3145736 | tf_op jit(solution)/shard_map/ppermute | solution.py:265
  87.8 24.2 %collective-permute-start.6 = (bf16[4,512,256]{2,1,0:T(8,128)(2,1)}, bf16[4,512,256]{2,1,0:T(8,128)(2,1)}, u32[]{:S(2)}, u32[]{:S(2)}) collective-permute-start(bf16[4,512,256]{2,1,0:T(8,128)(2,1)} %collective-permute-done.refs_1_), channel_id=1, source_target_pairs={{0,32},{8,104},{32,64},{40,8},{64,96},{72,40},{96,0},{104,72},{1,3... | collective-permute-start | bytes 3145736 | tf_op jit(solution)/shard_map/ppermute | solution.py:263
  90.6 22.7 %collective-permute-start.9 = (bf16[4,512,256]{2,1,0:T(8,128)(2,1)}, bf16[4,512,256]{2,1,0:T(8,128)(2,1)}, u32[]{:S(2)}, u32[]{:S(2)}) collective-permute-start(bf16[4,512,256]{2,1,0:T(8,128)(2,1)} %collective-permute-done.4.refs_1_), channel_id=1, source_target_pairs={{0,32},{8,104},{32,64},{40,8},{64,96},{72,40},{96,0},{104,72},{1,3... | collective-permute-start | bytes 3145736 | tf_op jit(solution)/shard_map/ppermute | solution.py:263
  90.6 22.8 %collective-permute-start.10 = (bf16[3,2,4,128,256]{4,3,2,1,0:T(8,128)(2,1)}, bf16[3,2,4,128,256]{4,3,2,1,0:T(8,128)(2,1)}, u32[]{:S(2)}, u32[]{:S(2)}) collective-permute-start(bf16[3,2,4,128,256]{4,3,2,1,0:T(8,128)(2,1)} %get-tuple-element.41), channel_id=1, source_target_pairs={{0,8},{8,0},{1,9},{9,1},{2,10},{10,2},{3,11},{11,3},{4,12},{12,4},... | collective-permute-start | bytes 4718600 | tf_op jit(solution)/shard_map/ppermute | solution.py:266
  92.5 6.2 %copy-start = (bf16[4,512,512]{2,1,0:T(8,128)(2,1)}, bf16[4,512,512]{2,1,0:T(8,128)(2,1)S(1)}, u32[]{:S(2)}) copy-start(bf16[4,512,512]{2,1,0:T(8,128)(2,1)S(1)} %rows.3.mine1_ref) | copy-start | bytes 6291460
  98.7 46.1 %collective-permute-start.17 = (bf16[4,2,4,128,256]{4,3,2,1,0:T(8,128)(2,1)}, bf16[4,2,4,128,256]{4,3,2,1,0:T(8,128)(2,1)}, u32[]{:S(2)}, u32[]{:S(2)}) collective-permute-start(bf16[4,2,4,128,256]{4,3,2,1,0:T(8,128)(2,1)} %get-tuple-element.48), channel_id=1, source_target_pairs={{0,8},{8,0},{1,9},{9,1},{2,10},{10,2},{3,11},{11,3},{4,12},{12,4},... | collective-permute-start | bytes 6291464 | tf_op jit(solution)/shard_map/ppermute | solution.py:266
  109.3 23.5 %collective-permute-start.3 = (bf16[4,512,256]{2,1,0:T(8,128)(2,1)}, bf16[4,512,256]{2,1,0:T(8,128)(2,1)}, u32[]{:S(2)}, u32[]{:S(2)}) collective-permute-start(bf16[4,512,256]{2,1,0:T(8,128)(2,1)} %collective-permute-done.refs_1_), channel_id=1, source_target_pairs={{0,16},{16,0},{1,17},{17,1},{2,18},{18,2},{3,19},{19,3},{4,20},{20... | collective-permute-start | bytes 3145736 | tf_op jit(solution)/shard_map/ppermute | solution.py:265
  112.0 23.5 %collective-permute-start.8 = (bf16[4,512,256]{2,1,0:T(8,128)(2,1)}, bf16[4,512,256]{2,1,0:T(8,128)(2,1)}, u32[]{:S(2)}, u32[]{:S(2)}) collective-permute-start(bf16[4,512,256]{2,1,0:T(8,128)(2,1)} %collective-permute-done.1.refs_3_), channel_id=1, source_target_pairs={{0,96},{8,40},{32,0},{40,72},{64,32},{72,104},{96,64},{104,8},{1,9... | collective-permute-start | bytes 3145736 | tf_op jit(solution)/shard_map/ppermute | solution.py:264
  113.3 26.7 %collective-permute-start.12 = (bf16[4,512,256]{2,1,0:T(8,128)(2,1)}, bf16[4,512,256]{2,1,0:T(8,128)(2,1)}, u32[]{:S(2)}, u32[]{:S(2)}) collective-permute-start(bf16[4,512,256]{2,1,0:T(8,128)(2,1)} %collective-permute-done.2.refs_2_), channel_id=1, source_target_pairs={{0,96},{8,40},{32,0},{40,72},{64,32},{72,104},{96,64},{104,8},{1,9... | collective-permute-start | bytes 3145736 | tf_op jit(solution)/shard_map/ppermute | solution.py:264
  113.4 1.6 copy-start.1
  120.4 1.1 copy-start.6
  132.8 22.4 %collective-permute-start.14 = (bf16[4,512,256]{2,1,0:T(8,128)(2,1)}, bf16[4,512,256]{2,1,0:T(8,128)(2,1)S(1)}, u32[]{:S(2)}, u32[]{:S(2)}) collective-permute-start(bf16[4,512,256]{2,1,0:T(8,128)(2,1)} %collective-permute-done.9.refs_1_), channel_id=1, source_target_pairs={{0,16},{16,0},{1,17},{17,1},{2,18},{18,2},{3,19},{19,3},{4,20},{20... | collective-permute-start | bytes 3145736 | tf_op jit(solution)/shard_map/ppermute | solution.py:265
  135.4 19.8 %collective-permute-start.11 = (bf16[4,512,256]{2,1,0:T(8,128)(2,1)}, bf16[4,512,256]{2,1,0:T(8,128)(2,1)}, u32[]{:S(2)}, u32[]{:S(2)}) collective-permute-start(bf16[4,512,256]{2,1,0:T(8,128)(2,1)} %collective-permute-done.3.refs_2_), channel_id=1, source_target_pairs={{0,32},{8,104},{32,64},{40,8},{64,96},{72,40},{96,0},{104,72},{1,3... | collective-permute-start | bytes 3145736 | tf_op jit(solution)/shard_map/ppermute | solution.py:263
  140.0 23.7 %collective-permute-start.13 = (bf16[4,512,256]{2,1,0:T(8,128)(2,1)}, bf16[4,512,256]{2,1,0:T(8,128)(2,1)}, u32[]{:S(2)}, u32[]{:S(2)}) collective-permute-start(bf16[4,512,256]{2,1,0:T(8,128)(2,1)} %collective-permute-done.2.refs_2_), channel_id=1, source_target_pairs={{0,32},{8,104},{32,64},{40,8},{64,96},{72,40},{96,0},{104,72},{1,3... | collective-permute-start | bytes 3145736 | tf_op jit(solution)/shard_map/ppermute | solution.py:263
  140.3 31.1 %collective-permute-start.16 = (bf16[3,2,4,128,256]{4,3,2,1,0:T(8,128)(2,1)}, bf16[3,2,4,128,256]{4,3,2,1,0:T(8,128)(2,1)}, u32[]{:S(2)}, u32[]{:S(2)}) collective-permute-start(bf16[3,2,4,128,256]{4,3,2,1,0:T(8,128)(2,1)} %copy-done.6), channel_id=1, source_target_pairs={{0,8},{8,0},{1,9},{9,1},{2,10},{10,2},{3,11},{11,3},{4,12},{12,4},... | collective-permute-start | bytes 4718600 | tf_op jit(solution)/shard_map/ppermute | solution.py:266
  144.8 1.6 copy-start.2
  152.2 19.2 %collective-permute-start.18 = (bf16[3,2,4,128,256]{4,3,2,1,0:T(8,128)(2,1)}, bf16[3,2,4,128,256]{4,3,2,1,0:T(8,128)(2,1)}, u32[]{:S(2)}, u32[]{:S(2)}) collective-permute-start(bf16[3,2,4,128,256]{4,3,2,1,0:T(8,128)(2,1)} %get-tuple-element.49), channel_id=1, source_target_pairs={{0,8},{8,0},{1,9},{9,1},{2,10},{10,2},{3,11},{11,3},{4,12},{12,4},... | collective-permute-start | bytes 4718600 | tf_op jit(solution)/shard_map/ppermute | solution.py:266
  167.6 10.2 %collective-permute-start.15 = (bf16[3,2,4,128,256]{4,3,2,1,0:T(8,128)(2,1)}, bf16[3,2,4,128,256]{4,3,2,1,0:T(8,128)(2,1)}, u32[]{:S(2)}, u32[]{:S(2)}) collective-permute-start(bf16[3,2,4,128,256]{4,3,2,1,0:T(8,128)(2,1)} %gram.9), channel_id=1, source_target_pairs={{0,8},{8,0},{1,9},{9,1},{2,10},{10,2},{3,11},{11,3},{4,12},{12,4},... | collective-permute-start | bytes 4718600 | tf_op jit(solution)/shard_map/ppermute | solution.py:266
  171.4 1.6 copy-start.3

commit v7 on v6

--- a/solution.py
+++ b/solution.py
@@ -74,27 +74,25 @@
 
 
 def rows_kernel(panel_ref, mine_ref):
-    bins, depth, width = panel_ref.shape
-    half, rows = depth // 2, width // 2
-    for f in range(bins):
-        for core in range(2):
-            real = panel_ref[f, :half, core * rows : (core + 1) * rows].T
-            imag = panel_ref[f, half:, core * rows : (core + 1) * rows].T
-            base = 2 * rows * core
-            mine_ref[f, base : base + rows, :half] = real
-            mine_ref[f, base : base + rows, half:] = imag
-            mine_ref[f, base + rows : base + 2 * rows, :half] = imag
-            mine_ref[f, base + rows : base + 2 * rows, half:] = -real
+    sources, _, depth, rows = panel_ref.shape
+    panel = panel_ref[:, 0].reshape(sources // 2, 2, 2, depth // 2, rows)
+    for core in range(2):
+        part = panel[:, core]
+        turned = jnp.stack([part[:, 1], -part[:, 0]], axis=1)
+        base = 2 * rows * core
+        mine_ref[0, base : base + rows] = part.reshape(-1, rows).T
+        mine_ref[0, base + rows : base + 2 * rows] = turned.reshape(-1, rows).T
 
 
 def rows_of(panel):
-    bins, depth, width = panel.shape
+    sources, bins, depth, rows = panel.shape
+    block = (1, 4 * rows, sources // 2 * depth)
     return pl.pallas_call(
         rows_kernel,
         grid=(bins,),
-        in_specs=[pl.BlockSpec((1, depth, width), lambda f: (f, 0, 0))],
-        out_specs=pl.BlockSpec((1, 2 * width, depth), lambda f: (f, 0, 0)),
-        out_shape=jax.ShapeDtypeStruct((bins, 2 * width, depth), panel.dtype),
+        in_specs=[pl.BlockSpec((sources, 1, depth, rows), lambda f: (0, f, 0, 0))],
+        out_specs=pl.BlockSpec(block, lambda f: (f, 0, 0)),
+        out_shape=jax.ShapeDtypeStruct((bins, *block[1:]), panel.dtype),
         compiler_params=pltpu.CompilerParams(vmem_limit_bytes=24 * MIB),
         name="rows",
     )(panel)
@@ -111,7 +109,7 @@
     out_ref, send_ref = rest[-5 - (own and other)], rest[-5]
     step, steps = pl.program_id(0), pl.num_programs(0)
     bins = mine0_ref.shape[0]
-    rows, cols = mine0_ref.shape[1] // 4, panels[0].shape[2]
+    rows, cols = mine0_ref.shape[1] // 4, 2 * panels[0].shape[3]
     slot, core = lax.rem(step, 2), where[count]
     received = [(which, at, chunk) for which, some in enumerate(placed) for at, chunk in enumerate(some)]
 
@@ -152,7 +150,9 @@
             else:
                 target = core if own else 1 - core
                 mine = mine_ref[f, pl.ds(pl.multiple_of(target * 2 * rows, 2 * rows), 2 * rows), :]
-            gram = jnp.dot(mine, panels[block][f], preferred_element_type=jnp.float32) * scale
+            panel = panels[block][:, f].reshape(-1, 2, *panels[block].shape[2:])
+            panel = jnp.concatenate([panel[:, side].reshape(-1, rows) for side in range(2)], axis=1)
+            gram = jnp.dot(mine, panel, preferred_element_type=jnp.float32) * scale
             gram = gram.astype(jnp.bfloat16)
             for target in range(own + other):
                 for part in range(2):
@@ -175,8 +175,8 @@
 
 
 def gram(core, mine, blocks, shape, out, *sent, own=True, other=True):
-    bins, depth, cols = blocks[0][3].shape
-    rows, step = shape[2], 2
+    sources, bins, part, rows = blocks[0][3].shape
+    depth, cols, step = sources // 2 * part, 2 * rows, 2
     count = len(blocks)
     chunks = [block[0] for block in blocks]
     received = [block for some, _ in sent for block in some]
@@ -196,7 +196,7 @@
             num_scalar_prefetch=1,
             grid=(bins // step,),
             in_specs=used
-            + [pl.BlockSpec((step, depth, cols), lambda f, w: (f, 0, 0))] * count
+            + [pl.BlockSpec((sources, step, part, rows), lambda f, w: (0, f, 0, 0))] * count
             + [sent_spec(results, step) for _, results in sent]
             + [pl.BlockSpec(memory_space=pl.ANY)] * len(held),
             out_specs=[pl.BlockSpec(memory_space=pl.ANY)] * (own + other),
@@ -268,8 +268,7 @@
 
     def owned(chunk):
         got = lax.all_to_all(chunk, ("yl", "z", "core"), split_axis=0, concat_axis=0, tiled=True)
-        got = got.reshape(OWNERS, 2, *got.shape[1:])
-        return jnp.transpose(got, (2, 3, 0, 4, 1, 5)).reshape(CHUNK, -1, 2 * stations)
+        return got.reshape(2 * OWNERS, CHUNK, -1, stations)
 
     def entry(chunk, dx, dy, panel):
         sign = 1 - 2 * core
@@ -304,10 +303,14 @@
     out, sent = gram(core, mine, blocks4, shape, out, sent2)
 
     sent4 = blocks4, swap(sent)
-    blocks5 = [entry(0, 2, 1, foa), entry(1, 1, 1, nob), entry(1, 2, 1, fob)]
-    (sent,) = gram(core, mine, blocks5, shape, None, own=False)
-    (out,) = gram(core, mine, blocks5, shape, out, sent3, sent4, other=False)
-    return place(core, (blocks5, swap(sent)), out)
+    blocks5 = [entry(0, 2, 1, foa)]
+    out, sent = gram(core, mine, blocks5, shape, out, sent3)
+
+    sent5 = blocks5, swap(sent)
+    blocks6 = [entry(1, 1, 1, after(nob, out)), entry(1, 2, 1, fob)]
+    (sent,) = gram(core, mine, blocks6, shape, None, own=False)
+    (out,) = gram(core, mine, blocks6, shape, out, sent4, sent5, other=False)
+    return place(core, (blocks6, swap(sent)), out)
 
 
 def solution(mesh):

time: 183 us -> 179 us (0.978)
  waiting for transfers between devices: 51.2 us -> 39.2 us
  starting transfers between devices: 27.6 us -> 37.3 us
  local copies, waits for them, and re-layouts: 13.6 us -> 9.96 us
  Pallas kernels: 45.4 us -> 48.3 us
    ppermute x4, waiting for transfers between devices: 37.2 us -> 21.3 us  [shards(): over = lambda v: lax.ppermute(v, 'yh', [(0, 1), (1, 0)])]
    ppermute x5 -> x6, starting transfers between devices: 9.54 us -> 19.2 us  [shards(): swap = lambda v: lax.ppermute(v, 'core', [(0, 1), (1, 0)])]
    reshape x4 -> x0, local copies, waits for them, and re-layouts: 6.37 us -> none  [the longest x2 3.24 us: owned(): jnp.transpose(got, (2, 3, 0, 4, 1, 5)).reshape(CHUNK, -1, 2 * stations)]
    ppermute x4, waiting for transfers between devices: 4.18 us -> 10.3 us  [shards(): bwd = lambda v: lax.ppermute(v, ('x', 'core'), mirrored(-1))]
    ppermute x6, waiting for transfers between devices: 9.77 us -> 4.54 us  [shards(): fwd = lambda v: lax.ppermute(v, ('x', 'core'), mirrored(1))]
    ppermute x5 -> x6, waiting for transfers between devices: 0.01 us -> 3.14 us  [shards(): swap = lambda v: lax.ppermute(v, 'core', [(0, 1), (1, 0)])]
    unnamed x16 -> x20, local copies, waits for them, and re-layouts: 6.89 us -> 9.54 us
    pallas_call x6 -> x7, Pallas kernels: 31.3 us -> 33.8 us  [gram(): pl.pallas_call(functools.partial(gram_kernel, 2.0 / depth, chunks, [[bloc...]
  transfers between devices with their start and end apart: 19 -> 20, of which waited for: 8 -> 10; matrix products, arithmetic and copies ran while one was open for 2% -> 0% of each run, Pallas kernels for 19% -> 21%
where the time goes in v7:
time: 179 us
  Pallas kernels  48.3 us (27%)
  blocking collectives  43.3 us (24%)
  waiting for transfers between devices  39.2 us (22%)
  starting transfers between devices  37.3 us (21%)
  local copies, waits for them, and re-layouts  9.96 us (6%)
    all_to_all x2, blocking collectives, owned(): lax.all_to_all(chunk, ('yl', 'z', 'core'), split_axis=0, concat_axis=0, t...  43.3 us
    pallas_call x7, Pallas kernels, gram(): pl.pallas_call(functools.partial(gram_kernel, 2.0 / depth, chunks, [[bloc...  33.8 us
    ppermute x4, waiting for transfers between devices, shards(): over = lambda v: lax.ppermute(v, 'yh', [(0, 1), (1, 0)])  21.3 us
    ppermute x6, starting transfers between devices, shards(): swap = lambda v: lax.ppermute(v, 'core', [(0, 1), (1, 0)])  19.2 us
    ppermute x4, starting transfers between devices, shards(): over = lambda v: lax.ppermute(v, 'yh', [(0, 1), (1, 0)])  10.5 us
    ppermute x4, waiting for transfers between devices, shards(): bwd = lambda v: lax.ppermute(v, ('x', 'core'), mirrored(-1))  10.3 us
    unnamed x20, local copies, waits for them, and re-layouts  9.54 us
    pallas_call x1, Pallas kernels, whiten(): pl.pallas_call(whiten_kernel, grid=(segments // SEG_STEP,), in_specs=[pl....  7.78 us
  transfers between devices with their start and end apart: 20, of which 10 were waited for; matrix products, arithmetic and copies ran while one was open for 0% of the time, Pallas kernels for 21%

profile of v7, /device:TPU:1, one launch (start us, length us, event | category | flops | bytes accessed | tf_op | source)
XLA Modules:
  0.0 178.6 jit_solution(5619246665225881758)
XLA Ops:
  0.0 7.8 %whiten.1 = (bf16[16,4,2,32,128]{4,3,2,1,0:T(8,128)(2,1)}, bf16[16,4,2,32,128]{4,3,2,1,0:T(8,128)(2,1)}) custom-call(bf16[128,32,512]{2,1,0:T(8,128)(2,1)} %records_ref.1, s32[32,128]{1,0:T(8,128)} %bitcast.23, bf16[512,256]{1,0:T(8,128)(2,1)} %constant.183.clone.high_ref, bf16[512,256]{1,0:T(8,128)(2,1)} %constant.184.clone.low_ref), custom_call_target="tpu_custom_call" | custom-call | tf_op jit(solution)/shard_map/whiten/pallas_call | solution.py:56
  7.8 23.5 %all_to_all.10 = bf16[16,4,2,32,128]{4,3,2,1,0:T(8,128)(2,1)} all-to-all(bf16[16,4,2,32,128]{4,3,2,1,0:T(8,128)(2,1)} %get-tuple-element.31), channel_id=1, replica_groups=mesh['x'=4,'yh'=2,'core'=2,'yl'=2,'z'=4] {'yl','z','core'}, dimensions={0} | all-to-all | bytes 2097152 | tf_op jit(solution)/shard_map/all_to_all | solution.py:270
  31.3 2.5 %collective-permute-start.2 = (bf16[16,4,64,128]{3,2,1,0:T(8,128)(2,1)}, bf16[16,4,64,128]{3,2,1,0:T(8,128)(2,1)}, u32[]{:S(2)}, u32[]{:S(2)}) collective-permute-start(bf16[16,4,64,128]{3,2,1,0:T(8,128)(2,1)} %bitcast.6.panel_ref.refs_0_), channel_id=1, source_target_pairs={{0,32},{8,104},{32,64},{40,8},{64,96},{72,40},{96,0},{104,72},{1,3... | collective-permute-start | bytes 3145736 | tf_op jit(solution)/shard_map/ppermute | solution.py:263
  33.8 0.0 collective-permute-start.4
  33.8 19.8 %all_to_all.11 = bf16[16,4,2,32,128]{4,3,2,1,0:T(8,128)(2,1)S(1)} all-to-all(bf16[16,4,2,32,128]{4,3,2,1,0:T(8,128)(2,1)S(1)} %copy-done.9), channel_id=1, replica_groups=mesh['x'=4,'yh'=2,'core'=2,'yl'=2,'z'=4] {'yl','z','core'}, dimensions={0} | all-to-all | bytes 2097152 | tf_op jit(solution)/shard_map/all_to_all | solution.py:270
  53.6 2.6 %collective-permute-start = (bf16[16,4,64,128]{3,2,1,0:T(8,128)(2,1)}, bf16[16,4,64,128]{3,2,1,0:T(8,128)(2,1)}, u32[]{:S(2)}, u32[]{:S(2)}) collective-permute-start(bf16[16,4,64,128]{3,2,1,0:T(8,128)(2,1)} %bitcast.6.panel_ref.refs_0_), channel_id=1, source_target_pairs={{0,16},{16,0},{1,17},{17,1},{2,18},{18,2},{3,19},{19,3},{4,20},{20... | collective-permute-start | bytes 3145736 | tf_op jit(solution)/shard_map/ppermute | solution.py:265
  56.2 0.0 collective-permute-done.2.refs_1_
  56.2 1.9 %collective-permute-start.3 = (bf16[16,4,64,128]{3,2,1,0:T(8,128)(2,1)S(1)}, bf16[16,4,64,128]{3,2,1,0:T(8,128)(2,1)}, u32[]{:S(2)}, u32[]{:S(2)}) collective-permute-start(bf16[16,4,64,128]{3,2,1,0:T(8,128)(2,1)S(1)} %bitcast.18), channel_id=1, source_target_pairs={{0,32},{8,104},{32,64},{40,8},{64,96},{72,40},{96,0},{104,72},{1,3... | collective-permute-start | bytes 3145736 | tf_op jit(solution)/shard_map/ppermute | solution.py:263
  58.2 1.0 collective-permute-done.4.refs_2_
  59.2 1.0 copy-done.7
  60.2 0.0 collective-permute-start.5
  60.2 0.1 pad_add_fusion.where
  60.3 2.6 %rows.2.mine0_ref.mine1_ref = bf16[4,512,512]{2,1,0:T(8,128)(2,1)S(1)} custom-call(bf16[16,4,64,128]{3,2,1,0:T(8,128)(2,1)} %bitcast.6.panel_ref.refs_0_), custom_call_target="tpu_custom_call" | custom-call | tf_op jit(solution)/shard_map/rows/pallas_call | solution.py:90
  62.9 5.1 %gram.7 = (bf16[2,16,128,2048]{3,2,1,0:T(8,128)(2,1)}, bf16[3,2,4,128,256]{4,3,2,1,0:T(8,128)(2,1)}) custom-call(s32[4]{0:T(128)S(1)} %pad_add_fusion.where, bf16[4,512,512]{2,1,0:T(8,128)(2,1)S(1)} %rows.2.mine0_ref.mine1_ref, bf16[4,512,512]{2,1,0:T(8,128)(2,1)S(1)} %rows.2.mine0_ref.mine1_ref, bf16[16,4,64,128]{3,2,1,0:T(8,128)(2,1)} %bitcast.6.panel_ref.refs_0_, ...), custom_call_target="tpu_custom_call" | custom-call | flops 1610612736 | bytes 10485760 | tf_op jit(solution)/shard_map/gram/pallas_call | solution.py:191
  68.0 3.3 %collective-permute-start.12 = (bf16[3,2,4,128,256]{4,3,2,1,0:T(8,128)(2,1)}, bf16[3,2,4,128,256]{4,3,2,1,0:T(8,128)(2,1)}, u32[]{:S(2)}, u32[]{:S(2)}) collective-permute-start(bf16[3,2,4,128,256]{4,3,2,1,0:T(8,128)(2,1)} %get-tuple-element.46), channel_id=1, source_target_pairs={{0,8},{8,0},{1,9},{9,1},{2,10},{10,2},{3,11},{11,3},{4,12},{12,4},... | collective-permute-start | bytes 4718600 | tf_op jit(solution)/shard_map/ppermute | solution.py:266
  71.3 7.6 %collective-permute-done.refs_3_ = bf16[16,4,64,128]{3,2,1,0:T(8,128)(2,1)} collective-permute-done((bf16[16,4,64,128]{3,2,1,0:T(8,128)(2,1)}, bf16[16,4,64,128]{3,2,1,0:T(8,128)(2,1)}, u32[]{:S(2)}, u32[]{:S(2)}) %collective-permute-start) | collective-permute-done | bytes 1048608 | tf_op jit(solution)/shard_map/ppermute | solution.py:265
  78.9 2.6 %collective-permute-start.1 = (bf16[16,4,64,128]{3,2,1,0:T(8,128)(2,1)S(1)}, bf16[16,4,64,128]{3,2,1,0:T(8,128)(2,1)}, u32[]{:S(2)}, u32[]{:S(2)}) collective-permute-start(bf16[16,4,64,128]{3,2,1,0:T(8,128)(2,1)S(1)} %bitcast.20), channel_id=1, source_target_pairs={{0,16},{16,0},{1,17},{17,1},{2,18},{18,2},{3,19},{19,3},{4,20},{20... | collective-permute-start | bytes 3145736 | tf_op jit(solution)/shard_map/ppermute | solution.py:265
  81.5 1.6 collective-permute-start.10
  83.1 3.0 %collective-permute-done.5.refs_2_ = bf16[16,4,64,128]{3,2,1,0:T(8,128)(2,1)} collective-permute-done((bf16[16,4,64,128]{3,2,1,0:T(8,128)(2,1)S(1)}, bf16[16,4,64,128]{3,2,1,0:T(8,128)(2,1)}, u32[]{:S(2)}, u32[]{:S(2)}) %collective-permute-start.5) | collective-permute-done | bytes 1048608 | tf_op jit(solution)/shard_map/ppermute | solution.py:264
  86.1 0.0 collective-permute-start.6
  86.1 0.1 stack.110.where
  86.2 0.9 rows.3.mine1_ref
  87.1 6.1 %gram.8 = (bf16[2,16,128,2048]{3,2,1,0:T(8,128)(2,1)}, bf16[4,2,4,128,256]{4,3,2,1,0:T(8,128)(2,1)}) custom-call(s32[5]{0:T(128)S(1)} %stack.110.where, bf16[4,512,512]{2,1,0:T(8,128)(2,1)S(1)} %rows.2.mine0_ref.mine1_ref, bf16[4,512,512]{2,1,0:T(8,128)(2,1)S(1)} %rows.3.mine1_ref, ...), custom_call_target="tpu_custom_call", output_to_operand_aliasing={{0}: (7, {})} | custom-call | flops 2147483648 | bytes 12582912 | tf_op jit(solution)/shard_map/gram/pallas_call | solution.py:191
  93.3 0.1 collective-permute-start.15
  93.4 9.7 %collective-permute-done.1.refs_2_ = bf16[16,4,64,128]{3,2,1,0:T(8,128)(2,1)} collective-permute-done((bf16[16,4,64,128]{3,2,1,0:T(8,128)(2,1)S(1)}, bf16[16,4,64,128]{3,2,1,0:T(8,128)(2,1)}, u32[]{:S(2)}, u32[]{:S(2)}) %collective-permute-start.1) | collective-permute-done | bytes 1048608 | tf_op jit(solution)/shard_map/ppermute | solution.py:265
  103.1 2.6 %collective-permute-start.9 = (bf16[16,4,64,128]{3,2,1,0:T(8,128)(2,1)}, bf16[16,4,64,128]{3,2,1,0:T(8,128)(2,1)}, u32[]{:S(2)}, u32[]{:S(2)}) collective-permute-start(bf16[16,4,64,128]{3,2,1,0:T(8,128)(2,1)} %collective-permute-done.2.refs_1_), channel_id=1, source_target_pairs={{0,16},{16,0},{1,17},{17,1},{2,18},{18,2},{3,19},{19,3},{4,20},{20... | collective-permute-start | bytes 3145736 | tf_op jit(solution)/shard_map/ppermute | solution.py:265
  105.7 0.0 collective-permute-done.10.refs_0_
  105.7 0.0 collective-permute-start.11
  105.7 1.3 collective-permute-done.6.refs_1_
  107.0 0.0 collective-permute-start.7
  107.0 0.1 stack.114.where
  107.1 0.0 collective-permute-done.12.refs_3_
  107.1 1.6 copy-done.1
  108.7 5.7 %gram.9 = (bf16[2,16,128,2048]{3,2,1,0:T(8,128)(2,1)}, bf16[3,2,4,128,256]{4,3,2,1,0:T(8,128)(2,1)}) custom-call(s32[7]{0:T(128)S(1)} %stack.114.where, bf16[4,512,512]{2,1,0:T(8,128)(2,1)S(1)} %rows.2.mine0_ref.mine1_ref, bf16[4,512,512]{2,1,0:T(8,128)(2,1)S(1)} %copy-done.1, ...), custom_call_target="tpu_custom_call", output_to_operand_aliasing={{0}: (7, {})} | custom-call | flops 1610612736 | bytes 10485760 | tf_op jit(solution)/shard_map/gram/pallas_call | solution.py:191
  114.4 9.8 %collective-permute-start.14 = (bf16[3,2,4,128,256]{4,3,2,1,0:T(8,128)(2,1)}, bf16[3,2,4,128,256]{4,3,2,1,0:T(8,128)(2,1)}, u32[]{:S(2)}, u32[]{:S(2)}) collective-permute-start(bf16[3,2,4,128,256]{4,3,2,1,0:T(8,128)(2,1)} %get-tuple-element.49), channel_id=1, source_target_pairs={{0,8},{8,0},{1,9},{9,1},{2,10},{10,2},{3,11},{11,3},{4,12},{12,4},... | collective-permute-start | bytes 4718600 | tf_op jit(solution)/shard_map/ppermute | solution.py:266
  124.3 2.3 %collective-permute-done.9.refs_2_ = bf16[16,4,64,128]{3,2,1,0:T(8,128)(2,1)} collective-permute-done((bf16[16,4,64,128]{3,2,1,0:T(8,128)(2,1)}, bf16[16,4,64,128]{3,2,1,0:T(8,128)(2,1)}, u32[]{:S(2)}, u32[]{:S(2)}) %collective-permute-start.9) | collective-permute-done | bytes 1048608 | tf_op jit(solution)/shard_map/ppermute | solution.py:265
  126.6 1.0 copy-done.5
  127.5 1.6 collective-permute-start.13
  129.1 6.2 %collective-permute-done.7.refs_1_ = bf16[16,4,64,128]{3,2,1,0:T(8,128)(2,1)} collective-permute-done((bf16[16,4,64,128]{3,2,1,0:T(8,128)(2,1)}, bf16[16,4,64,128]{3,2,1,0:T(8,128)(2,1)}, u32[]{:S(2)}, u32[]{:S(2)}) %collective-permute-start.7) | collective-permute-done | bytes 1048608 | tf_op jit(solution)/shard_map/ppermute | solution.py:264
  135.4 0.0 collective-permute-start.8
  135.4 2.6 %collective-permute-start.16 = (bf16[16,4,64,128]{3,2,1,0:T(8,128)(2,1)}, bf16[16,4,64,128]{3,2,1,0:T(8,128)(2,1)}, u32[]{:S(2)}, u32[]{:S(2)}) collective-permute-start(bf16[16,4,64,128]{3,2,1,0:T(8,128)(2,1)} %collective-permute-done.6.refs_1_), channel_id=1, source_target_pairs={{0,16},{16,0},{1,17},{17,1},{2,18},{18,2},{3,19},{19,3},{4,20},{20... | collective-permute-start | bytes 3145736 | tf_op jit(solution)/shard_map/ppermute | solution.py:265
  138.0 0.1 stack.116.where
  138.1 1.6 copy-done.2
  139.7 1.2 copy-done.6
  140.9 5.7 %gram.10 = (bf16[2,16,128,2048]{3,2,1,0:T(8,128)(2,1)}, bf16[3,2,4,128,256]{4,3,2,1,0:T(8,128)(2,1)}) custom-call(s32[8]{0:T(128)S(1)} %stack.116.where, bf16[4,512,512]{2,1,0:T(8,128)(2,1)S(1)} %rows.2.mine0_ref.mine1_ref, bf16[4,512,512]{2,1,0:T(8,128)(2,1)S(1)} %copy-done.2, ...), custom_call_target="tpu_custom_call", output_to_operand_aliasing={{0}: (7, {})} | custom-call | flops 1610612736 | bytes 10485760 | tf_op jit(solution)/shard_map/gram/pallas_call | solution.py:191
  146.6 2.1 %collective-permute-start.18 = (bf16[3,2,4,128,256]{4,3,2,1,0:T(8,128)(2,1)}, bf16[3,2,4,128,256]{4,3,2,1,0:T(8,128)(2,1)}, u32[]{:S(2)}, u32[]{:S(2)}) collective-permute-start(bf16[3,2,4,128,256]{4,3,2,1,0:T(8,128)(2,1)} %get-tuple-element.55), channel_id=1, source_target_pairs={{0,8},{8,0},{1,9},{9,1},{2,10},{10,2},{3,11},{11,3},{4,12},{12,4},... | collective-permute-start | bytes 4718600 | tf_op jit(solution)/shard_map/ppermute | solution.py:266
  148.7 0.1 stack.105.where
  148.7 0.1 add_add_fusion.1.where
  148.8 0.0 collective-permute-done.14.refs_1_
  148.8 0.0 collective-permute-done.13.refs_0_
  148.8 1.6 copy-done.3
  150.4 3.8 %gram.11 = (bf16[2,16,128,2048]{3,2,1,0:T(8,128)(2,1)}, bf16[1,2,4,128,256]{4,3,2,1,0:T(8,128)(2,1)}) custom-call(s32[5]{0:T(128)S(1)} %stack.105.where, bf16[4,512,512]{2,1,0:T(8,128)(2,1)S(1)} %rows.2.mine0_ref.mine1_ref, bf16[4,512,512]{2,1,0:T(8,128)(2,1)S(1)} %copy-done.3, ...), custom_call_target="tpu_custom_call", output_to_operand_aliasing={{0}: (5, {})} | custom-call | flops 536870912 | bytes 6291456 | tf_op jit(solution)/shard_map/gram/pallas_call | solution.py:191
  154.2 3.2 %collective-permute-done.8.refs_0_ = bf16[16,4,64,128]{3,2,1,0:T(8,128)(2,1)S(1)} collective-permute-done((bf16[16,4,64,128]{3,2,1,0:T(8,128)(2,1)}, bf16[16,4,64,128]{3,2,1,0:T(8,128)(2,1)S(1)}, u32[]{:S(2)}, u32[]{:S(2)}) %collective-permute-start.8) | collective-permute-done | bytes 1048608 | tf_op jit(solution)/shard_map/ppermute | solution.py:263
  157.4 1.6 collective-permute-done.16.refs_1_
  159.1 3.4 %gram.12 = bf16[2,2,4,128,256]{4,3,2,1,0:T(8,128)(2,1)} custom-call(s32[3]{0:T(128)S(1)} %add_add_fusion.1.where, bf16[4,512,512]{2,1,0:T(8,128)(2,1)S(1)} %rows.2.mine0_ref.mine1_ref, bf16[4,512,512]{2,1,0:T(8,128)(2,1)S(1)} %copy-done.3, bf16[16,4,64,128]{3,2,1,0:T(8,128)(2,1)S(1)} %collective-permute-done.8.refs_0_, ...), custom_call_target="tpu_custom_call" | custom-call | flops 1073741824 | bytes 8388608 | tf_op jit(solution)/shard_map/gram/pallas_call | solution.py:191
  162.5 3.8 %collective-permute-start.17 = (bf16[2,2,4,128,256]{4,3,2,1,0:T(8,128)(2,1)}, bf16[2,2,4,128,256]{4,3,2,1,0:T(8,128)(2,1)}, u32[]{:S(2)}, u32[]{:S(2)}) collective-permute-start(bf16[2,2,4,128,256]{4,3,2,1,0:T(8,128)(2,1)} %gram.12), channel_id=1, source_target_pairs={{0,8},{8,0},{1,9},{9,1},{2,10},{10,2},{3,11},{11,3},{4,12},{12,4},... | collective-permute-start | bytes 3145736 | tf_op jit(solution)/shard_map/ppermute | solution.py:266
  166.3 0.1 collective-permute-start.19
  166.4 0.1 stack.118.where
  166.5 0.1 add_add_fusion.where
  166.5 3.1 %collective-permute-done.19.refs_3_ = bf16[1,2,4,128,256]{4,3,2,1,0:T(8,128)(2,1)} collective-permute-done((bf16[1,2,4,128,256]{4,3,2,1,0:T(8,128)(2,1)}, bf16[1,2,4,128,256]{4,3,2,1,0:T(8,128)(2,1)}, u32[]{:S(2)}, u32[]{:S(2)}) %collective-permute-start.19) | collective-permute-done | bytes 524320 | tf_op jit(solution)/shard_map/ppermute | solution.py:266
  169.7 0.0 collective-permute-done.18.refs_2_
  169.7 1.6 copy-done.4
  171.3 4.0 %gram.13._ = bf16[2,16,128,2048]{3,2,1,0:T(8,128)(2,1)} custom-call(s32[7]{0:T(128)S(1)} %stack.118.where, bf16[4,512,512]{2,1,0:T(8,128)(2,1)S(1)} %rows.2.mine0_ref.mine1_ref, bf16[4,512,512]{2,1,0:T(8,128)(2,1)S(1)} %copy-done.4, bf16[16,4,64,128]{3,2,1,0:T(8,128)(2,1)S(1)} %collective-permute-done.8.refs_0_, ...), custom_call_target="tpu_custom_call", output_to_operand_aliasing={{}: (7, {})} | custom-call | flops 1073741824 | bytes 8388608 | tf_op jit(solution)/shard_map/gram/pallas_call | solution.py:191
  175.3 3.2 %place.1 = bf16[2,16,128,2048]{3,2,1,0:T(8,128)(2,1)} custom-call(s32[3]{0:T(128)S(1)} %add_add_fusion.where, bf16[2,2,4,128,256]{4,3,2,1,0:T(8,128)(2,1)} %collective-permute-done.17.sent_ref, bf16[2,16,128,2048]{3,2,1,0:T(8,128)(2,1)} %gram.13._), custom_call_target="tpu_custom_call", output_to_operand_aliasing={{}: (2, {})} | custom-call | tf_op jit(solution)/shard_map/place/pallas_call | solution.py:238
  (17 shorter events, 0.0 us)
Async XLA Ops:
  7.8 26.0 %copy-start.9 = (bf16[16,4,2,32,128]{4,3,2,1,0:T(8,128)(2,1)S(1)}, bf16[16,4,2,32,128]{4,3,2,1,0:T(8,128)(2,1)}, u32[]{:S(2)}) copy-start(bf16[16,4,2,32,128]{4,3,2,1,0:T(8,128)(2,1)} %get-tuple-element.33) | copy-start | bytes 3145732
  31.3 25.0 %collective-permute-start.2 = (bf16[16,4,64,128]{3,2,1,0:T(8,128)(2,1)}, bf16[16,4,64,128]{3,2,1,0:T(8,128)(2,1)}, u32[]{:S(2)}, u32[]{:S(2)}) collective-permute-start(bf16[16,4,64,128]{3,2,1,0:T(8,128)(2,1)} %bitcast.6.panel_ref.refs_0_), channel_id=1, source_target_pairs={{0,32},{8,104},{32,64},{40,8},{64,96},{72,40},{96,0},{104,72},{1,3... | collective-permute-start | bytes 3145736 | tf_op jit(solution)/shard_map/ppermute | solution.py:263
  33.8 25.5 %collective-permute-start.4 = (bf16[16,4,64,128]{3,2,1,0:T(8,128)(2,1)}, bf16[16,4,64,128]{3,2,1,0:T(8,128)(2,1)S(1)}, u32[]{:S(2)}, u32[]{:S(2)}) collective-permute-start(bf16[16,4,64,128]{3,2,1,0:T(8,128)(2,1)} %bitcast.6.panel_ref.refs_0_), channel_id=1, source_target_pairs={{0,96},{8,40},{32,0},{40,72},{64,32},{72,104},{96,64},{104,8},{1,9... | collective-permute-start | bytes 3145736 | tf_op jit(solution)/shard_map/ppermute | solution.py:264
  53.6 25.3 %collective-permute-start = (bf16[16,4,64,128]{3,2,1,0:T(8,128)(2,1)}, bf16[16,4,64,128]{3,2,1,0:T(8,128)(2,1)}, u32[]{:S(2)}, u32[]{:S(2)}) collective-permute-start(bf16[16,4,64,128]{3,2,1,0:T(8,128)(2,1)} %bitcast.6.panel_ref.refs_0_), channel_id=1, source_target_pairs={{0,16},{16,0},{1,17},{17,1},{2,18},{18,2},{3,19},{19,3},{4,20},{20... | collective-permute-start | bytes 3145736 | tf_op jit(solution)/shard_map/ppermute | solution.py:265
  56.2 25.3 %collective-permute-start.3 = (bf16[16,4,64,128]{3,2,1,0:T(8,128)(2,1)S(1)}, bf16[16,4,64,128]{3,2,1,0:T(8,128)(2,1)}, u32[]{:S(2)}, u32[]{:S(2)}) collective-permute-start(bf16[16,4,64,128]{3,2,1,0:T(8,128)(2,1)S(1)} %bitcast.18), channel_id=1, source_target_pairs={{0,32},{8,104},{32,64},{40,8},{64,96},{72,40},{96,0},{104,72},{1,3... | collective-permute-start | bytes 3145736 | tf_op jit(solution)/shard_map/ppermute | solution.py:263
  59.2 1.0 copy-start.7
  60.2 25.9 %collective-permute-start.5 = (bf16[16,4,64,128]{3,2,1,0:T(8,128)(2,1)S(1)}, bf16[16,4,64,128]{3,2,1,0:T(8,128)(2,1)}, u32[]{:S(2)}, u32[]{:S(2)}) collective-permute-start(bf16[16,4,64,128]{3,2,1,0:T(8,128)(2,1)S(1)} %bitcast.19), channel_id=1, source_target_pairs={{0,96},{8,40},{32,0},{40,72},{64,32},{72,104},{96,64},{104,8},{1,9... | collective-permute-start | bytes 3145736 | tf_op jit(solution)/shard_map/ppermute | solution.py:264
  60.2 2.7 %copy-start.8 = (bf16[16,4,64,128]{3,2,1,0:T(8,128)(2,1)S(1)}, bf16[16,4,64,128]{3,2,1,0:T(8,128)(2,1)}, u32[]{:S(2)}) copy-start(bf16[16,4,64,128]{3,2,1,0:T(8,128)(2,1)} %copy-done.7) | copy-start | bytes 3145732
  68.0 39.1 %collective-permute-start.12 = (bf16[3,2,4,128,256]{4,3,2,1,0:T(8,128)(2,1)}, bf16[3,2,4,128,256]{4,3,2,1,0:T(8,128)(2,1)}, u32[]{:S(2)}, u32[]{:S(2)}) collective-permute-start(bf16[3,2,4,128,256]{4,3,2,1,0:T(8,128)(2,1)} %get-tuple-element.46), channel_id=1, source_target_pairs={{0,8},{8,0},{1,9},{9,1},{2,10},{10,2},{3,11},{11,3},{4,12},{12,4},... | collective-permute-start | bytes 4718600 | tf_op jit(solution)/shard_map/ppermute | solution.py:266
  78.9 24.2 %collective-permute-start.1 = (bf16[16,4,64,128]{3,2,1,0:T(8,128)(2,1)S(1)}, bf16[16,4,64,128]{3,2,1,0:T(8,128)(2,1)}, u32[]{:S(2)}, u32[]{:S(2)}) collective-permute-start(bf16[16,4,64,128]{3,2,1,0:T(8,128)(2,1)S(1)} %bitcast.20), channel_id=1, source_target_pairs={{0,16},{16,0},{1,17},{17,1},{2,18},{18,2},{3,19},{19,3},{4,20},{20... | collective-permute-start | bytes 3145736 | tf_op jit(solution)/shard_map/ppermute | solution.py:265
  81.5 24.2 %collective-permute-start.10 = (bf16[16,4,64,128]{3,2,1,0:T(8,128)(2,1)}, bf16[16,4,64,128]{3,2,1,0:T(8,128)(2,1)}, u32[]{:S(2)}, u32[]{:S(2)}) collective-permute-start(bf16[16,4,64,128]{3,2,1,0:T(8,128)(2,1)} %collective-permute-done.2.refs_1_), channel_id=1, source_target_pairs={{0,32},{8,104},{32,64},{40,8},{64,96},{72,40},{96,0},{104,72},{1,3... | collective-permute-start | bytes 3145736 | tf_op jit(solution)/shard_map/ppermute | solution.py:263
  86.1 20.9 %collective-permute-start.6 = (bf16[16,4,64,128]{3,2,1,0:T(8,128)(2,1)}, bf16[16,4,64,128]{3,2,1,0:T(8,128)(2,1)}, u32[]{:S(2)}, u32[]{:S(2)}) collective-permute-start(bf16[16,4,64,128]{3,2,1,0:T(8,128)(2,1)} %collective-permute-done.3.refs_1_), channel_id=1, source_target_pairs={{0,32},{8,104},{32,64},{40,8},{64,96},{72,40},{96,0},{104,72},{1,3... | collective-permute-start | bytes 3145736 | tf_op jit(solution)/shard_map/ppermute | solution.py:263
  87.1 6.1 %copy-start = (bf16[4,512,512]{2,1,0:T(8,128)(2,1)}, bf16[4,512,512]{2,1,0:T(8,128)(2,1)S(1)}, u32[]{:S(2)}) copy-start(bf16[4,512,512]{2,1,0:T(8,128)(2,1)S(1)} %rows.3.mine1_ref) | copy-start | bytes 6291460
  93.3 44.8 %collective-permute-start.15 = (bf16[4,2,4,128,256]{4,3,2,1,0:T(8,128)(2,1)}, bf16[4,2,4,128,256]{4,3,2,1,0:T(8,128)(2,1)}, u32[]{:S(2)}, u32[]{:S(2)}) collective-permute-start(bf16[4,2,4,128,256]{4,3,2,1,0:T(8,128)(2,1)} %get-tuple-element.50), channel_id=1, source_target_pairs={{0,8},{8,0},{1,9},{9,1},{2,10},{10,2},{3,11},{11,3},{4,12},{12,4},... | collective-permute-start | bytes 6291464 | tf_op jit(solution)/shard_map/ppermute | solution.py:266
  103.1 23.5 %collective-permute-start.9 = (bf16[16,4,64,128]{3,2,1,0:T(8,128)(2,1)}, bf16[16,4,64,128]{3,2,1,0:T(8,128)(2,1)}, u32[]{:S(2)}, u32[]{:S(2)}) collective-permute-start(bf16[16,4,64,128]{3,2,1,0:T(8,128)(2,1)} %collective-permute-done.2.refs_1_), channel_id=1, source_target_pairs={{0,16},{16,0},{1,17},{17,1},{2,18},{18,2},{3,19},{19,3},{4,20},{20... | collective-permute-start | bytes 3145736 | tf_op jit(solution)/shard_map/ppermute | solution.py:265
  105.7 20.8 %collective-permute-start.11 = (bf16[16,4,64,128]{3,2,1,0:T(8,128)(2,1)}, bf16[16,4,64,128]{3,2,1,0:T(8,128)(2,1)S(1)}, u32[]{:S(2)}, u32[]{:S(2)}) collective-permute-start(bf16[16,4,64,128]{3,2,1,0:T(8,128)(2,1)} %collective-permute-done.refs_3_), channel_id=1, source_target_pairs={{0,96},{8,40},{32,0},{40,72},{64,32},{72,104},{96,64},{104,8},{1,9... | collective-permute-start | bytes 3145736 | tf_op jit(solution)/shard_map/ppermute | solution.py:264
  107.0 28.3 %collective-permute-start.7 = (bf16[16,4,64,128]{3,2,1,0:T(8,128)(2,1)}, bf16[16,4,64,128]{3,2,1,0:T(8,128)(2,1)}, u32[]{:S(2)}, u32[]{:S(2)}) collective-permute-start(bf16[16,4,64,128]{3,2,1,0:T(8,128)(2,1)} %collective-permute-done.1.refs_2_), channel_id=1, source_target_pairs={{0,96},{8,40},{32,0},{40,72},{64,32},{72,104},{96,64},{104,8},{1,9... | collective-permute-start | bytes 3145736 | tf_op jit(solution)/shard_map/ppermute | solution.py:264
  107.1 1.6 copy-start.1
  114.4 34.4 %collective-permute-start.14 = (bf16[3,2,4,128,256]{4,3,2,1,0:T(8,128)(2,1)}, bf16[3,2,4,128,256]{4,3,2,1,0:T(8,128)(2,1)}, u32[]{:S(2)}, u32[]{:S(2)}) collective-permute-start(bf16[3,2,4,128,256]{4,3,2,1,0:T(8,128)(2,1)} %get-tuple-element.49), channel_id=1, source_target_pairs={{0,8},{8,0},{1,9},{9,1},{2,10},{10,2},{3,11},{11,3},{4,12},{12,4},... | collective-permute-start | bytes 4718600 | tf_op jit(solution)/shard_map/ppermute | solution.py:266
  126.6 1.0 copy-start.5
  127.5 21.3 %collective-permute-start.13 = (bf16[16,4,64,128]{3,2,1,0:T(8,128)(2,1)}, bf16[16,4,64,128]{3,2,1,0:T(8,128)(2,1)}, u32[]{:S(2)}, u32[]{:S(2)}) collective-permute-start(bf16[16,4,64,128]{3,2,1,0:T(8,128)(2,1)} %collective-permute-done.9.refs_2_), channel_id=1, source_target_pairs={{0,32},{8,104},{32,64},{40,8},{64,96},{72,40},{96,0},{104,72},{1,3... | collective-permute-start | bytes 3145736 | tf_op jit(solution)/shard_map/ppermute | solution.py:263
  135.4 22.1 %collective-permute-start.8 = (bf16[16,4,64,128]{3,2,1,0:T(8,128)(2,1)}, bf16[16,4,64,128]{3,2,1,0:T(8,128)(2,1)S(1)}, u32[]{:S(2)}, u32[]{:S(2)}) collective-permute-start(bf16[16,4,64,128]{3,2,1,0:T(8,128)(2,1)} %collective-permute-done.1.refs_2_), channel_id=1, source_target_pairs={{0,32},{8,104},{32,64},{40,8},{64,96},{72,40},{96,0},{104,72},{1,3... | collective-permute-start | bytes 3145736 | tf_op jit(solution)/shard_map/ppermute | solution.py:263
  135.4 23.7 %collective-permute-start.16 = (bf16[16,4,64,128]{3,2,1,0:T(8,128)(2,1)}, bf16[16,4,64,128]{3,2,1,0:T(8,128)(2,1)}, u32[]{:S(2)}, u32[]{:S(2)}) collective-permute-start(bf16[16,4,64,128]{3,2,1,0:T(8,128)(2,1)} %collective-permute-done.6.refs_1_), channel_id=1, source_target_pairs={{0,16},{16,0},{1,17},{17,1},{2,18},{18,2},{3,19},{19,3},{4,20},{20... | collective-permute-start | bytes 3145736 | tf_op jit(solution)/shard_map/ppermute | solution.py:265
  138.1 1.6 copy-start.2
  139.7 1.2 copy-start.6
  146.6 23.1 %collective-permute-start.18 = (bf16[3,2,4,128,256]{4,3,2,1,0:T(8,128)(2,1)}, bf16[3,2,4,128,256]{4,3,2,1,0:T(8,128)(2,1)}, u32[]{:S(2)}, u32[]{:S(2)}) collective-permute-start(bf16[3,2,4,128,256]{4,3,2,1,0:T(8,128)(2,1)} %get-tuple-element.55), channel_id=1, source_target_pairs={{0,8},{8,0},{1,9},{9,1},{2,10},{10,2},{3,11},{11,3},{4,12},{12,4},... | collective-permute-start | bytes 4718600 | tf_op jit(solution)/shard_map/ppermute | solution.py:266
  148.8 1.6 copy-start.3
  162.5 12.8 %collective-permute-start.17 = (bf16[2,2,4,128,256]{4,3,2,1,0:T(8,128)(2,1)}, bf16[2,2,4,128,256]{4,3,2,1,0:T(8,128)(2,1)}, u32[]{:S(2)}, u32[]{:S(2)}) collective-permute-start(bf16[2,2,4,128,256]{4,3,2,1,0:T(8,128)(2,1)} %gram.12), channel_id=1, source_target_pairs={{0,8},{8,0},{1,9},{9,1},{2,10},{10,2},{3,11},{11,3},{4,12},{12,4},... | collective-permute-start | bytes 3145736 | tf_op jit(solution)/shard_map/ppermute | solution.py:266
  166.3 3.4 %collective-permute-start.19 = (bf16[1,2,4,128,256]{4,3,2,1,0:T(8,128)(2,1)}, bf16[1,2,4,128,256]{4,3,2,1,0:T(8,128)(2,1)}, u32[]{:S(2)}, u32[]{:S(2)}) collective-permute-start(bf16[1,2,4,128,256]{4,3,2,1,0:T(8,128)(2,1)} %get-tuple-element.56), channel_id=1, source_target_pairs={{0,8},{8,0},{1,9},{9,1},{2,10},{10,2},{3,11},{11,3},{4,12},{12,4},... | collective-permute-start | bytes 1572872 | tf_op jit(solution)/shard_map/ppermute | solution.py:266
  169.7 1.6 copy-start.4

commit v8 on v7

--- a/solution.py
+++ b/solution.py
@@ -92,7 +92,7 @@
         grid=(bins,),
         in_specs=[pl.BlockSpec((sources, 1, depth, rows), lambda f: (0, f, 0, 0))],
         out_specs=pl.BlockSpec(block, lambda f: (f, 0, 0)),
-        out_shape=jax.ShapeDtypeStruct((bins, *block[1:]), panel.dtype),
+        out_shape=pltpu.HBM((bins, *block[1:]), panel.dtype),
         compiler_params=pltpu.CompilerParams(vmem_limit_bytes=24 * MIB),
         name="rows",
     )(panel)
@@ -167,6 +167,10 @@
             copy.wait()
         for copy in (*writes(step, slot), *places(step, slot)):
             copy.wait()
+
+
+def far(value):
+    return pltpu.with_memory_space_constraint(value, pltpu.HBM)
 
 
 def sent_spec(results, step):
@@ -216,39 +220,41 @@
         ),
         compiler_params=pltpu.CompilerParams(vmem_limit_bytes=24 * MIB),
         name="gram",
-    )(jnp.stack(where).astype(jnp.int32), *mine, *[block[3] for block in blocks], *[r for _, r in sent], *held)
-
-
-def place_kernel(chunks, where, sent_ref, _, out_ref, sems):
-    bins, cols = sent_ref.shape[2], sent_ref.shape[4]
-    step, core = pl.program_id(0), where[len(chunks)]
-    copies = []
-    for k, chunk in enumerate(chunks):
-        first = (1 - core) * 2 * CHUNK + chunk * CHUNK + step * bins
-        spot = out_ref.at[:, pl.ds(first, bins), :, spot_of(where, k, cols)]
-        copies.append(pltpu.make_async_copy(sent_ref.at[k], spot, sems.at[k]))
+    )(jnp.stack(where).astype(jnp.int32), *map(far, mine), *[block[3] for block in blocks], *[r for _, r in sent], *held)
+
+
+def place_kernel(placed, where, *refs):
+    sent, (out_ref, sems) = refs[: len(placed)], refs[-2:]
+    step, count = pl.program_id(0), sum(map(len, placed))
+    core, copies = where[count], []
+    for which, chunks in enumerate(placed):
+        bins, cols = sent[which].shape[2], sent[which].shape[4]
+        for at, chunk in enumerate(chunks):
+            first = (1 - core) * 2 * CHUNK + chunk * CHUNK + step * bins
+            spot = out_ref.at[:, pl.ds(first, bins), :, spot_of(where, len(copies), cols)]
+            copies.append(pltpu.make_async_copy(sent[which].at[at], spot, sems.at[len(copies)]))
     for copy in copies:
         copy.start()
     for copy in copies:
         copy.wait()
 
 
-def place(core, sent, out):
-    blocks, results = sent
+def place(core, out, *sent):
+    received = [block for blocks, _ in sent for block in blocks]
     return pl.pallas_call(
-        functools.partial(place_kernel, [block[0] for block in blocks]),
+        functools.partial(place_kernel, [[block[0] for block in blocks] for blocks, _ in sent]),
         grid_spec=pltpu.PrefetchScalarGridSpec(
             num_scalar_prefetch=1,
-            grid=(results.shape[2] // 2,),
-            in_specs=[sent_spec(results, 2), pl.BlockSpec(memory_space=pl.ANY)],
+            grid=(CHUNK // 2,),
+            in_specs=[sent_spec(results, 2) for _, results in sent] + [pl.BlockSpec(memory_space=pl.ANY)],
             out_specs=pl.BlockSpec(memory_space=pl.ANY),
-            scratch_shapes=[pltpu.SemaphoreType.DMA((len(blocks),))],
+            scratch_shapes=[pltpu.SemaphoreType.DMA((len(received),))],
         ),
         out_shape=jax.ShapeDtypeStruct(out.shape, out.dtype),
-        input_output_aliases={2: 0},
+        input_output_aliases={1 + len(sent): 0},
         compiler_params=pltpu.CompilerParams(vmem_limit_bytes=24 * MIB),
         name="place",
-    )(jnp.stack([block[2] for block in blocks] + [core]).astype(jnp.int32), results, out)
+    )(jnp.stack([block[2] for block in received] + [core]).astype(jnp.int32), *[r for _, r in sent], out)
 
 
 def mirrored(step):
@@ -282,35 +288,35 @@
     pb = owned(after(second, pa))
     ma = rows_of(pa)
 
-    nb, bb, oa = fwd(after(pb, na)), bwd(after(pb, ba)), over(after(pa, pb))
+    fa, nb, oa = fwd(after(na, pb)), fwd(after(pb, na)), over(after(pa, pb))
     blocks1 = [entry(0, 0, 0, pa), entry(0, 1, 0, na), entry(0, -1, 0, ba)]
     out, sent = gram(core, (ma, ma), blocks1, shape, None)
     mine = ma, rows_of(pb)
 
-    fa, fb, ob = fwd(after(na, nb, out)), fwd(after(nb, bb)), over(after(pb, oa))
+    bb, fb, ob = bwd(after(pb, fa, out)), fwd(after(nb, out)), over(after(pb, oa, fa))
     sent1 = blocks1, swap(sent)
-    blocks2 = [entry(1, 0, 0, pb), entry(1, 1, 0, nb), entry(1, -1, 0, bb), entry(0, 0, 1, oa)]
+    blocks2 = [entry(1, 0, 0, pb), entry(0, 2, 0, fa), entry(1, 1, 0, nb), entry(0, 0, 1, oa)]
     out, sent = gram(core, mine, blocks2, shape, out)
 
-    boa, bob, noa = bwd(after(oa, fa, out)), bwd(after(ob, fb)), over(after(na, ob))
+    boa, bob, noa = bwd(after(oa, bb, out)), bwd(after(ob, fb)), over(after(na, ob, bb))
     sent2 = blocks2, swap(sent)
-    blocks3 = [entry(0, 2, 0, fa), entry(1, 2, 0, fb), entry(1, 0, 1, ob)]
+    blocks3 = [entry(1, -1, 0, bb), entry(1, 2, 0, fb), entry(1, 0, 1, ob)]
     out, sent = gram(core, mine, blocks3, shape, out, sent1)
 
-    foa, nob, fob = fwd(after(noa, boa, out)), fwd(after(ob, bob)), over(after(fb, noa))
+    nob, foa, fob = fwd(after(ob, boa, out)), fwd(after(noa, bob)), over(after(fb, noa, boa))
     sent3 = blocks3, swap(sent)
     blocks4 = [entry(0, -1, 1, boa), entry(1, -1, 1, bob), entry(0, 1, 1, noa)]
     out, sent = gram(core, mine, blocks4, shape, out, sent2)
 
     sent4 = blocks4, swap(sent)
-    blocks5 = [entry(0, 2, 1, foa)]
+    blocks5 = [entry(1, 1, 1, nob)]
     out, sent = gram(core, mine, blocks5, shape, out, sent3)
 
     sent5 = blocks5, swap(sent)
-    blocks6 = [entry(1, 1, 1, after(nob, out)), entry(1, 2, 1, fob)]
+    blocks6 = [entry(0, 2, 1, after(foa, out)), entry(1, 2, 1, fob)]
     (sent,) = gram(core, mine, blocks6, shape, None, own=False)
-    (out,) = gram(core, mine, blocks6, shape, out, sent4, sent5, other=False)
-    return place(core, (blocks6, swap(sent)), out)
+    (out,) = gram(core, mine, blocks6, shape, out, sent4, other=False)
+    return place(core, out, sent5, (blocks6, swap(sent)))
 
 
 def solution(mesh):

time: 179 us -> 175 us (0.978)
  blocking collectives: 43.3 us -> 23.3 us
  waiting for transfers between devices: 39.2 us -> 52.2 us
  local copies, waits for them, and re-layouts: 9.96 us -> 0.42 us
  Pallas kernels: 48.3 us -> 54.8 us
  starting transfers between devices: 37.3 us -> 43.6 us
    all_to_all x2 -> x1, blocking collectives: 43.3 us -> 23.3 us  [owned(): lax.all_to_all(chunk, ('yl', 'z', 'core'), split_axis=0, concat_axis=0, t...]
    all_to_all x0 -> x1, waiting for transfers between devices: none -> 14.7 us  [owned(): lax.all_to_all(chunk, ('yl', 'z', 'core'), split_axis=0, concat_axis=0, t...]
    unnamed x20 -> x0, local copies, waits for them, and re-layouts: 9.54 us -> none
    ppermute x6, starting transfers between devices: 19.2 us -> 13.4 us  [shards(): swap = lambda v: lax.ppermute(v, 'core', [(0, 1), (1, 0)])]
    pallas_call x7, Pallas kernels: 33.8 us -> 39.3 us  [gram(): pl.pallas_call(functools.partial(gram_kernel, 2.0 / depth, chunks, [[bloc...]
    ppermute x4, waiting for transfers between devices: 10.3 us -> 14.9 us  [shards(): bwd = lambda v: lax.ppermute(v, ('x', 'core'), mirrored(-1))]
    ppermute x4, starting transfers between devices: 0.01 us -> 3.77 us  [shards(): bwd = lambda v: lax.ppermute(v, ('x', 'core'), mirrored(-1))]
    all_to_all x0 -> x1, starting transfers between devices: none -> 3.62 us  [owned(): lax.all_to_all(chunk, ('yl', 'z', 'core'), split_axis=0, concat_axis=0, t...]
  transfers between devices with their start and end apart: 20 -> 21, of which waited for: 10 -> 6; matrix products, arithmetic and copies ran while one was open for 0% -> 0% of each run, Pallas kernels for 21% -> 25%
where the time goes in v8:
time: 175 us
  Pallas kernels  54.8 us (31%)
  waiting for transfers between devices  52.2 us (30%)
  starting transfers between devices  43.6 us (25%)
  blocking collectives  23.3 us (13%)
    pallas_call x7, Pallas kernels, gram(): pl.pallas_call(functools.partial(gram_kernel, 2.0 / depth, chunks, [[bloc...  39.3 us
    all_to_all x1, blocking collectives, owned(): lax.all_to_all(chunk, ('yl', 'z', 'core'), split_axis=0, concat_axis=0, t...  23.3 us
    ppermute x4, waiting for transfers between devices, shards(): over = lambda v: lax.ppermute(v, 'yh', [(0, 1), (1, 0)])  20.6 us
    ppermute x4, waiting for transfers between devices, shards(): bwd = lambda v: lax.ppermute(v, ('x', 'core'), mirrored(-1))  14.9 us
    all_to_all x1, waiting for transfers between devices, owned(): lax.all_to_all(chunk, ('yl', 'z', 'core'), split_axis=0, concat_axis=0, t...  14.7 us
    ppermute x6, starting transfers between devices, shards(): swap = lambda v: lax.ppermute(v, 'core', [(0, 1), (1, 0)])  13.4 us
    ppermute x4, starting transfers between devices, shards(): over = lambda v: lax.ppermute(v, 'yh', [(0, 1), (1, 0)])  13.4 us
    ppermute x6, starting transfers between devices, shards(): fwd = lambda v: lax.ppermute(v, ('x', 'core'), mirrored(1))  9.51 us
  transfers between devices with their start and end apart: 21, of which 6 were waited for; matrix products, arithmetic and copies ran while one was open for 0% of the time, Pallas kernels for 25%

profile of v8, /device:TPU:1, one launch (start us, length us, event | category | flops | bytes accessed | tf_op | source)
XLA Modules:
  0.0 174.8 jit_solution(4028296491873386002)
XLA Ops:
  0.0 7.8 %whiten.1 = (bf16[16,4,2,32,128]{4,3,2,1,0:T(8,128)(2,1)}, bf16[16,4,2,32,128]{4,3,2,1,0:T(8,128)(2,1)}) custom-call(bf16[128,32,512]{2,1,0:T(8,128)(2,1)} %records_ref.1, s32[32,128]{1,0:T(8,128)} %bitcast.28, bf16[512,256]{1,0:T(8,128)(2,1)} %constant.183.clone.high_ref, bf16[512,256]{1,0:T(8,128)(2,1)} %constant.184.clone.low_ref), custom_call_target="tpu_custom_call" | custom-call | tf_op jit(solution)/shard_map/whiten/pallas_call | solution.py:56
  7.8 23.3 %all_to_all.10 = bf16[16,4,2,32,128]{4,3,2,1,0:T(8,128)(2,1)S(1)} all-to-all(bf16[16,4,2,32,128]{4,3,2,1,0:T(8,128)(2,1)} %get-tuple-element.31), channel_id=1, replica_groups=mesh['x'=4,'yh'=2,'core'=2,'yl'=2,'z'=4] {'yl','z','core'}, dimensions={0} | all-to-all | bytes 2097152 | tf_op jit(solution)/shard_map/all_to_all | solution.py:276
  31.0 2.5 %collective-permute-start.1 = (bf16[16,4,64,128]{3,2,1,0:T(8,128)(2,1)S(1)}, bf16[16,4,64,128]{3,2,1,0:T(8,128)(2,1)}, u32[]{:S(2)}, u32[]{:S(2)}) collective-permute-start(bf16[16,4,64,128]{3,2,1,0:T(8,128)(2,1)S(1)} %bitcast.23), channel_id=1, source_target_pairs={{0,32},{8,104},{32,64},{40,8},{64,96},{72,40},{96,0},{104,72},{1,3... | collective-permute-start | bytes 3145736 | tf_op jit(solution)/shard_map/ppermute | solution.py:269
  33.5 3.6 %all-to-all-start.1 = ((bf16[16,4,2,32,128]{4,3,2,1,0:T(8,128)(2,1)}), bf16[16,4,2,32,128]{4,3,2,1,0:T(8,128)(2,1)S(1)}, u32[]{:S(2)}, u32[]{:S(2)}) async-start(bf16[16,4,2,32,128]{4,3,2,1,0:T(8,128)(2,1)} %get-tuple-element.33), calls=%async_computation.1 | async-start | bytes 2097152 | tf_op jit(solution)/shard_map/all_to_all | solution.py:276
  37.1 1.2 collective-permute-start.4
  38.3 14.7 %all-to-all-done.1 = bf16[16,4,2,32,128]{4,3,2,1,0:T(8,128)(2,1)S(1)} async-done(((bf16[16,4,2,32,128]{4,3,2,1,0:T(8,128)(2,1)}), bf16[16,4,2,32,128]{4,3,2,1,0:T(8,128)(2,1)S(1)}, u32[]{:S(2)}, u32[]{:S(2)}) %all-to-all-start.1) | async-done | bytes 1048608 | tf_op jit(solution)/shard_map/all_to_all | solution.py:276
  53.0 0.0 collective-permute-done.1.refs_1_
  53.0 1.5 collective-permute-start.2
  54.5 2.6 %collective-permute-start = (bf16[16,4,64,128]{3,2,1,0:T(8,128)(2,1)S(1)}, bf16[16,4,64,128]{3,2,1,0:T(8,128)(2,1)S(1)}, u32[]{:S(2)}, u32[]{:S(2)}) collective-permute-start(bf16[16,4,64,128]{3,2,1,0:T(8,128)(2,1)S(1)} %bitcast.25), channel_id=1, source_target_pairs={{0,16},{16,0},{1,17},{17,1},{2,18},{18,2},{3,19},{19,3},{4,20},{20... | collective-permute-start | bytes 3145736 | tf_op jit(solution)/shard_map/ppermute | solution.py:271
  57.1 1.3 collective-permute-start.6
  58.4 0.1 add_add_fusion.1.where
  58.5 2.3 %rows.2.mine0_ref.mine1_ref = bf16[4,512,512]{2,1,0:T(8,128)(2,1)} custom-call(bf16[16,4,64,128]{3,2,1,0:T(8,128)(2,1)S(1)} %bitcast.26), custom_call_target="tpu_custom_call" | custom-call | tf_op jit(solution)/shard_map/rows/pallas_call | solution.py:90
  60.7 0.0 collective-permute-done.4.refs_2_
  60.7 6.3 %gram.7 = (bf16[2,16,128,2048]{3,2,1,0:T(8,128)(2,1)}, bf16[3,2,4,128,256]{4,3,2,1,0:T(8,128)(2,1)}) custom-call(s32[4]{0:T(128)S(1)} %add_add_fusion.1.where, bf16[4,512,512]{2,1,0:T(8,128)(2,1)} %rows.2.mine0_ref.mine1_ref, bf16[4,512,512]{2,1,0:T(8,128)(2,1)} %rows.2.mine0_ref.mine1_ref, bf16[16,4,64,128]{3,2,1,0:T(8,128)(2,1)S(1)} %bitcast.27, ...), custom_call_target="tpu_custom_call" | custom-call | flops 1610612736 | bytes 10485760 | tf_op jit(solution)/shard_map/gram/pallas_call | solution.py:195
  67.0 1.6 collective-permute-start.9
  68.6 0.0 collective-permute-done.2.refs_1_
  68.6 1.6 collective-permute-start.5
  70.3 9.5 %collective-permute-done.refs_3_ = bf16[16,4,64,128]{3,2,1,0:T(8,128)(2,1)S(1)} collective-permute-done((bf16[16,4,64,128]{3,2,1,0:T(8,128)(2,1)S(1)}, bf16[16,4,64,128]{3,2,1,0:T(8,128)(2,1)S(1)}, u32[]{:S(2)}, u32[]{:S(2)}) %collective-permute-start) | collective-permute-done | bytes 1048608 | tf_op jit(solution)/shard_map/ppermute | solution.py:271
  79.8 2.7 %collective-permute-start.3 = (bf16[16,4,64,128]{3,2,1,0:T(8,128)(2,1)S(1)}, bf16[16,4,64,128]{3,2,1,0:T(8,128)(2,1)}, u32[]{:S(2)}, u32[]{:S(2)}) collective-permute-start(bf16[16,4,64,128]{3,2,1,0:T(8,128)(2,1)S(1)} %bitcast.20), channel_id=1, source_target_pairs={{0,16},{16,0},{1,17},{17,1},{2,18},{18,2},{3,19},{19,3},{4,20},{20... | collective-permute-start | bytes 3145736 | tf_op jit(solution)/shard_map/ppermute | solution.py:271
  82.5 2.0 %collective-permute-done.6.refs_2_ = bf16[16,4,64,128]{3,2,1,0:T(8,128)(2,1)} collective-permute-done((bf16[16,4,64,128]{3,2,1,0:T(8,128)(2,1)S(1)}, bf16[16,4,64,128]{3,2,1,0:T(8,128)(2,1)}, u32[]{:S(2)}, u32[]{:S(2)}) %collective-permute-start.6) | collective-permute-done | bytes 1048608 | tf_op jit(solution)/shard_map/ppermute | solution.py:269
  84.5 3.5 %collective-permute-start.8 = (bf16[16,4,64,128]{3,2,1,0:T(8,128)(2,1)}, bf16[16,4,64,128]{3,2,1,0:T(8,128)(2,1)S(1)}, u32[]{:S(2)}, u32[]{:S(2)}) collective-permute-start(bf16[16,4,64,128]{3,2,1,0:T(8,128)(2,1)} %collective-permute-done.6.refs_2_), channel_id=1, source_target_pairs={{0,32},{8,104},{32,64},{40,8},{64,96},{72,40},{96,0},{104,72},{1,3... | collective-permute-start | bytes 3145736 | tf_op jit(solution)/shard_map/ppermute | solution.py:269
  88.0 0.1 stack.110.where
  88.1 2.2 %rows.3.mine1_ref = bf16[4,512,512]{2,1,0:T(8,128)(2,1)} custom-call(bf16[16,4,64,128]{3,2,1,0:T(8,128)(2,1)S(1)} %bitcast.21), custom_call_target="tpu_custom_call" | custom-call | tf_op jit(solution)/shard_map/rows/pallas_call | solution.py:90
  90.3 6.4 %gram.8 = (bf16[2,16,128,2048]{3,2,1,0:T(8,128)(2,1)}, bf16[4,2,4,128,256]{4,3,2,1,0:T(8,128)(2,1)}) custom-call(s32[5]{0:T(128)S(1)} %stack.110.where, bf16[4,512,512]{2,1,0:T(8,128)(2,1)} %rows.2.mine0_ref.mine1_ref, bf16[4,512,512]{2,1,0:T(8,128)(2,1)} %rows.3.mine1_ref, bf16[16,4,64,128]{3,2,1,0:T(8,128)(2,1)S(1)} %bitcast.22, ...), custom_call_target="tpu_custom_call", output_to_operand_aliasing={{0}: (7, {})} | custom-call | flops 2147483648 | bytes 12582912 | tf_op jit(solution)/shard_map/gram/pallas_call | solution.py:195
  96.8 4.0 %collective-permute-start.14 = (bf16[4,2,4,128,256]{4,3,2,1,0:T(8,128)(2,1)}, bf16[4,2,4,128,256]{4,3,2,1,0:T(8,128)(2,1)}, u32[]{:S(2)}, u32[]{:S(2)}) collective-permute-start(bf16[4,2,4,128,256]{4,3,2,1,0:T(8,128)(2,1)} %get-tuple-element.49), channel_id=1, source_target_pairs={{0,8},{8,0},{1,9},{9,1},{2,10},{10,2},{3,11},{11,3},{4,12},{12,4},... | collective-permute-start | bytes 6291464 | tf_op jit(solution)/shard_map/ppermute | solution.py:272
  100.7 0.0 collective-permute-done.5.refs_0_
  100.7 0.9 collective-permute-start.7
  101.7 2.6 %collective-permute-done.3.refs_2_ = bf16[16,4,64,128]{3,2,1,0:T(8,128)(2,1)} collective-permute-done((bf16[16,4,64,128]{3,2,1,0:T(8,128)(2,1)S(1)}, bf16[16,4,64,128]{3,2,1,0:T(8,128)(2,1)}, u32[]{:S(2)}, u32[]{:S(2)}) %collective-permute-start.3) | collective-permute-done | bytes 1048608 | tf_op jit(solution)/shard_map/ppermute | solution.py:271
  104.2 0.0 collective-permute-done.8.refs_1_
  104.2 0.0 collective-permute-start.12
  104.2 2.8 %collective-permute-start.13 = (bf16[16,4,64,128]{3,2,1,0:T(8,128)(2,1)}, bf16[16,4,64,128]{3,2,1,0:T(8,128)(2,1)}, u32[]{:S(2)}, u32[]{:S(2)}) collective-permute-start(bf16[16,4,64,128]{3,2,1,0:T(8,128)(2,1)} %collective-permute-done.1.refs_1_), channel_id=1, source_target_pairs={{0,16},{16,0},{1,17},{17,1},{2,18},{18,2},{3,19},{19,3},{4,20},{20... | collective-permute-start | bytes 3145736 | tf_op jit(solution)/shard_map/ppermute | solution.py:271
  107.1 0.1 stack.112.where
  107.1 0.0 collective-permute-done.9.refs_3_
  107.1 6.2 %gram.9 = (bf16[2,16,128,2048]{3,2,1,0:T(8,128)(2,1)}, bf16[3,2,4,128,256]{4,3,2,1,0:T(8,128)(2,1)}) custom-call(s32[7]{0:T(128)S(1)} %stack.112.where, bf16[4,512,512]{2,1,0:T(8,128)(2,1)} %rows.2.mine0_ref.mine1_ref, bf16[4,512,512]{2,1,0:T(8,128)(2,1)} %rows.3.mine1_ref, ...), custom_call_target="tpu_custom_call", output_to_operand_aliasing={{0}: (7, {})} | custom-call | flops 1610612736 | bytes 10485760 | tf_op jit(solution)/shard_map/gram/pallas_call | solution.py:195
  113.3 7.1 %collective-permute-start.11 = (bf16[3,2,4,128,256]{4,3,2,1,0:T(8,128)(2,1)}, bf16[3,2,4,128,256]{4,3,2,1,0:T(8,128)(2,1)}, u32[]{:S(2)}, u32[]{:S(2)}) collective-permute-start(bf16[3,2,4,128,256]{4,3,2,1,0:T(8,128)(2,1)} %get-tuple-element.46), channel_id=1, source_target_pairs={{0,8},{8,0},{1,9},{9,1},{2,10},{10,2},{3,11},{11,3},{4,12},{12,4},... | collective-permute-start | bytes 4718600 | tf_op jit(solution)/shard_map/ppermute | solution.py:272
  120.4 0.0 collective-permute-done.7.refs_0_
  120.4 0.0 collective-permute-start.10
  120.4 14.9 %collective-permute-done.12.refs_1_ = bf16[16,4,64,128]{3,2,1,0:T(8,128)(2,1)} collective-permute-done((bf16[16,4,64,128]{3,2,1,0:T(8,128)(2,1)}, bf16[16,4,64,128]{3,2,1,0:T(8,128)(2,1)}, u32[]{:S(2)}, u32[]{:S(2)}) %collective-permute-start.12) | collective-permute-done | bytes 1048608 | tf_op jit(solution)/shard_map/ppermute | solution.py:270
  135.3 0.0 collective-permute-done.13.refs_2_
  135.3 0.8 collective-permute-start.16
  136.1 5.2 %collective-permute-start.17 = (bf16[16,4,64,128]{3,2,1,0:T(8,128)(2,1)S(1)}, bf16[16,4,64,128]{3,2,1,0:T(8,128)(2,1)S(1)}, u32[]{:S(2)}, u32[]{:S(2)}) collective-permute-start(bf16[16,4,64,128]{3,2,1,0:T(8,128)(2,1)S(1)} %collective-permute-done.8.refs_1_), channel_id=1, source_target_pairs={{0,16},{16,0},{1,17},{17,1},{2,18},{18,2},{3,19},{19,3},{4,20},{20... | collective-permute-start | bytes 3145736 | tf_op jit(solution)/shard_map/ppermute | solution.py:271
  141.3 0.1 stack.114.where
  141.4 0.0 collective-permute-done.14.refs_3_
  141.4 7.1 %gram.10 = (bf16[2,16,128,2048]{3,2,1,0:T(8,128)(2,1)}, bf16[3,2,4,128,256]{4,3,2,1,0:T(8,128)(2,1)}) custom-call(s32[8]{0:T(128)S(1)} %stack.114.where, bf16[4,512,512]{2,1,0:T(8,128)(2,1)} %rows.2.mine0_ref.mine1_ref, bf16[4,512,512]{2,1,0:T(8,128)(2,1)} %rows.3.mine1_ref, ...), custom_call_target="tpu_custom_call", output_to_operand_aliasing={{0}: (7, {})} | custom-call | flops 1610612736 | bytes 10485760 | tf_op jit(solution)/shard_map/gram/pallas_call | solution.py:195
  148.4 0.1 collective-permute-start.19
  148.5 0.1 stack.104.where
  148.6 0.1 pad_add_fusion.where
  148.7 0.0 collective-permute-done.11.refs_1_
  148.7 0.0 collective-permute-done.10.refs_0_
  148.7 4.6 %gram.11 = (bf16[2,16,128,2048]{3,2,1,0:T(8,128)(2,1)}, bf16[1,2,4,128,256]{4,3,2,1,0:T(8,128)(2,1)}) custom-call(s32[5]{0:T(128)S(1)} %stack.104.where, bf16[4,512,512]{2,1,0:T(8,128)(2,1)} %rows.2.mine0_ref.mine1_ref, bf16[4,512,512]{2,1,0:T(8,128)(2,1)} %rows.3.mine1_ref, ...), custom_call_target="tpu_custom_call", output_to_operand_aliasing={{0}: (5, {})} | custom-call | flops 536870912 | bytes 6291456 | tf_op jit(solution)/shard_map/gram/pallas_call | solution.py:195
  153.3 0.0 collective-permute-done.16.refs_0_
  153.3 8.5 %collective-permute-done.17.refs_1_ = bf16[16,4,64,128]{3,2,1,0:T(8,128)(2,1)S(1)} collective-permute-done((bf16[16,4,64,128]{3,2,1,0:T(8,128)(2,1)S(1)}, bf16[16,4,64,128]{3,2,1,0:T(8,128)(2,1)S(1)}, u32[]{:S(2)}, u32[]{:S(2)}) %collective-permute-start.17) | collective-permute-done | bytes 1048608 | tf_op jit(solution)/shard_map/ppermute | solution.py:271
  161.9 4.1 %gram.12 = bf16[2,2,4,128,256]{4,3,2,1,0:T(8,128)(2,1)} custom-call(s32[3]{0:T(128)S(1)} %pad_add_fusion.where, bf16[4,512,512]{2,1,0:T(8,128)(2,1)} %rows.2.mine0_ref.mine1_ref, bf16[4,512,512]{2,1,0:T(8,128)(2,1)} %rows.3.mine1_ref, bf16[16,4,64,128]{3,2,1,0:T(8,128)(2,1)S(1)} %collective-permute-done.16.refs_0_, ...), custom_call_target="tpu_custom_call" | custom-call | flops 1073741824 | bytes 8388608 | tf_op jit(solution)/shard_map/gram/pallas_call | solution.py:195
  166.0 0.1 collective-permute-start.18
  166.1 0.5 collective-permute-start.15
  166.6 0.1 stack.118.where
  166.6 0.1 add_add_fusion.where
  166.7 0.0 collective-permute-done.19.refs_2_
  166.7 4.7 %gram.13.refs_2_ = bf16[2,16,128,2048]{3,2,1,0:T(8,128)(2,1)} custom-call(s32[6]{0:T(128)S(1)} %stack.118.where, bf16[4,512,512]{2,1,0:T(8,128)(2,1)} %rows.2.mine0_ref.mine1_ref, bf16[4,512,512]{2,1,0:T(8,128)(2,1)} %rows.3.mine1_ref, bf16[16,4,64,128]{3,2,1,0:T(8,128)(2,1)S(1)} %collective-permute-done.16.refs_0_, ...), custom_call_target="tpu_custom_call", output_to_operand_aliasing={{}: (6, {})} | custom-call | flops 1073741824 | bytes 8388608 | tf_op jit(solution)/shard_map/gram/pallas_call | solution.py:195
  171.4 0.0 collective-permute-done.15.refs_0_
  171.4 0.0 collective-permute-done.18.refs_1_
  171.4 3.3 %place.1 = bf16[2,16,128,2048]{3,2,1,0:T(8,128)(2,1)} custom-call(s32[4]{0:T(128)S(1)} %add_add_fusion.where, bf16[1,2,4,128,256]{4,3,2,1,0:T(8,128)(2,1)} %collective-permute-done.15.refs_0_, bf16[2,2,4,128,256]{4,3,2,1,0:T(8,128)(2,1)S(1)} %collective-permute-done.18.refs_1_, bf16[2,16,128,2048]{3,2,1,0:T(8,128)(2,1)} %gram.13.refs_2_), custom_call_target="tpu_custom_call", output_to_operand_aliasing={{}: (3, {})} | custom-call | tf_op jit(solution)/shard_map/place/pallas_call | solution.py:244
Async XLA Ops:
  31.0 22.0 %collective-permute-start.1 = (bf16[16,4,64,128]{3,2,1,0:T(8,128)(2,1)S(1)}, bf16[16,4,64,128]{3,2,1,0:T(8,128)(2,1)}, u32[]{:S(2)}, u32[]{:S(2)}) collective-permute-start(bf16[16,4,64,128]{3,2,1,0:T(8,128)(2,1)S(1)} %bitcast.23), channel_id=1, source_target_pairs={{0,32},{8,104},{32,64},{40,8},{64,96},{72,40},{96,0},{104,72},{1,3... | collective-permute-start | bytes 3145736 | tf_op jit(solution)/shard_map/ppermute | solution.py:269
  33.5 19.5 %all-to-all-start.1 = ((bf16[16,4,2,32,128]{4,3,2,1,0:T(8,128)(2,1)}), bf16[16,4,2,32,128]{4,3,2,1,0:T(8,128)(2,1)S(1)}, u32[]{:S(2)}, u32[]{:S(2)}) async-start(bf16[16,4,2,32,128]{4,3,2,1,0:T(8,128)(2,1)} %get-tuple-element.33), calls=%async_computation.1 | async-start | bytes 2097152 | tf_op jit(solution)/shard_map/all_to_all | solution.py:276
  37.1 23.6 %collective-permute-start.4 = (bf16[16,4,64,128]{3,2,1,0:T(8,128)(2,1)S(1)}, bf16[16,4,64,128]{3,2,1,0:T(8,128)(2,1)}, u32[]{:S(2)}, u32[]{:S(2)}) collective-permute-start(bf16[16,4,64,128]{3,2,1,0:T(8,128)(2,1)S(1)} %bitcast.24), channel_id=1, source_target_pairs={{0,96},{8,40},{32,0},{40,72},{64,32},{72,104},{96,64},{104,8},{1,9... | collective-permute-start | bytes 3145736 | tf_op jit(solution)/shard_map/ppermute | solution.py:270
  53.0 15.6 %collective-permute-start.2 = (bf16[16,4,64,128]{3,2,1,0:T(8,128)(2,1)}, bf16[16,4,64,128]{3,2,1,0:T(8,128)(2,1)}, u32[]{:S(2)}, u32[]{:S(2)}) collective-permute-start(bf16[16,4,64,128]{3,2,1,0:T(8,128)(2,1)} %collective-permute-done.1.refs_1_), channel_id=1, source_target_pairs={{0,32},{8,104},{32,64},{40,8},{64,96},{72,40},{96,0},{104,72},{1,3... | collective-permute-start | bytes 3145736 | tf_op jit(solution)/shard_map/ppermute | solution.py:269
  54.5 25.3 %collective-permute-start = (bf16[16,4,64,128]{3,2,1,0:T(8,128)(2,1)S(1)}, bf16[16,4,64,128]{3,2,1,0:T(8,128)(2,1)S(1)}, u32[]{:S(2)}, u32[]{:S(2)}) collective-permute-start(bf16[16,4,64,128]{3,2,1,0:T(8,128)(2,1)S(1)} %bitcast.25), channel_id=1, source_target_pairs={{0,16},{16,0},{1,17},{17,1},{2,18},{18,2},{3,19},{19,3},{4,20},{20... | collective-permute-start | bytes 3145736 | tf_op jit(solution)/shard_map/ppermute | solution.py:271
  57.1 27.4 %collective-permute-start.6 = (bf16[16,4,64,128]{3,2,1,0:T(8,128)(2,1)S(1)}, bf16[16,4,64,128]{3,2,1,0:T(8,128)(2,1)}, u32[]{:S(2)}, u32[]{:S(2)}) collective-permute-start(bf16[16,4,64,128]{3,2,1,0:T(8,128)(2,1)S(1)} %bitcast.18), channel_id=1, source_target_pairs={{0,32},{8,104},{32,64},{40,8},{64,96},{72,40},{96,0},{104,72},{1,3... | collective-permute-start | bytes 3145736 | tf_op jit(solution)/shard_map/ppermute | solution.py:269
  67.0 40.2 %collective-permute-start.9 = (bf16[3,2,4,128,256]{4,3,2,1,0:T(8,128)(2,1)}, bf16[3,2,4,128,256]{4,3,2,1,0:T(8,128)(2,1)}, u32[]{:S(2)}, u32[]{:S(2)}) collective-permute-start(bf16[3,2,4,128,256]{4,3,2,1,0:T(8,128)(2,1)} %get-tuple-element.43), channel_id=1, source_target_pairs={{0,8},{8,0},{1,9},{9,1},{2,10},{10,2},{3,11},{11,3},{4,12},{12,4},... | collective-permute-start | bytes 4718600 | tf_op jit(solution)/shard_map/ppermute | solution.py:272
  68.6 32.1 %collective-permute-start.5 = (bf16[16,4,64,128]{3,2,1,0:T(8,128)(2,1)S(1)}, bf16[16,4,64,128]{3,2,1,0:T(8,128)(2,1)}, u32[]{:S(2)}, u32[]{:S(2)}) collective-permute-start(bf16[16,4,64,128]{3,2,1,0:T(8,128)(2,1)S(1)} %bitcast.19), channel_id=1, source_target_pairs={{0,96},{8,40},{32,0},{40,72},{64,32},{72,104},{96,64},{104,8},{1,9... | collective-permute-start | bytes 3145736 | tf_op jit(solution)/shard_map/ppermute | solution.py:270
  79.8 24.5 %collective-permute-start.3 = (bf16[16,4,64,128]{3,2,1,0:T(8,128)(2,1)S(1)}, bf16[16,4,64,128]{3,2,1,0:T(8,128)(2,1)}, u32[]{:S(2)}, u32[]{:S(2)}) collective-permute-start(bf16[16,4,64,128]{3,2,1,0:T(8,128)(2,1)S(1)} %bitcast.20), channel_id=1, source_target_pairs={{0,16},{16,0},{1,17},{17,1},{2,18},{18,2},{3,19},{19,3},{4,20},{20... | collective-permute-start | bytes 3145736 | tf_op jit(solution)/shard_map/ppermute | solution.py:271
  84.5 19.8 %collective-permute-start.8 = (bf16[16,4,64,128]{3,2,1,0:T(8,128)(2,1)}, bf16[16,4,64,128]{3,2,1,0:T(8,128)(2,1)S(1)}, u32[]{:S(2)}, u32[]{:S(2)}) collective-permute-start(bf16[16,4,64,128]{3,2,1,0:T(8,128)(2,1)} %collective-permute-done.6.refs_2_), channel_id=1, source_target_pairs={{0,32},{8,104},{32,64},{40,8},{64,96},{72,40},{96,0},{104,72},{1,3... | collective-permute-start | bytes 3145736 | tf_op jit(solution)/shard_map/ppermute | solution.py:269
  96.8 44.6 %collective-permute-start.14 = (bf16[4,2,4,128,256]{4,3,2,1,0:T(8,128)(2,1)}, bf16[4,2,4,128,256]{4,3,2,1,0:T(8,128)(2,1)}, u32[]{:S(2)}, u32[]{:S(2)}) collective-permute-start(bf16[4,2,4,128,256]{4,3,2,1,0:T(8,128)(2,1)} %get-tuple-element.49), channel_id=1, source_target_pairs={{0,8},{8,0},{1,9},{9,1},{2,10},{10,2},{3,11},{11,3},{4,12},{12,4},... | collective-permute-start | bytes 6291464 | tf_op jit(solution)/shard_map/ppermute | solution.py:272
  100.7 19.7 %collective-permute-start.7 = (bf16[16,4,64,128]{3,2,1,0:T(8,128)(2,1)S(1)}, bf16[16,4,64,128]{3,2,1,0:T(8,128)(2,1)}, u32[]{:S(2)}, u32[]{:S(2)}) collective-permute-start(bf16[16,4,64,128]{3,2,1,0:T(8,128)(2,1)S(1)} %collective-permute-done.refs_3_), channel_id=1, source_target_pairs={{0,96},{8,40},{32,0},{40,72},{64,32},{72,104},{96,64},{104,8},{1,9... | collective-permute-start | bytes 3145736 | tf_op jit(solution)/shard_map/ppermute | solution.py:270
  104.2 31.1 %collective-permute-start.12 = (bf16[16,4,64,128]{3,2,1,0:T(8,128)(2,1)}, bf16[16,4,64,128]{3,2,1,0:T(8,128)(2,1)}, u32[]{:S(2)}, u32[]{:S(2)}) collective-permute-start(bf16[16,4,64,128]{3,2,1,0:T(8,128)(2,1)} %collective-permute-done.3.refs_2_), channel_id=1, source_target_pairs={{0,96},{8,40},{32,0},{40,72},{64,32},{72,104},{96,64},{104,8},{1,9... | collective-permute-start | bytes 3145736 | tf_op jit(solution)/shard_map/ppermute | solution.py:270
  104.2 31.1 %collective-permute-start.13 = (bf16[16,4,64,128]{3,2,1,0:T(8,128)(2,1)}, bf16[16,4,64,128]{3,2,1,0:T(8,128)(2,1)}, u32[]{:S(2)}, u32[]{:S(2)}) collective-permute-start(bf16[16,4,64,128]{3,2,1,0:T(8,128)(2,1)} %collective-permute-done.1.refs_1_), channel_id=1, source_target_pairs={{0,16},{16,0},{1,17},{17,1},{2,18},{18,2},{3,19},{19,3},{4,20},{20... | collective-permute-start | bytes 3145736 | tf_op jit(solution)/shard_map/ppermute | solution.py:271
  113.3 35.4 %collective-permute-start.11 = (bf16[3,2,4,128,256]{4,3,2,1,0:T(8,128)(2,1)}, bf16[3,2,4,128,256]{4,3,2,1,0:T(8,128)(2,1)}, u32[]{:S(2)}, u32[]{:S(2)}) collective-permute-start(bf16[3,2,4,128,256]{4,3,2,1,0:T(8,128)(2,1)} %get-tuple-element.46), channel_id=1, source_target_pairs={{0,8},{8,0},{1,9},{9,1},{2,10},{10,2},{3,11},{11,3},{4,12},{12,4},... | collective-permute-start | bytes 4718600 | tf_op jit(solution)/shard_map/ppermute | solution.py:272
  120.4 28.3 %collective-permute-start.10 = (bf16[16,4,64,128]{3,2,1,0:T(8,128)(2,1)}, bf16[16,4,64,128]{3,2,1,0:T(8,128)(2,1)}, u32[]{:S(2)}, u32[]{:S(2)}) collective-permute-start(bf16[16,4,64,128]{3,2,1,0:T(8,128)(2,1)} %collective-permute-done.3.refs_2_), channel_id=1, source_target_pairs={{0,32},{8,104},{32,64},{40,8},{64,96},{72,40},{96,0},{104,72},{1,3... | collective-permute-start | bytes 3145736 | tf_op jit(solution)/shard_map/ppermute | solution.py:269
  135.3 18.0 %collective-permute-start.16 = (bf16[16,4,64,128]{3,2,1,0:T(8,128)(2,1)}, bf16[16,4,64,128]{3,2,1,0:T(8,128)(2,1)S(1)}, u32[]{:S(2)}, u32[]{:S(2)}) collective-permute-start(bf16[16,4,64,128]{3,2,1,0:T(8,128)(2,1)} %collective-permute-done.13.refs_2_), channel_id=1, source_target_pairs={{0,32},{8,104},{32,64},{40,8},{64,96},{72,40},{96,0},{104,72},{1,3... | collective-permute-start | bytes 3145736 | tf_op jit(solution)/shard_map/ppermute | solution.py:269
  136.1 25.8 %collective-permute-start.17 = (bf16[16,4,64,128]{3,2,1,0:T(8,128)(2,1)S(1)}, bf16[16,4,64,128]{3,2,1,0:T(8,128)(2,1)S(1)}, u32[]{:S(2)}, u32[]{:S(2)}) collective-permute-start(bf16[16,4,64,128]{3,2,1,0:T(8,128)(2,1)S(1)} %collective-permute-done.8.refs_1_), channel_id=1, source_target_pairs={{0,16},{16,0},{1,17},{17,1},{2,18},{18,2},{3,19},{19,3},{4,20},{20... | collective-permute-start | bytes 3145736 | tf_op jit(solution)/shard_map/ppermute | solution.py:271
  148.4 18.3 %collective-permute-start.19 = (bf16[3,2,4,128,256]{4,3,2,1,0:T(8,128)(2,1)}, bf16[3,2,4,128,256]{4,3,2,1,0:T(8,128)(2,1)}, u32[]{:S(2)}, u32[]{:S(2)}) collective-permute-start(bf16[3,2,4,128,256]{4,3,2,1,0:T(8,128)(2,1)} %get-tuple-element.56), channel_id=1, source_target_pairs={{0,8},{8,0},{1,9},{9,1},{2,10},{10,2},{3,11},{11,3},{4,12},{12,4},... | collective-permute-start | bytes 4718600 | tf_op jit(solution)/shard_map/ppermute | solution.py:272
  166.0 5.4 %collective-permute-start.18 = (bf16[2,2,4,128,256]{4,3,2,1,0:T(8,128)(2,1)}, bf16[2,2,4,128,256]{4,3,2,1,0:T(8,128)(2,1)S(1)}, u32[]{:S(2)}, u32[]{:S(2)}) collective-permute-start(bf16[2,2,4,128,256]{4,3,2,1,0:T(8,128)(2,1)} %gram.12), channel_id=1, source_target_pairs={{0,8},{8,0},{1,9},{9,1},{2,10},{10,2},{3,11},{11,3},{4,12},{12,4},... | collective-permute-start | bytes 3145736 | tf_op jit(solution)/shard_map/ppermute | solution.py:272
  166.1 5.3 %collective-permute-start.15 = (bf16[1,2,4,128,256]{4,3,2,1,0:T(8,128)(2,1)}, bf16[1,2,4,128,256]{4,3,2,1,0:T(8,128)(2,1)}, u32[]{:S(2)}, u32[]{:S(2)}) collective-permute-start(bf16[1,2,4,128,256]{4,3,2,1,0:T(8,128)(2,1)} %get-tuple-element.51), channel_id=1, source_target_pairs={{0,8},{8,0},{1,9},{9,1},{2,10},{10,2},{3,11},{11,3},{4,12},{12,4},... | collective-permute-start | bytes 1572872 | tf_op jit(solution)/shard_map/ppermute | solution.py:272

commit v9 on v8

--- a/solution.py
+++ b/solution.py
@@ -288,35 +288,36 @@
     pb = owned(after(second, pa))
     ma = rows_of(pa)
 
-    fa, nb, oa = fwd(after(na, pb)), fwd(after(pb, na)), over(after(pa, pb))
+    fa, nb, oa = fwd(after(na, pb)), fwd(after(pb, na)), over(pa)
     blocks1 = [entry(0, 0, 0, pa), entry(0, 1, 0, na), entry(0, -1, 0, ba)]
     out, sent = gram(core, (ma, ma), blocks1, shape, None)
     mine = ma, rows_of(pb)
 
-    bb, fb, ob = bwd(after(pb, fa, out)), fwd(after(nb, out)), over(after(pb, oa, fa))
+    bb, fb, ob = bwd(after(pb, fa, out)), fwd(after(nb, out)), over(after(pb, oa))
     sent1 = blocks1, swap(sent)
     blocks2 = [entry(1, 0, 0, pb), entry(0, 2, 0, fa), entry(1, 1, 0, nb), entry(0, 0, 1, oa)]
     out, sent = gram(core, mine, blocks2, shape, out)
 
-    boa, bob, noa = bwd(after(oa, bb, out)), bwd(after(ob, fb)), over(after(na, ob, bb))
+    boa, bob, noa = bwd(after(oa, bb, out)), bwd(after(ob, fb)), over(after(na, ob))
     sent2 = blocks2, swap(sent)
     blocks3 = [entry(1, -1, 0, bb), entry(1, 2, 0, fb), entry(1, 0, 1, ob)]
     out, sent = gram(core, mine, blocks3, shape, out, sent1)
 
-    nob, foa, fob = fwd(after(ob, boa, out)), fwd(after(noa, bob)), over(after(fb, noa, boa))
+    nob, foa, fob = fwd(after(ob, boa, out)), fwd(after(noa, bob)), over(after(fb, noa))
     sent3 = blocks3, swap(sent)
     blocks4 = [entry(0, -1, 1, boa), entry(1, -1, 1, bob), entry(0, 1, 1, noa)]
     out, sent = gram(core, mine, blocks4, shape, out, sent2)
 
     sent4 = blocks4, swap(sent)
-    blocks5 = [entry(1, 1, 1, nob)]
-    out, sent = gram(core, mine, blocks5, shape, out, sent3)
+    blocks5 = [entry(1, 2, 1, fob)]
+    out, sent = gram(core, mine, blocks5, shape, out)
 
     sent5 = blocks5, swap(sent)
-    blocks6 = [entry(0, 2, 1, after(foa, out)), entry(1, 2, 1, fob)]
+    out = place(core, out, sent3)
+    blocks6 = [entry(0, 2, 1, after(foa, sent5[1], out)), entry(1, 1, 1, nob)]
     (sent,) = gram(core, mine, blocks6, shape, None, own=False)
-    (out,) = gram(core, mine, blocks6, shape, out, sent4, other=False)
-    return place(core, out, sent5, (blocks6, swap(sent)))
+    (out,) = gram(core, mine, blocks6, shape, out, sent4, sent5, other=False)
+    return place(core, out, (blocks6, swap(sent)))
 
 
 def solution(mesh):

time: 175 us -> 175 us (level)
  starting transfers between devices: 43.6 us -> 30.6 us
  waiting for transfers between devices: 52.2 us -> 62.2 us
    ppermute x4, waiting for transfers between devices: 20.6 us -> 40.5 us  [shards(): over = lambda v: lax.ppermute(v, 'yh', [(0, 1), (1, 0)])]
    ppermute x4, waiting for transfers between devices: 14.9 us -> 2.16 us  [shards(): bwd = lambda v: lax.ppermute(v, ('x', 'core'), mirrored(-1))]
    ppermute x4, starting transfers between devices: 13.4 us -> 3.73 us  [shards(): over = lambda v: lax.ppermute(v, 'yh', [(0, 1), (1, 0)])]
    ppermute x6, waiting for transfers between devices: 1.99 us -> 7.41 us  [shards(): fwd = lambda v: lax.ppermute(v, ('x', 'core'), mirrored(1))]
    all_to_all x1, waiting for transfers between devices: 14.7 us -> 12.2 us  [owned(): lax.all_to_all(chunk, ('yl', 'z', 'core'), split_axis=0, concat_axis=0, t...]
    pallas_call x1 -> x2, Pallas kernels: 3.28 us -> 5.71 us  [place(): pl.pallas_call(functools.partial(place_kernel, [[block[0] for block in bl...]
    ppermute x6, starting transfers between devices: 13.4 us -> 11.2 us  [shards(): swap = lambda v: lax.ppermute(v, 'core', [(0, 1), (1, 0)])]
  transfers between devices with their start and end apart: 21 -> 21, of which waited for: 6 -> 7; matrix products, arithmetic and copies ran while one was open for 0% -> 0% of each run, Pallas kernels for 25% -> 27%
where the time goes in v9:
time: 175 us
  waiting for transfers between devices  62.2 us (36%)
  Pallas kernels  56.5 us (32%)
  starting transfers between devices  30.6 us (17%)
  blocking collectives  23.3 us (13%)
    ppermute x4, waiting for transfers between devices, shards(): over = lambda v: lax.ppermute(v, 'yh', [(0, 1), (1, 0)])  40.5 us
    pallas_call x7, Pallas kernels, gram(): pl.pallas_call(functools.partial(gram_kernel, 2.0 / depth, chunks, [[bloc...  38.5 us
    all_to_all x1, blocking collectives, owned(): lax.all_to_all(chunk, ('yl', 'z', 'core'), split_axis=0, concat_axis=0, t...  23.3 us
    all_to_all x1, waiting for transfers between devices, owned(): lax.all_to_all(chunk, ('yl', 'z', 'core'), split_axis=0, concat_axis=0, t...  12.2 us
    ppermute x6, starting transfers between devices, shards(): swap = lambda v: lax.ppermute(v, 'core', [(0, 1), (1, 0)])  11.2 us
    ppermute x6, starting transfers between devices, shards(): fwd = lambda v: lax.ppermute(v, ('x', 'core'), mirrored(1))  9.42 us
    pallas_call x1, Pallas kernels, whiten(): pl.pallas_call(whiten_kernel, grid=(segments // SEG_STEP,), in_specs=[pl....  7.77 us
    ppermute x6, waiting for transfers between devices, shards(): fwd = lambda v: lax.ppermute(v, ('x', 'core'), mirrored(1))  7.41 us
  transfers between devices with their start and end apart: 21, of which 7 were waited for; matrix products, arithmetic and copies ran while one was open for 0% of the time, Pallas kernels for 27%

profile of v9, /device:TPU:1, one launch (start us, length us, event | category | flops | bytes accessed | tf_op | source)
XLA Modules:
  0.0 174.7 jit_solution(11066282323852688951)
XLA Ops:
  0.0 7.8 %whiten.1 = (bf16[16,4,2,32,128]{4,3,2,1,0:T(8,128)(2,1)}, bf16[16,4,2,32,128]{4,3,2,1,0:T(8,128)(2,1)}) custom-call(bf16[128,32,512]{2,1,0:T(8,128)(2,1)} %records_ref.1, s32[32,128]{1,0:T(8,128)} %bitcast.28, bf16[512,256]{1,0:T(8,128)(2,1)} %constant.183.clone.high_ref, bf16[512,256]{1,0:T(8,128)(2,1)} %constant.184.clone.low_ref), custom_call_target="tpu_custom_call" | custom-call | tf_op jit(solution)/shard_map/whiten/pallas_call | solution.py:56
  7.8 23.3 %all_to_all.10 = bf16[16,4,2,32,128]{4,3,2,1,0:T(8,128)(2,1)S(1)} all-to-all(bf16[16,4,2,32,128]{4,3,2,1,0:T(8,128)(2,1)} %get-tuple-element.30), channel_id=1, replica_groups=mesh['x'=4,'yh'=2,'core'=2,'yl'=2,'z'=4] {'yl','z','core'}, dimensions={0} | all-to-all | bytes 2097152 | tf_op jit(solution)/shard_map/all_to_all | solution.py:276
  31.0 2.5 %collective-permute-start = (bf16[16,4,64,128]{3,2,1,0:T(8,128)(2,1)S(1)}, bf16[16,4,64,128]{3,2,1,0:T(8,128)(2,1)}, u32[]{:S(2)}, u32[]{:S(2)}) collective-permute-start(bf16[16,4,64,128]{3,2,1,0:T(8,128)(2,1)S(1)} %bitcast.23), channel_id=1, source_target_pairs={{0,32},{8,104},{32,64},{40,8},{64,96},{72,40},{96,0},{104,72},{1,3... | collective-permute-start | bytes 3145736 | tf_op jit(solution)/shard_map/ppermute | solution.py:269
  33.5 3.6 %all-to-all-start.1 = ((bf16[16,4,2,32,128]{4,3,2,1,0:T(8,128)(2,1)}), bf16[16,4,2,32,128]{4,3,2,1,0:T(8,128)(2,1)S(1)}, u32[]{:S(2)}, u32[]{:S(2)}) async-start(bf16[16,4,2,32,128]{4,3,2,1,0:T(8,128)(2,1)} %get-tuple-element.32), calls=%async_computation.1 | async-start | bytes 2097152 | tf_op jit(solution)/shard_map/all_to_all | solution.py:276
  37.1 2.7 %collective-permute-start.1 = (bf16[16,4,64,128]{3,2,1,0:T(8,128)(2,1)S(1)}, bf16[16,4,64,128]{3,2,1,0:T(8,128)(2,1)}, u32[]{:S(2)}, u32[]{:S(2)}) collective-permute-start(bf16[16,4,64,128]{3,2,1,0:T(8,128)(2,1)S(1)} %bitcast.24), channel_id=1, source_target_pairs={{0,16},{16,0},{1,17},{17,1},{2,18},{18,2},{3,19},{19,3},{4,20},{20... | collective-permute-start | bytes 3145736 | tf_op jit(solution)/shard_map/ppermute | solution.py:271
  39.8 1.2 collective-permute-start.5
  41.0 12.2 %all-to-all-done.1 = bf16[16,4,2,32,128]{4,3,2,1,0:T(8,128)(2,1)S(1)} async-done(((bf16[16,4,2,32,128]{4,3,2,1,0:T(8,128)(2,1)}), bf16[16,4,2,32,128]{4,3,2,1,0:T(8,128)(2,1)S(1)}, u32[]{:S(2)}, u32[]{:S(2)}) %all-to-all-start.1) | async-done | bytes 1048608 | tf_op jit(solution)/shard_map/all_to_all | solution.py:276
  53.1 0.0 collective-permute-done.refs_1_
  53.1 1.5 collective-permute-start.4
  54.6 1.3 collective-permute-start.10
  55.9 18.9 %collective-permute-done.1.refs_3_ = bf16[16,4,64,128]{3,2,1,0:T(8,128)(2,1)} collective-permute-done((bf16[16,4,64,128]{3,2,1,0:T(8,128)(2,1)S(1)}, bf16[16,4,64,128]{3,2,1,0:T(8,128)(2,1)}, u32[]{:S(2)}, u32[]{:S(2)}) %collective-permute-start.1) | collective-permute-done | bytes 1048608 | tf_op jit(solution)/shard_map/ppermute | solution.py:271
  74.8 0.3 collective-permute-start.2
  75.1 0.1 add_add_fusion.2.where
  75.2 2.3 %rows.2.mine0_ref.mine1_ref = bf16[4,512,512]{2,1,0:T(8,128)(2,1)} custom-call(bf16[16,4,64,128]{3,2,1,0:T(8,128)(2,1)S(1)} %bitcast.26), custom_call_target="tpu_custom_call" | custom-call | tf_op jit(solution)/shard_map/rows/pallas_call | solution.py:90
  77.5 0.0 collective-permute-done.5.refs_2_
  77.5 6.0 %gram.7 = (bf16[2,16,128,2048]{3,2,1,0:T(8,128)(2,1)}, bf16[3,2,4,128,256]{4,3,2,1,0:T(8,128)(2,1)}) custom-call(s32[4]{0:T(128)S(1)} %add_add_fusion.2.where, bf16[4,512,512]{2,1,0:T(8,128)(2,1)} %rows.2.mine0_ref.mine1_ref, bf16[4,512,512]{2,1,0:T(8,128)(2,1)} %rows.2.mine0_ref.mine1_ref, bf16[16,4,64,128]{3,2,1,0:T(8,128)(2,1)S(1)} %bitcast.27, ...), custom_call_target="tpu_custom_call" | custom-call | flops 1610612736 | bytes 10485760 | tf_op jit(solution)/shard_map/gram/pallas_call | solution.py:195
  83.5 1.1 collective-permute-start.14
  84.5 0.0 collective-permute-done.4.refs_2_
  84.5 1.5 collective-permute-start.6
  86.0 0.0 collective-permute-done.10.refs_1_
  86.0 0.0 collective-permute-start.11
  86.0 0.1 stack.118.where
  86.1 2.3 %rows.3.mine1_ref = bf16[4,512,512]{2,1,0:T(8,128)(2,1)} custom-call(bf16[16,4,64,128]{3,2,1,0:T(8,128)(2,1)S(1)} %bitcast.21), custom_call_target="tpu_custom_call" | custom-call | tf_op jit(solution)/shard_map/rows/pallas_call | solution.py:90
  88.3 6.6 %gram.8 = (bf16[2,16,128,2048]{3,2,1,0:T(8,128)(2,1)}, bf16[4,2,4,128,256]{4,3,2,1,0:T(8,128)(2,1)}) custom-call(s32[5]{0:T(128)S(1)} %stack.118.where, bf16[4,512,512]{2,1,0:T(8,128)(2,1)} %rows.2.mine0_ref.mine1_ref, bf16[4,512,512]{2,1,0:T(8,128)(2,1)} %rows.3.mine1_ref, bf16[16,4,64,128]{3,2,1,0:T(8,128)(2,1)S(1)} %bitcast.22, ...), custom_call_target="tpu_custom_call", output_to_operand_aliasing={{0}: (7, {})} | custom-call | flops 2147483648 | bytes 12582912 | tf_op jit(solution)/shard_map/gram/pallas_call | solution.py:195
  95.0 1.9 %collective-permute-start.13 = (bf16[4,2,4,128,256]{4,3,2,1,0:T(8,128)(2,1)}, bf16[4,2,4,128,256]{4,3,2,1,0:T(8,128)(2,1)}, u32[]{:S(2)}, u32[]{:S(2)}) collective-permute-start(bf16[4,2,4,128,256]{4,3,2,1,0:T(8,128)(2,1)} %get-tuple-element.45), channel_id=1, source_target_pairs={{0,8},{8,0},{1,9},{9,1},{2,10},{10,2},{3,11},{11,3},{4,12},{12,4},... | collective-permute-start | bytes 6291464 | tf_op jit(solution)/shard_map/ppermute | solution.py:272
  96.9 3.5 %collective-permute-done.2.refs_2_ = bf16[16,4,64,128]{3,2,1,0:T(8,128)(2,1)} collective-permute-done((bf16[16,4,64,128]{3,2,1,0:T(8,128)(2,1)S(1)}, bf16[16,4,64,128]{3,2,1,0:T(8,128)(2,1)}, u32[]{:S(2)}, u32[]{:S(2)}) %collective-permute-start.2) | collective-permute-done | bytes 1048608 | tf_op jit(solution)/shard_map/ppermute | solution.py:271
  100.4 0.3 collective-permute-start.3
  100.7 7.4 %collective-permute-done.6.refs_1_ = bf16[16,4,64,128]{3,2,1,0:T(8,128)(2,1)} collective-permute-done((bf16[16,4,64,128]{3,2,1,0:T(8,128)(2,1)}, bf16[16,4,64,128]{3,2,1,0:T(8,128)(2,1)}, u32[]{:S(2)}, u32[]{:S(2)}) %collective-permute-start.6) | collective-permute-done | bytes 1048608 | tf_op jit(solution)/shard_map/ppermute | solution.py:269
  108.1 1.5 collective-permute-start.7
  109.6 2.2 %collective-permute-done.11.refs_0_ = bf16[16,4,64,128]{3,2,1,0:T(8,128)(2,1)} collective-permute-done((bf16[16,4,64,128]{3,2,1,0:T(8,128)(2,1)S(1)}, bf16[16,4,64,128]{3,2,1,0:T(8,128)(2,1)}, u32[]{:S(2)}, u32[]{:S(2)}) %collective-permute-start.11) | collective-permute-done | bytes 1048608 | tf_op jit(solution)/shard_map/ppermute | solution.py:270
  111.8 0.0 collective-permute-start.12
  111.8 0.1 stack.120.where
  111.9 13.4 %collective-permute-done.3.refs_2_ = bf16[16,4,64,128]{3,2,1,0:T(8,128)(2,1)} collective-permute-done((bf16[16,4,64,128]{3,2,1,0:T(8,128)(2,1)}, bf16[16,4,64,128]{3,2,1,0:T(8,128)(2,1)}, u32[]{:S(2)}, u32[]{:S(2)}) %collective-permute-start.3) | collective-permute-done | bytes 1048608 | tf_op jit(solution)/shard_map/ppermute | solution.py:271
  125.3 0.3 collective-permute-start.9
  125.6 0.0 collective-permute-done.14.refs_3_
  125.6 6.1 %gram.9 = (bf16[2,16,128,2048]{3,2,1,0:T(8,128)(2,1)}, bf16[3,2,4,128,256]{4,3,2,1,0:T(8,128)(2,1)}) custom-call(s32[7]{0:T(128)S(1)} %stack.120.where, bf16[4,512,512]{2,1,0:T(8,128)(2,1)} %rows.2.mine0_ref.mine1_ref, bf16[4,512,512]{2,1,0:T(8,128)(2,1)} %rows.3.mine1_ref, ...), custom_call_target="tpu_custom_call", output_to_operand_aliasing={{0}: (7, {})} | custom-call | flops 1610612736 | bytes 10485760 | tf_op jit(solution)/shard_map/gram/pallas_call | solution.py:195
  131.7 2.9 %collective-permute-start.16 = (bf16[3,2,4,128,256]{4,3,2,1,0:T(8,128)(2,1)}, bf16[3,2,4,128,256]{4,3,2,1,0:T(8,128)(2,1)}, u32[]{:S(2)}, u32[]{:S(2)}) collective-permute-start(bf16[3,2,4,128,256]{4,3,2,1,0:T(8,128)(2,1)} %get-tuple-element.50), channel_id=1, source_target_pairs={{0,8},{8,0},{1,9},{9,1},{2,10},{10,2},{3,11},{11,3},{4,12},{12,4},... | collective-permute-start | bytes 4718600 | tf_op jit(solution)/shard_map/ppermute | solution.py:272
  134.6 0.0 collective-permute-done.7.refs_1_
  134.6 1.5 collective-permute-start.8
  136.1 0.0 collective-permute-done.12.refs_0_
  136.1 1.3 collective-permute-start.17
  137.3 0.1 stack.116.where
  137.4 0.1 pad_add_fusion.where
  137.5 0.0 collective-permute-done.13.refs_3_
  137.5 7.1 %gram.10 = (bf16[2,16,128,2048]{3,2,1,0:T(8,128)(2,1)}, bf16[3,2,4,128,256]{4,3,2,1,0:T(8,128)(2,1)}) custom-call(s32[8]{0:T(128)S(1)} %stack.116.where, bf16[4,512,512]{2,1,0:T(8,128)(2,1)} %rows.2.mine0_ref.mine1_ref, bf16[4,512,512]{2,1,0:T(8,128)(2,1)} %rows.3.mine1_ref, ...), custom_call_target="tpu_custom_call", output_to_operand_aliasing={{0}: (7, {})} | custom-call | flops 1610612736 | bytes 10485760 | tf_op jit(solution)/shard_map/gram/pallas_call | solution.py:195
  144.6 4.7 %collective-permute-done.9.refs_0_ = bf16[16,4,64,128]{3,2,1,0:T(8,128)(2,1)} collective-permute-done((bf16[16,4,64,128]{3,2,1,0:T(8,128)(2,1)}, bf16[16,4,64,128]{3,2,1,0:T(8,128)(2,1)}, u32[]{:S(2)}, u32[]{:S(2)}) %collective-permute-start.9) | collective-permute-done | bytes 1048608 | tf_op jit(solution)/shard_map/ppermute | solution.py:271
  149.3 3.9 %gram.11 = (bf16[2,16,128,2048]{3,2,1,0:T(8,128)(2,1)}, bf16[1,2,4,128,256]{4,3,2,1,0:T(8,128)(2,1)S(1)}) custom-call(s32[2]{0:T(128)S(1)} %pad_add_fusion.where, bf16[4,512,512]{2,1,0:T(8,128)(2,1)} %rows.2.mine0_ref.mine1_ref, bf16[4,512,512]{2,1,0:T(8,128)(2,1)} %rows.3.mine1_ref, ...), custom_call_target="tpu_custom_call", output_to_operand_aliasing={{0}: (4, {})} | custom-call | flops 536870912 | bytes 6291456 | tf_op jit(solution)/shard_map/gram/pallas_call | solution.py:195
  153.2 3.5 %collective-permute-start.15 = (bf16[1,2,4,128,256]{4,3,2,1,0:T(8,128)(2,1)S(1)}, bf16[1,2,4,128,256]{4,3,2,1,0:T(8,128)(2,1)S(1)}, u32[]{:S(2)}, u32[]{:S(2)}) collective-permute-start(bf16[1,2,4,128,256]{4,3,2,1,0:T(8,128)(2,1)S(1)} %get-tuple-element.49), channel_id=1, source_target_pairs={{0,8},{8,0},{1,9},{9,1},{2,10},{10,2},{3,11},{11,3},{4,12},{12,4},... | collective-permute-start | bytes 1572872 | tf_op jit(solution)/shard_map/ppermute | solution.py:272
  156.7 0.1 collective-permute-start.19
  156.8 0.1 add_add_fusion.3.where
  156.9 0.1 add_add_fusion.1.where
  157.0 0.0 collective-permute-done.16.refs_0_
  157.0 3.5 %place.2.refs_4_ = bf16[2,16,128,2048]{3,2,1,0:T(8,128)(2,1)} custom-call(s32[4]{0:T(128)S(1)} %add_add_fusion.3.where, bf16[3,2,4,128,256]{4,3,2,1,0:T(8,128)(2,1)} %collective-permute-done.16.refs_0_, bf16[2,16,128,2048]{3,2,1,0:T(8,128)(2,1)} %get-tuple-element.51.refs_1_), custom_call_target="tpu_custom_call", output_to_operand_aliasing={{}: (2, {})} | custom-call | tf_op jit(solution)/shard_map/place/pallas_call | solution.py:244
  160.4 0.0 collective-permute-done.15.refs_3_
  160.4 0.0 collective-permute-done.8.refs_0_
  160.5 0.0 collective-permute-done.17.refs_1_
  160.5 4.1 %gram.12 = bf16[2,2,4,128,256]{4,3,2,1,0:T(8,128)(2,1)} custom-call(s32[3]{0:T(128)S(1)} %add_add_fusion.1.where, bf16[4,512,512]{2,1,0:T(8,128)(2,1)} %rows.2.mine0_ref.mine1_ref, bf16[4,512,512]{2,1,0:T(8,128)(2,1)} %rows.3.mine1_ref, bf16[16,4,64,128]{3,2,1,0:T(8,128)(2,1)S(1)} %collective-permute-done.8.refs_0_, ...), custom_call_target="tpu_custom_call" | custom-call | flops 1073741824 | bytes 8388608 | tf_op jit(solution)/shard_map/gram/pallas_call | solution.py:195
  164.6 1.8 %collective-permute-start.18 = (bf16[2,2,4,128,256]{4,3,2,1,0:T(8,128)(2,1)}, bf16[2,2,4,128,256]{4,3,2,1,0:T(8,128)(2,1)S(1)}, u32[]{:S(2)}, u32[]{:S(2)}) collective-permute-start(bf16[2,2,4,128,256]{4,3,2,1,0:T(8,128)(2,1)} %gram.12), channel_id=1, source_target_pairs={{0,8},{8,0},{1,9},{9,1},{2,10},{10,2},{3,11},{11,3},{4,12},{12,4},... | collective-permute-start | bytes 3145736 | tf_op jit(solution)/shard_map/ppermute | solution.py:272
  166.4 0.1 stack.123.where
  166.4 0.1 add_add_fusion.where
  166.5 0.0 collective-permute-done.19.refs_2_
  166.5 1.0 copy-done.1
  167.6 4.7 %gram.13.refs_1_ = bf16[2,16,128,2048]{3,2,1,0:T(8,128)(2,1)} custom-call(s32[7]{0:T(128)S(1)} %stack.123.where, bf16[4,512,512]{2,1,0:T(8,128)(2,1)} %rows.2.mine0_ref.mine1_ref, bf16[4,512,512]{2,1,0:T(8,128)(2,1)} %rows.3.mine1_ref, bf16[16,4,64,128]{3,2,1,0:T(8,128)(2,1)S(1)} %collective-permute-done.8.refs_0_, ...), custom_call_target="tpu_custom_call", output_to_operand_aliasing={{}: (7, {})} | custom-call | flops 1073741824 | bytes 8388608 | tf_op jit(solution)/shard_map/gram/pallas_call | solution.py:195
  172.3 2.2 %place.3 = bf16[2,16,128,2048]{3,2,1,0:T(8,128)(2,1)} custom-call(s32[3]{0:T(128)S(1)} %add_add_fusion.where, bf16[2,2,4,128,256]{4,3,2,1,0:T(8,128)(2,1)S(1)} %collective-permute-done.18.refs_0_, bf16[2,16,128,2048]{3,2,1,0:T(8,128)(2,1)} %gram.13.refs_1_), custom_call_target="tpu_custom_call", output_to_operand_aliasing={{}: (2, {})} | custom-call | tf_op jit(solution)/shard_map/place/pallas_call | solution.py:244
  (4 shorter events, 0.0 us)
Async XLA Ops:
  31.0 22.1 %collective-permute-start = (bf16[16,4,64,128]{3,2,1,0:T(8,128)(2,1)S(1)}, bf16[16,4,64,128]{3,2,1,0:T(8,128)(2,1)}, u32[]{:S(2)}, u32[]{:S(2)}) collective-permute-start(bf16[16,4,64,128]{3,2,1,0:T(8,128)(2,1)S(1)} %bitcast.23), channel_id=1, source_target_pairs={{0,32},{8,104},{32,64},{40,8},{64,96},{72,40},{96,0},{104,72},{1,3... | collective-permute-start | bytes 3145736 | tf_op jit(solution)/shard_map/ppermute | solution.py:269
  33.5 19.6 %all-to-all-start.1 = ((bf16[16,4,2,32,128]{4,3,2,1,0:T(8,128)(2,1)}), bf16[16,4,2,32,128]{4,3,2,1,0:T(8,128)(2,1)S(1)}, u32[]{:S(2)}, u32[]{:S(2)}) async-start(bf16[16,4,2,32,128]{4,3,2,1,0:T(8,128)(2,1)} %get-tuple-element.32), calls=%async_computation.1 | async-start | bytes 2097152 | tf_op jit(solution)/shard_map/all_to_all | solution.py:276
  37.1 37.7 %collective-permute-start.1 = (bf16[16,4,64,128]{3,2,1,0:T(8,128)(2,1)S(1)}, bf16[16,4,64,128]{3,2,1,0:T(8,128)(2,1)}, u32[]{:S(2)}, u32[]{:S(2)}) collective-permute-start(bf16[16,4,64,128]{3,2,1,0:T(8,128)(2,1)S(1)} %bitcast.24), channel_id=1, source_target_pairs={{0,16},{16,0},{1,17},{17,1},{2,18},{18,2},{3,19},{19,3},{4,20},{20... | collective-permute-start | bytes 3145736 | tf_op jit(solution)/shard_map/ppermute | solution.py:271
  39.8 37.7 %collective-permute-start.5 = (bf16[16,4,64,128]{3,2,1,0:T(8,128)(2,1)S(1)}, bf16[16,4,64,128]{3,2,1,0:T(8,128)(2,1)S(1)}, u32[]{:S(2)}, u32[]{:S(2)}) collective-permute-start(bf16[16,4,64,128]{3,2,1,0:T(8,128)(2,1)S(1)} %bitcast.25), channel_id=1, source_target_pairs={{0,96},{8,40},{32,0},{40,72},{64,32},{72,104},{96,64},{104,8},{1,9... | collective-permute-start | bytes 3145736 | tf_op jit(solution)/shard_map/ppermute | solution.py:270
  53.1 31.4 %collective-permute-start.4 = (bf16[16,4,64,128]{3,2,1,0:T(8,128)(2,1)S(1)}, bf16[16,4,64,128]{3,2,1,0:T(8,128)(2,1)}, u32[]{:S(2)}, u32[]{:S(2)}) collective-permute-start(bf16[16,4,64,128]{3,2,1,0:T(8,128)(2,1)S(1)} %bitcast.18), channel_id=1, source_target_pairs={{0,32},{8,104},{32,64},{40,8},{64,96},{72,40},{96,0},{104,72},{1,3... | collective-permute-start | bytes 3145736 | tf_op jit(solution)/shard_map/ppermute | solution.py:269
  54.6 31.4 %collective-permute-start.10 = (bf16[16,4,64,128]{3,2,1,0:T(8,128)(2,1)}, bf16[16,4,64,128]{3,2,1,0:T(8,128)(2,1)}, u32[]{:S(2)}, u32[]{:S(2)}) collective-permute-start(bf16[16,4,64,128]{3,2,1,0:T(8,128)(2,1)} %collective-permute-done.refs_1_), channel_id=1, source_target_pairs={{0,32},{8,104},{32,64},{40,8},{64,96},{72,40},{96,0},{104,72},{1,3... | collective-permute-start | bytes 3145736 | tf_op jit(solution)/shard_map/ppermute | solution.py:269
  74.8 25.6 %collective-permute-start.2 = (bf16[16,4,64,128]{3,2,1,0:T(8,128)(2,1)S(1)}, bf16[16,4,64,128]{3,2,1,0:T(8,128)(2,1)}, u32[]{:S(2)}, u32[]{:S(2)}) collective-permute-start(bf16[16,4,64,128]{3,2,1,0:T(8,128)(2,1)S(1)} %bitcast.19), channel_id=1, source_target_pairs={{0,16},{16,0},{1,17},{17,1},{2,18},{18,2},{3,19},{19,3},{4,20},{20... | collective-permute-start | bytes 3145736 | tf_op jit(solution)/shard_map/ppermute | solution.py:271
  83.5 42.2 %collective-permute-start.14 = (bf16[3,2,4,128,256]{4,3,2,1,0:T(8,128)(2,1)}, bf16[3,2,4,128,256]{4,3,2,1,0:T(8,128)(2,1)S(1)}, u32[]{:S(2)}, u32[]{:S(2)}) collective-permute-start(bf16[3,2,4,128,256]{4,3,2,1,0:T(8,128)(2,1)} %get-tuple-element.46), channel_id=1, source_target_pairs={{0,8},{8,0},{1,9},{9,1},{2,10},{10,2},{3,11},{11,3},{4,12},{12,4},... | collective-permute-start | bytes 4718600 | tf_op jit(solution)/shard_map/ppermute | solution.py:272
  84.5 23.6 %collective-permute-start.6 = (bf16[16,4,64,128]{3,2,1,0:T(8,128)(2,1)}, bf16[16,4,64,128]{3,2,1,0:T(8,128)(2,1)}, u32[]{:S(2)}, u32[]{:S(2)}) collective-permute-start(bf16[16,4,64,128]{3,2,1,0:T(8,128)(2,1)} %collective-permute-done.4.refs_2_), channel_id=1, source_target_pairs={{0,32},{8,104},{32,64},{40,8},{64,96},{72,40},{96,0},{104,72},{1,3... | collective-permute-start | bytes 3145736 | tf_op jit(solution)/shard_map/ppermute | solution.py:269
  86.0 25.8 %collective-permute-start.11 = (bf16[16,4,64,128]{3,2,1,0:T(8,128)(2,1)S(1)}, bf16[16,4,64,128]{3,2,1,0:T(8,128)(2,1)}, u32[]{:S(2)}, u32[]{:S(2)}) collective-permute-start(bf16[16,4,64,128]{3,2,1,0:T(8,128)(2,1)S(1)} %bitcast.20), channel_id=1, source_target_pairs={{0,96},{8,40},{32,0},{40,72},{64,32},{72,104},{96,64},{104,8},{1,9... | collective-permute-start | bytes 3145736 | tf_op jit(solution)/shard_map/ppermute | solution.py:270
  95.0 42.5 %collective-permute-start.13 = (bf16[4,2,4,128,256]{4,3,2,1,0:T(8,128)(2,1)}, bf16[4,2,4,128,256]{4,3,2,1,0:T(8,128)(2,1)}, u32[]{:S(2)}, u32[]{:S(2)}) collective-permute-start(bf16[4,2,4,128,256]{4,3,2,1,0:T(8,128)(2,1)} %get-tuple-element.45), channel_id=1, source_target_pairs={{0,8},{8,0},{1,9},{9,1},{2,10},{10,2},{3,11},{11,3},{4,12},{12,4},... | collective-permute-start | bytes 6291464 | tf_op jit(solution)/shard_map/ppermute | solution.py:272
  100.4 24.9 %collective-permute-start.3 = (bf16[16,4,64,128]{3,2,1,0:T(8,128)(2,1)}, bf16[16,4,64,128]{3,2,1,0:T(8,128)(2,1)}, u32[]{:S(2)}, u32[]{:S(2)}) collective-permute-start(bf16[16,4,64,128]{3,2,1,0:T(8,128)(2,1)} %collective-permute-done.refs_1_), channel_id=1, source_target_pairs={{0,16},{16,0},{1,17},{17,1},{2,18},{18,2},{3,19},{19,3},{4,20},{20... | collective-permute-start | bytes 3145736 | tf_op jit(solution)/shard_map/ppermute | solution.py:271
  108.1 26.5 %collective-permute-start.7 = (bf16[16,4,64,128]{3,2,1,0:T(8,128)(2,1)}, bf16[16,4,64,128]{3,2,1,0:T(8,128)(2,1)}, u32[]{:S(2)}, u32[]{:S(2)}) collective-permute-start(bf16[16,4,64,128]{3,2,1,0:T(8,128)(2,1)} %collective-permute-done.2.refs_2_), channel_id=1, source_target_pairs={{0,96},{8,40},{32,0},{40,72},{64,32},{72,104},{96,64},{104,8},{1,9... | collective-permute-start | bytes 3145736 | tf_op jit(solution)/shard_map/ppermute | solution.py:270
  111.8 24.3 %collective-permute-start.12 = (bf16[16,4,64,128]{3,2,1,0:T(8,128)(2,1)}, bf16[16,4,64,128]{3,2,1,0:T(8,128)(2,1)}, u32[]{:S(2)}, u32[]{:S(2)}) collective-permute-start(bf16[16,4,64,128]{3,2,1,0:T(8,128)(2,1)} %collective-permute-done.1.refs_3_), channel_id=1, source_target_pairs={{0,96},{8,40},{32,0},{40,72},{64,32},{72,104},{96,64},{104,8},{1,9... | collective-permute-start | bytes 3145736 | tf_op jit(solution)/shard_map/ppermute | solution.py:270
  125.3 24.0 %collective-permute-start.9 = (bf16[16,4,64,128]{3,2,1,0:T(8,128)(2,1)}, bf16[16,4,64,128]{3,2,1,0:T(8,128)(2,1)}, u32[]{:S(2)}, u32[]{:S(2)}) collective-permute-start(bf16[16,4,64,128]{3,2,1,0:T(8,128)(2,1)} %collective-permute-done.6.refs_1_), channel_id=1, source_target_pairs={{0,16},{16,0},{1,17},{17,1},{2,18},{18,2},{3,19},{19,3},{4,20},{20... | collective-permute-start | bytes 3145736 | tf_op jit(solution)/shard_map/ppermute | solution.py:271
  131.7 25.2 %collective-permute-start.16 = (bf16[3,2,4,128,256]{4,3,2,1,0:T(8,128)(2,1)}, bf16[3,2,4,128,256]{4,3,2,1,0:T(8,128)(2,1)}, u32[]{:S(2)}, u32[]{:S(2)}) collective-permute-start(bf16[3,2,4,128,256]{4,3,2,1,0:T(8,128)(2,1)} %get-tuple-element.50), channel_id=1, source_target_pairs={{0,8},{8,0},{1,9},{9,1},{2,10},{10,2},{3,11},{11,3},{4,12},{12,4},... | collective-permute-start | bytes 4718600 | tf_op jit(solution)/shard_map/ppermute | solution.py:272
  134.6 25.9 %collective-permute-start.8 = (bf16[16,4,64,128]{3,2,1,0:T(8,128)(2,1)}, bf16[16,4,64,128]{3,2,1,0:T(8,128)(2,1)S(1)}, u32[]{:S(2)}, u32[]{:S(2)}) collective-permute-start(bf16[16,4,64,128]{3,2,1,0:T(8,128)(2,1)} %collective-permute-done.3.refs_2_), channel_id=1, source_target_pairs={{0,32},{8,104},{32,64},{40,8},{64,96},{72,40},{96,0},{104,72},{1,3... | collective-permute-start | bytes 3145736 | tf_op jit(solution)/shard_map/ppermute | solution.py:269
  136.1 24.4 %collective-permute-start.17 = (bf16[16,4,64,128]{3,2,1,0:T(8,128)(2,1)}, bf16[16,4,64,128]{3,2,1,0:T(8,128)(2,1)S(1)}, u32[]{:S(2)}, u32[]{:S(2)}) collective-permute-start(bf16[16,4,64,128]{3,2,1,0:T(8,128)(2,1)} %collective-permute-done.2.refs_2_), channel_id=1, source_target_pairs={{0,32},{8,104},{32,64},{40,8},{64,96},{72,40},{96,0},{104,72},{1,3... | collective-permute-start | bytes 3145736 | tf_op jit(solution)/shard_map/ppermute | solution.py:269
  153.2 7.2 %collective-permute-start.15 = (bf16[1,2,4,128,256]{4,3,2,1,0:T(8,128)(2,1)S(1)}, bf16[1,2,4,128,256]{4,3,2,1,0:T(8,128)(2,1)S(1)}, u32[]{:S(2)}, u32[]{:S(2)}) collective-permute-start(bf16[1,2,4,128,256]{4,3,2,1,0:T(8,128)(2,1)S(1)} %get-tuple-element.49), channel_id=1, source_target_pairs={{0,8},{8,0},{1,9},{9,1},{2,10},{10,2},{3,11},{11,3},{4,12},{12,4},... | collective-permute-start | bytes 1572872 | tf_op jit(solution)/shard_map/ppermute | solution.py:272
  156.7 9.8 %collective-permute-start.19 = (bf16[3,2,4,128,256]{4,3,2,1,0:T(8,128)(2,1)}, bf16[3,2,4,128,256]{4,3,2,1,0:T(8,128)(2,1)}, u32[]{:S(2)}, u32[]{:S(2)}) collective-permute-start(bf16[3,2,4,128,256]{4,3,2,1,0:T(8,128)(2,1)} %get-tuple-element.54), channel_id=1, source_target_pairs={{0,8},{8,0},{1,9},{9,1},{2,10},{10,2},{3,11},{11,3},{4,12},{12,4},... | collective-permute-start | bytes 4718600 | tf_op jit(solution)/shard_map/ppermute | solution.py:272
  160.4 4.2 %copy-start = (bf16[1,2,4,128,256]{4,3,2,1,0:T(8,128)(2,1)}, bf16[1,2,4,128,256]{4,3,2,1,0:T(8,128)(2,1)S(1)}, u32[]{:S(2)}) copy-start(bf16[1,2,4,128,256]{4,3,2,1,0:T(8,128)(2,1)S(1)} %collective-permute-done.15.refs_3_) | copy-start | bytes 1572868
  164.6 7.7 %collective-permute-start.18 = (bf16[2,2,4,128,256]{4,3,2,1,0:T(8,128)(2,1)}, bf16[2,2,4,128,256]{4,3,2,1,0:T(8,128)(2,1)S(1)}, u32[]{:S(2)}, u32[]{:S(2)}) collective-permute-start(bf16[2,2,4,128,256]{4,3,2,1,0:T(8,128)(2,1)} %gram.12), channel_id=1, source_target_pairs={{0,8},{8,0},{1,9},{9,1},{2,10},{10,2},{3,11},{11,3},{4,12},{12,4},... | collective-permute-start | bytes 3145736 | tf_op jit(solution)/shard_map/ppermute | solution.py:272
  166.5 1.0 copy-start.1

commit v10 on v8

--- a/solution.py
+++ b/solution.py
@@ -298,22 +298,24 @@
     blocks2 = [entry(1, 0, 0, pb), entry(0, 2, 0, fa), entry(1, 1, 0, nb), entry(0, 0, 1, oa)]
     out, sent = gram(core, mine, blocks2, shape, out)
 
-    boa, bob, noa = bwd(after(oa, bb, out)), bwd(after(ob, fb)), over(after(na, ob, bb))
+    boa, nob, noa = bwd(after(oa, bb, out)), fwd(after(ob, fb)), over(after(na, ob, bb))
     sent2 = blocks2, swap(sent)
     blocks3 = [entry(1, -1, 0, bb), entry(1, 2, 0, fb), entry(1, 0, 1, ob)]
     out, sent = gram(core, mine, blocks3, shape, out, sent1)
 
-    nob, foa, fob = fwd(after(ob, boa, out)), fwd(after(noa, bob)), over(after(fb, noa, boa))
+    half = CHUNK // 2
+    foa, bob = fwd(after(noa, boa, out)), bwd(after(ob, nob))
+    fob = over(after(fb[:, :half], noa)), fwd(nob[:, half:])
     sent3 = blocks3, swap(sent)
-    blocks4 = [entry(0, -1, 1, boa), entry(1, -1, 1, bob), entry(0, 1, 1, noa)]
+    blocks4 = [entry(0, -1, 1, boa), entry(1, 1, 1, nob), entry(0, 1, 1, noa)]
     out, sent = gram(core, mine, blocks4, shape, out, sent2)
 
     sent4 = blocks4, swap(sent)
-    blocks5 = [entry(1, 1, 1, nob)]
+    blocks5 = [entry(0, 2, 1, foa)]
     out, sent = gram(core, mine, blocks5, shape, out, sent3)
 
     sent5 = blocks5, swap(sent)
-    blocks6 = [entry(0, 2, 1, after(foa, out)), entry(1, 2, 1, fob)]
+    blocks6 = [entry(1, -1, 1, after(bob, out)), entry(1, 2, 1, jnp.concatenate([after(fob[0], out), after(fob[1], out)], axis=1))]
     (sent,) = gram(core, mine, blocks6, shape, None, own=False)
     (out,) = gram(core, mine, blocks6, shape, out, sent4, other=False)
     return place(core, out, sent5, (blocks6, swap(sent)))

time: 175 us -> 176 us (level); the launches traced: 175 us -> 174 us
  waiting for transfers between devices: 52.2 us -> 47.9 us
  local copies, waits for them, and re-layouts: 0.42 us -> 3.28 us
    ppermute x4, waiting for transfers between devices: 14.9 us -> 4.95 us  [shards(): bwd = lambda v: lax.ppermute(v, ('x', 'core'), mirrored(-1))]
    ppermute x6 -> x7, waiting for transfers between devices: 1.99 us -> 8.51 us  [shards(): fwd = lambda v: lax.ppermute(v, ('x', 'core'), mirrored(1))]
    ppermute x4, starting transfers between devices: 13.4 us -> 11.1 us  [shards(): over = lambda v: lax.ppermute(v, 'yh', [(0, 1), (1, 0)])]
    ppermute x6 -> x7, starting transfers between devices: 9.51 us -> 9.95 us  [shards(): fwd = lambda v: lax.ppermute(v, ('x', 'core'), mirrored(1))]
  transfers between devices with their start and end apart: 21 -> 22, of which waited for: 6 -> 8; matrix products, arithmetic and copies ran while one was open for 0% -> 1% of each run, Pallas kernels for 25% -> 25%
where the time goes in v10:
time: 176 us; the launch traced here: 174 us
  Pallas kernels  54.2 us (31%)
  waiting for transfers between devices  47.9 us (27%)
  starting transfers between devices  44.7 us (25%)
  blocking collectives  23.3 us (13%)
  local copies, waits for them, and re-layouts  3.28 us (2%)
    pallas_call x7, Pallas kernels, gram(): pl.pallas_call(functools.partial(gram_kernel, 2.0 / depth, chunks, [[bloc...  38.6 us
    all_to_all x1, blocking collectives, owned(): lax.all_to_all(chunk, ('yl', 'z', 'core'), split_axis=0, concat_axis=0, t...  23.3 us
    ppermute x4, waiting for transfers between devices, shards(): over = lambda v: lax.ppermute(v, 'yh', [(0, 1), (1, 0)])  19.7 us
    ppermute x6, starting transfers between devices, shards(): swap = lambda v: lax.ppermute(v, 'core', [(0, 1), (1, 0)])  14.8 us
    all_to_all x1, waiting for transfers between devices, owned(): lax.all_to_all(chunk, ('yl', 'z', 'core'), split_axis=0, concat_axis=0, t...  14.7 us
    ppermute x4, starting transfers between devices, shards(): over = lambda v: lax.ppermute(v, 'yh', [(0, 1), (1, 0)])  11.1 us
    ppermute x7, starting transfers between devices, shards(): fwd = lambda v: lax.ppermute(v, ('x', 'core'), mirrored(1))  9.95 us
    ppermute x7, waiting for transfers between devices, shards(): fwd = lambda v: lax.ppermute(v, ('x', 'core'), mirrored(1))  8.51 us
  transfers between devices with their start and end apart: 22, of which 8 were waited for; matrix products, arithmetic and copies ran while one was open for 1% of the time, Pallas kernels for 25%

profile of v10, /device:TPU:1, one launch (start us, length us, event | category | flops | bytes accessed | tf_op | source)
XLA Modules:
  0.0 173.9 jit_solution(14777921764760724344)
XLA Ops:
  0.0 7.8 %whiten.1 = (bf16[16,4,2,32,128]{4,3,2,1,0:T(8,128)(2,1)}, bf16[16,4,2,32,128]{4,3,2,1,0:T(8,128)(2,1)}) custom-call(bf16[128,32,512]{2,1,0:T(8,128)(2,1)} %records_ref.1, s32[32,128]{1,0:T(8,128)} %bitcast.28, bf16[512,256]{1,0:T(8,128)(2,1)} %constant.183.clone.high_ref, bf16[512,256]{1,0:T(8,128)(2,1)} %constant.184.clone.low_ref), custom_call_target="tpu_custom_call" | custom-call | tf_op jit(solution)/shard_map/whiten/pallas_call | solution.py:56
  7.8 23.3 %all_to_all.10 = bf16[16,4,2,32,128]{4,3,2,1,0:T(8,128)(2,1)S(1)} all-to-all(bf16[16,4,2,32,128]{4,3,2,1,0:T(8,128)(2,1)} %get-tuple-element.33), channel_id=1, replica_groups=mesh['x'=4,'yh'=2,'core'=2,'yl'=2,'z'=4] {'yl','z','core'}, dimensions={0} | all-to-all | bytes 2097152 | tf_op jit(solution)/shard_map/all_to_all | solution.py:276
  31.0 2.5 %collective-permute-start = (bf16[16,4,64,128]{3,2,1,0:T(8,128)(2,1)S(1)}, bf16[16,4,64,128]{3,2,1,0:T(8,128)(2,1)}, u32[]{:S(2)}, u32[]{:S(2)}) collective-permute-start(bf16[16,4,64,128]{3,2,1,0:T(8,128)(2,1)S(1)} %bitcast.23), channel_id=1, source_target_pairs={{0,32},{8,104},{32,64},{40,8},{64,96},{72,40},{96,0},{104,72},{1,3... | collective-permute-start | bytes 3145736 | tf_op jit(solution)/shard_map/ppermute | solution.py:269
  33.5 3.6 %all-to-all-start.1 = ((bf16[16,4,2,32,128]{4,3,2,1,0:T(8,128)(2,1)}), bf16[16,4,2,32,128]{4,3,2,1,0:T(8,128)(2,1)S(1)}, u32[]{:S(2)}, u32[]{:S(2)}) async-start(bf16[16,4,2,32,128]{4,3,2,1,0:T(8,128)(2,1)} %get-tuple-element.35), calls=%async_computation.1 | async-start | bytes 2097152 | tf_op jit(solution)/shard_map/all_to_all | solution.py:276
  37.1 1.2 collective-permute-start.4
  38.3 14.7 %all-to-all-done.1 = bf16[16,4,2,32,128]{4,3,2,1,0:T(8,128)(2,1)S(1)} async-done(((bf16[16,4,2,32,128]{4,3,2,1,0:T(8,128)(2,1)}), bf16[16,4,2,32,128]{4,3,2,1,0:T(8,128)(2,1)S(1)}, u32[]{:S(2)}, u32[]{:S(2)}) %all-to-all-start.1) | async-done | bytes 1048608 | tf_op jit(solution)/shard_map/all_to_all | solution.py:276
  53.0 0.0 collective-permute-done.refs_1_
  53.0 1.5 collective-permute-start.2
  54.5 2.6 %collective-permute-start.1 = (bf16[16,4,64,128]{3,2,1,0:T(8,128)(2,1)S(1)}, bf16[16,4,64,128]{3,2,1,0:T(8,128)(2,1)S(1)}, u32[]{:S(2)}, u32[]{:S(2)}) collective-permute-start(bf16[16,4,64,128]{3,2,1,0:T(8,128)(2,1)S(1)} %bitcast.25), channel_id=1, source_target_pairs={{0,16},{16,0},{1,17},{17,1},{2,18},{18,2},{3,19},{19,3},{4,20},{20... | collective-permute-start | bytes 3145736 | tf_op jit(solution)/shard_map/ppermute | solution.py:271
  57.1 1.3 collective-permute-start.7
  58.4 0.1 add_add_fusion.1.where
  58.5 2.3 %rows.2.mine0_ref.mine1_ref = bf16[4,512,512]{2,1,0:T(8,128)(2,1)} custom-call(bf16[16,4,64,128]{3,2,1,0:T(8,128)(2,1)S(1)} %bitcast.26), custom_call_target="tpu_custom_call" | custom-call | tf_op jit(solution)/shard_map/rows/pallas_call | solution.py:90
  60.7 0.0 collective-permute-done.4.refs_2_
  60.7 6.3 %gram.7 = (bf16[2,16,128,2048]{3,2,1,0:T(8,128)(2,1)}, bf16[3,2,4,128,256]{4,3,2,1,0:T(8,128)(2,1)}) custom-call(s32[4]{0:T(128)S(1)} %add_add_fusion.1.where, bf16[4,512,512]{2,1,0:T(8,128)(2,1)} %rows.2.mine0_ref.mine1_ref, bf16[4,512,512]{2,1,0:T(8,128)(2,1)} %rows.2.mine0_ref.mine1_ref, bf16[16,4,64,128]{3,2,1,0:T(8,128)(2,1)S(1)} %bitcast.27, ...), custom_call_target="tpu_custom_call" | custom-call | flops 1610612736 | bytes 10485760 | tf_op jit(solution)/shard_map/gram/pallas_call | solution.py:195
  67.1 1.7 collective-permute-start.10
  68.7 0.0 collective-permute-done.2.refs_1_
  68.7 1.6 collective-permute-start.5
  70.4 9.4 %collective-permute-done.1.refs_3_ = bf16[16,4,64,128]{3,2,1,0:T(8,128)(2,1)S(1)} collective-permute-done((bf16[16,4,64,128]{3,2,1,0:T(8,128)(2,1)S(1)}, bf16[16,4,64,128]{3,2,1,0:T(8,128)(2,1)S(1)}, u32[]{:S(2)}, u32[]{:S(2)}) %collective-permute-start.1) | collective-permute-done | bytes 1048608 | tf_op jit(solution)/shard_map/ppermute | solution.py:271
  79.8 1.0 copy-done
  80.8 2.7 %collective-permute-start.3 = (bf16[16,4,64,128]{3,2,1,0:T(8,128)(2,1)S(1)}, bf16[16,4,64,128]{3,2,1,0:T(8,128)(2,1)}, u32[]{:S(2)}, u32[]{:S(2)}) collective-permute-start(bf16[16,4,64,128]{3,2,1,0:T(8,128)(2,1)S(1)} %bitcast.20), channel_id=1, source_target_pairs={{0,16},{16,0},{1,17},{17,1},{2,18},{18,2},{3,19},{19,3},{4,20},{20... | collective-permute-start | bytes 3145736 | tf_op jit(solution)/shard_map/ppermute | solution.py:271
  83.5 1.0 collective-permute-done.7.refs_2_
  84.5 3.5 %collective-permute-start.9 = (bf16[16,4,64,128]{3,2,1,0:T(8,128)(2,1)}, bf16[16,4,64,128]{3,2,1,0:T(8,128)(2,1)S(1)}, u32[]{:S(2)}, u32[]{:S(2)}) collective-permute-start(bf16[16,4,64,128]{3,2,1,0:T(8,128)(2,1)} %collective-permute-done.7.refs_2_), channel_id=1, source_target_pairs={{0,32},{8,104},{32,64},{40,8},{64,96},{72,40},{96,0},{104,72},{1,3... | collective-permute-start | bytes 3145736 | tf_op jit(solution)/shard_map/ppermute | solution.py:269
  88.0 0.1 stack.110.where
  88.1 2.3 %rows.3.mine1_ref = bf16[4,512,512]{2,1,0:T(8,128)(2,1)} custom-call(bf16[16,4,64,128]{3,2,1,0:T(8,128)(2,1)S(1)} %bitcast.21), custom_call_target="tpu_custom_call" | custom-call | tf_op jit(solution)/shard_map/rows/pallas_call | solution.py:90
  90.3 6.5 %gram.8 = (bf16[2,16,128,2048]{3,2,1,0:T(8,128)(2,1)}, bf16[4,2,4,128,256]{4,3,2,1,0:T(8,128)(2,1)}) custom-call(s32[5]{0:T(128)S(1)} %stack.110.where, bf16[4,512,512]{2,1,0:T(8,128)(2,1)} %rows.2.mine0_ref.mine1_ref, bf16[4,512,512]{2,1,0:T(8,128)(2,1)} %rows.3.mine1_ref, bf16[16,4,64,128]{3,2,1,0:T(8,128)(2,1)S(1)} %bitcast.22, ...), custom_call_target="tpu_custom_call", output_to_operand_aliasing={{0}: (7, {})} | custom-call | flops 2147483648 | bytes 12582912 | tf_op jit(solution)/shard_map/gram/pallas_call | solution.py:195
  96.8 3.9 %collective-permute-start.14 = (bf16[4,2,4,128,256]{4,3,2,1,0:T(8,128)(2,1)}, bf16[4,2,4,128,256]{4,3,2,1,0:T(8,128)(2,1)}, u32[]{:S(2)}, u32[]{:S(2)}) collective-permute-start(bf16[4,2,4,128,256]{4,3,2,1,0:T(8,128)(2,1)} %get-tuple-element.51), channel_id=1, source_target_pairs={{0,8},{8,0},{1,9},{9,1},{2,10},{10,2},{3,11},{11,3},{4,12},{12,4},... | collective-permute-start | bytes 6291464 | tf_op jit(solution)/shard_map/ppermute | solution.py:272
  100.7 0.0 collective-permute-done.5.refs_0_
  100.7 0.9 collective-permute-start.8
  101.6 3.6 %collective-permute-done.3.refs_2_ = bf16[16,4,64,128]{3,2,1,0:T(8,128)(2,1)} collective-permute-done((bf16[16,4,64,128]{3,2,1,0:T(8,128)(2,1)S(1)}, bf16[16,4,64,128]{3,2,1,0:T(8,128)(2,1)}, u32[]{:S(2)}, u32[]{:S(2)}) %collective-permute-start.3) | collective-permute-done | bytes 1048608 | tf_op jit(solution)/shard_map/ppermute | solution.py:271
  105.2 2.8 %collective-permute-start.6 = (bf16[16,4,64,128]{3,2,1,0:T(8,128)(2,1)}, bf16[16,4,64,128]{3,2,1,0:T(8,128)(2,1)}, u32[]{:S(2)}, u32[]{:S(2)}) collective-permute-start(bf16[16,4,64,128]{3,2,1,0:T(8,128)(2,1)} %collective-permute-done.refs_1_), channel_id=1, source_target_pairs={{0,16},{16,0},{1,17},{17,1},{2,18},{18,2},{3,19},{19,3},{4,20},{20... | collective-permute-start | bytes 3145736 | tf_op jit(solution)/shard_map/ppermute | solution.py:271
  108.1 0.0 collective-permute-done.9.refs_1_
  108.1 0.0 collective-permute-start.13
  108.1 0.1 stack.112.where
  108.2 6.2 %gram.9 = (bf16[2,16,128,2048]{3,2,1,0:T(8,128)(2,1)}, bf16[3,2,4,128,256]{4,3,2,1,0:T(8,128)(2,1)}) custom-call(s32[7]{0:T(128)S(1)} %stack.112.where, bf16[4,512,512]{2,1,0:T(8,128)(2,1)} %rows.2.mine0_ref.mine1_ref, bf16[4,512,512]{2,1,0:T(8,128)(2,1)} %rows.3.mine1_ref, ...), custom_call_target="tpu_custom_call", output_to_operand_aliasing={{0}: (7, {})} | custom-call | flops 1610612736 | bytes 10485760 | tf_op jit(solution)/shard_map/gram/pallas_call | solution.py:195
  114.3 3.0 %collective-permute-start.12 = (bf16[3,2,4,128,256]{4,3,2,1,0:T(8,128)(2,1)}, bf16[3,2,4,128,256]{4,3,2,1,0:T(8,128)(2,1)}, u32[]{:S(2)}, u32[]{:S(2)}) collective-permute-start(bf16[3,2,4,128,256]{4,3,2,1,0:T(8,128)(2,1)} %get-tuple-element.49), channel_id=1, source_target_pairs={{0,8},{8,0},{1,9},{9,1},{2,10},{10,2},{3,11},{11,3},{4,12},{12,4},... | collective-permute-start | bytes 4718600 | tf_op jit(solution)/shard_map/ppermute | solution.py:272
  117.3 4.9 %collective-permute-done.8.refs_0_ = bf16[16,4,64,128]{3,2,1,0:T(8,128)(2,1)} collective-permute-done((bf16[16,4,64,128]{3,2,1,0:T(8,128)(2,1)S(1)}, bf16[16,4,64,128]{3,2,1,0:T(8,128)(2,1)}, u32[]{:S(2)}, u32[]{:S(2)}) %collective-permute-start.8) | collective-permute-done | bytes 1048608 | tf_op jit(solution)/shard_map/ppermute | solution.py:270
  122.3 6.7 %collective-permute-done.6.refs_2_ = bf16[16,4,64,128]{3,2,1,0:T(8,128)(2,1)} collective-permute-done((bf16[16,4,64,128]{3,2,1,0:T(8,128)(2,1)}, bf16[16,4,64,128]{3,2,1,0:T(8,128)(2,1)}, u32[]{:S(2)}, u32[]{:S(2)}) %collective-permute-start.6) | collective-permute-done | bytes 1048608 | tf_op jit(solution)/shard_map/ppermute | solution.py:271
  129.0 0.0 collective-permute-start.11
  129.0 0.0 collective-permute-done.13.refs_1_
  129.0 1.5 collective-permute-start.16
  130.5 0.9 slice.8
  131.3 0.9 slice.9
  132.2 1.2 collective-permute-start.18
  133.4 2.9 %collective-permute-start.17 = (bf16[16,2,64,128]{3,2,1,0:T(8,128)(2,1)}, bf16[16,2,64,128]{3,2,1,0:T(8,128)(2,1)S(1)}, u32[]{:S(2)}, u32[]{:S(2)}) collective-permute-start(bf16[16,2,64,128]{3,2,1,0:T(8,128)(2,1)} %slice.8), channel_id=1, source_target_pairs={{0,16},{16,0},{1,17},{17,1},{2,18},{18,2},{3,19},{19,3},{4,20},{20... | collective-permute-start | bytes 1572872 | tf_op jit(solution)/shard_map/ppermute | solution.py:271
  136.3 0.1 stack.115.where
  136.4 6.8 %gram.10 = (bf16[2,16,128,2048]{3,2,1,0:T(8,128)(2,1)}, bf16[3,2,4,128,256]{4,3,2,1,0:T(8,128)(2,1)}) custom-call(s32[8]{0:T(128)S(1)} %stack.115.where, bf16[4,512,512]{2,1,0:T(8,128)(2,1)} %rows.2.mine0_ref.mine1_ref, bf16[4,512,512]{2,1,0:T(8,128)(2,1)} %rows.3.mine1_ref, ...), custom_call_target="tpu_custom_call", output_to_operand_aliasing={{0}: (7, {})} | custom-call | flops 1610612736 | bytes 10485760 | tf_op jit(solution)/shard_map/gram/pallas_call | solution.py:195
  143.2 0.0 collective-permute-done.12.refs_1_
  143.2 4.5 %collective-permute-start.20 = (bf16[3,2,4,128,256]{4,3,2,1,0:T(8,128)(2,1)}, bf16[3,2,4,128,256]{4,3,2,1,0:T(8,128)(2,1)}, u32[]{:S(2)}, u32[]{:S(2)}) collective-permute-start(bf16[3,2,4,128,256]{4,3,2,1,0:T(8,128)(2,1)} %get-tuple-element.60), channel_id=1, source_target_pairs={{0,8},{8,0},{1,9},{9,1},{2,10},{10,2},{3,11},{11,3},{4,12},{12,4},... | collective-permute-start | bytes 4718600 | tf_op jit(solution)/shard_map/ppermute | solution.py:272
  147.7 0.1 stack.104.where
  147.8 0.1 pad_add_fusion.where
  147.9 2.4 %collective-permute-done.11.refs_0_ = bf16[16,4,64,128]{3,2,1,0:T(8,128)(2,1)} collective-permute-done((bf16[16,4,64,128]{3,2,1,0:T(8,128)(2,1)}, bf16[16,4,64,128]{3,2,1,0:T(8,128)(2,1)}, u32[]{:S(2)}, u32[]{:S(2)}) %collective-permute-start.11) | collective-permute-done | bytes 1048608 | tf_op jit(solution)/shard_map/ppermute | solution.py:269
  150.3 4.6 %gram.11 = (bf16[2,16,128,2048]{3,2,1,0:T(8,128)(2,1)}, bf16[1,2,4,128,256]{4,3,2,1,0:T(8,128)(2,1)}) custom-call(s32[5]{0:T(128)S(1)} %stack.104.where, bf16[4,512,512]{2,1,0:T(8,128)(2,1)} %rows.2.mine0_ref.mine1_ref, bf16[4,512,512]{2,1,0:T(8,128)(2,1)} %rows.3.mine1_ref, ...), custom_call_target="tpu_custom_call", output_to_operand_aliasing={{0}: (5, {})} | custom-call | flops 536870912 | bytes 6291456 | tf_op jit(solution)/shard_map/gram/pallas_call | solution.py:195
  154.9 5.1 %collective-permute-done.18 = bf16[16,2,64,128]{3,2,1,0:T(8,128)(2,1)S(1)} collective-permute-done((bf16[16,2,64,128]{3,2,1,0:T(8,128)(2,1)}, bf16[16,2,64,128]{3,2,1,0:T(8,128)(2,1)S(1)}, u32[]{:S(2)}, u32[]{:S(2)}) %collective-permute-start.18) | collective-permute-done | bytes 524320 | tf_op jit(solution)/shard_map/ppermute | solution.py:269
  160.0 0.0 collective-permute-done.17
  160.0 0.0 collective-permute-done.16.refs_0_
  160.0 0.1 constant_dynamic-update-slice_fusion.refs_1_
  160.1 4.0 %gram.12 = bf16[2,2,4,128,256]{4,3,2,1,0:T(8,128)(2,1)} custom-call(s32[3]{0:T(128)S(1)} %pad_add_fusion.where, bf16[4,512,512]{2,1,0:T(8,128)(2,1)} %rows.2.mine0_ref.mine1_ref, bf16[4,512,512]{2,1,0:T(8,128)(2,1)} %rows.3.mine1_ref, bf16[16,4,64,128]{3,2,1,0:T(8,128)(2,1)S(1)} %collective-permute-done.16.refs_0_, ...), custom_call_target="tpu_custom_call" | custom-call | flops 1073741824 | bytes 8388608 | tf_op jit(solution)/shard_map/gram/pallas_call | solution.py:195
  164.1 1.7 collective-permute-start.19
  165.8 0.1 collective-permute-start.15
  165.9 0.1 stack.118.where
  166.0 0.1 add_add_fusion.where
  166.0 0.0 collective-permute-done.20.refs_2_
  166.0 4.3 %gram.13.refs_2_ = bf16[2,16,128,2048]{3,2,1,0:T(8,128)(2,1)} custom-call(s32[6]{0:T(128)S(1)} %stack.118.where, bf16[4,512,512]{2,1,0:T(8,128)(2,1)} %rows.2.mine0_ref.mine1_ref, bf16[4,512,512]{2,1,0:T(8,128)(2,1)} %rows.3.mine1_ref, bf16[16,4,64,128]{3,2,1,0:T(8,128)(2,1)S(1)} %collective-permute-done.16.refs_0_, ...), custom_call_target="tpu_custom_call", output_to_operand_aliasing={{}: (6, {})} | custom-call | flops 1073741824 | bytes 8388608 | tf_op jit(solution)/shard_map/gram/pallas_call | solution.py:195
  170.4 3.3 %place.1 = bf16[2,16,128,2048]{3,2,1,0:T(8,128)(2,1)} custom-call(s32[4]{0:T(128)S(1)} %add_add_fusion.where, bf16[1,2,4,128,256]{4,3,2,1,0:T(8,128)(2,1)} %collective-permute-done.15.refs_0_, bf16[2,2,4,128,256]{4,3,2,1,0:T(8,128)(2,1)S(1)} %collective-permute-done.19.refs_1_, bf16[2,16,128,2048]{3,2,1,0:T(8,128)(2,1)} %gram.13.refs_2_), custom_call_target="tpu_custom_call", output_to_operand_aliasing={{}: (3, {})} | custom-call | tf_op jit(solution)/shard_map/place/pallas_call | solution.py:244
  (8 shorter events, 0.1 us)
Async XLA Ops:
  31.0 22.0 %collective-permute-start = (bf16[16,4,64,128]{3,2,1,0:T(8,128)(2,1)S(1)}, bf16[16,4,64,128]{3,2,1,0:T(8,128)(2,1)}, u32[]{:S(2)}, u32[]{:S(2)}) collective-permute-start(bf16[16,4,64,128]{3,2,1,0:T(8,128)(2,1)S(1)} %bitcast.23), channel_id=1, source_target_pairs={{0,32},{8,104},{32,64},{40,8},{64,96},{72,40},{96,0},{104,72},{1,3... | collective-permute-start | bytes 3145736 | tf_op jit(solution)/shard_map/ppermute | solution.py:269
  33.5 19.5 %all-to-all-start.1 = ((bf16[16,4,2,32,128]{4,3,2,1,0:T(8,128)(2,1)}), bf16[16,4,2,32,128]{4,3,2,1,0:T(8,128)(2,1)S(1)}, u32[]{:S(2)}, u32[]{:S(2)}) async-start(bf16[16,4,2,32,128]{4,3,2,1,0:T(8,128)(2,1)} %get-tuple-element.35), calls=%async_computation.1 | async-start | bytes 2097152 | tf_op jit(solution)/shard_map/all_to_all | solution.py:276
  37.1 23.6 %collective-permute-start.4 = (bf16[16,4,64,128]{3,2,1,0:T(8,128)(2,1)S(1)}, bf16[16,4,64,128]{3,2,1,0:T(8,128)(2,1)}, u32[]{:S(2)}, u32[]{:S(2)}) collective-permute-start(bf16[16,4,64,128]{3,2,1,0:T(8,128)(2,1)S(1)} %bitcast.24), channel_id=1, source_target_pairs={{0,96},{8,40},{32,0},{40,72},{64,32},{72,104},{96,64},{104,8},{1,9... | collective-permute-start | bytes 3145736 | tf_op jit(solution)/shard_map/ppermute | solution.py:270
  53.0 15.7 %collective-permute-start.2 = (bf16[16,4,64,128]{3,2,1,0:T(8,128)(2,1)}, bf16[16,4,64,128]{3,2,1,0:T(8,128)(2,1)}, u32[]{:S(2)}, u32[]{:S(2)}) collective-permute-start(bf16[16,4,64,128]{3,2,1,0:T(8,128)(2,1)} %collective-permute-done.refs_1_), channel_id=1, source_target_pairs={{0,32},{8,104},{32,64},{40,8},{64,96},{72,40},{96,0},{104,72},{1,3... | collective-permute-start | bytes 3145736 | tf_op jit(solution)/shard_map/ppermute | solution.py:269
  54.5 25.3 %collective-permute-start.1 = (bf16[16,4,64,128]{3,2,1,0:T(8,128)(2,1)S(1)}, bf16[16,4,64,128]{3,2,1,0:T(8,128)(2,1)S(1)}, u32[]{:S(2)}, u32[]{:S(2)}) collective-permute-start(bf16[16,4,64,128]{3,2,1,0:T(8,128)(2,1)S(1)} %bitcast.25), channel_id=1, source_target_pairs={{0,16},{16,0},{1,17},{17,1},{2,18},{18,2},{3,19},{19,3},{4,20},{20... | collective-permute-start | bytes 3145736 | tf_op jit(solution)/shard_map/ppermute | solution.py:271
  57.1 27.4 %collective-permute-start.7 = (bf16[16,4,64,128]{3,2,1,0:T(8,128)(2,1)S(1)}, bf16[16,4,64,128]{3,2,1,0:T(8,128)(2,1)}, u32[]{:S(2)}, u32[]{:S(2)}) collective-permute-start(bf16[16,4,64,128]{3,2,1,0:T(8,128)(2,1)S(1)} %bitcast.18), channel_id=1, source_target_pairs={{0,32},{8,104},{32,64},{40,8},{64,96},{72,40},{96,0},{104,72},{1,3... | collective-permute-start | bytes 3145736 | tf_op jit(solution)/shard_map/ppermute | solution.py:269
  67.1 41.1 %collective-permute-start.10 = (bf16[3,2,4,128,256]{4,3,2,1,0:T(8,128)(2,1)}, bf16[3,2,4,128,256]{4,3,2,1,0:T(8,128)(2,1)}, u32[]{:S(2)}, u32[]{:S(2)}) collective-permute-start(bf16[3,2,4,128,256]{4,3,2,1,0:T(8,128)(2,1)} %get-tuple-element.46), channel_id=1, source_target_pairs={{0,8},{8,0},{1,9},{9,1},{2,10},{10,2},{3,11},{11,3},{4,12},{12,4},... | collective-permute-start | bytes 4718600 | tf_op jit(solution)/shard_map/ppermute | solution.py:272
  68.7 32.0 %collective-permute-start.5 = (bf16[16,4,64,128]{3,2,1,0:T(8,128)(2,1)S(1)}, bf16[16,4,64,128]{3,2,1,0:T(8,128)(2,1)}, u32[]{:S(2)}, u32[]{:S(2)}) collective-permute-start(bf16[16,4,64,128]{3,2,1,0:T(8,128)(2,1)S(1)} %bitcast.19), channel_id=1, source_target_pairs={{0,96},{8,40},{32,0},{40,72},{64,32},{72,104},{96,64},{104,8},{1,9... | collective-permute-start | bytes 3145736 | tf_op jit(solution)/shard_map/ppermute | solution.py:270
  79.8 1.0 copy-start
  80.8 24.5 %collective-permute-start.3 = (bf16[16,4,64,128]{3,2,1,0:T(8,128)(2,1)S(1)}, bf16[16,4,64,128]{3,2,1,0:T(8,128)(2,1)}, u32[]{:S(2)}, u32[]{:S(2)}) collective-permute-start(bf16[16,4,64,128]{3,2,1,0:T(8,128)(2,1)S(1)} %bitcast.20), channel_id=1, source_target_pairs={{0,16},{16,0},{1,17},{17,1},{2,18},{18,2},{3,19},{19,3},{4,20},{20... | collective-permute-start | bytes 3145736 | tf_op jit(solution)/shard_map/ppermute | solution.py:271
  83.5 6.8 %copy-start.1 = (bf16[16,4,64,128]{3,2,1,0:T(8,128)(2,1)S(1)}, bf16[16,4,64,128]{3,2,1,0:T(8,128)(2,1)}, u32[]{:S(2)}) copy-start(bf16[16,4,64,128]{3,2,1,0:T(8,128)(2,1)} %copy-done) | copy-start | bytes 3145732
  84.5 23.6 %collective-permute-start.9 = (bf16[16,4,64,128]{3,2,1,0:T(8,128)(2,1)}, bf16[16,4,64,128]{3,2,1,0:T(8,128)(2,1)S(1)}, u32[]{:S(2)}, u32[]{:S(2)}) collective-permute-start(bf16[16,4,64,128]{3,2,1,0:T(8,128)(2,1)} %collective-permute-done.7.refs_2_), channel_id=1, source_target_pairs={{0,32},{8,104},{32,64},{40,8},{64,96},{72,40},{96,0},{104,72},{1,3... | collective-permute-start | bytes 3145736 | tf_op jit(solution)/shard_map/ppermute | solution.py:269
  96.8 36.6 %collective-permute-start.14 = (bf16[4,2,4,128,256]{4,3,2,1,0:T(8,128)(2,1)}, bf16[4,2,4,128,256]{4,3,2,1,0:T(8,128)(2,1)}, u32[]{:S(2)}, u32[]{:S(2)}) collective-permute-start(bf16[4,2,4,128,256]{4,3,2,1,0:T(8,128)(2,1)} %get-tuple-element.51), channel_id=1, source_target_pairs={{0,8},{8,0},{1,9},{9,1},{2,10},{10,2},{3,11},{11,3},{4,12},{12,4},... | collective-permute-start | bytes 6291464 | tf_op jit(solution)/shard_map/ppermute | solution.py:272
  100.7 21.5 %collective-permute-start.8 = (bf16[16,4,64,128]{3,2,1,0:T(8,128)(2,1)S(1)}, bf16[16,4,64,128]{3,2,1,0:T(8,128)(2,1)}, u32[]{:S(2)}, u32[]{:S(2)}) collective-permute-start(bf16[16,4,64,128]{3,2,1,0:T(8,128)(2,1)S(1)} %copy-done.1), channel_id=1, source_target_pairs={{0,96},{8,40},{32,0},{40,72},{64,32},{72,104},{96,64},{104,8},{1,9... | collective-permute-start | bytes 3145736 | tf_op jit(solution)/shard_map/ppermute | solution.py:270
  105.2 23.7 %collective-permute-start.6 = (bf16[16,4,64,128]{3,2,1,0:T(8,128)(2,1)}, bf16[16,4,64,128]{3,2,1,0:T(8,128)(2,1)}, u32[]{:S(2)}, u32[]{:S(2)}) collective-permute-start(bf16[16,4,64,128]{3,2,1,0:T(8,128)(2,1)} %collective-permute-done.refs_1_), channel_id=1, source_target_pairs={{0,16},{16,0},{1,17},{17,1},{2,18},{18,2},{3,19},{19,3},{4,20},{20... | collective-permute-start | bytes 3145736 | tf_op jit(solution)/shard_map/ppermute | solution.py:271
  108.1 20.9 %collective-permute-start.13 = (bf16[16,4,64,128]{3,2,1,0:T(8,128)(2,1)}, bf16[16,4,64,128]{3,2,1,0:T(8,128)(2,1)S(1)}, u32[]{:S(2)}, u32[]{:S(2)}) collective-permute-start(bf16[16,4,64,128]{3,2,1,0:T(8,128)(2,1)} %collective-permute-done.3.refs_2_), channel_id=1, source_target_pairs={{0,32},{8,104},{32,64},{40,8},{64,96},{72,40},{96,0},{104,72},{1,3... | collective-permute-start | bytes 3145736 | tf_op jit(solution)/shard_map/ppermute | solution.py:269
  114.3 28.9 %collective-permute-start.12 = (bf16[3,2,4,128,256]{4,3,2,1,0:T(8,128)(2,1)}, bf16[3,2,4,128,256]{4,3,2,1,0:T(8,128)(2,1)}, u32[]{:S(2)}, u32[]{:S(2)}) collective-permute-start(bf16[3,2,4,128,256]{4,3,2,1,0:T(8,128)(2,1)} %get-tuple-element.49), channel_id=1, source_target_pairs={{0,8},{8,0},{1,9},{9,1},{2,10},{10,2},{3,11},{11,3},{4,12},{12,4},... | collective-permute-start | bytes 4718600 | tf_op jit(solution)/shard_map/ppermute | solution.py:272
  129.0 21.3 %collective-permute-start.11 = (bf16[16,4,64,128]{3,2,1,0:T(8,128)(2,1)}, bf16[16,4,64,128]{3,2,1,0:T(8,128)(2,1)}, u32[]{:S(2)}, u32[]{:S(2)}) collective-permute-start(bf16[16,4,64,128]{3,2,1,0:T(8,128)(2,1)} %collective-permute-done.6.refs_2_), channel_id=1, source_target_pairs={{0,32},{8,104},{32,64},{40,8},{64,96},{72,40},{96,0},{104,72},{1,3... | collective-permute-start | bytes 3145736 | tf_op jit(solution)/shard_map/ppermute | solution.py:269
  129.0 31.0 %collective-permute-start.16 = (bf16[16,4,64,128]{3,2,1,0:T(8,128)(2,1)}, bf16[16,4,64,128]{3,2,1,0:T(8,128)(2,1)S(1)}, u32[]{:S(2)}, u32[]{:S(2)}) collective-permute-start(bf16[16,4,64,128]{3,2,1,0:T(8,128)(2,1)} %collective-permute-done.3.refs_2_), channel_id=1, source_target_pairs={{0,96},{8,40},{32,0},{40,72},{64,32},{72,104},{96,64},{104,8},{1,9... | collective-permute-start | bytes 3145736 | tf_op jit(solution)/shard_map/ppermute | solution.py:270
  132.2 27.8 %collective-permute-start.18 = (bf16[16,2,64,128]{3,2,1,0:T(8,128)(2,1)}, bf16[16,2,64,128]{3,2,1,0:T(8,128)(2,1)S(1)}, u32[]{:S(2)}, u32[]{:S(2)}) collective-permute-start(bf16[16,2,64,128]{3,2,1,0:T(8,128)(2,1)} %slice.9), channel_id=1, source_target_pairs={{0,32},{8,104},{32,64},{40,8},{64,96},{72,40},{96,0},{104,72},{1,3... | collective-permute-start | bytes 1572872 | tf_op jit(solution)/shard_map/ppermute | solution.py:269
  133.4 26.6 %collective-permute-start.17 = (bf16[16,2,64,128]{3,2,1,0:T(8,128)(2,1)}, bf16[16,2,64,128]{3,2,1,0:T(8,128)(2,1)S(1)}, u32[]{:S(2)}, u32[]{:S(2)}) collective-permute-start(bf16[16,2,64,128]{3,2,1,0:T(8,128)(2,1)} %slice.8), channel_id=1, source_target_pairs={{0,16},{16,0},{1,17},{17,1},{2,18},{18,2},{3,19},{19,3},{4,20},{20... | collective-permute-start | bytes 1572872 | tf_op jit(solution)/shard_map/ppermute | solution.py:271
  143.2 22.8 %collective-permute-start.20 = (bf16[3,2,4,128,256]{4,3,2,1,0:T(8,128)(2,1)}, bf16[3,2,4,128,256]{4,3,2,1,0:T(8,128)(2,1)}, u32[]{:S(2)}, u32[]{:S(2)}) collective-permute-start(bf16[3,2,4,128,256]{4,3,2,1,0:T(8,128)(2,1)} %get-tuple-element.60), channel_id=1, source_target_pairs={{0,8},{8,0},{1,9},{9,1},{2,10},{10,2},{3,11},{11,3},{4,12},{12,4},... | collective-permute-start | bytes 4718600 | tf_op jit(solution)/shard_map/ppermute | solution.py:272
  164.1 6.3 %collective-permute-start.19 = (bf16[2,2,4,128,256]{4,3,2,1,0:T(8,128)(2,1)}, bf16[2,2,4,128,256]{4,3,2,1,0:T(8,128)(2,1)S(1)}, u32[]{:S(2)}, u32[]{:S(2)}) collective-permute-start(bf16[2,2,4,128,256]{4,3,2,1,0:T(8,128)(2,1)} %gram.12), channel_id=1, source_target_pairs={{0,8},{8,0},{1,9},{9,1},{2,10},{10,2},{3,11},{11,3},{4,12},{12,4},... | collective-permute-start | bytes 3145736 | tf_op jit(solution)/shard_map/ppermute | solution.py:272
  165.8 4.6 %collective-permute-start.15 = (bf16[1,2,4,128,256]{4,3,2,1,0:T(8,128)(2,1)}, bf16[1,2,4,128,256]{4,3,2,1,0:T(8,128)(2,1)}, u32[]{:S(2)}, u32[]{:S(2)}) collective-permute-start(bf16[1,2,4,128,256]{4,3,2,1,0:T(8,128)(2,1)} %get-tuple-element.53), channel_id=1, source_target_pairs={{0,8},{8,0},{1,9},{9,1},{2,10},{10,2},{3,11},{11,3},{4,12},{12,4},... | collective-permute-start | bytes 1572872 | tf_op jit(solution)/shard_map/ppermute | solution.py:272

commit v11 on v10

--- a/solution.py
+++ b/solution.py
@@ -295,29 +295,29 @@
 
     bb, fb, ob = bwd(after(pb, fa, out)), fwd(after(nb, out)), over(after(pb, oa, fa))
     sent1 = blocks1, swap(sent)
-    blocks2 = [entry(1, 0, 0, pb), entry(0, 2, 0, fa), entry(1, 1, 0, nb), entry(0, 0, 1, oa)]
+    blocks2 = [entry(1, 0, 0, after(pb, bb)), entry(0, 2, 0, fa), entry(1, 1, 0, nb), entry(0, 0, 1, oa)]
     out, sent = gram(core, mine, blocks2, shape, out)
 
-    boa, nob, noa = bwd(after(oa, bb, out)), fwd(after(ob, fb)), over(after(na, ob, bb))
+    boa, nob, noa = bwd(after(oa, bb)), fwd(after(ob, fb)), over(after(na, ob, bb))
     sent2 = blocks2, swap(sent)
     blocks3 = [entry(1, -1, 0, bb), entry(1, 2, 0, fb), entry(1, 0, 1, ob)]
     out, sent = gram(core, mine, blocks3, shape, out, sent1)
 
     half = CHUNK // 2
-    foa, bob = fwd(after(noa, boa, out)), bwd(after(ob, nob))
+    bob, foa = bwd(after(ob, boa, out)), fwd(after(noa, nob))
     fob = over(after(fb[:, :half], noa)), fwd(nob[:, half:])
     sent3 = blocks3, swap(sent)
     blocks4 = [entry(0, -1, 1, boa), entry(1, 1, 1, nob), entry(0, 1, 1, noa)]
-    out, sent = gram(core, mine, blocks4, shape, out, sent2)
+    out, sent = gram(core, mine, blocks4, shape, out)
 
     sent4 = blocks4, swap(sent)
-    blocks5 = [entry(0, 2, 1, foa)]
-    out, sent = gram(core, mine, blocks5, shape, out, sent3)
+    blocks5 = [entry(1, -1, 1, bob)]
+    out, sent = gram(core, mine, blocks5, shape, out, sent2)
 
     sent5 = blocks5, swap(sent)
-    blocks6 = [entry(1, -1, 1, after(bob, out)), entry(1, 2, 1, jnp.concatenate([after(fob[0], out), after(fob[1], out)], axis=1))]
+    blocks6 = [entry(0, 2, 1, after(foa, out)), entry(1, 2, 1, jnp.concatenate([after(fob[0], out), after(fob[1], out)], axis=1))]
     (sent,) = gram(core, mine, blocks6, shape, None, own=False)
-    (out,) = gram(core, mine, blocks6, shape, out, sent4, other=False)
+    (out,) = gram(core, mine, blocks6, shape, out, sent3, sent4, other=False)
     return place(core, out, sent5, (blocks6, swap(sent)))
 
 

time: 176 us -> 176 us (level)
  waiting for transfers between devices: 47.9 us -> 44.7 us
  starting transfers between devices: 44.7 us -> 47.5 us
    ppermute x4, waiting for transfers between devices: 19.7 us -> 8.93 us  [shards(): over = lambda v: lax.ppermute(v, 'yh', [(0, 1), (1, 0)])]
    ppermute x7, waiting for transfers between devices: 8.51 us -> 19.3 us  [shards(): fwd = lambda v: lax.ppermute(v, ('x', 'core'), mirrored(1))]
    ppermute x6, starting transfers between devices: 14.8 us -> 20.4 us  [shards(): swap = lambda v: lax.ppermute(v, 'core', [(0, 1), (1, 0)])]
    ppermute x4, waiting for transfers between devices: 4.95 us -> 1.81 us  [shards(): bwd = lambda v: lax.ppermute(v, ('x', 'core'), mirrored(-1))]
where the time goes in v11:
time: 176 us; the launch traced here: 174 us
  Pallas kernels  54.5 us (31%)
  starting transfers between devices  47.5 us (27%)
  waiting for transfers between devices  44.7 us (25%)
  blocking collectives  23.3 us (13%)
  local copies, waits for them, and re-layouts  3.18 us (2%)
    pallas_call x7, Pallas kernels, gram(): pl.pallas_call(functools.partial(gram_kernel, 2.0 / depth, chunks, [[bloc...  38.9 us
    all_to_all x1, blocking collectives, owned(): lax.all_to_all(chunk, ('yl', 'z', 'core'), split_axis=0, concat_axis=0, t...  23.3 us
    ppermute x6, starting transfers between devices, shards(): swap = lambda v: lax.ppermute(v, 'core', [(0, 1), (1, 0)])  20.4 us
    ppermute x7, waiting for transfers between devices, shards(): fwd = lambda v: lax.ppermute(v, ('x', 'core'), mirrored(1))  19.3 us
    all_to_all x1, waiting for transfers between devices, owned(): lax.all_to_all(chunk, ('yl', 'z', 'core'), split_axis=0, concat_axis=0, t...  14.7 us
    ppermute x4, starting transfers between devices, shards(): over = lambda v: lax.ppermute(v, 'yh', [(0, 1), (1, 0)])  9.86 us
    ppermute x4, waiting for transfers between devices, shards(): over = lambda v: lax.ppermute(v, 'yh', [(0, 1), (1, 0)])  8.93 us
    ppermute x7, starting transfers between devices, shards(): fwd = lambda v: lax.ppermute(v, ('x', 'core'), mirrored(1))  8.74 us
  transfers between devices with their start and end apart: 22, of which 8 were waited for; matrix products, arithmetic and copies ran while one was open for 1% of the time, Pallas kernels for 25%

profile of v11, /device:TPU:1, one launch (start us, length us, event | category | flops | bytes accessed | tf_op | source)
XLA Modules:
  0.0 173.8 jit_solution(11499968844389929552)
XLA Ops:
  0.0 7.8 %whiten.1 = (bf16[16,4,2,32,128]{4,3,2,1,0:T(8,128)(2,1)}, bf16[16,4,2,32,128]{4,3,2,1,0:T(8,128)(2,1)}) custom-call(bf16[128,32,512]{2,1,0:T(8,128)(2,1)} %records_ref.1, s32[32,128]{1,0:T(8,128)} %bitcast.28, bf16[512,256]{1,0:T(8,128)(2,1)} %constant.183.clone.high_ref, bf16[512,256]{1,0:T(8,128)(2,1)} %constant.184.clone.low_ref), custom_call_target="tpu_custom_call" | custom-call | tf_op jit(solution)/shard_map/whiten/pallas_call | solution.py:56
  7.8 23.3 %all_to_all.10 = bf16[16,4,2,32,128]{4,3,2,1,0:T(8,128)(2,1)S(1)} all-to-all(bf16[16,4,2,32,128]{4,3,2,1,0:T(8,128)(2,1)} %get-tuple-element.34), channel_id=1, replica_groups=mesh['x'=4,'yh'=2,'core'=2,'yl'=2,'z'=4] {'yl','z','core'}, dimensions={0} | all-to-all | bytes 2097152 | tf_op jit(solution)/shard_map/all_to_all | solution.py:276
  31.0 2.5 %collective-permute-start.1 = (bf16[16,4,64,128]{3,2,1,0:T(8,128)(2,1)S(1)}, bf16[16,4,64,128]{3,2,1,0:T(8,128)(2,1)}, u32[]{:S(2)}, u32[]{:S(2)}) collective-permute-start(bf16[16,4,64,128]{3,2,1,0:T(8,128)(2,1)S(1)} %bitcast.23), channel_id=1, source_target_pairs={{0,32},{8,104},{32,64},{40,8},{64,96},{72,40},{96,0},{104,72},{1,3... | collective-permute-start | bytes 3145736 | tf_op jit(solution)/shard_map/ppermute | solution.py:269
  33.5 3.6 %all-to-all-start.1 = ((bf16[16,4,2,32,128]{4,3,2,1,0:T(8,128)(2,1)}), bf16[16,4,2,32,128]{4,3,2,1,0:T(8,128)(2,1)S(1)}, u32[]{:S(2)}, u32[]{:S(2)}) async-start(bf16[16,4,2,32,128]{4,3,2,1,0:T(8,128)(2,1)} %get-tuple-element.36), calls=%async_computation.1 | async-start | bytes 2097152 | tf_op jit(solution)/shard_map/all_to_all | solution.py:276
  37.1 1.2 collective-permute-start.4
  38.3 14.7 %all-to-all-done.1 = bf16[16,4,2,32,128]{4,3,2,1,0:T(8,128)(2,1)S(1)} async-done(((bf16[16,4,2,32,128]{4,3,2,1,0:T(8,128)(2,1)}), bf16[16,4,2,32,128]{4,3,2,1,0:T(8,128)(2,1)S(1)}, u32[]{:S(2)}, u32[]{:S(2)}) %all-to-all-start.1) | async-done | bytes 1048608 | tf_op jit(solution)/shard_map/all_to_all | solution.py:276
  53.0 0.0 collective-permute-done.1.refs_1_
  53.0 1.5 collective-permute-start.2
  54.5 1.3 collective-permute-start.7
  55.8 2.6 %collective-permute-start = (bf16[16,4,64,128]{3,2,1,0:T(8,128)(2,1)S(1)}, bf16[16,4,64,128]{3,2,1,0:T(8,128)(2,1)}, u32[]{:S(2)}, u32[]{:S(2)}) collective-permute-start(bf16[16,4,64,128]{3,2,1,0:T(8,128)(2,1)S(1)} %bitcast.25), channel_id=1, source_target_pairs={{0,16},{16,0},{1,17},{17,1},{2,18},{18,2},{3,19},{19,3},{4,20},{20... | collective-permute-start | bytes 3145736 | tf_op jit(solution)/shard_map/ppermute | solution.py:271
  58.4 0.1 add_add_fusion.1.where
  58.5 2.3 %rows.2.mine0_ref.mine1_ref = bf16[4,512,512]{2,1,0:T(8,128)(2,1)} custom-call(bf16[16,4,64,128]{3,2,1,0:T(8,128)(2,1)S(1)} %bitcast.26), custom_call_target="tpu_custom_call" | custom-call | tf_op jit(solution)/shard_map/rows/pallas_call | solution.py:90
  60.7 0.0 collective-permute-done.4.refs_2_
  60.8 6.3 %gram.7 = (bf16[2,16,128,2048]{3,2,1,0:T(8,128)(2,1)}, bf16[3,2,4,128,256]{4,3,2,1,0:T(8,128)(2,1)}) custom-call(s32[4]{0:T(128)S(1)} %add_add_fusion.1.where, bf16[4,512,512]{2,1,0:T(8,128)(2,1)} %rows.2.mine0_ref.mine1_ref, bf16[4,512,512]{2,1,0:T(8,128)(2,1)} %rows.2.mine0_ref.mine1_ref, bf16[16,4,64,128]{3,2,1,0:T(8,128)(2,1)S(1)} %bitcast.27, ...), custom_call_target="tpu_custom_call" | custom-call | flops 1610612736 | bytes 10485760 | tf_op jit(solution)/shard_map/gram/pallas_call | solution.py:195
  67.0 0.8 collective-permute-done.2.refs_1_
  67.8 1.0 copy-done
  68.8 0.9 collective-permute-start.5
  69.8 13.8 %collective-permute-done.7.refs_2_ = bf16[16,4,64,128]{3,2,1,0:T(8,128)(2,1)} collective-permute-done((bf16[16,4,64,128]{3,2,1,0:T(8,128)(2,1)S(1)}, bf16[16,4,64,128]{3,2,1,0:T(8,128)(2,1)}, u32[]{:S(2)}, u32[]{:S(2)}) %collective-permute-start.7) | collective-permute-done | bytes 1048608 | tf_op jit(solution)/shard_map/ppermute | solution.py:269
  83.6 3.5 %collective-permute-start.8 = (bf16[16,4,64,128]{3,2,1,0:T(8,128)(2,1)}, bf16[16,4,64,128]{3,2,1,0:T(8,128)(2,1)S(1)}, u32[]{:S(2)}, u32[]{:S(2)}) collective-permute-start(bf16[16,4,64,128]{3,2,1,0:T(8,128)(2,1)} %collective-permute-done.7.refs_2_), channel_id=1, source_target_pairs={{0,32},{8,104},{32,64},{40,8},{64,96},{72,40},{96,0},{104,72},{1,3... | collective-permute-start | bytes 3145736 | tf_op jit(solution)/shard_map/ppermute | solution.py:269
  87.1 0.0 collective-permute-done.refs_3_
  87.1 2.6 %collective-permute-start.3 = (bf16[16,4,64,128]{3,2,1,0:T(8,128)(2,1)S(1)}, bf16[16,4,64,128]{3,2,1,0:T(8,128)(2,1)}, u32[]{:S(2)}, u32[]{:S(2)}) collective-permute-start(bf16[16,4,64,128]{3,2,1,0:T(8,128)(2,1)S(1)} %bitcast.20), channel_id=1, source_target_pairs={{0,16},{16,0},{1,17},{17,1},{2,18},{18,2},{3,19},{19,3},{4,20},{20... | collective-permute-start | bytes 3145736 | tf_op jit(solution)/shard_map/ppermute | solution.py:271
  89.7 4.5 %collective-permute-start.9 = (bf16[3,2,4,128,256]{4,3,2,1,0:T(8,128)(2,1)}, bf16[3,2,4,128,256]{4,3,2,1,0:T(8,128)(2,1)}, u32[]{:S(2)}, u32[]{:S(2)}) collective-permute-start(bf16[3,2,4,128,256]{4,3,2,1,0:T(8,128)(2,1)} %get-tuple-element.45), channel_id=1, source_target_pairs={{0,8},{8,0},{1,9},{9,1},{2,10},{10,2},{3,11},{11,3},{4,12},{12,4},... | collective-permute-start | bytes 4718600 | tf_op jit(solution)/shard_map/ppermute | solution.py:272
  94.2 0.1 stack.112.where
  94.3 2.3 %rows.3.mine1_ref = bf16[4,512,512]{2,1,0:T(8,128)(2,1)} custom-call(bf16[16,4,64,128]{3,2,1,0:T(8,128)(2,1)S(1)} %bitcast.21), custom_call_target="tpu_custom_call" | custom-call | tf_op jit(solution)/shard_map/rows/pallas_call | solution.py:90
  96.5 0.0 collective-permute-done.5.refs_0_
  96.5 1.2 collective-permute-start.6
  97.8 6.5 %gram.8 = (bf16[2,16,128,2048]{3,2,1,0:T(8,128)(2,1)}, bf16[4,2,4,128,256]{4,3,2,1,0:T(8,128)(2,1)}) custom-call(s32[5]{0:T(128)S(1)} %stack.112.where, bf16[4,512,512]{2,1,0:T(8,128)(2,1)} %rows.2.mine0_ref.mine1_ref, bf16[4,512,512]{2,1,0:T(8,128)(2,1)} %rows.3.mine1_ref, bf16[16,4,64,128]{3,2,1,0:T(8,128)(2,1)S(1)} %bitcast.22, ...), custom_call_target="tpu_custom_call", output_to_operand_aliasing={{0}: (7, {})} | custom-call | flops 2147483648 | bytes 12582912 | tf_op jit(solution)/shard_map/gram/pallas_call | solution.py:195
  104.2 2.0 %collective-permute-start.11 = (bf16[4,2,4,128,256]{4,3,2,1,0:T(8,128)(2,1)}, bf16[4,2,4,128,256]{4,3,2,1,0:T(8,128)(2,1)}, u32[]{:S(2)}, u32[]{:S(2)}) collective-permute-start(bf16[4,2,4,128,256]{4,3,2,1,0:T(8,128)(2,1)} %get-tuple-element.50), channel_id=1, source_target_pairs={{0,8},{8,0},{1,9},{9,1},{2,10},{10,2},{3,11},{11,3},{4,12},{12,4},... | collective-permute-start | bytes 6291464 | tf_op jit(solution)/shard_map/ppermute | solution.py:272
  106.2 0.0 collective-permute-done.8.refs_1_
  106.2 3.0 %collective-permute-done.3.refs_2_ = bf16[16,4,64,128]{3,2,1,0:T(8,128)(2,1)} collective-permute-done((bf16[16,4,64,128]{3,2,1,0:T(8,128)(2,1)S(1)}, bf16[16,4,64,128]{3,2,1,0:T(8,128)(2,1)}, u32[]{:S(2)}, u32[]{:S(2)}) %collective-permute-start.3) | collective-permute-done | bytes 1048608 | tf_op jit(solution)/shard_map/ppermute | solution.py:271
  109.2 2.6 %collective-permute-start.13 = (bf16[16,4,64,128]{3,2,1,0:T(8,128)(2,1)}, bf16[16,4,64,128]{3,2,1,0:T(8,128)(2,1)}, u32[]{:S(2)}, u32[]{:S(2)}) collective-permute-start(bf16[16,4,64,128]{3,2,1,0:T(8,128)(2,1)} %collective-permute-done.1.refs_1_), channel_id=1, source_target_pairs={{0,16},{16,0},{1,17},{17,1},{2,18},{18,2},{3,19},{19,3},{4,20},{20... | collective-permute-start | bytes 3145736 | tf_op jit(solution)/shard_map/ppermute | solution.py:271
  111.8 0.1 stack.111.where
  111.9 0.0 collective-permute-done.9.refs_3_
  111.9 6.2 %gram.9 = (bf16[2,16,128,2048]{3,2,1,0:T(8,128)(2,1)}, bf16[3,2,4,128,256]{4,3,2,1,0:T(8,128)(2,1)}) custom-call(s32[7]{0:T(128)S(1)} %stack.111.where, bf16[4,512,512]{2,1,0:T(8,128)(2,1)} %rows.2.mine0_ref.mine1_ref, bf16[4,512,512]{2,1,0:T(8,128)(2,1)} %rows.3.mine1_ref, ...), custom_call_target="tpu_custom_call", output_to_operand_aliasing={{0}: (7, {})} | custom-call | flops 1610612736 | bytes 10485760 | tf_op jit(solution)/shard_map/gram/pallas_call | solution.py:195
  118.1 0.0 collective-permute-done.6.refs_0_
  118.1 1.5 collective-permute-start.10
  119.6 4.4 %collective-permute-done.12.refs_1_ = bf16[16,4,64,128]{3,2,1,0:T(8,128)(2,1)S(1)} collective-permute-done((bf16[16,4,64,128]{3,2,1,0:T(8,128)(2,1)}, bf16[16,4,64,128]{3,2,1,0:T(8,128)(2,1)S(1)}, u32[]{:S(2)}, u32[]{:S(2)}) %collective-permute-start.12) | collective-permute-done | bytes 1048608 | tf_op jit(solution)/shard_map/ppermute | solution.py:269
  124.0 5.9 %collective-permute-done.13.refs_2_ = bf16[16,4,64,128]{3,2,1,0:T(8,128)(2,1)} collective-permute-done((bf16[16,4,64,128]{3,2,1,0:T(8,128)(2,1)}, bf16[16,4,64,128]{3,2,1,0:T(8,128)(2,1)}, u32[]{:S(2)}, u32[]{:S(2)}) %collective-permute-start.13) | collective-permute-done | bytes 1048608 | tf_op jit(solution)/shard_map/ppermute | solution.py:271
  130.0 0.9 slice.8
  130.8 0.9 slice.9
  131.7 2.0 %collective-permute-start.16 = (bf16[16,2,64,128]{3,2,1,0:T(8,128)(2,1)}, bf16[16,2,64,128]{3,2,1,0:T(8,128)(2,1)S(1)}, u32[]{:S(2)}, u32[]{:S(2)}) collective-permute-start(bf16[16,2,64,128]{3,2,1,0:T(8,128)(2,1)} %slice.8), channel_id=1, source_target_pairs={{0,16},{16,0},{1,17},{17,1},{2,18},{18,2},{3,19},{19,3},{4,20},{20... | collective-permute-start | bytes 1572872 | tf_op jit(solution)/shard_map/ppermute | solution.py:271
  133.7 0.1 add_add_fusion.2.where
  133.8 5.7 %gram.10 = (bf16[2,16,128,2048]{3,2,1,0:T(8,128)(2,1)}, bf16[3,2,4,128,256]{4,3,2,1,0:T(8,128)(2,1)}) custom-call(s32[4]{0:T(128)S(1)} %add_add_fusion.2.where, bf16[4,512,512]{2,1,0:T(8,128)(2,1)} %rows.2.mine0_ref.mine1_ref, bf16[4,512,512]{2,1,0:T(8,128)(2,1)} %rows.3.mine1_ref, ...), custom_call_target="tpu_custom_call", output_to_operand_aliasing={{0}: (6, {})} | custom-call | flops 1610612736 | bytes 10485760 | tf_op jit(solution)/shard_map/gram/pallas_call | solution.py:195
  139.5 1.8 %collective-permute-done.10.refs_0_ = bf16[16,4,64,128]{3,2,1,0:T(8,128)(2,1)} collective-permute-done((bf16[16,4,64,128]{3,2,1,0:T(8,128)(2,1)}, bf16[16,4,64,128]{3,2,1,0:T(8,128)(2,1)}, u32[]{:S(2)}, u32[]{:S(2)}) %collective-permute-start.10) | collective-permute-done | bytes 1048608 | tf_op jit(solution)/shard_map/ppermute | solution.py:270
  141.3 10.8 %collective-permute-start.19 = (bf16[3,2,4,128,256]{4,3,2,1,0:T(8,128)(2,1)}, bf16[3,2,4,128,256]{4,3,2,1,0:T(8,128)(2,1)}, u32[]{:S(2)}, u32[]{:S(2)}) collective-permute-start(bf16[3,2,4,128,256]{4,3,2,1,0:T(8,128)(2,1)} %get-tuple-element.61), channel_id=1, source_target_pairs={{0,8},{8,0},{1,9},{9,1},{2,10},{10,2},{3,11},{11,3},{4,12},{12,4},... | collective-permute-start | bytes 4718600 | tf_op jit(solution)/shard_map/ppermute | solution.py:272
  152.1 0.0 collective-permute-done.11.refs_1_
  152.1 0.1 collective-permute-start.20
  152.2 0.1 stack.105.where
  152.3 0.1 pad_add_fusion.where
  152.3 4.8 %gram.11 = (bf16[2,16,128,2048]{3,2,1,0:T(8,128)(2,1)}, bf16[1,2,4,128,256]{4,3,2,1,0:T(8,128)(2,1)}) custom-call(s32[6]{0:T(128)S(1)} %stack.105.where, bf16[4,512,512]{2,1,0:T(8,128)(2,1)} %rows.2.mine0_ref.mine1_ref, bf16[4,512,512]{2,1,0:T(8,128)(2,1)} %rows.3.mine1_ref, ...), custom_call_target="tpu_custom_call", output_to_operand_aliasing={{0}: (5, {})} | custom-call | flops 536870912 | bytes 6291456 | tf_op jit(solution)/shard_map/gram/pallas_call | solution.py:195
  157.1 0.3 collective-permute-done.17
  157.4 0.0 collective-permute-done.16
  157.4 0.0 collective-permute-done.15.refs_0_
  157.5 0.1 constant_dynamic-update-slice_fusion.refs_1_
  157.6 4.1 %gram.12 = bf16[2,2,4,128,256]{4,3,2,1,0:T(8,128)(2,1)} custom-call(s32[3]{0:T(128)S(1)} %pad_add_fusion.where, bf16[4,512,512]{2,1,0:T(8,128)(2,1)} %rows.2.mine0_ref.mine1_ref, bf16[4,512,512]{2,1,0:T(8,128)(2,1)} %rows.3.mine1_ref, bf16[16,4,64,128]{3,2,1,0:T(8,128)(2,1)S(1)} %collective-permute-done.15.refs_0_, ...), custom_call_target="tpu_custom_call" | custom-call | flops 1073741824 | bytes 8388608 | tf_op jit(solution)/shard_map/gram/pallas_call | solution.py:195
  161.7 3.0 %collective-permute-start.18 = (bf16[2,2,4,128,256]{4,3,2,1,0:T(8,128)(2,1)}, bf16[2,2,4,128,256]{4,3,2,1,0:T(8,128)(2,1)S(1)}, u32[]{:S(2)}, u32[]{:S(2)}) collective-permute-start(bf16[2,2,4,128,256]{4,3,2,1,0:T(8,128)(2,1)} %gram.12), channel_id=1, source_target_pairs={{0,8},{8,0},{1,9},{9,1},{2,10},{10,2},{3,11},{11,3},{4,12},{12,4},... | collective-permute-start | bytes 3145736 | tf_op jit(solution)/shard_map/ppermute | solution.py:272
  164.6 0.1 collective-permute-start.14
  164.7 0.1 stack.118.where
  164.8 0.1 add_add_fusion.where
  164.9 0.0 collective-permute-done.19.refs_2_
  164.9 0.0 collective-permute-done.20.refs_3_
  164.9 5.4 %gram.13.refs_2_ = bf16[2,16,128,2048]{3,2,1,0:T(8,128)(2,1)} custom-call(s32[9]{0:T(128)S(1)} %stack.118.where, bf16[4,512,512]{2,1,0:T(8,128)(2,1)} %rows.2.mine0_ref.mine1_ref, bf16[4,512,512]{2,1,0:T(8,128)(2,1)} %rows.3.mine1_ref, bf16[16,4,64,128]{3,2,1,0:T(8,128)(2,1)S(1)} %collective-permute-done.15.refs_0_, ...), custom_call_target="tpu_custom_call", output_to_operand_aliasing={{}: (7, {})} | custom-call | flops 1073741824 | bytes 8388608 | tf_op jit(solution)/shard_map/gram/pallas_call | solution.py:195
  170.3 0.0 collective-permute-done.14.refs_0_
  170.3 3.3 %place.1 = bf16[2,16,128,2048]{3,2,1,0:T(8,128)(2,1)} custom-call(s32[4]{0:T(128)S(1)} %add_add_fusion.where, bf16[1,2,4,128,256]{4,3,2,1,0:T(8,128)(2,1)} %collective-permute-done.14.refs_0_, bf16[2,2,4,128,256]{4,3,2,1,0:T(8,128)(2,1)S(1)} %collective-permute-done.18.refs_1_, bf16[2,16,128,2048]{3,2,1,0:T(8,128)(2,1)} %gram.13.refs_2_), custom_call_target="tpu_custom_call", output_to_operand_aliasing={{}: (3, {})} | custom-call | tf_op jit(solution)/shard_map/place/pallas_call | solution.py:244
  (8 shorter events, 0.1 us)
Async XLA Ops:
  31.0 22.0 %collective-permute-start.1 = (bf16[16,4,64,128]{3,2,1,0:T(8,128)(2,1)S(1)}, bf16[16,4,64,128]{3,2,1,0:T(8,128)(2,1)}, u32[]{:S(2)}, u32[]{:S(2)}) collective-permute-start(bf16[16,4,64,128]{3,2,1,0:T(8,128)(2,1)S(1)} %bitcast.23), channel_id=1, source_target_pairs={{0,32},{8,104},{32,64},{40,8},{64,96},{72,40},{96,0},{104,72},{1,3... | collective-permute-start | bytes 3145736 | tf_op jit(solution)/shard_map/ppermute | solution.py:269
  33.5 19.5 %all-to-all-start.1 = ((bf16[16,4,2,32,128]{4,3,2,1,0:T(8,128)(2,1)}), bf16[16,4,2,32,128]{4,3,2,1,0:T(8,128)(2,1)S(1)}, u32[]{:S(2)}, u32[]{:S(2)}) async-start(bf16[16,4,2,32,128]{4,3,2,1,0:T(8,128)(2,1)} %get-tuple-element.36), calls=%async_computation.1 | async-start | bytes 2097152 | tf_op jit(solution)/shard_map/all_to_all | solution.py:276
  37.1 23.6 %collective-permute-start.4 = (bf16[16,4,64,128]{3,2,1,0:T(8,128)(2,1)S(1)}, bf16[16,4,64,128]{3,2,1,0:T(8,128)(2,1)}, u32[]{:S(2)}, u32[]{:S(2)}) collective-permute-start(bf16[16,4,64,128]{3,2,1,0:T(8,128)(2,1)S(1)} %bitcast.24), channel_id=1, source_target_pairs={{0,96},{8,40},{32,0},{40,72},{64,32},{72,104},{96,64},{104,8},{1,9... | collective-permute-start | bytes 3145736 | tf_op jit(solution)/shard_map/ppermute | solution.py:270
  53.0 14.8 %collective-permute-start.2 = (bf16[16,4,64,128]{3,2,1,0:T(8,128)(2,1)}, bf16[16,4,64,128]{3,2,1,0:T(8,128)(2,1)S(1)}, u32[]{:S(2)}, u32[]{:S(2)}) collective-permute-start(bf16[16,4,64,128]{3,2,1,0:T(8,128)(2,1)} %collective-permute-done.1.refs_1_), channel_id=1, source_target_pairs={{0,32},{8,104},{32,64},{40,8},{64,96},{72,40},{96,0},{104,72},{1,3... | collective-permute-start | bytes 3145736 | tf_op jit(solution)/shard_map/ppermute | solution.py:269
  54.5 29.1 %collective-permute-start.7 = (bf16[16,4,64,128]{3,2,1,0:T(8,128)(2,1)S(1)}, bf16[16,4,64,128]{3,2,1,0:T(8,128)(2,1)}, u32[]{:S(2)}, u32[]{:S(2)}) collective-permute-start(bf16[16,4,64,128]{3,2,1,0:T(8,128)(2,1)S(1)} %bitcast.18), channel_id=1, source_target_pairs={{0,32},{8,104},{32,64},{40,8},{64,96},{72,40},{96,0},{104,72},{1,3... | collective-permute-start | bytes 3145736 | tf_op jit(solution)/shard_map/ppermute | solution.py:269
  55.8 31.3 %collective-permute-start = (bf16[16,4,64,128]{3,2,1,0:T(8,128)(2,1)S(1)}, bf16[16,4,64,128]{3,2,1,0:T(8,128)(2,1)}, u32[]{:S(2)}, u32[]{:S(2)}) collective-permute-start(bf16[16,4,64,128]{3,2,1,0:T(8,128)(2,1)S(1)} %bitcast.25), channel_id=1, source_target_pairs={{0,16},{16,0},{1,17},{17,1},{2,18},{18,2},{3,19},{19,3},{4,20},{20... | collective-permute-start | bytes 3145736 | tf_op jit(solution)/shard_map/ppermute | solution.py:271
  67.8 1.0 copy-start
  68.8 27.7 %collective-permute-start.5 = (bf16[16,4,64,128]{3,2,1,0:T(8,128)(2,1)S(1)}, bf16[16,4,64,128]{3,2,1,0:T(8,128)(2,1)}, u32[]{:S(2)}, u32[]{:S(2)}) collective-permute-start(bf16[16,4,64,128]{3,2,1,0:T(8,128)(2,1)S(1)} %bitcast.19), channel_id=1, source_target_pairs={{0,96},{8,40},{32,0},{40,72},{64,32},{72,104},{96,64},{104,8},{1,9... | collective-permute-start | bytes 3145736 | tf_op jit(solution)/shard_map/ppermute | solution.py:270
  83.6 22.6 %collective-permute-start.8 = (bf16[16,4,64,128]{3,2,1,0:T(8,128)(2,1)}, bf16[16,4,64,128]{3,2,1,0:T(8,128)(2,1)S(1)}, u32[]{:S(2)}, u32[]{:S(2)}) collective-permute-start(bf16[16,4,64,128]{3,2,1,0:T(8,128)(2,1)} %collective-permute-done.7.refs_2_), channel_id=1, source_target_pairs={{0,32},{8,104},{32,64},{40,8},{64,96},{72,40},{96,0},{104,72},{1,3... | collective-permute-start | bytes 3145736 | tf_op jit(solution)/shard_map/ppermute | solution.py:269
  87.1 10.7 %copy-start.1 = (bf16[16,4,64,128]{3,2,1,0:T(8,128)(2,1)S(1)}, bf16[16,4,64,128]{3,2,1,0:T(8,128)(2,1)}, u32[]{:S(2)}) copy-start(bf16[16,4,64,128]{3,2,1,0:T(8,128)(2,1)} %copy-done) | copy-start | bytes 3145732
  87.1 22.1 %collective-permute-start.3 = (bf16[16,4,64,128]{3,2,1,0:T(8,128)(2,1)S(1)}, bf16[16,4,64,128]{3,2,1,0:T(8,128)(2,1)}, u32[]{:S(2)}, u32[]{:S(2)}) collective-permute-start(bf16[16,4,64,128]{3,2,1,0:T(8,128)(2,1)S(1)} %bitcast.20), channel_id=1, source_target_pairs={{0,16},{16,0},{1,17},{17,1},{2,18},{18,2},{3,19},{19,3},{4,20},{20... | collective-permute-start | bytes 3145736 | tf_op jit(solution)/shard_map/ppermute | solution.py:271
  89.7 22.2 %collective-permute-start.9 = (bf16[3,2,4,128,256]{4,3,2,1,0:T(8,128)(2,1)}, bf16[3,2,4,128,256]{4,3,2,1,0:T(8,128)(2,1)}, u32[]{:S(2)}, u32[]{:S(2)}) collective-permute-start(bf16[3,2,4,128,256]{4,3,2,1,0:T(8,128)(2,1)} %get-tuple-element.45), channel_id=1, source_target_pairs={{0,8},{8,0},{1,9},{9,1},{2,10},{10,2},{3,11},{11,3},{4,12},{12,4},... | collective-permute-start | bytes 4718600 | tf_op jit(solution)/shard_map/ppermute | solution.py:272
  96.5 21.5 %collective-permute-start.6 = (bf16[16,4,64,128]{3,2,1,0:T(8,128)(2,1)}, bf16[16,4,64,128]{3,2,1,0:T(8,128)(2,1)}, u32[]{:S(2)}, u32[]{:S(2)}) collective-permute-start(bf16[16,4,64,128]{3,2,1,0:T(8,128)(2,1)} %collective-permute-done.refs_3_), channel_id=1, source_target_pairs={{0,96},{8,40},{32,0},{40,72},{64,32},{72,104},{96,64},{104,8},{1,9... | collective-permute-start | bytes 3145736 | tf_op jit(solution)/shard_map/ppermute | solution.py:270
  104.2 47.8 %collective-permute-start.11 = (bf16[4,2,4,128,256]{4,3,2,1,0:T(8,128)(2,1)}, bf16[4,2,4,128,256]{4,3,2,1,0:T(8,128)(2,1)}, u32[]{:S(2)}, u32[]{:S(2)}) collective-permute-start(bf16[4,2,4,128,256]{4,3,2,1,0:T(8,128)(2,1)} %get-tuple-element.50), channel_id=1, source_target_pairs={{0,8},{8,0},{1,9},{9,1},{2,10},{10,2},{3,11},{11,3},{4,12},{12,4},... | collective-permute-start | bytes 6291464 | tf_op jit(solution)/shard_map/ppermute | solution.py:272
  109.2 14.8 %collective-permute-start.12 = (bf16[16,4,64,128]{3,2,1,0:T(8,128)(2,1)}, bf16[16,4,64,128]{3,2,1,0:T(8,128)(2,1)S(1)}, u32[]{:S(2)}, u32[]{:S(2)}) collective-permute-start(bf16[16,4,64,128]{3,2,1,0:T(8,128)(2,1)} %collective-permute-done.3.refs_2_), channel_id=1, source_target_pairs={{0,32},{8,104},{32,64},{40,8},{64,96},{72,40},{96,0},{104,72},{1,3... | collective-permute-start | bytes 3145736 | tf_op jit(solution)/shard_map/ppermute | solution.py:269
  109.2 20.8 %collective-permute-start.13 = (bf16[16,4,64,128]{3,2,1,0:T(8,128)(2,1)}, bf16[16,4,64,128]{3,2,1,0:T(8,128)(2,1)}, u32[]{:S(2)}, u32[]{:S(2)}) collective-permute-start(bf16[16,4,64,128]{3,2,1,0:T(8,128)(2,1)} %collective-permute-done.1.refs_1_), channel_id=1, source_target_pairs={{0,16},{16,0},{1,17},{17,1},{2,18},{18,2},{3,19},{19,3},{4,20},{20... | collective-permute-start | bytes 3145736 | tf_op jit(solution)/shard_map/ppermute | solution.py:271
  118.1 23.2 %collective-permute-start.10 = (bf16[16,4,64,128]{3,2,1,0:T(8,128)(2,1)}, bf16[16,4,64,128]{3,2,1,0:T(8,128)(2,1)}, u32[]{:S(2)}, u32[]{:S(2)}) collective-permute-start(bf16[16,4,64,128]{3,2,1,0:T(8,128)(2,1)} %collective-permute-done.3.refs_2_), channel_id=1, source_target_pairs={{0,96},{8,40},{32,0},{40,72},{64,32},{72,104},{96,64},{104,8},{1,9... | collective-permute-start | bytes 3145736 | tf_op jit(solution)/shard_map/ppermute | solution.py:270
  130.0 27.5 %collective-permute-start.15 = (bf16[16,4,64,128]{3,2,1,0:T(8,128)(2,1)}, bf16[16,4,64,128]{3,2,1,0:T(8,128)(2,1)S(1)}, u32[]{:S(2)}, u32[]{:S(2)}) collective-permute-start(bf16[16,4,64,128]{3,2,1,0:T(8,128)(2,1)} %collective-permute-done.13.refs_2_), channel_id=1, source_target_pairs={{0,32},{8,104},{32,64},{40,8},{64,96},{72,40},{96,0},{104,72},{1,3... | collective-permute-start | bytes 3145736 | tf_op jit(solution)/shard_map/ppermute | solution.py:269
  131.7 25.8 %collective-permute-start.17 = (bf16[16,2,64,128]{3,2,1,0:T(8,128)(2,1)}, bf16[16,2,64,128]{3,2,1,0:T(8,128)(2,1)S(1)}, u32[]{:S(2)}, u32[]{:S(2)}) collective-permute-start(bf16[16,2,64,128]{3,2,1,0:T(8,128)(2,1)} %slice.9), channel_id=1, source_target_pairs={{0,32},{8,104},{32,64},{40,8},{64,96},{72,40},{96,0},{104,72},{1,3... | collective-permute-start | bytes 1572872 | tf_op jit(solution)/shard_map/ppermute | solution.py:269
  131.7 25.8 %collective-permute-start.16 = (bf16[16,2,64,128]{3,2,1,0:T(8,128)(2,1)}, bf16[16,2,64,128]{3,2,1,0:T(8,128)(2,1)S(1)}, u32[]{:S(2)}, u32[]{:S(2)}) collective-permute-start(bf16[16,2,64,128]{3,2,1,0:T(8,128)(2,1)} %slice.8), channel_id=1, source_target_pairs={{0,16},{16,0},{1,17},{17,1},{2,18},{18,2},{3,19},{19,3},{4,20},{20... | collective-permute-start | bytes 1572872 | tf_op jit(solution)/shard_map/ppermute | solution.py:271
  141.3 23.6 %collective-permute-start.19 = (bf16[3,2,4,128,256]{4,3,2,1,0:T(8,128)(2,1)}, bf16[3,2,4,128,256]{4,3,2,1,0:T(8,128)(2,1)}, u32[]{:S(2)}, u32[]{:S(2)}) collective-permute-start(bf16[3,2,4,128,256]{4,3,2,1,0:T(8,128)(2,1)} %get-tuple-element.61), channel_id=1, source_target_pairs={{0,8},{8,0},{1,9},{9,1},{2,10},{10,2},{3,11},{11,3},{4,12},{12,4},... | collective-permute-start | bytes 4718600 | tf_op jit(solution)/shard_map/ppermute | solution.py:272
  152.1 12.8 %collective-permute-start.20 = (bf16[3,2,4,128,256]{4,3,2,1,0:T(8,128)(2,1)}, bf16[3,2,4,128,256]{4,3,2,1,0:T(8,128)(2,1)}, u32[]{:S(2)}, u32[]{:S(2)}) collective-permute-start(bf16[3,2,4,128,256]{4,3,2,1,0:T(8,128)(2,1)} %get-tuple-element.62), channel_id=1, source_target_pairs={{0,8},{8,0},{1,9},{9,1},{2,10},{10,2},{3,11},{11,3},{4,12},{12,4},... | collective-permute-start | bytes 4718600 | tf_op jit(solution)/shard_map/ppermute | solution.py:272
  161.7 8.6 %collective-permute-start.18 = (bf16[2,2,4,128,256]{4,3,2,1,0:T(8,128)(2,1)}, bf16[2,2,4,128,256]{4,3,2,1,0:T(8,128)(2,1)S(1)}, u32[]{:S(2)}, u32[]{:S(2)}) collective-permute-start(bf16[2,2,4,128,256]{4,3,2,1,0:T(8,128)(2,1)} %gram.12), channel_id=1, source_target_pairs={{0,8},{8,0},{1,9},{9,1},{2,10},{10,2},{3,11},{11,3},{4,12},{12,4},... | collective-permute-start | bytes 3145736 | tf_op jit(solution)/shard_map/ppermute | solution.py:272
  164.6 5.7 %collective-permute-start.14 = (bf16[1,2,4,128,256]{4,3,2,1,0:T(8,128)(2,1)}, bf16[1,2,4,128,256]{4,3,2,1,0:T(8,128)(2,1)}, u32[]{:S(2)}, u32[]{:S(2)}) collective-permute-start(bf16[1,2,4,128,256]{4,3,2,1,0:T(8,128)(2,1)} %get-tuple-element.54), channel_id=1, source_target_pairs={{0,8},{8,0},{1,9},{9,1},{2,10},{10,2},{3,11},{11,3},{4,12},{12,4},... | collective-permute-start | bytes 1572872 | tf_op jit(solution)/shard_map/ppermute | solution.py:272

commit v12 on v11

--- a/solution.py
+++ b/solution.py
@@ -293,12 +293,12 @@
     out, sent = gram(core, (ma, ma), blocks1, shape, None)
     mine = ma, rows_of(pb)
 
-    bb, fb, ob = bwd(after(pb, fa, out)), fwd(after(nb, out)), over(after(pb, oa, fa))
+    bb, fb, ob = bwd(after(pb, fa, out)), fwd(after(nb, oa, out)), over(after(pb, oa))
     sent1 = blocks1, swap(sent)
     blocks2 = [entry(1, 0, 0, after(pb, bb)), entry(0, 2, 0, fa), entry(1, 1, 0, nb), entry(0, 0, 1, oa)]
     out, sent = gram(core, mine, blocks2, shape, out)
 
-    boa, nob, noa = bwd(after(oa, bb)), fwd(after(ob, fb)), over(after(na, ob, bb))
+    boa, nob, noa = bwd(after(oa, bb)), fwd(after(ob, fb)), over(after(na, ob))
     sent2 = blocks2, swap(sent)
     blocks3 = [entry(1, -1, 0, bb), entry(1, 2, 0, fb), entry(1, 0, 1, ob)]
     out, sent = gram(core, mine, blocks3, shape, out, sent1)

time: 176 us -> 179 us (1.017); the launches traced: 174 us -> 179 us
  starting transfers between devices: 47.5 us -> 52.7 us
    ppermute x7, waiting for transfers between devices: 19.3 us -> 2.76 us  [shards(): fwd = lambda v: lax.ppermute(v, ('x', 'core'), mirrored(1))]
    ppermute x4, waiting for transfers between devices: 8.93 us -> 19.7 us  [shards(): over = lambda v: lax.ppermute(v, 'yh', [(0, 1), (1, 0)])]
    ppermute x4, waiting for transfers between devices: 1.81 us -> 8.45 us  [shards(): bwd = lambda v: lax.ppermute(v, ('x', 'core'), mirrored(-1))]
    ppermute x7, starting transfers between devices: 8.74 us -> 12.2 us  [shards(): fwd = lambda v: lax.ppermute(v, ('x', 'core'), mirrored(1))]
    ppermute x6, starting transfers between devices: 20.4 us -> 22.5 us  [shards(): swap = lambda v: lax.ppermute(v, 'core', [(0, 1), (1, 0)])]
  transfers between devices with their start and end apart: 22 -> 22, of which waited for: 8 -> 7; matrix products, arithmetic and copies ran while one was open for 1% -> 1% of each run, Pallas kernels for 25% -> 24%
where the time goes in v12:
time: 179 us
  Pallas kernels  54.5 us (30%)
  starting transfers between devices  52.7 us (29%)
  waiting for transfers between devices  45.7 us (26%)
  blocking collectives  23.3 us (13%)
  local copies, waits for them, and re-layouts  2.18 us (1%)
    pallas_call x7, Pallas kernels, gram(): pl.pallas_call(functools.partial(gram_kernel, 2.0 / depth, chunks, [[bloc...  38.9 us
    all_to_all x1, blocking collectives, owned(): lax.all_to_all(chunk, ('yl', 'z', 'core'), split_axis=0, concat_axis=0, t...  23.3 us
    ppermute x6, starting transfers between devices, shards(): swap = lambda v: lax.ppermute(v, 'core', [(0, 1), (1, 0)])  22.5 us
    ppermute x4, waiting for transfers between devices, shards(): over = lambda v: lax.ppermute(v, 'yh', [(0, 1), (1, 0)])  19.7 us
    all_to_all x1, waiting for transfers between devices, owned(): lax.all_to_all(chunk, ('yl', 'z', 'core'), split_axis=0, concat_axis=0, t...  14.7 us
    ppermute x7, starting transfers between devices, shards(): fwd = lambda v: lax.ppermute(v, ('x', 'core'), mirrored(1))  12.2 us
    ppermute x4, starting transfers between devices, shards(): over = lambda v: lax.ppermute(v, 'yh', [(0, 1), (1, 0)])  11.1 us
    ppermute x4, waiting for transfers between devices, shards(): bwd = lambda v: lax.ppermute(v, ('x', 'core'), mirrored(-1))  8.45 us
  transfers between devices with their start and end apart: 22, of which 7 were waited for; matrix products, arithmetic and copies ran while one was open for 1% of the time, Pallas kernels for 24%

profile of v12, /device:TPU:1, one launch (start us, length us, event | category | flops | bytes accessed | tf_op | source)
XLA Modules:
  0.0 178.9 jit_solution(16354836626041981410)
XLA Ops:
  0.0 7.8 %whiten.1 = (bf16[16,4,2,32,128]{4,3,2,1,0:T(8,128)(2,1)}, bf16[16,4,2,32,128]{4,3,2,1,0:T(8,128)(2,1)}) custom-call(bf16[128,32,512]{2,1,0:T(8,128)(2,1)} %records_ref.1, s32[32,128]{1,0:T(8,128)} %bitcast.28, bf16[512,256]{1,0:T(8,128)(2,1)} %constant.183.clone.high_ref, bf16[512,256]{1,0:T(8,128)(2,1)} %constant.184.clone.low_ref), custom_call_target="tpu_custom_call" | custom-call | tf_op jit(solution)/shard_map/whiten/pallas_call | solution.py:56
  7.8 23.3 %all_to_all.10 = bf16[16,4,2,32,128]{4,3,2,1,0:T(8,128)(2,1)S(1)} all-to-all(bf16[16,4,2,32,128]{4,3,2,1,0:T(8,128)(2,1)} %get-tuple-element.34), channel_id=1, replica_groups=mesh['x'=4,'yh'=2,'core'=2,'yl'=2,'z'=4] {'yl','z','core'}, dimensions={0} | all-to-all | bytes 2097152 | tf_op jit(solution)/shard_map/all_to_all | solution.py:276
  31.0 2.5 %collective-permute-start.2 = (bf16[16,4,64,128]{3,2,1,0:T(8,128)(2,1)S(1)}, bf16[16,4,64,128]{3,2,1,0:T(8,128)(2,1)}, u32[]{:S(2)}, u32[]{:S(2)}) collective-permute-start(bf16[16,4,64,128]{3,2,1,0:T(8,128)(2,1)S(1)} %bitcast.23), channel_id=1, source_target_pairs={{0,32},{8,104},{32,64},{40,8},{64,96},{72,40},{96,0},{104,72},{1,3... | collective-permute-start | bytes 3145736 | tf_op jit(solution)/shard_map/ppermute | solution.py:269
  33.5 3.6 %all-to-all-start.1 = ((bf16[16,4,2,32,128]{4,3,2,1,0:T(8,128)(2,1)}), bf16[16,4,2,32,128]{4,3,2,1,0:T(8,128)(2,1)S(1)}, u32[]{:S(2)}, u32[]{:S(2)}) async-start(bf16[16,4,2,32,128]{4,3,2,1,0:T(8,128)(2,1)} %get-tuple-element.36), calls=%async_computation.1 | async-start | bytes 2097152 | tf_op jit(solution)/shard_map/all_to_all | solution.py:276
  37.1 1.2 collective-permute-start.4
  38.3 14.7 %all-to-all-done.1 = bf16[16,4,2,32,128]{4,3,2,1,0:T(8,128)(2,1)S(1)} async-done(((bf16[16,4,2,32,128]{4,3,2,1,0:T(8,128)(2,1)}), bf16[16,4,2,32,128]{4,3,2,1,0:T(8,128)(2,1)S(1)}, u32[]{:S(2)}, u32[]{:S(2)}) %all-to-all-start.1) | async-done | bytes 1048608 | tf_op jit(solution)/shard_map/all_to_all | solution.py:276
  53.0 0.0 collective-permute-done.2.refs_1_
  53.0 1.5 collective-permute-start.3
  54.5 2.6 %collective-permute-start = (bf16[16,4,64,128]{3,2,1,0:T(8,128)(2,1)S(1)}, bf16[16,4,64,128]{3,2,1,0:T(8,128)(2,1)S(1)}, u32[]{:S(2)}, u32[]{:S(2)}) collective-permute-start(bf16[16,4,64,128]{3,2,1,0:T(8,128)(2,1)S(1)} %bitcast.25), channel_id=1, source_target_pairs={{0,16},{16,0},{1,17},{17,1},{2,18},{18,2},{3,19},{19,3},{4,20},{20... | collective-permute-start | bytes 3145736 | tf_op jit(solution)/shard_map/ppermute | solution.py:271
  57.1 1.3 collective-permute-start.7
  58.4 0.1 add_add_fusion.1.where
  58.5 2.3 %rows.2.mine0_ref.mine1_ref = bf16[4,512,512]{2,1,0:T(8,128)(2,1)} custom-call(bf16[16,4,64,128]{3,2,1,0:T(8,128)(2,1)S(1)} %bitcast.26), custom_call_target="tpu_custom_call" | custom-call | tf_op jit(solution)/shard_map/rows/pallas_call | solution.py:90
  60.7 0.0 collective-permute-done.4.refs_2_
  60.8 6.3 %gram.7 = (bf16[2,16,128,2048]{3,2,1,0:T(8,128)(2,1)}, bf16[3,2,4,128,256]{4,3,2,1,0:T(8,128)(2,1)}) custom-call(s32[4]{0:T(128)S(1)} %add_add_fusion.1.where, bf16[4,512,512]{2,1,0:T(8,128)(2,1)} %rows.2.mine0_ref.mine1_ref, bf16[4,512,512]{2,1,0:T(8,128)(2,1)} %rows.2.mine0_ref.mine1_ref, bf16[16,4,64,128]{3,2,1,0:T(8,128)(2,1)S(1)} %bitcast.27, ...), custom_call_target="tpu_custom_call" | custom-call | flops 1610612736 | bytes 10485760 | tf_op jit(solution)/shard_map/gram/pallas_call | solution.py:195
  67.0 0.8 collective-permute-done.3.refs_1_
  67.8 0.9 collective-permute-start.5
  68.8 11.0 %collective-permute-done.refs_3_ = bf16[16,4,64,128]{3,2,1,0:T(8,128)(2,1)S(1)} collective-permute-done((bf16[16,4,64,128]{3,2,1,0:T(8,128)(2,1)S(1)}, bf16[16,4,64,128]{3,2,1,0:T(8,128)(2,1)S(1)}, u32[]{:S(2)}, u32[]{:S(2)}) %collective-permute-start) | collective-permute-done | bytes 1048608 | tf_op jit(solution)/shard_map/ppermute | solution.py:271
  79.8 2.7 %collective-permute-start.1 = (bf16[16,4,64,128]{3,2,1,0:T(8,128)(2,1)S(1)}, bf16[16,4,64,128]{3,2,1,0:T(8,128)(2,1)}, u32[]{:S(2)}, u32[]{:S(2)}) collective-permute-start(bf16[16,4,64,128]{3,2,1,0:T(8,128)(2,1)S(1)} %bitcast.20), channel_id=1, source_target_pairs={{0,16},{16,0},{1,17},{17,1},{2,18},{18,2},{3,19},{19,3},{4,20},{20... | collective-permute-start | bytes 3145736 | tf_op jit(solution)/shard_map/ppermute | solution.py:271
  82.5 2.0 %collective-permute-done.7.refs_2_ = bf16[16,4,64,128]{3,2,1,0:T(8,128)(2,1)} collective-permute-done((bf16[16,4,64,128]{3,2,1,0:T(8,128)(2,1)S(1)}, bf16[16,4,64,128]{3,2,1,0:T(8,128)(2,1)}, u32[]{:S(2)}, u32[]{:S(2)}) %collective-permute-start.7) | collective-permute-done | bytes 1048608 | tf_op jit(solution)/shard_map/ppermute | solution.py:269
  84.5 3.5 %collective-permute-start.8 = (bf16[16,4,64,128]{3,2,1,0:T(8,128)(2,1)}, bf16[16,4,64,128]{3,2,1,0:T(8,128)(2,1)S(1)}, u32[]{:S(2)}, u32[]{:S(2)}) collective-permute-start(bf16[16,4,64,128]{3,2,1,0:T(8,128)(2,1)} %collective-permute-done.7.refs_2_), channel_id=1, source_target_pairs={{0,32},{8,104},{32,64},{40,8},{64,96},{72,40},{96,0},{104,72},{1,3... | collective-permute-start | bytes 3145736 | tf_op jit(solution)/shard_map/ppermute | solution.py:269
  88.0 4.3 %collective-permute-start.9 = (bf16[3,2,4,128,256]{4,3,2,1,0:T(8,128)(2,1)}, bf16[3,2,4,128,256]{4,3,2,1,0:T(8,128)(2,1)}, u32[]{:S(2)}, u32[]{:S(2)}) collective-permute-start(bf16[3,2,4,128,256]{4,3,2,1,0:T(8,128)(2,1)} %get-tuple-element.45), channel_id=1, source_target_pairs={{0,8},{8,0},{1,9},{9,1},{2,10},{10,2},{3,11},{11,3},{4,12},{12,4},... | collective-permute-start | bytes 4718600 | tf_op jit(solution)/shard_map/ppermute | solution.py:272
  92.3 0.1 stack.112.where
  92.4 2.3 %rows.3.mine1_ref = bf16[4,512,512]{2,1,0:T(8,128)(2,1)} custom-call(bf16[16,4,64,128]{3,2,1,0:T(8,128)(2,1)S(1)} %bitcast.21), custom_call_target="tpu_custom_call" | custom-call | tf_op jit(solution)/shard_map/rows/pallas_call | solution.py:90
  94.6 0.0 collective-permute-done.5.refs_0_
  94.6 1.2 collective-permute-start.6
  95.9 6.5 %gram.8 = (bf16[2,16,128,2048]{3,2,1,0:T(8,128)(2,1)}, bf16[4,2,4,128,256]{4,3,2,1,0:T(8,128)(2,1)}) custom-call(s32[5]{0:T(128)S(1)} %stack.112.where, bf16[4,512,512]{2,1,0:T(8,128)(2,1)} %rows.2.mine0_ref.mine1_ref, bf16[4,512,512]{2,1,0:T(8,128)(2,1)} %rows.3.mine1_ref, bf16[16,4,64,128]{3,2,1,0:T(8,128)(2,1)S(1)} %bitcast.22, ...), custom_call_target="tpu_custom_call", output_to_operand_aliasing={{0}: (7, {})} | custom-call | flops 2147483648 | bytes 12582912 | tf_op jit(solution)/shard_map/gram/pallas_call | solution.py:195
  102.3 1.9 %collective-permute-start.11 = (bf16[4,2,4,128,256]{4,3,2,1,0:T(8,128)(2,1)}, bf16[4,2,4,128,256]{4,3,2,1,0:T(8,128)(2,1)}, u32[]{:S(2)}, u32[]{:S(2)}) collective-permute-start(bf16[4,2,4,128,256]{4,3,2,1,0:T(8,128)(2,1)} %get-tuple-element.50), channel_id=1, source_target_pairs={{0,8},{8,0},{1,9},{9,1},{2,10},{10,2},{3,11},{11,3},{4,12},{12,4},... | collective-permute-start | bytes 6291464 | tf_op jit(solution)/shard_map/ppermute | solution.py:272
  104.2 0.0 collective-permute-done.1.refs_2_
  104.2 2.8 %collective-permute-start.13 = (bf16[16,4,64,128]{3,2,1,0:T(8,128)(2,1)}, bf16[16,4,64,128]{3,2,1,0:T(8,128)(2,1)}, u32[]{:S(2)}, u32[]{:S(2)}) collective-permute-start(bf16[16,4,64,128]{3,2,1,0:T(8,128)(2,1)} %collective-permute-done.2.refs_1_), channel_id=1, source_target_pairs={{0,16},{16,0},{1,17},{17,1},{2,18},{18,2},{3,19},{19,3},{4,20},{20... | collective-permute-start | bytes 3145736 | tf_op jit(solution)/shard_map/ppermute | solution.py:271
  107.1 0.8 collective-permute-start.12
  107.9 0.1 stack.111.where
  108.0 0.0 collective-permute-done.9.refs_3_
  108.0 6.2 %gram.9 = (bf16[2,16,128,2048]{3,2,1,0:T(8,128)(2,1)}, bf16[3,2,4,128,256]{4,3,2,1,0:T(8,128)(2,1)}) custom-call(s32[7]{0:T(128)S(1)} %stack.111.where, bf16[4,512,512]{2,1,0:T(8,128)(2,1)} %rows.2.mine0_ref.mine1_ref, bf16[4,512,512]{2,1,0:T(8,128)(2,1)} %rows.3.mine1_ref, ...), custom_call_target="tpu_custom_call", output_to_operand_aliasing={{0}: (7, {})} | custom-call | flops 1610612736 | bytes 10485760 | tf_op jit(solution)/shard_map/gram/pallas_call | solution.py:195
  114.2 5.1 %collective-permute-done.6.refs_0_ = bf16[16,4,64,128]{3,2,1,0:T(8,128)(2,1)} collective-permute-done((bf16[16,4,64,128]{3,2,1,0:T(8,128)(2,1)S(1)}, bf16[16,4,64,128]{3,2,1,0:T(8,128)(2,1)}, u32[]{:S(2)}, u32[]{:S(2)}) %collective-permute-start.6) | collective-permute-done | bytes 1048608 | tf_op jit(solution)/shard_map/ppermute | solution.py:270
  119.3 0.0 collective-permute-start.10
  119.3 8.7 %collective-permute-done.13.refs_2_ = bf16[16,4,64,128]{3,2,1,0:T(8,128)(2,1)} collective-permute-done((bf16[16,4,64,128]{3,2,1,0:T(8,128)(2,1)}, bf16[16,4,64,128]{3,2,1,0:T(8,128)(2,1)}, u32[]{:S(2)}, u32[]{:S(2)}) %collective-permute-start.13) | collective-permute-done | bytes 1048608 | tf_op jit(solution)/shard_map/ppermute | solution.py:271
  128.0 0.0 collective-permute-done.12.refs_1_
  128.0 0.0 collective-permute-start.15
  128.0 0.9 slice.8
  128.8 2.9 %collective-permute-start.16 = (bf16[16,2,64,128]{3,2,1,0:T(8,128)(2,1)}, bf16[16,2,64,128]{3,2,1,0:T(8,128)(2,1)S(1)}, u32[]{:S(2)}, u32[]{:S(2)}) collective-permute-start(bf16[16,2,64,128]{3,2,1,0:T(8,128)(2,1)} %slice.8), channel_id=1, source_target_pairs={{0,16},{16,0},{1,17},{17,1},{2,18},{18,2},{3,19},{19,3},{4,20},{20... | collective-permute-start | bytes 1572872 | tf_op jit(solution)/shard_map/ppermute | solution.py:271
  131.8 0.9 slice.9
  132.7 2.6 %collective-permute-start.17 = (bf16[16,2,64,128]{3,2,1,0:T(8,128)(2,1)}, bf16[16,2,64,128]{3,2,1,0:T(8,128)(2,1)S(1)}, u32[]{:S(2)}, u32[]{:S(2)}) collective-permute-start(bf16[16,2,64,128]{3,2,1,0:T(8,128)(2,1)} %slice.9), channel_id=1, source_target_pairs={{0,32},{8,104},{32,64},{40,8},{64,96},{72,40},{96,0},{104,72},{1,3... | collective-permute-start | bytes 1572872 | tf_op jit(solution)/shard_map/ppermute | solution.py:269
  135.2 0.1 add_add_fusion.2.where
  135.3 5.7 %gram.10 = (bf16[2,16,128,2048]{3,2,1,0:T(8,128)(2,1)}, bf16[3,2,4,128,256]{4,3,2,1,0:T(8,128)(2,1)}) custom-call(s32[4]{0:T(128)S(1)} %add_add_fusion.2.where, bf16[4,512,512]{2,1,0:T(8,128)(2,1)} %rows.2.mine0_ref.mine1_ref, bf16[4,512,512]{2,1,0:T(8,128)(2,1)} %rows.3.mine1_ref, ...), custom_call_target="tpu_custom_call", output_to_operand_aliasing={{0}: (6, {})} | custom-call | flops 1610612736 | bytes 10485760 | tf_op jit(solution)/shard_map/gram/pallas_call | solution.py:195
  141.0 3.4 %collective-permute-done.10.refs_0_ = bf16[16,4,64,128]{3,2,1,0:T(8,128)(2,1)} collective-permute-done((bf16[16,4,64,128]{3,2,1,0:T(8,128)(2,1)}, bf16[16,4,64,128]{3,2,1,0:T(8,128)(2,1)}, u32[]{:S(2)}, u32[]{:S(2)}) %collective-permute-start.10) | collective-permute-done | bytes 1048608 | tf_op jit(solution)/shard_map/ppermute | solution.py:270
  144.4 10.1 %collective-permute-start.19 = (bf16[3,2,4,128,256]{4,3,2,1,0:T(8,128)(2,1)}, bf16[3,2,4,128,256]{4,3,2,1,0:T(8,128)(2,1)}, u32[]{:S(2)}, u32[]{:S(2)}) collective-permute-start(bf16[3,2,4,128,256]{4,3,2,1,0:T(8,128)(2,1)} %get-tuple-element.61), channel_id=1, source_target_pairs={{0,8},{8,0},{1,9},{9,1},{2,10},{10,2},{3,11},{11,3},{4,12},{12,4},... | collective-permute-start | bytes 4718600 | tf_op jit(solution)/shard_map/ppermute | solution.py:272
  154.5 0.0 collective-permute-done.11.refs_1_
  154.5 0.1 collective-permute-start.20
  154.6 0.1 stack.105.where
  154.7 0.1 pad_add_fusion.where
  154.7 4.8 %gram.11 = (bf16[2,16,128,2048]{3,2,1,0:T(8,128)(2,1)}, bf16[1,2,4,128,256]{4,3,2,1,0:T(8,128)(2,1)}) custom-call(s32[6]{0:T(128)S(1)} %stack.105.where, bf16[4,512,512]{2,1,0:T(8,128)(2,1)} %rows.2.mine0_ref.mine1_ref, bf16[4,512,512]{2,1,0:T(8,128)(2,1)} %rows.3.mine1_ref, ...), custom_call_target="tpu_custom_call", output_to_operand_aliasing={{0}: (5, {})} | custom-call | flops 536870912 | bytes 6291456 | tf_op jit(solution)/shard_map/gram/pallas_call | solution.py:195
  159.5 0.0 collective-permute-done.17
  159.6 0.0 collective-permute-done.16
  159.6 0.1 constant_dynamic-update-slice_fusion.refs_1_
  159.7 4.1 %gram.12 = bf16[2,2,4,128,256]{4,3,2,1,0:T(8,128)(2,1)} custom-call(s32[3]{0:T(128)S(1)} %pad_add_fusion.where, bf16[4,512,512]{2,1,0:T(8,128)(2,1)} %rows.2.mine0_ref.mine1_ref, bf16[4,512,512]{2,1,0:T(8,128)(2,1)} %rows.3.mine1_ref, bf16[16,4,64,128]{3,2,1,0:T(8,128)(2,1)S(1)} %collective-permute-done.15.refs_0_, ...), custom_call_target="tpu_custom_call" | custom-call | flops 1073741824 | bytes 8388608 | tf_op jit(solution)/shard_map/gram/pallas_call | solution.py:195
  163.8 6.0 %collective-permute-start.18 = (bf16[2,2,4,128,256]{4,3,2,1,0:T(8,128)(2,1)}, bf16[2,2,4,128,256]{4,3,2,1,0:T(8,128)(2,1)S(1)}, u32[]{:S(2)}, u32[]{:S(2)}) collective-permute-start(bf16[2,2,4,128,256]{4,3,2,1,0:T(8,128)(2,1)} %gram.12), channel_id=1, source_target_pairs={{0,8},{8,0},{1,9},{9,1},{2,10},{10,2},{3,11},{11,3},{4,12},{12,4},... | collective-permute-start | bytes 3145736 | tf_op jit(solution)/shard_map/ppermute | solution.py:272
  169.8 0.1 collective-permute-start.14
  169.9 0.1 stack.118.where
  170.0 0.1 add_add_fusion.where
  170.0 0.0 collective-permute-done.19.refs_2_
  170.1 5.4 %gram.13.refs_2_ = bf16[2,16,128,2048]{3,2,1,0:T(8,128)(2,1)} custom-call(s32[9]{0:T(128)S(1)} %stack.118.where, bf16[4,512,512]{2,1,0:T(8,128)(2,1)} %rows.2.mine0_ref.mine1_ref, bf16[4,512,512]{2,1,0:T(8,128)(2,1)} %rows.3.mine1_ref, bf16[16,4,64,128]{3,2,1,0:T(8,128)(2,1)S(1)} %collective-permute-done.15.refs_0_, ...), custom_call_target="tpu_custom_call", output_to_operand_aliasing={{}: (7, {})} | custom-call | flops 1073741824 | bytes 8388608 | tf_op jit(solution)/shard_map/gram/pallas_call | solution.py:195
  175.4 0.0 collective-permute-done.14.refs_0_
  175.5 0.0 collective-permute-done.18.refs_1_
  175.5 3.3 %place.1 = bf16[2,16,128,2048]{3,2,1,0:T(8,128)(2,1)} custom-call(s32[4]{0:T(128)S(1)} %add_add_fusion.where, bf16[1,2,4,128,256]{4,3,2,1,0:T(8,128)(2,1)} %collective-permute-done.14.refs_0_, bf16[2,2,4,128,256]{4,3,2,1,0:T(8,128)(2,1)S(1)} %collective-permute-done.18.refs_1_, bf16[2,16,128,2048]{3,2,1,0:T(8,128)(2,1)} %gram.13.refs_2_), custom_call_target="tpu_custom_call", output_to_operand_aliasing={{}: (3, {})} | custom-call | tf_op jit(solution)/shard_map/place/pallas_call | solution.py:244
  (8 shorter events, 0.1 us)
Async XLA Ops:
  31.0 22.0 %collective-permute-start.2 = (bf16[16,4,64,128]{3,2,1,0:T(8,128)(2,1)S(1)}, bf16[16,4,64,128]{3,2,1,0:T(8,128)(2,1)}, u32[]{:S(2)}, u32[]{:S(2)}) collective-permute-start(bf16[16,4,64,128]{3,2,1,0:T(8,128)(2,1)S(1)} %bitcast.23), channel_id=1, source_target_pairs={{0,32},{8,104},{32,64},{40,8},{64,96},{72,40},{96,0},{104,72},{1,3... | collective-permute-start | bytes 3145736 | tf_op jit(solution)/shard_map/ppermute | solution.py:269
  33.5 19.5 %all-to-all-start.1 = ((bf16[16,4,2,32,128]{4,3,2,1,0:T(8,128)(2,1)}), bf16[16,4,2,32,128]{4,3,2,1,0:T(8,128)(2,1)S(1)}, u32[]{:S(2)}, u32[]{:S(2)}) async-start(bf16[16,4,2,32,128]{4,3,2,1,0:T(8,128)(2,1)} %get-tuple-element.36), calls=%async_computation.1 | async-start | bytes 2097152 | tf_op jit(solution)/shard_map/all_to_all | solution.py:276
  37.1 23.6 %collective-permute-start.4 = (bf16[16,4,64,128]{3,2,1,0:T(8,128)(2,1)S(1)}, bf16[16,4,64,128]{3,2,1,0:T(8,128)(2,1)}, u32[]{:S(2)}, u32[]{:S(2)}) collective-permute-start(bf16[16,4,64,128]{3,2,1,0:T(8,128)(2,1)S(1)} %bitcast.24), channel_id=1, source_target_pairs={{0,96},{8,40},{32,0},{40,72},{64,32},{72,104},{96,64},{104,8},{1,9... | collective-permute-start | bytes 3145736 | tf_op jit(solution)/shard_map/ppermute | solution.py:270
  53.0 14.8 %collective-permute-start.3 = (bf16[16,4,64,128]{3,2,1,0:T(8,128)(2,1)}, bf16[16,4,64,128]{3,2,1,0:T(8,128)(2,1)}, u32[]{:S(2)}, u32[]{:S(2)}) collective-permute-start(bf16[16,4,64,128]{3,2,1,0:T(8,128)(2,1)} %collective-permute-done.2.refs_1_), channel_id=1, source_target_pairs={{0,32},{8,104},{32,64},{40,8},{64,96},{72,40},{96,0},{104,72},{1,3... | collective-permute-start | bytes 3145736 | tf_op jit(solution)/shard_map/ppermute | solution.py:269
  54.5 25.3 %collective-permute-start = (bf16[16,4,64,128]{3,2,1,0:T(8,128)(2,1)S(1)}, bf16[16,4,64,128]{3,2,1,0:T(8,128)(2,1)S(1)}, u32[]{:S(2)}, u32[]{:S(2)}) collective-permute-start(bf16[16,4,64,128]{3,2,1,0:T(8,128)(2,1)S(1)} %bitcast.25), channel_id=1, source_target_pairs={{0,16},{16,0},{1,17},{17,1},{2,18},{18,2},{3,19},{19,3},{4,20},{20... | collective-permute-start | bytes 3145736 | tf_op jit(solution)/shard_map/ppermute | solution.py:271
  57.1 27.4 %collective-permute-start.7 = (bf16[16,4,64,128]{3,2,1,0:T(8,128)(2,1)S(1)}, bf16[16,4,64,128]{3,2,1,0:T(8,128)(2,1)}, u32[]{:S(2)}, u32[]{:S(2)}) collective-permute-start(bf16[16,4,64,128]{3,2,1,0:T(8,128)(2,1)S(1)} %bitcast.18), channel_id=1, source_target_pairs={{0,32},{8,104},{32,64},{40,8},{64,96},{72,40},{96,0},{104,72},{1,3... | collective-permute-start | bytes 3145736 | tf_op jit(solution)/shard_map/ppermute | solution.py:269
  67.8 26.8 %collective-permute-start.5 = (bf16[16,4,64,128]{3,2,1,0:T(8,128)(2,1)S(1)}, bf16[16,4,64,128]{3,2,1,0:T(8,128)(2,1)}, u32[]{:S(2)}, u32[]{:S(2)}) collective-permute-start(bf16[16,4,64,128]{3,2,1,0:T(8,128)(2,1)S(1)} %bitcast.19), channel_id=1, source_target_pairs={{0,96},{8,40},{32,0},{40,72},{64,32},{72,104},{96,64},{104,8},{1,9... | collective-permute-start | bytes 3145736 | tf_op jit(solution)/shard_map/ppermute | solution.py:270
  79.8 2.7 %copy-start = (bf16[16,4,64,128]{3,2,1,0:T(8,128)(2,1)}, bf16[16,4,64,128]{3,2,1,0:T(8,128)(2,1)S(1)}, u32[]{:S(2)}) copy-start(bf16[16,4,64,128]{3,2,1,0:T(8,128)(2,1)S(1)} %collective-permute-done.refs_3_) | copy-start | bytes 3145732
  79.8 24.5 %collective-permute-start.1 = (bf16[16,4,64,128]{3,2,1,0:T(8,128)(2,1)S(1)}, bf16[16,4,64,128]{3,2,1,0:T(8,128)(2,1)}, u32[]{:S(2)}, u32[]{:S(2)}) collective-permute-start(bf16[16,4,64,128]{3,2,1,0:T(8,128)(2,1)S(1)} %bitcast.20), channel_id=1, source_target_pairs={{0,16},{16,0},{1,17},{17,1},{2,18},{18,2},{3,19},{19,3},{4,20},{20... | collective-permute-start | bytes 3145736 | tf_op jit(solution)/shard_map/ppermute | solution.py:271
  84.5 10.2 %copy-start.1 = (bf16[16,4,64,128]{3,2,1,0:T(8,128)(2,1)S(1)}, bf16[16,4,64,128]{3,2,1,0:T(8,128)(2,1)}, u32[]{:S(2)}) copy-start(bf16[16,4,64,128]{3,2,1,0:T(8,128)(2,1)} %copy-done) | copy-start | bytes 3145732
  84.5 22.6 %collective-permute-start.8 = (bf16[16,4,64,128]{3,2,1,0:T(8,128)(2,1)}, bf16[16,4,64,128]{3,2,1,0:T(8,128)(2,1)S(1)}, u32[]{:S(2)}, u32[]{:S(2)}) collective-permute-start(bf16[16,4,64,128]{3,2,1,0:T(8,128)(2,1)} %collective-permute-done.7.refs_2_), channel_id=1, source_target_pairs={{0,32},{8,104},{32,64},{40,8},{64,96},{72,40},{96,0},{104,72},{1,3... | collective-permute-start | bytes 3145736 | tf_op jit(solution)/shard_map/ppermute | solution.py:269
  88.0 20.0 %collective-permute-start.9 = (bf16[3,2,4,128,256]{4,3,2,1,0:T(8,128)(2,1)}, bf16[3,2,4,128,256]{4,3,2,1,0:T(8,128)(2,1)}, u32[]{:S(2)}, u32[]{:S(2)}) collective-permute-start(bf16[3,2,4,128,256]{4,3,2,1,0:T(8,128)(2,1)} %get-tuple-element.45), channel_id=1, source_target_pairs={{0,8},{8,0},{1,9},{9,1},{2,10},{10,2},{3,11},{11,3},{4,12},{12,4},... | collective-permute-start | bytes 4718600 | tf_op jit(solution)/shard_map/ppermute | solution.py:272
  94.6 24.6 %collective-permute-start.6 = (bf16[16,4,64,128]{3,2,1,0:T(8,128)(2,1)S(1)}, bf16[16,4,64,128]{3,2,1,0:T(8,128)(2,1)}, u32[]{:S(2)}, u32[]{:S(2)}) collective-permute-start(bf16[16,4,64,128]{3,2,1,0:T(8,128)(2,1)S(1)} %copy-done.1), channel_id=1, source_target_pairs={{0,96},{8,40},{32,0},{40,72},{64,32},{72,104},{96,64},{104,8},{1,9... | collective-permute-start | bytes 3145736 | tf_op jit(solution)/shard_map/ppermute | solution.py:270
  102.3 52.2 %collective-permute-start.11 = (bf16[4,2,4,128,256]{4,3,2,1,0:T(8,128)(2,1)}, bf16[4,2,4,128,256]{4,3,2,1,0:T(8,128)(2,1)}, u32[]{:S(2)}, u32[]{:S(2)}) collective-permute-start(bf16[4,2,4,128,256]{4,3,2,1,0:T(8,128)(2,1)} %get-tuple-element.50), channel_id=1, source_target_pairs={{0,8},{8,0},{1,9},{9,1},{2,10},{10,2},{3,11},{11,3},{4,12},{12,4},... | collective-permute-start | bytes 6291464 | tf_op jit(solution)/shard_map/ppermute | solution.py:272
  104.2 23.7 %collective-permute-start.13 = (bf16[16,4,64,128]{3,2,1,0:T(8,128)(2,1)}, bf16[16,4,64,128]{3,2,1,0:T(8,128)(2,1)}, u32[]{:S(2)}, u32[]{:S(2)}) collective-permute-start(bf16[16,4,64,128]{3,2,1,0:T(8,128)(2,1)} %collective-permute-done.2.refs_1_), channel_id=1, source_target_pairs={{0,16},{16,0},{1,17},{17,1},{2,18},{18,2},{3,19},{19,3},{4,20},{20... | collective-permute-start | bytes 3145736 | tf_op jit(solution)/shard_map/ppermute | solution.py:271
  107.1 20.9 %collective-permute-start.12 = (bf16[16,4,64,128]{3,2,1,0:T(8,128)(2,1)}, bf16[16,4,64,128]{3,2,1,0:T(8,128)(2,1)S(1)}, u32[]{:S(2)}, u32[]{:S(2)}) collective-permute-start(bf16[16,4,64,128]{3,2,1,0:T(8,128)(2,1)} %collective-permute-done.1.refs_2_), channel_id=1, source_target_pairs={{0,32},{8,104},{32,64},{40,8},{64,96},{72,40},{96,0},{104,72},{1,3... | collective-permute-start | bytes 3145736 | tf_op jit(solution)/shard_map/ppermute | solution.py:269
  119.3 25.1 %collective-permute-start.10 = (bf16[16,4,64,128]{3,2,1,0:T(8,128)(2,1)}, bf16[16,4,64,128]{3,2,1,0:T(8,128)(2,1)}, u32[]{:S(2)}, u32[]{:S(2)}) collective-permute-start(bf16[16,4,64,128]{3,2,1,0:T(8,128)(2,1)} %collective-permute-done.1.refs_2_), channel_id=1, source_target_pairs={{0,96},{8,40},{32,0},{40,72},{64,32},{72,104},{96,64},{104,8},{1,9... | collective-permute-start | bytes 3145736 | tf_op jit(solution)/shard_map/ppermute | solution.py:270
  128.0 31.6 %collective-permute-start.15 = (bf16[16,4,64,128]{3,2,1,0:T(8,128)(2,1)}, bf16[16,4,64,128]{3,2,1,0:T(8,128)(2,1)S(1)}, u32[]{:S(2)}, u32[]{:S(2)}) collective-permute-start(bf16[16,4,64,128]{3,2,1,0:T(8,128)(2,1)} %collective-permute-done.13.refs_2_), channel_id=1, source_target_pairs={{0,32},{8,104},{32,64},{40,8},{64,96},{72,40},{96,0},{104,72},{1,3... | collective-permute-start | bytes 3145736 | tf_op jit(solution)/shard_map/ppermute | solution.py:269
  128.8 30.7 %collective-permute-start.16 = (bf16[16,2,64,128]{3,2,1,0:T(8,128)(2,1)}, bf16[16,2,64,128]{3,2,1,0:T(8,128)(2,1)S(1)}, u32[]{:S(2)}, u32[]{:S(2)}) collective-permute-start(bf16[16,2,64,128]{3,2,1,0:T(8,128)(2,1)} %slice.8), channel_id=1, source_target_pairs={{0,16},{16,0},{1,17},{17,1},{2,18},{18,2},{3,19},{19,3},{4,20},{20... | collective-permute-start | bytes 1572872 | tf_op jit(solution)/shard_map/ppermute | solution.py:271
  132.7 26.9 %collective-permute-start.17 = (bf16[16,2,64,128]{3,2,1,0:T(8,128)(2,1)}, bf16[16,2,64,128]{3,2,1,0:T(8,128)(2,1)S(1)}, u32[]{:S(2)}, u32[]{:S(2)}) collective-permute-start(bf16[16,2,64,128]{3,2,1,0:T(8,128)(2,1)} %slice.9), channel_id=1, source_target_pairs={{0,32},{8,104},{32,64},{40,8},{64,96},{72,40},{96,0},{104,72},{1,3... | collective-permute-start | bytes 1572872 | tf_op jit(solution)/shard_map/ppermute | solution.py:269
  144.4 25.7 %collective-permute-start.19 = (bf16[3,2,4,128,256]{4,3,2,1,0:T(8,128)(2,1)}, bf16[3,2,4,128,256]{4,3,2,1,0:T(8,128)(2,1)}, u32[]{:S(2)}, u32[]{:S(2)}) collective-permute-start(bf16[3,2,4,128,256]{4,3,2,1,0:T(8,128)(2,1)} %get-tuple-element.61), channel_id=1, source_target_pairs={{0,8},{8,0},{1,9},{9,1},{2,10},{10,2},{3,11},{11,3},{4,12},{12,4},... | collective-permute-start | bytes 4718600 | tf_op jit(solution)/shard_map/ppermute | solution.py:272
  154.5 15.6 %collective-permute-start.20 = (bf16[3,2,4,128,256]{4,3,2,1,0:T(8,128)(2,1)}, bf16[3,2,4,128,256]{4,3,2,1,0:T(8,128)(2,1)}, u32[]{:S(2)}, u32[]{:S(2)}) collective-permute-start(bf16[3,2,4,128,256]{4,3,2,1,0:T(8,128)(2,1)} %get-tuple-element.62), channel_id=1, source_target_pairs={{0,8},{8,0},{1,9},{9,1},{2,10},{10,2},{3,11},{11,3},{4,12},{12,4},... | collective-permute-start | bytes 4718600 | tf_op jit(solution)/shard_map/ppermute | solution.py:272
  163.8 11.6 %collective-permute-start.18 = (bf16[2,2,4,128,256]{4,3,2,1,0:T(8,128)(2,1)}, bf16[2,2,4,128,256]{4,3,2,1,0:T(8,128)(2,1)S(1)}, u32[]{:S(2)}, u32[]{:S(2)}) collective-permute-start(bf16[2,2,4,128,256]{4,3,2,1,0:T(8,128)(2,1)} %gram.12), channel_id=1, source_target_pairs={{0,8},{8,0},{1,9},{9,1},{2,10},{10,2},{3,11},{11,3},{4,12},{12,4},... | collective-permute-start | bytes 3145736 | tf_op jit(solution)/shard_map/ppermute | solution.py:272
  169.8 5.7 %collective-permute-start.14 = (bf16[1,2,4,128,256]{4,3,2,1,0:T(8,128)(2,1)}, bf16[1,2,4,128,256]{4,3,2,1,0:T(8,128)(2,1)}, u32[]{:S(2)}, u32[]{:S(2)}) collective-permute-start(bf16[1,2,4,128,256]{4,3,2,1,0:T(8,128)(2,1)} %get-tuple-element.54), channel_id=1, source_target_pairs={{0,8},{8,0},{1,9},{9,1},{2,10},{10,2},{3,11},{11,3},{4,12},{12,4},... | collective-permute-start | bytes 1572872 | tf_op jit(solution)/shard_map/ppermute | solution.py:272

commit v13 on v8

--- a/solution.py
+++ b/solution.py
@@ -23,16 +23,13 @@
     phase = (sample[:, None] * bins[None, :] % FFT_LEN) * (2.0 * np.pi / FFT_LEN)
     taper = 0.5 - 0.5 * np.cos(2.0 * np.pi * sample / FFT_LEN)
     table = np.stack([np.cos(phase), -np.sin(phase)], axis=2).reshape(FFT_LEN, 2 * BINS) * taper[:, None]
-    high = table.astype(jnp.bfloat16)
-    low = (table - high.astype(np.float64)).astype(jnp.bfloat16)
-    return high, low
-
-
-def whiten_kernel(records_ref, available_ref, high_ref, low_ref, first_ref, second_ref, rows_ref, turned_ref):
+    return table.astype(jnp.bfloat16)
+
+
+def whiten_kernel(records_ref, available_ref, table_ref, first_ref, second_ref, rows_ref, turned_ref):
     stations, segs, samples = records_ref.shape
     flat = records_ref[...].reshape(stations * segs, samples)
-    spectra = jnp.dot(flat, high_ref[...], preferred_element_type=jnp.float32)
-    spectra += jnp.dot(flat, low_ref[...], preferred_element_type=jnp.float32)
+    spectra = jnp.dot(flat, table_ref[...], preferred_element_type=jnp.float32)
     wide = spectra.shape[1]
     for part in range(2):
         rows_ref[part] = spectra[:, part * BINS : (part + 1) * BINS]
@@ -50,7 +47,6 @@
 
 def whiten(records, available):
     stations, segments, samples = records.shape
-    high, low = spectra_table()
     half = jax.ShapeDtypeStruct((2 * OWNERS, CHUNK, 2, segments, stations), jnp.bfloat16)
     half_spec = pl.BlockSpec((2 * OWNERS, CHUNK, 2, SEG_STEP, stations), lambda i: (0, 0, 0, i, 0))
     return pl.pallas_call(
@@ -59,7 +55,6 @@
         in_specs=[
             pl.BlockSpec((stations, SEG_STEP, samples), lambda i: (0, i, 0)),
             pl.BlockSpec((SEG_STEP, stations), lambda i: (i, 0)),
-            pl.BlockSpec((samples, 2 * BINS), lambda i: (0, 0)),
             pl.BlockSpec((samples, 2 * BINS), lambda i: (0, 0)),
         ],
         out_specs=[half_spec, half_spec],
@@ -70,7 +65,7 @@
         ],
         compiler_params=pltpu.CompilerParams(vmem_limit_bytes=60 * MIB),
         name="whiten",
-    )(records, available.T, jnp.asarray(high), jnp.asarray(low))
+    )(records, available.T, jnp.asarray(spectra_table()))
 
 
 def rows_kernel(panel_ref, mine_ref):

time: 175 us -> 174 us (level)
  no operation moved by 1% of the time
where the time goes in v13:
time: 174 us
  Pallas kernels  54 us (31%)
  waiting for transfers between devices  52.2 us (30%)
  starting transfers between devices  43.7 us (25%)
  blocking collectives  23.2 us (13%)
    pallas_call x7, Pallas kernels, gram(): pl.pallas_call(functools.partial(gram_kernel, 2.0 / depth, chunks, [[bloc...  39.3 us
    all_to_all x1, blocking collectives, owned(): lax.all_to_all(chunk, ('yl', 'z', 'core'), split_axis=0, concat_axis=0, t...  23.2 us
    ppermute x4, waiting for transfers between devices, shards(): over = lambda v: lax.ppermute(v, 'yh', [(0, 1), (1, 0)])  20.6 us
    ppermute x4, waiting for transfers between devices, shards(): bwd = lambda v: lax.ppermute(v, ('x', 'core'), mirrored(-1))  14.9 us
    all_to_all x1, waiting for transfers between devices, owned(): lax.all_to_all(chunk, ('yl', 'z', 'core'), split_axis=0, concat_axis=0, t...  14.7 us
    ppermute x4, starting transfers between devices, shards(): over = lambda v: lax.ppermute(v, 'yh', [(0, 1), (1, 0)])  13.4 us
    ppermute x6, starting transfers between devices, shards(): swap = lambda v: lax.ppermute(v, 'core', [(0, 1), (1, 0)])  13.4 us
    ppermute x6, starting transfers between devices, shards(): fwd = lambda v: lax.ppermute(v, ('x', 'core'), mirrored(1))  9.5 us
  transfers between devices with their start and end apart: 21, of which 6 were waited for; matrix products, arithmetic and copies ran while one was open for 0% of the time, Pallas kernels for 25%

profile of v13, /device:TPU:1, one launch (start us, length us, event | category | flops | bytes accessed | tf_op | source)
XLA Modules:
  0.0 173.8 jit_solution(17032856585643798976)
XLA Ops:
  0.0 6.9 %whiten.1 = (bf16[16,4,2,32,128]{4,3,2,1,0:T(8,128)(2,1)}, bf16[16,4,2,32,128]{4,3,2,1,0:T(8,128)(2,1)}) custom-call(bf16[128,32,512]{2,1,0:T(8,128)(2,1)} %records_ref.1, s32[32,128]{1,0:T(8,128)} %bitcast.28, bf16[512,256]{1,0:T(8,128)(2,1)} %constant.181.clone.table_ref), custom_call_target="tpu_custom_call" | custom-call | tf_op jit(solution)/shard_map/whiten/pallas_call | solution.py:52
  6.9 23.2 %all_to_all.10 = bf16[16,4,2,32,128]{4,3,2,1,0:T(8,128)(2,1)S(1)} all-to-all(bf16[16,4,2,32,128]{4,3,2,1,0:T(8,128)(2,1)} %get-tuple-element.31), channel_id=1, replica_groups=mesh['x'=4,'yh'=2,'core'=2,'yl'=2,'z'=4] {'yl','z','core'}, dimensions={0} | all-to-all | bytes 2097152 | tf_op jit(solution)/shard_map/all_to_all | solution.py:271
  30.1 2.5 %collective-permute-start.1 = (bf16[16,4,64,128]{3,2,1,0:T(8,128)(2,1)S(1)}, bf16[16,4,64,128]{3,2,1,0:T(8,128)(2,1)}, u32[]{:S(2)}, u32[]{:S(2)}) collective-permute-start(bf16[16,4,64,128]{3,2,1,0:T(8,128)(2,1)S(1)} %bitcast.23), channel_id=1, source_target_pairs={{0,32},{8,104},{32,64},{40,8},{64,96},{72,40},{96,0},{104,72},{1,3... | collective-permute-start | bytes 3145736 | tf_op jit(solution)/shard_map/ppermute | solution.py:264
  32.6 3.6 %all-to-all-start.1 = ((bf16[16,4,2,32,128]{4,3,2,1,0:T(8,128)(2,1)}), bf16[16,4,2,32,128]{4,3,2,1,0:T(8,128)(2,1)S(1)}, u32[]{:S(2)}, u32[]{:S(2)}) async-start(bf16[16,4,2,32,128]{4,3,2,1,0:T(8,128)(2,1)} %get-tuple-element.33), calls=%async_computation.1 | async-start | bytes 2097152 | tf_op jit(solution)/shard_map/all_to_all | solution.py:271
  36.2 1.2 collective-permute-start.4
  37.4 14.7 %all-to-all-done.1 = bf16[16,4,2,32,128]{4,3,2,1,0:T(8,128)(2,1)S(1)} async-done(((bf16[16,4,2,32,128]{4,3,2,1,0:T(8,128)(2,1)}), bf16[16,4,2,32,128]{4,3,2,1,0:T(8,128)(2,1)S(1)}, u32[]{:S(2)}, u32[]{:S(2)}) %all-to-all-start.1) | async-done | bytes 1048608 | tf_op jit(solution)/shard_map/all_to_all | solution.py:271
  52.1 0.0 collective-permute-done.1.refs_1_
  52.1 1.5 collective-permute-start.2
  53.6 2.6 %collective-permute-start = (bf16[16,4,64,128]{3,2,1,0:T(8,128)(2,1)S(1)}, bf16[16,4,64,128]{3,2,1,0:T(8,128)(2,1)S(1)}, u32[]{:S(2)}, u32[]{:S(2)}) collective-permute-start(bf16[16,4,64,128]{3,2,1,0:T(8,128)(2,1)S(1)} %bitcast.25), channel_id=1, source_target_pairs={{0,16},{16,0},{1,17},{17,1},{2,18},{18,2},{3,19},{19,3},{4,20},{20... | collective-permute-start | bytes 3145736 | tf_op jit(solution)/shard_map/ppermute | solution.py:266
  56.2 1.3 collective-permute-start.6
  57.5 0.1 add_add_fusion.1.where
  57.6 2.3 %rows.2.mine0_ref.mine1_ref = bf16[4,512,512]{2,1,0:T(8,128)(2,1)} custom-call(bf16[16,4,64,128]{3,2,1,0:T(8,128)(2,1)S(1)} %bitcast.26), custom_call_target="tpu_custom_call" | custom-call | tf_op jit(solution)/shard_map/rows/pallas_call | solution.py:85
  59.8 0.0 collective-permute-done.4.refs_2_
  59.8 6.3 %gram.7 = (bf16[2,16,128,2048]{3,2,1,0:T(8,128)(2,1)}, bf16[3,2,4,128,256]{4,3,2,1,0:T(8,128)(2,1)}) custom-call(s32[4]{0:T(128)S(1)} %add_add_fusion.1.where, bf16[4,512,512]{2,1,0:T(8,128)(2,1)} %rows.2.mine0_ref.mine1_ref, bf16[4,512,512]{2,1,0:T(8,128)(2,1)} %rows.2.mine0_ref.mine1_ref, bf16[16,4,64,128]{3,2,1,0:T(8,128)(2,1)S(1)} %bitcast.27, ...), custom_call_target="tpu_custom_call" | custom-call | flops 1610612736 | bytes 10485760 | tf_op jit(solution)/shard_map/gram/pallas_call | solution.py:190
  66.1 1.6 collective-permute-start.9
  67.7 0.0 collective-permute-done.2.refs_1_
  67.7 1.6 collective-permute-start.5
  69.4 9.5 %collective-permute-done.refs_3_ = bf16[16,4,64,128]{3,2,1,0:T(8,128)(2,1)S(1)} collective-permute-done((bf16[16,4,64,128]{3,2,1,0:T(8,128)(2,1)S(1)}, bf16[16,4,64,128]{3,2,1,0:T(8,128)(2,1)S(1)}, u32[]{:S(2)}, u32[]{:S(2)}) %collective-permute-start) | collective-permute-done | bytes 1048608 | tf_op jit(solution)/shard_map/ppermute | solution.py:266
  78.9 2.7 %collective-permute-start.3 = (bf16[16,4,64,128]{3,2,1,0:T(8,128)(2,1)S(1)}, bf16[16,4,64,128]{3,2,1,0:T(8,128)(2,1)}, u32[]{:S(2)}, u32[]{:S(2)}) collective-permute-start(bf16[16,4,64,128]{3,2,1,0:T(8,128)(2,1)S(1)} %bitcast.20), channel_id=1, source_target_pairs={{0,16},{16,0},{1,17},{17,1},{2,18},{18,2},{3,19},{19,3},{4,20},{20... | collective-permute-start | bytes 3145736 | tf_op jit(solution)/shard_map/ppermute | solution.py:266
  81.6 2.0 %collective-permute-done.6.refs_2_ = bf16[16,4,64,128]{3,2,1,0:T(8,128)(2,1)} collective-permute-done((bf16[16,4,64,128]{3,2,1,0:T(8,128)(2,1)S(1)}, bf16[16,4,64,128]{3,2,1,0:T(8,128)(2,1)}, u32[]{:S(2)}, u32[]{:S(2)}) %collective-permute-start.6) | collective-permute-done | bytes 1048608 | tf_op jit(solution)/shard_map/ppermute | solution.py:264
  83.6 3.5 %collective-permute-start.8 = (bf16[16,4,64,128]{3,2,1,0:T(8,128)(2,1)}, bf16[16,4,64,128]{3,2,1,0:T(8,128)(2,1)S(1)}, u32[]{:S(2)}, u32[]{:S(2)}) collective-permute-start(bf16[16,4,64,128]{3,2,1,0:T(8,128)(2,1)} %collective-permute-done.6.refs_2_), channel_id=1, source_target_pairs={{0,32},{8,104},{32,64},{40,8},{64,96},{72,40},{96,0},{104,72},{1,3... | collective-permute-start | bytes 3145736 | tf_op jit(solution)/shard_map/ppermute | solution.py:264
  87.1 0.1 stack.110.where
  87.2 2.2 %rows.3.mine1_ref = bf16[4,512,512]{2,1,0:T(8,128)(2,1)} custom-call(bf16[16,4,64,128]{3,2,1,0:T(8,128)(2,1)S(1)} %bitcast.21), custom_call_target="tpu_custom_call" | custom-call | tf_op jit(solution)/shard_map/rows/pallas_call | solution.py:85
  89.4 6.4 %gram.8 = (bf16[2,16,128,2048]{3,2,1,0:T(8,128)(2,1)}, bf16[4,2,4,128,256]{4,3,2,1,0:T(8,128)(2,1)}) custom-call(s32[5]{0:T(128)S(1)} %stack.110.where, bf16[4,512,512]{2,1,0:T(8,128)(2,1)} %rows.2.mine0_ref.mine1_ref, bf16[4,512,512]{2,1,0:T(8,128)(2,1)} %rows.3.mine1_ref, bf16[16,4,64,128]{3,2,1,0:T(8,128)(2,1)S(1)} %bitcast.22, ...), custom_call_target="tpu_custom_call", output_to_operand_aliasing={{0}: (7, {})} | custom-call | flops 2147483648 | bytes 12582912 | tf_op jit(solution)/shard_map/gram/pallas_call | solution.py:190
  95.9 4.0 %collective-permute-start.14 = (bf16[4,2,4,128,256]{4,3,2,1,0:T(8,128)(2,1)}, bf16[4,2,4,128,256]{4,3,2,1,0:T(8,128)(2,1)}, u32[]{:S(2)}, u32[]{:S(2)}) collective-permute-start(bf16[4,2,4,128,256]{4,3,2,1,0:T(8,128)(2,1)} %get-tuple-element.49), channel_id=1, source_target_pairs={{0,8},{8,0},{1,9},{9,1},{2,10},{10,2},{3,11},{11,3},{4,12},{12,4},... | collective-permute-start | bytes 6291464 | tf_op jit(solution)/shard_map/ppermute | solution.py:267
  99.9 0.0 collective-permute-done.5.refs_0_
  99.9 0.9 collective-permute-start.7
  100.8 2.5 %collective-permute-done.3.refs_2_ = bf16[16,4,64,128]{3,2,1,0:T(8,128)(2,1)} collective-permute-done((bf16[16,4,64,128]{3,2,1,0:T(8,128)(2,1)S(1)}, bf16[16,4,64,128]{3,2,1,0:T(8,128)(2,1)}, u32[]{:S(2)}, u32[]{:S(2)}) %collective-permute-start.3) | collective-permute-done | bytes 1048608 | tf_op jit(solution)/shard_map/ppermute | solution.py:266
  103.3 0.0 collective-permute-done.8.refs_1_
  103.3 0.0 collective-permute-start.12
  103.3 2.9 %collective-permute-start.13 = (bf16[16,4,64,128]{3,2,1,0:T(8,128)(2,1)}, bf16[16,4,64,128]{3,2,1,0:T(8,128)(2,1)}, u32[]{:S(2)}, u32[]{:S(2)}) collective-permute-start(bf16[16,4,64,128]{3,2,1,0:T(8,128)(2,1)} %collective-permute-done.1.refs_1_), channel_id=1, source_target_pairs={{0,16},{16,0},{1,17},{17,1},{2,18},{18,2},{3,19},{19,3},{4,20},{20... | collective-permute-start | bytes 3145736 | tf_op jit(solution)/shard_map/ppermute | solution.py:266
  106.2 0.1 stack.112.where
  106.3 0.0 collective-permute-done.9.refs_3_
  106.3 6.2 %gram.9 = (bf16[2,16,128,2048]{3,2,1,0:T(8,128)(2,1)}, bf16[3,2,4,128,256]{4,3,2,1,0:T(8,128)(2,1)}) custom-call(s32[7]{0:T(128)S(1)} %stack.112.where, bf16[4,512,512]{2,1,0:T(8,128)(2,1)} %rows.2.mine0_ref.mine1_ref, bf16[4,512,512]{2,1,0:T(8,128)(2,1)} %rows.3.mine1_ref, ...), custom_call_target="tpu_custom_call", output_to_operand_aliasing={{0}: (7, {})} | custom-call | flops 1610612736 | bytes 10485760 | tf_op jit(solution)/shard_map/gram/pallas_call | solution.py:190
  112.4 7.1 %collective-permute-start.11 = (bf16[3,2,4,128,256]{4,3,2,1,0:T(8,128)(2,1)}, bf16[3,2,4,128,256]{4,3,2,1,0:T(8,128)(2,1)}, u32[]{:S(2)}, u32[]{:S(2)}) collective-permute-start(bf16[3,2,4,128,256]{4,3,2,1,0:T(8,128)(2,1)} %get-tuple-element.46), channel_id=1, source_target_pairs={{0,8},{8,0},{1,9},{9,1},{2,10},{10,2},{3,11},{11,3},{4,12},{12,4},... | collective-permute-start | bytes 4718600 | tf_op jit(solution)/shard_map/ppermute | solution.py:267
  119.5 0.0 collective-permute-done.7.refs_0_
  119.5 0.0 collective-permute-start.10
  119.5 14.9 %collective-permute-done.12.refs_1_ = bf16[16,4,64,128]{3,2,1,0:T(8,128)(2,1)} collective-permute-done((bf16[16,4,64,128]{3,2,1,0:T(8,128)(2,1)}, bf16[16,4,64,128]{3,2,1,0:T(8,128)(2,1)}, u32[]{:S(2)}, u32[]{:S(2)}) %collective-permute-start.12) | collective-permute-done | bytes 1048608 | tf_op jit(solution)/shard_map/ppermute | solution.py:265
  134.4 0.0 collective-permute-done.13.refs_2_
  134.4 0.8 collective-permute-start.16
  135.2 5.2 %collective-permute-start.17 = (bf16[16,4,64,128]{3,2,1,0:T(8,128)(2,1)S(1)}, bf16[16,4,64,128]{3,2,1,0:T(8,128)(2,1)S(1)}, u32[]{:S(2)}, u32[]{:S(2)}) collective-permute-start(bf16[16,4,64,128]{3,2,1,0:T(8,128)(2,1)S(1)} %collective-permute-done.8.refs_1_), channel_id=1, source_target_pairs={{0,16},{16,0},{1,17},{17,1},{2,18},{18,2},{3,19},{19,3},{4,20},{20... | collective-permute-start | bytes 3145736 | tf_op jit(solution)/shard_map/ppermute | solution.py:266
  140.4 0.1 stack.114.where
  140.5 0.0 collective-permute-done.14.refs_3_
  140.5 7.1 %gram.10 = (bf16[2,16,128,2048]{3,2,1,0:T(8,128)(2,1)}, bf16[3,2,4,128,256]{4,3,2,1,0:T(8,128)(2,1)}) custom-call(s32[8]{0:T(128)S(1)} %stack.114.where, bf16[4,512,512]{2,1,0:T(8,128)(2,1)} %rows.2.mine0_ref.mine1_ref, bf16[4,512,512]{2,1,0:T(8,128)(2,1)} %rows.3.mine1_ref, ...), custom_call_target="tpu_custom_call", output_to_operand_aliasing={{0}: (7, {})} | custom-call | flops 1610612736 | bytes 10485760 | tf_op jit(solution)/shard_map/gram/pallas_call | solution.py:190
  147.6 0.1 collective-permute-start.19
  147.6 0.1 stack.104.where
  147.7 0.1 pad_add_fusion.where
  147.8 0.0 collective-permute-done.11.refs_1_
  147.8 0.0 collective-permute-done.10.refs_0_
  147.8 4.6 %gram.11 = (bf16[2,16,128,2048]{3,2,1,0:T(8,128)(2,1)}, bf16[1,2,4,128,256]{4,3,2,1,0:T(8,128)(2,1)}) custom-call(s32[5]{0:T(128)S(1)} %stack.104.where, bf16[4,512,512]{2,1,0:T(8,128)(2,1)} %rows.2.mine0_ref.mine1_ref, bf16[4,512,512]{2,1,0:T(8,128)(2,1)} %rows.3.mine1_ref, ...), custom_call_target="tpu_custom_call", output_to_operand_aliasing={{0}: (5, {})} | custom-call | flops 536870912 | bytes 6291456 | tf_op jit(solution)/shard_map/gram/pallas_call | solution.py:190
  152.4 0.0 collective-permute-done.16.refs_0_
  152.4 8.5 %collective-permute-done.17.refs_1_ = bf16[16,4,64,128]{3,2,1,0:T(8,128)(2,1)S(1)} collective-permute-done((bf16[16,4,64,128]{3,2,1,0:T(8,128)(2,1)S(1)}, bf16[16,4,64,128]{3,2,1,0:T(8,128)(2,1)S(1)}, u32[]{:S(2)}, u32[]{:S(2)}) %collective-permute-start.17) | collective-permute-done | bytes 1048608 | tf_op jit(solution)/shard_map/ppermute | solution.py:266
  161.0 4.1 %gram.12 = bf16[2,2,4,128,256]{4,3,2,1,0:T(8,128)(2,1)} custom-call(s32[3]{0:T(128)S(1)} %pad_add_fusion.where, bf16[4,512,512]{2,1,0:T(8,128)(2,1)} %rows.2.mine0_ref.mine1_ref, bf16[4,512,512]{2,1,0:T(8,128)(2,1)} %rows.3.mine1_ref, bf16[16,4,64,128]{3,2,1,0:T(8,128)(2,1)S(1)} %collective-permute-done.16.refs_0_, ...), custom_call_target="tpu_custom_call" | custom-call | flops 1073741824 | bytes 8388608 | tf_op jit(solution)/shard_map/gram/pallas_call | solution.py:190
  165.1 0.1 collective-permute-start.18
  165.2 0.5 collective-permute-start.15
  165.7 0.1 stack.118.where
  165.8 0.1 add_add_fusion.where
  165.8 0.0 collective-permute-done.19.refs_2_
  165.8 4.7 %gram.13.refs_2_ = bf16[2,16,128,2048]{3,2,1,0:T(8,128)(2,1)} custom-call(s32[6]{0:T(128)S(1)} %stack.118.where, bf16[4,512,512]{2,1,0:T(8,128)(2,1)} %rows.2.mine0_ref.mine1_ref, bf16[4,512,512]{2,1,0:T(8,128)(2,1)} %rows.3.mine1_ref, bf16[16,4,64,128]{3,2,1,0:T(8,128)(2,1)S(1)} %collective-permute-done.16.refs_0_, ...), custom_call_target="tpu_custom_call", output_to_operand_aliasing={{}: (6, {})} | custom-call | flops 1073741824 | bytes 8388608 | tf_op jit(solution)/shard_map/gram/pallas_call | solution.py:190
  170.5 0.0 collective-permute-done.15.refs_0_
  170.5 0.0 collective-permute-done.18.refs_1_
  170.5 3.3 %place.1 = bf16[2,16,128,2048]{3,2,1,0:T(8,128)(2,1)} custom-call(s32[4]{0:T(128)S(1)} %add_add_fusion.where, bf16[1,2,4,128,256]{4,3,2,1,0:T(8,128)(2,1)} %collective-permute-done.15.refs_0_, bf16[2,2,4,128,256]{4,3,2,1,0:T(8,128)(2,1)S(1)} %collective-permute-done.18.refs_1_, bf16[2,16,128,2048]{3,2,1,0:T(8,128)(2,1)} %gram.13.refs_2_), custom_call_target="tpu_custom_call", output_to_operand_aliasing={{}: (3, {})} | custom-call | tf_op jit(solution)/shard_map/place/pallas_call | solution.py:239
Async XLA Ops:
  30.1 22.0 %collective-permute-start.1 = (bf16[16,4,64,128]{3,2,1,0:T(8,128)(2,1)S(1)}, bf16[16,4,64,128]{3,2,1,0:T(8,128)(2,1)}, u32[]{:S(2)}, u32[]{:S(2)}) collective-permute-start(bf16[16,4,64,128]{3,2,1,0:T(8,128)(2,1)S(1)} %bitcast.23), channel_id=1, source_target_pairs={{0,32},{8,104},{32,64},{40,8},{64,96},{72,40},{96,0},{104,72},{1,3... | collective-permute-start | bytes 3145736 | tf_op jit(solution)/shard_map/ppermute | solution.py:264
  32.6 19.5 %all-to-all-start.1 = ((bf16[16,4,2,32,128]{4,3,2,1,0:T(8,128)(2,1)}), bf16[16,4,2,32,128]{4,3,2,1,0:T(8,128)(2,1)S(1)}, u32[]{:S(2)}, u32[]{:S(2)}) async-start(bf16[16,4,2,32,128]{4,3,2,1,0:T(8,128)(2,1)} %get-tuple-element.33), calls=%async_computation.1 | async-start | bytes 2097152 | tf_op jit(solution)/shard_map/all_to_all | solution.py:271
  36.2 23.6 %collective-permute-start.4 = (bf16[16,4,64,128]{3,2,1,0:T(8,128)(2,1)S(1)}, bf16[16,4,64,128]{3,2,1,0:T(8,128)(2,1)}, u32[]{:S(2)}, u32[]{:S(2)}) collective-permute-start(bf16[16,4,64,128]{3,2,1,0:T(8,128)(2,1)S(1)} %bitcast.24), channel_id=1, source_target_pairs={{0,96},{8,40},{32,0},{40,72},{64,32},{72,104},{96,64},{104,8},{1,9... | collective-permute-start | bytes 3145736 | tf_op jit(solution)/shard_map/ppermute | solution.py:265
  52.1 15.6 %collective-permute-start.2 = (bf16[16,4,64,128]{3,2,1,0:T(8,128)(2,1)}, bf16[16,4,64,128]{3,2,1,0:T(8,128)(2,1)}, u32[]{:S(2)}, u32[]{:S(2)}) collective-permute-start(bf16[16,4,64,128]{3,2,1,0:T(8,128)(2,1)} %collective-permute-done.1.refs_1_), channel_id=1, source_target_pairs={{0,32},{8,104},{32,64},{40,8},{64,96},{72,40},{96,0},{104,72},{1,3... | collective-permute-start | bytes 3145736 | tf_op jit(solution)/shard_map/ppermute | solution.py:264
  53.6 25.3 %collective-permute-start = (bf16[16,4,64,128]{3,2,1,0:T(8,128)(2,1)S(1)}, bf16[16,4,64,128]{3,2,1,0:T(8,128)(2,1)S(1)}, u32[]{:S(2)}, u32[]{:S(2)}) collective-permute-start(bf16[16,4,64,128]{3,2,1,0:T(8,128)(2,1)S(1)} %bitcast.25), channel_id=1, source_target_pairs={{0,16},{16,0},{1,17},{17,1},{2,18},{18,2},{3,19},{19,3},{4,20},{20... | collective-permute-start | bytes 3145736 | tf_op jit(solution)/shard_map/ppermute | solution.py:266
  56.2 27.4 %collective-permute-start.6 = (bf16[16,4,64,128]{3,2,1,0:T(8,128)(2,1)S(1)}, bf16[16,4,64,128]{3,2,1,0:T(8,128)(2,1)}, u32[]{:S(2)}, u32[]{:S(2)}) collective-permute-start(bf16[16,4,64,128]{3,2,1,0:T(8,128)(2,1)S(1)} %bitcast.18), channel_id=1, source_target_pairs={{0,32},{8,104},{32,64},{40,8},{64,96},{72,40},{96,0},{104,72},{1,3... | collective-permute-start | bytes 3145736 | tf_op jit(solution)/shard_map/ppermute | solution.py:264
  66.1 40.2 %collective-permute-start.9 = (bf16[3,2,4,128,256]{4,3,2,1,0:T(8,128)(2,1)}, bf16[3,2,4,128,256]{4,3,2,1,0:T(8,128)(2,1)}, u32[]{:S(2)}, u32[]{:S(2)}) collective-permute-start(bf16[3,2,4,128,256]{4,3,2,1,0:T(8,128)(2,1)} %get-tuple-element.43), channel_id=1, source_target_pairs={{0,8},{8,0},{1,9},{9,1},{2,10},{10,2},{3,11},{11,3},{4,12},{12,4},... | collective-permute-start | bytes 4718600 | tf_op jit(solution)/shard_map/ppermute | solution.py:267
  67.7 32.1 %collective-permute-start.5 = (bf16[16,4,64,128]{3,2,1,0:T(8,128)(2,1)S(1)}, bf16[16,4,64,128]{3,2,1,0:T(8,128)(2,1)}, u32[]{:S(2)}, u32[]{:S(2)}) collective-permute-start(bf16[16,4,64,128]{3,2,1,0:T(8,128)(2,1)S(1)} %bitcast.19), channel_id=1, source_target_pairs={{0,96},{8,40},{32,0},{40,72},{64,32},{72,104},{96,64},{104,8},{1,9... | collective-permute-start | bytes 3145736 | tf_op jit(solution)/shard_map/ppermute | solution.py:265
  78.9 24.5 %collective-permute-start.3 = (bf16[16,4,64,128]{3,2,1,0:T(8,128)(2,1)S(1)}, bf16[16,4,64,128]{3,2,1,0:T(8,128)(2,1)}, u32[]{:S(2)}, u32[]{:S(2)}) collective-permute-start(bf16[16,4,64,128]{3,2,1,0:T(8,128)(2,1)S(1)} %bitcast.20), channel_id=1, source_target_pairs={{0,16},{16,0},{1,17},{17,1},{2,18},{18,2},{3,19},{19,3},{4,20},{20... | collective-permute-start | bytes 3145736 | tf_op jit(solution)/shard_map/ppermute | solution.py:266
  83.6 19.8 %collective-permute-start.8 = (bf16[16,4,64,128]{3,2,1,0:T(8,128)(2,1)}, bf16[16,4,64,128]{3,2,1,0:T(8,128)(2,1)S(1)}, u32[]{:S(2)}, u32[]{:S(2)}) collective-permute-start(bf16[16,4,64,128]{3,2,1,0:T(8,128)(2,1)} %collective-permute-done.6.refs_2_), channel_id=1, source_target_pairs={{0,32},{8,104},{32,64},{40,8},{64,96},{72,40},{96,0},{104,72},{1,3... | collective-permute-start | bytes 3145736 | tf_op jit(solution)/shard_map/ppermute | solution.py:264
  95.9 44.6 %collective-permute-start.14 = (bf16[4,2,4,128,256]{4,3,2,1,0:T(8,128)(2,1)}, bf16[4,2,4,128,256]{4,3,2,1,0:T(8,128)(2,1)}, u32[]{:S(2)}, u32[]{:S(2)}) collective-permute-start(bf16[4,2,4,128,256]{4,3,2,1,0:T(8,128)(2,1)} %get-tuple-element.49), channel_id=1, source_target_pairs={{0,8},{8,0},{1,9},{9,1},{2,10},{10,2},{3,11},{11,3},{4,12},{12,4},... | collective-permute-start | bytes 6291464 | tf_op jit(solution)/shard_map/ppermute | solution.py:267
  99.9 19.7 %collective-permute-start.7 = (bf16[16,4,64,128]{3,2,1,0:T(8,128)(2,1)S(1)}, bf16[16,4,64,128]{3,2,1,0:T(8,128)(2,1)}, u32[]{:S(2)}, u32[]{:S(2)}) collective-permute-start(bf16[16,4,64,128]{3,2,1,0:T(8,128)(2,1)S(1)} %collective-permute-done.refs_3_), channel_id=1, source_target_pairs={{0,96},{8,40},{32,0},{40,72},{64,32},{72,104},{96,64},{104,8},{1,9... | collective-permute-start | bytes 3145736 | tf_op jit(solution)/shard_map/ppermute | solution.py:265
  103.3 31.1 %collective-permute-start.12 = (bf16[16,4,64,128]{3,2,1,0:T(8,128)(2,1)}, bf16[16,4,64,128]{3,2,1,0:T(8,128)(2,1)}, u32[]{:S(2)}, u32[]{:S(2)}) collective-permute-start(bf16[16,4,64,128]{3,2,1,0:T(8,128)(2,1)} %collective-permute-done.3.refs_2_), channel_id=1, source_target_pairs={{0,96},{8,40},{32,0},{40,72},{64,32},{72,104},{96,64},{104,8},{1,9... | collective-permute-start | bytes 3145736 | tf_op jit(solution)/shard_map/ppermute | solution.py:265
  103.3 31.1 %collective-permute-start.13 = (bf16[16,4,64,128]{3,2,1,0:T(8,128)(2,1)}, bf16[16,4,64,128]{3,2,1,0:T(8,128)(2,1)}, u32[]{:S(2)}, u32[]{:S(2)}) collective-permute-start(bf16[16,4,64,128]{3,2,1,0:T(8,128)(2,1)} %collective-permute-done.1.refs_1_), channel_id=1, source_target_pairs={{0,16},{16,0},{1,17},{17,1},{2,18},{18,2},{3,19},{19,3},{4,20},{20... | collective-permute-start | bytes 3145736 | tf_op jit(solution)/shard_map/ppermute | solution.py:266
  112.4 35.4 %collective-permute-start.11 = (bf16[3,2,4,128,256]{4,3,2,1,0:T(8,128)(2,1)}, bf16[3,2,4,128,256]{4,3,2,1,0:T(8,128)(2,1)}, u32[]{:S(2)}, u32[]{:S(2)}) collective-permute-start(bf16[3,2,4,128,256]{4,3,2,1,0:T(8,128)(2,1)} %get-tuple-element.46), channel_id=1, source_target_pairs={{0,8},{8,0},{1,9},{9,1},{2,10},{10,2},{3,11},{11,3},{4,12},{12,4},... | collective-permute-start | bytes 4718600 | tf_op jit(solution)/shard_map/ppermute | solution.py:267
  119.5 28.3 %collective-permute-start.10 = (bf16[16,4,64,128]{3,2,1,0:T(8,128)(2,1)}, bf16[16,4,64,128]{3,2,1,0:T(8,128)(2,1)}, u32[]{:S(2)}, u32[]{:S(2)}) collective-permute-start(bf16[16,4,64,128]{3,2,1,0:T(8,128)(2,1)} %collective-permute-done.3.refs_2_), channel_id=1, source_target_pairs={{0,32},{8,104},{32,64},{40,8},{64,96},{72,40},{96,0},{104,72},{1,3... | collective-permute-start | bytes 3145736 | tf_op jit(solution)/shard_map/ppermute | solution.py:264
  134.4 18.0 %collective-permute-start.16 = (bf16[16,4,64,128]{3,2,1,0:T(8,128)(2,1)}, bf16[16,4,64,128]{3,2,1,0:T(8,128)(2,1)S(1)}, u32[]{:S(2)}, u32[]{:S(2)}) collective-permute-start(bf16[16,4,64,128]{3,2,1,0:T(8,128)(2,1)} %collective-permute-done.13.refs_2_), channel_id=1, source_target_pairs={{0,32},{8,104},{32,64},{40,8},{64,96},{72,40},{96,0},{104,72},{1,3... | collective-permute-start | bytes 3145736 | tf_op jit(solution)/shard_map/ppermute | solution.py:264
  135.2 25.8 %collective-permute-start.17 = (bf16[16,4,64,128]{3,2,1,0:T(8,128)(2,1)S(1)}, bf16[16,4,64,128]{3,2,1,0:T(8,128)(2,1)S(1)}, u32[]{:S(2)}, u32[]{:S(2)}) collective-permute-start(bf16[16,4,64,128]{3,2,1,0:T(8,128)(2,1)S(1)} %collective-permute-done.8.refs_1_), channel_id=1, source_target_pairs={{0,16},{16,0},{1,17},{17,1},{2,18},{18,2},{3,19},{19,3},{4,20},{20... | collective-permute-start | bytes 3145736 | tf_op jit(solution)/shard_map/ppermute | solution.py:266
  147.6 18.3 %collective-permute-start.19 = (bf16[3,2,4,128,256]{4,3,2,1,0:T(8,128)(2,1)}, bf16[3,2,4,128,256]{4,3,2,1,0:T(8,128)(2,1)}, u32[]{:S(2)}, u32[]{:S(2)}) collective-permute-start(bf16[3,2,4,128,256]{4,3,2,1,0:T(8,128)(2,1)} %get-tuple-element.56), channel_id=1, source_target_pairs={{0,8},{8,0},{1,9},{9,1},{2,10},{10,2},{3,11},{11,3},{4,12},{12,4},... | collective-permute-start | bytes 4718600 | tf_op jit(solution)/shard_map/ppermute | solution.py:267
  165.1 5.4 %collective-permute-start.18 = (bf16[2,2,4,128,256]{4,3,2,1,0:T(8,128)(2,1)}, bf16[2,2,4,128,256]{4,3,2,1,0:T(8,128)(2,1)S(1)}, u32[]{:S(2)}, u32[]{:S(2)}) collective-permute-start(bf16[2,2,4,128,256]{4,3,2,1,0:T(8,128)(2,1)} %gram.12), channel_id=1, source_target_pairs={{0,8},{8,0},{1,9},{9,1},{2,10},{10,2},{3,11},{11,3},{4,12},{12,4},... | collective-permute-start | bytes 3145736 | tf_op jit(solution)/shard_map/ppermute | solution.py:267
  165.2 5.3 %collective-permute-start.15 = (bf16[1,2,4,128,256]{4,3,2,1,0:T(8,128)(2,1)}, bf16[1,2,4,128,256]{4,3,2,1,0:T(8,128)(2,1)}, u32[]{:S(2)}, u32[]{:S(2)}) collective-permute-start(bf16[1,2,4,128,256]{4,3,2,1,0:T(8,128)(2,1)} %get-tuple-element.51), channel_id=1, source_target_pairs={{0,8},{8,0},{1,9},{9,1},{2,10},{10,2},{3,11},{11,3},{4,12},{12,4},... | collective-permute-start | bytes 1572872 | tf_op jit(solution)/shard_map/ppermute | solution.py:267

commit v14 on v12

--- a/solution.py
+++ b/solution.py
@@ -298,24 +298,22 @@
     blocks2 = [entry(1, 0, 0, after(pb, bb)), entry(0, 2, 0, fa), entry(1, 1, 0, nb), entry(0, 0, 1, oa)]
     out, sent = gram(core, mine, blocks2, shape, out)
 
-    boa, nob, noa = bwd(after(oa, bb)), fwd(after(ob, fb)), over(after(na, ob))
+    boa, bob, noa = bwd(after(oa, bb)), bwd(after(ob, fb)), over(after(na, ob, bb))
     sent2 = blocks2, swap(sent)
     blocks3 = [entry(1, -1, 0, bb), entry(1, 2, 0, fb), entry(1, 0, 1, ob)]
     out, sent = gram(core, mine, blocks3, shape, out, sent1)
 
-    half = CHUNK // 2
-    bob, foa = bwd(after(ob, boa, out)), fwd(after(noa, nob))
-    fob = over(after(fb[:, :half], noa)), fwd(nob[:, half:])
+    nob, foa, fob = fwd(after(ob, boa, out)), fwd(after(noa, bob)), over(after(fb, noa))
     sent3 = blocks3, swap(sent)
-    blocks4 = [entry(0, -1, 1, boa), entry(1, 1, 1, nob), entry(0, 1, 1, noa)]
+    blocks4 = [entry(0, -1, 1, boa), entry(1, -1, 1, bob), entry(0, 1, 1, noa)]
     out, sent = gram(core, mine, blocks4, shape, out)
 
     sent4 = blocks4, swap(sent)
-    blocks5 = [entry(1, -1, 1, bob)]
+    blocks5 = [entry(1, 1, 1, nob)]
     out, sent = gram(core, mine, blocks5, shape, out, sent2)
 
     sent5 = blocks5, swap(sent)
-    blocks6 = [entry(0, 2, 1, after(foa, out)), entry(1, 2, 1, jnp.concatenate([after(fob[0], out), after(fob[1], out)], axis=1))]
+    blocks6 = [entry(0, 2, 1, after(foa, out)), entry(1, 2, 1, fob)]
     (sent,) = gram(core, mine, blocks6, shape, None, own=False)
     (out,) = gram(core, mine, blocks6, shape, out, sent3, sent4, other=False)
     return place(core, out, sent5, (blocks6, swap(sent)))

time: 179 us -> 174 us (0.972)
  waiting for transfers between devices: 45.7 us -> 41.9 us
  starting transfers between devices: 52.7 us -> 49.6 us
    ppermute x4, waiting for transfers between devices: 19.7 us -> 7.1 us  [shards(): over = lambda v: lax.ppermute(v, 'yh', [(0, 1), (1, 0)])]
    ppermute x4, waiting for transfers between devices: 8.45 us -> 17.3 us  [shards(): bwd = lambda v: lax.ppermute(v, ('x', 'core'), mirrored(-1))]
    unnamed x5 -> x6, local copies, waits for them, and re-layouts: 0.05 us -> 3.41 us
    ppermute x7 -> x6, starting transfers between devices: 12.2 us -> 9.54 us  [shards(): fwd = lambda v: lax.ppermute(v, ('x', 'core'), mirrored(1))]
  transfers between devices with their start and end apart: 22 -> 21, of which waited for: 7 -> 7; matrix products, arithmetic and copies ran while one was open for 1% -> 0% of each run, Pallas kernels for 24% -> 25%
where the time goes in v14:
time: 174 us; the launch traced here: 173 us
  Pallas kernels  54.3 us (31%)
  starting transfers between devices  49.6 us (29%)
  waiting for transfers between devices  41.9 us (24%)
  blocking collectives  23.3 us (13%)
  local copies, waits for them, and re-layouts  3.75 us (2%)
    pallas_call x7, Pallas kernels, gram(): pl.pallas_call(functools.partial(gram_kernel, 2.0 / depth, chunks, [[bloc...  38.7 us
    all_to_all x1, blocking collectives, owned(): lax.all_to_all(chunk, ('yl', 'z', 'core'), split_axis=0, concat_axis=0, t...  23.3 us
    ppermute x6, starting transfers between devices, shards(): swap = lambda v: lax.ppermute(v, 'core', [(0, 1), (1, 0)])  22.5 us
    ppermute x4, waiting for transfers between devices, shards(): bwd = lambda v: lax.ppermute(v, ('x', 'core'), mirrored(-1))  17.3 us
    all_to_all x1, waiting for transfers between devices, owned(): lax.all_to_all(chunk, ('yl', 'z', 'core'), split_axis=0, concat_axis=0, t...  14.7 us
    ppermute x4, starting transfers between devices, shards(): over = lambda v: lax.ppermute(v, 'yh', [(0, 1), (1, 0)])  10.6 us
    ppermute x6, starting transfers between devices, shards(): fwd = lambda v: lax.ppermute(v, ('x', 'core'), mirrored(1))  9.54 us
    pallas_call x1, Pallas kernels, whiten(): pl.pallas_call(whiten_kernel, grid=(segments // SEG_STEP,), in_specs=[pl....  7.77 us
  transfers between devices with their start and end apart: 21, of which 7 were waited for; matrix products, arithmetic and copies ran while one was open for 0% of the time, Pallas kernels for 25%

profile of v14, /device:TPU:1, one launch (start us, length us, event | category | flops | bytes accessed | tf_op | source)
XLA Modules:
  0.0 173.4 jit_solution(12807778313652528296)
XLA Ops:
  0.0 7.8 %whiten.1 = (bf16[16,4,2,32,128]{4,3,2,1,0:T(8,128)(2,1)}, bf16[16,4,2,32,128]{4,3,2,1,0:T(8,128)(2,1)}) custom-call(bf16[128,32,512]{2,1,0:T(8,128)(2,1)} %records_ref.1, s32[32,128]{1,0:T(8,128)} %bitcast.28, bf16[512,256]{1,0:T(8,128)(2,1)} %constant.183.clone.high_ref, bf16[512,256]{1,0:T(8,128)(2,1)} %constant.184.clone.low_ref), custom_call_target="tpu_custom_call" | custom-call | tf_op jit(solution)/shard_map/whiten/pallas_call | solution.py:56
  7.8 23.3 %all_to_all.10 = bf16[16,4,2,32,128]{4,3,2,1,0:T(8,128)(2,1)S(1)} all-to-all(bf16[16,4,2,32,128]{4,3,2,1,0:T(8,128)(2,1)} %get-tuple-element.32), channel_id=1, replica_groups=mesh['x'=4,'yh'=2,'core'=2,'yl'=2,'z'=4] {'yl','z','core'}, dimensions={0} | all-to-all | bytes 2097152 | tf_op jit(solution)/shard_map/all_to_all | solution.py:276
  31.0 2.5 %collective-permute-start.2 = (bf16[16,4,64,128]{3,2,1,0:T(8,128)(2,1)S(1)}, bf16[16,4,64,128]{3,2,1,0:T(8,128)(2,1)}, u32[]{:S(2)}, u32[]{:S(2)}) collective-permute-start(bf16[16,4,64,128]{3,2,1,0:T(8,128)(2,1)S(1)} %bitcast.23), channel_id=1, source_target_pairs={{0,32},{8,104},{32,64},{40,8},{64,96},{72,40},{96,0},{104,72},{1,3... | collective-permute-start | bytes 3145736 | tf_op jit(solution)/shard_map/ppermute | solution.py:269
  33.5 3.6 %all-to-all-start.1 = ((bf16[16,4,2,32,128]{4,3,2,1,0:T(8,128)(2,1)}), bf16[16,4,2,32,128]{4,3,2,1,0:T(8,128)(2,1)S(1)}, u32[]{:S(2)}, u32[]{:S(2)}) async-start(bf16[16,4,2,32,128]{4,3,2,1,0:T(8,128)(2,1)} %get-tuple-element.34), calls=%async_computation.1 | async-start | bytes 2097152 | tf_op jit(solution)/shard_map/all_to_all | solution.py:276
  37.1 1.2 collective-permute-start.4
  38.3 14.7 %all-to-all-done.1 = bf16[16,4,2,32,128]{4,3,2,1,0:T(8,128)(2,1)S(1)} async-done(((bf16[16,4,2,32,128]{4,3,2,1,0:T(8,128)(2,1)}), bf16[16,4,2,32,128]{4,3,2,1,0:T(8,128)(2,1)S(1)}, u32[]{:S(2)}, u32[]{:S(2)}) %all-to-all-start.1) | async-done | bytes 1048608 | tf_op jit(solution)/shard_map/all_to_all | solution.py:276
  53.0 0.0 collective-permute-done.2.refs_1_
  53.0 1.5 collective-permute-start.3
  54.5 2.6 %collective-permute-start = (bf16[16,4,64,128]{3,2,1,0:T(8,128)(2,1)S(1)}, bf16[16,4,64,128]{3,2,1,0:T(8,128)(2,1)S(1)}, u32[]{:S(2)}, u32[]{:S(2)}) collective-permute-start(bf16[16,4,64,128]{3,2,1,0:T(8,128)(2,1)S(1)} %bitcast.25), channel_id=1, source_target_pairs={{0,16},{16,0},{1,17},{17,1},{2,18},{18,2},{3,19},{19,3},{4,20},{20... | collective-permute-start | bytes 3145736 | tf_op jit(solution)/shard_map/ppermute | solution.py:271
  57.1 1.3 collective-permute-start.7
  58.4 0.1 add_add_fusion.1.where
  58.5 2.3 %rows.2.mine0_ref.mine1_ref = bf16[4,512,512]{2,1,0:T(8,128)(2,1)} custom-call(bf16[16,4,64,128]{3,2,1,0:T(8,128)(2,1)S(1)} %bitcast.26), custom_call_target="tpu_custom_call" | custom-call | tf_op jit(solution)/shard_map/rows/pallas_call | solution.py:90
  60.7 0.0 collective-permute-done.4.refs_2_
  60.8 6.3 %gram.7 = (bf16[2,16,128,2048]{3,2,1,0:T(8,128)(2,1)}, bf16[3,2,4,128,256]{4,3,2,1,0:T(8,128)(2,1)}) custom-call(s32[4]{0:T(128)S(1)} %add_add_fusion.1.where, bf16[4,512,512]{2,1,0:T(8,128)(2,1)} %rows.2.mine0_ref.mine1_ref, bf16[4,512,512]{2,1,0:T(8,128)(2,1)} %rows.2.mine0_ref.mine1_ref, bf16[16,4,64,128]{3,2,1,0:T(8,128)(2,1)S(1)} %bitcast.27, ...), custom_call_target="tpu_custom_call" | custom-call | flops 1610612736 | bytes 10485760 | tf_op jit(solution)/shard_map/gram/pallas_call | solution.py:195
  67.0 0.8 collective-permute-done.3.refs_1_
  67.8 0.9 collective-permute-start.5
  68.8 3.9 %collective-permute-start.9 = (bf16[3,2,4,128,256]{4,3,2,1,0:T(8,128)(2,1)}, bf16[3,2,4,128,256]{4,3,2,1,0:T(8,128)(2,1)}, u32[]{:S(2)}, u32[]{:S(2)}) collective-permute-start(bf16[3,2,4,128,256]{4,3,2,1,0:T(8,128)(2,1)} %get-tuple-element.43), channel_id=1, source_target_pairs={{0,8},{8,0},{1,9},{9,1},{2,10},{10,2},{3,11},{11,3},{4,12},{12,4},... | collective-permute-start | bytes 4718600 | tf_op jit(solution)/shard_map/ppermute | solution.py:272
  72.7 7.1 %collective-permute-done.refs_3_ = bf16[16,4,64,128]{3,2,1,0:T(8,128)(2,1)S(1)} collective-permute-done((bf16[16,4,64,128]{3,2,1,0:T(8,128)(2,1)S(1)}, bf16[16,4,64,128]{3,2,1,0:T(8,128)(2,1)S(1)}, u32[]{:S(2)}, u32[]{:S(2)}) %collective-permute-start) | collective-permute-done | bytes 1048608 | tf_op jit(solution)/shard_map/ppermute | solution.py:271
  79.8 2.7 %collective-permute-start.1 = (bf16[16,4,64,128]{3,2,1,0:T(8,128)(2,1)S(1)}, bf16[16,4,64,128]{3,2,1,0:T(8,128)(2,1)}, u32[]{:S(2)}, u32[]{:S(2)}) collective-permute-start(bf16[16,4,64,128]{3,2,1,0:T(8,128)(2,1)S(1)} %bitcast.20), channel_id=1, source_target_pairs={{0,16},{16,0},{1,17},{17,1},{2,18},{18,2},{3,19},{19,3},{4,20},{20... | collective-permute-start | bytes 3145736 | tf_op jit(solution)/shard_map/ppermute | solution.py:271
  82.5 2.0 %collective-permute-done.7.refs_2_ = bf16[16,4,64,128]{3,2,1,0:T(8,128)(2,1)} collective-permute-done((bf16[16,4,64,128]{3,2,1,0:T(8,128)(2,1)S(1)}, bf16[16,4,64,128]{3,2,1,0:T(8,128)(2,1)}, u32[]{:S(2)}, u32[]{:S(2)}) %collective-permute-start.7) | collective-permute-done | bytes 1048608 | tf_op jit(solution)/shard_map/ppermute | solution.py:269
  84.5 3.5 %collective-permute-start.8 = (bf16[16,4,64,128]{3,2,1,0:T(8,128)(2,1)}, bf16[16,4,64,128]{3,2,1,0:T(8,128)(2,1)S(1)}, u32[]{:S(2)}, u32[]{:S(2)}) collective-permute-start(bf16[16,4,64,128]{3,2,1,0:T(8,128)(2,1)} %collective-permute-done.7.refs_2_), channel_id=1, source_target_pairs={{0,32},{8,104},{32,64},{40,8},{64,96},{72,40},{96,0},{104,72},{1,3... | collective-permute-start | bytes 3145736 | tf_op jit(solution)/shard_map/ppermute | solution.py:269
  88.0 5.4 %collective-permute-done.5.refs_0_ = bf16[16,4,64,128]{3,2,1,0:T(8,128)(2,1)S(1)} collective-permute-done((bf16[16,4,64,128]{3,2,1,0:T(8,128)(2,1)S(1)}, bf16[16,4,64,128]{3,2,1,0:T(8,128)(2,1)S(1)}, u32[]{:S(2)}, u32[]{:S(2)}) %collective-permute-start.5) | collective-permute-done | bytes 1048608 | tf_op jit(solution)/shard_map/ppermute | solution.py:270
  93.4 1.0 copy-done
  94.4 0.0 collective-permute-start.6
  94.4 0.1 stack.112.where
  94.4 2.3 %rows.3.mine1_ref = bf16[4,512,512]{2,1,0:T(8,128)(2,1)} custom-call(bf16[16,4,64,128]{3,2,1,0:T(8,128)(2,1)S(1)} %bitcast.21), custom_call_target="tpu_custom_call" | custom-call | tf_op jit(solution)/shard_map/rows/pallas_call | solution.py:90
  96.7 6.5 %gram.8 = (bf16[2,16,128,2048]{3,2,1,0:T(8,128)(2,1)}, bf16[4,2,4,128,256]{4,3,2,1,0:T(8,128)(2,1)}) custom-call(s32[5]{0:T(128)S(1)} %stack.112.where, bf16[4,512,512]{2,1,0:T(8,128)(2,1)} %rows.2.mine0_ref.mine1_ref, bf16[4,512,512]{2,1,0:T(8,128)(2,1)} %rows.3.mine1_ref, bf16[16,4,64,128]{3,2,1,0:T(8,128)(2,1)S(1)} %bitcast.22, ...), custom_call_target="tpu_custom_call", output_to_operand_aliasing={{0}: (7, {})} | custom-call | flops 2147483648 | bytes 12582912 | tf_op jit(solution)/shard_map/gram/pallas_call | solution.py:195
  103.2 2.4 %collective-permute-start.11 = (bf16[4,2,4,128,256]{4,3,2,1,0:T(8,128)(2,1)}, bf16[4,2,4,128,256]{4,3,2,1,0:T(8,128)(2,1)}, u32[]{:S(2)}, u32[]{:S(2)}) collective-permute-start(bf16[4,2,4,128,256]{4,3,2,1,0:T(8,128)(2,1)} %get-tuple-element.48), channel_id=1, source_target_pairs={{0,8},{8,0},{1,9},{9,1},{2,10},{10,2},{3,11},{11,3},{4,12},{12,4},... | collective-permute-start | bytes 6291464 | tf_op jit(solution)/shard_map/ppermute | solution.py:272
  105.6 0.0 collective-permute-done.1.refs_2_
  105.6 0.0 collective-permute-done.8.refs_1_
  105.6 1.2 collective-permute-start.12
  106.8 2.6 %collective-permute-start.13 = (bf16[16,4,64,128]{3,2,1,0:T(8,128)(2,1)}, bf16[16,4,64,128]{3,2,1,0:T(8,128)(2,1)}, u32[]{:S(2)}, u32[]{:S(2)}) collective-permute-start(bf16[16,4,64,128]{3,2,1,0:T(8,128)(2,1)} %collective-permute-done.2.refs_1_), channel_id=1, source_target_pairs={{0,16},{16,0},{1,17},{17,1},{2,18},{18,2},{3,19},{19,3},{4,20},{20... | collective-permute-start | bytes 3145736 | tf_op jit(solution)/shard_map/ppermute | solution.py:271
  109.4 0.1 stack.111.where
  109.5 0.0 collective-permute-done.9.refs_3_
  109.5 1.2 copy-done.1
  110.7 5.8 %gram.9 = (bf16[2,16,128,2048]{3,2,1,0:T(8,128)(2,1)}, bf16[3,2,4,128,256]{4,3,2,1,0:T(8,128)(2,1)S(1)}) custom-call(s32[7]{0:T(128)S(1)} %stack.111.where, bf16[4,512,512]{2,1,0:T(8,128)(2,1)} %rows.2.mine0_ref.mine1_ref, bf16[4,512,512]{2,1,0:T(8,128)(2,1)} %rows.3.mine1_ref, ...), custom_call_target="tpu_custom_call", output_to_operand_aliasing={{0}: (7, {})} | custom-call | flops 1610612736 | bytes 10485760 | tf_op jit(solution)/shard_map/gram/pallas_call | solution.py:195
  116.6 1.2 copy-done.2
  117.7 1.2 collective-permute-done.6.refs_0_
  119.0 0.8 collective-permute-start.10
  119.8 10.7 %collective-permute-done.12.refs_1_ = bf16[16,4,64,128]{3,2,1,0:T(8,128)(2,1)} collective-permute-done((bf16[16,4,64,128]{3,2,1,0:T(8,128)(2,1)}, bf16[16,4,64,128]{3,2,1,0:T(8,128)(2,1)}, u32[]{:S(2)}, u32[]{:S(2)}) %collective-permute-start.12) | collective-permute-done | bytes 1048608 | tf_op jit(solution)/shard_map/ppermute | solution.py:270
  130.5 0.0 collective-permute-done.13.refs_2_
  130.5 0.0 collective-permute-start.15
  130.5 2.6 %collective-permute-start.16 = (bf16[16,4,64,128]{3,2,1,0:T(8,128)(2,1)S(1)}, bf16[16,4,64,128]{3,2,1,0:T(8,128)(2,1)S(1)}, u32[]{:S(2)}, u32[]{:S(2)}) collective-permute-start(bf16[16,4,64,128]{3,2,1,0:T(8,128)(2,1)S(1)} %collective-permute-done.8.refs_1_), channel_id=1, source_target_pairs={{0,16},{16,0},{1,17},{17,1},{2,18},{18,2},{3,19},{19,3},{4,20},{20... | collective-permute-start | bytes 3145736 | tf_op jit(solution)/shard_map/ppermute | solution.py:271
  133.1 0.1 add_add_fusion.2.where
  133.2 14.4 %collective-permute-start.18 = (bf16[3,2,4,128,256]{4,3,2,1,0:T(8,128)(2,1)}, bf16[3,2,4,128,256]{4,3,2,1,0:T(8,128)(2,1)}, u32[]{:S(2)}, u32[]{:S(2)}) collective-permute-start(bf16[3,2,4,128,256]{4,3,2,1,0:T(8,128)(2,1)} %copy-done.2), channel_id=1, source_target_pairs={{0,8},{8,0},{1,9},{9,1},{2,10},{10,2},{3,11},{11,3},{4,12},{12,4},... | collective-permute-start | bytes 4718600 | tf_op jit(solution)/shard_map/ppermute | solution.py:272
  147.6 5.9 %gram.10 = (bf16[2,16,128,2048]{3,2,1,0:T(8,128)(2,1)}, bf16[3,2,4,128,256]{4,3,2,1,0:T(8,128)(2,1)}) custom-call(s32[4]{0:T(128)S(1)} %add_add_fusion.2.where, bf16[4,512,512]{2,1,0:T(8,128)(2,1)} %rows.2.mine0_ref.mine1_ref, bf16[4,512,512]{2,1,0:T(8,128)(2,1)} %rows.3.mine1_ref, ...), custom_call_target="tpu_custom_call", output_to_operand_aliasing={{0}: (6, {})} | custom-call | flops 1610612736 | bytes 10485760 | tf_op jit(solution)/shard_map/gram/pallas_call | solution.py:195
  153.5 0.0 collective-permute-done.10.refs_0_
  153.5 0.1 collective-permute-start.19
  153.7 0.1 stack.105.where
  153.8 0.1 pad_add_fusion.where
  153.8 0.0 collective-permute-done.11.refs_1_
  153.8 4.8 %gram.11 = (bf16[2,16,128,2048]{3,2,1,0:T(8,128)(2,1)}, bf16[1,2,4,128,256]{4,3,2,1,0:T(8,128)(2,1)}) custom-call(s32[6]{0:T(128)S(1)} %stack.105.where, bf16[4,512,512]{2,1,0:T(8,128)(2,1)} %rows.2.mine0_ref.mine1_ref, bf16[4,512,512]{2,1,0:T(8,128)(2,1)} %rows.3.mine1_ref, ...), custom_call_target="tpu_custom_call", output_to_operand_aliasing={{0}: (5, {})} | custom-call | flops 536870912 | bytes 6291456 | tf_op jit(solution)/shard_map/gram/pallas_call | solution.py:195
  158.7 0.0 collective-permute-done.15.refs_0_
  158.7 0.0 collective-permute-done.16.refs_1_
  158.7 4.1 %gram.12 = bf16[2,2,4,128,256]{4,3,2,1,0:T(8,128)(2,1)} custom-call(s32[3]{0:T(128)S(1)} %pad_add_fusion.where, bf16[4,512,512]{2,1,0:T(8,128)(2,1)} %rows.2.mine0_ref.mine1_ref, bf16[4,512,512]{2,1,0:T(8,128)(2,1)} %rows.3.mine1_ref, bf16[16,4,64,128]{3,2,1,0:T(8,128)(2,1)S(1)} %collective-permute-done.15.refs_0_, ...), custom_call_target="tpu_custom_call" | custom-call | flops 1073741824 | bytes 8388608 | tf_op jit(solution)/shard_map/gram/pallas_call | solution.py:195
  162.8 1.5 collective-permute-start.17
  164.3 0.1 collective-permute-start.14
  164.4 0.1 stack.118.where
  164.5 0.1 add_add_fusion.where
  164.6 0.0 collective-permute-done.18.refs_2_
  164.6 0.0 collective-permute-done.19.refs_3_
  164.6 5.4 %gram.13.refs_2_ = bf16[2,16,128,2048]{3,2,1,0:T(8,128)(2,1)} custom-call(s32[9]{0:T(128)S(1)} %stack.118.where, bf16[4,512,512]{2,1,0:T(8,128)(2,1)} %rows.2.mine0_ref.mine1_ref, bf16[4,512,512]{2,1,0:T(8,128)(2,1)} %rows.3.mine1_ref, bf16[16,4,64,128]{3,2,1,0:T(8,128)(2,1)S(1)} %collective-permute-done.15.refs_0_, ...), custom_call_target="tpu_custom_call", output_to_operand_aliasing={{}: (7, {})} | custom-call | flops 1073741824 | bytes 8388608 | tf_op jit(solution)/shard_map/gram/pallas_call | solution.py:195
  170.0 0.0 collective-permute-done.17.refs_1_
  170.0 3.3 %place.1 = bf16[2,16,128,2048]{3,2,1,0:T(8,128)(2,1)} custom-call(s32[4]{0:T(128)S(1)} %add_add_fusion.where, bf16[1,2,4,128,256]{4,3,2,1,0:T(8,128)(2,1)} %collective-permute-done.14.refs_0_, bf16[2,2,4,128,256]{4,3,2,1,0:T(8,128)(2,1)S(1)} %collective-permute-done.17.refs_1_, bf16[2,16,128,2048]{3,2,1,0:T(8,128)(2,1)} %gram.13.refs_2_), custom_call_target="tpu_custom_call", output_to_operand_aliasing={{}: (3, {})} | custom-call | tf_op jit(solution)/shard_map/place/pallas_call | solution.py:244
  (4 shorter events, 0.0 us)
Async XLA Ops:
  31.0 22.0 %collective-permute-start.2 = (bf16[16,4,64,128]{3,2,1,0:T(8,128)(2,1)S(1)}, bf16[16,4,64,128]{3,2,1,0:T(8,128)(2,1)}, u32[]{:S(2)}, u32[]{:S(2)}) collective-permute-start(bf16[16,4,64,128]{3,2,1,0:T(8,128)(2,1)S(1)} %bitcast.23), channel_id=1, source_target_pairs={{0,32},{8,104},{32,64},{40,8},{64,96},{72,40},{96,0},{104,72},{1,3... | collective-permute-start | bytes 3145736 | tf_op jit(solution)/shard_map/ppermute | solution.py:269
  33.5 19.5 %all-to-all-start.1 = ((bf16[16,4,2,32,128]{4,3,2,1,0:T(8,128)(2,1)}), bf16[16,4,2,32,128]{4,3,2,1,0:T(8,128)(2,1)S(1)}, u32[]{:S(2)}, u32[]{:S(2)}) async-start(bf16[16,4,2,32,128]{4,3,2,1,0:T(8,128)(2,1)} %get-tuple-element.34), calls=%async_computation.1 | async-start | bytes 2097152 | tf_op jit(solution)/shard_map/all_to_all | solution.py:276
  37.1 23.6 %collective-permute-start.4 = (bf16[16,4,64,128]{3,2,1,0:T(8,128)(2,1)S(1)}, bf16[16,4,64,128]{3,2,1,0:T(8,128)(2,1)}, u32[]{:S(2)}, u32[]{:S(2)}) collective-permute-start(bf16[16,4,64,128]{3,2,1,0:T(8,128)(2,1)S(1)} %bitcast.24), channel_id=1, source_target_pairs={{0,96},{8,40},{32,0},{40,72},{64,32},{72,104},{96,64},{104,8},{1,9... | collective-permute-start | bytes 3145736 | tf_op jit(solution)/shard_map/ppermute | solution.py:270
  53.0 14.8 %collective-permute-start.3 = (bf16[16,4,64,128]{3,2,1,0:T(8,128)(2,1)}, bf16[16,4,64,128]{3,2,1,0:T(8,128)(2,1)}, u32[]{:S(2)}, u32[]{:S(2)}) collective-permute-start(bf16[16,4,64,128]{3,2,1,0:T(8,128)(2,1)} %collective-permute-done.2.refs_1_), channel_id=1, source_target_pairs={{0,32},{8,104},{32,64},{40,8},{64,96},{72,40},{96,0},{104,72},{1,3... | collective-permute-start | bytes 3145736 | tf_op jit(solution)/shard_map/ppermute | solution.py:269
  54.5 25.3 %collective-permute-start = (bf16[16,4,64,128]{3,2,1,0:T(8,128)(2,1)S(1)}, bf16[16,4,64,128]{3,2,1,0:T(8,128)(2,1)S(1)}, u32[]{:S(2)}, u32[]{:S(2)}) collective-permute-start(bf16[16,4,64,128]{3,2,1,0:T(8,128)(2,1)S(1)} %bitcast.25), channel_id=1, source_target_pairs={{0,16},{16,0},{1,17},{17,1},{2,18},{18,2},{3,19},{19,3},{4,20},{20... | collective-permute-start | bytes 3145736 | tf_op jit(solution)/shard_map/ppermute | solution.py:271
  57.1 27.4 %collective-permute-start.7 = (bf16[16,4,64,128]{3,2,1,0:T(8,128)(2,1)S(1)}, bf16[16,4,64,128]{3,2,1,0:T(8,128)(2,1)}, u32[]{:S(2)}, u32[]{:S(2)}) collective-permute-start(bf16[16,4,64,128]{3,2,1,0:T(8,128)(2,1)S(1)} %bitcast.18), channel_id=1, source_target_pairs={{0,32},{8,104},{32,64},{40,8},{64,96},{72,40},{96,0},{104,72},{1,3... | collective-permute-start | bytes 3145736 | tf_op jit(solution)/shard_map/ppermute | solution.py:269
  67.8 25.5 %collective-permute-start.5 = (bf16[16,4,64,128]{3,2,1,0:T(8,128)(2,1)S(1)}, bf16[16,4,64,128]{3,2,1,0:T(8,128)(2,1)S(1)}, u32[]{:S(2)}, u32[]{:S(2)}) collective-permute-start(bf16[16,4,64,128]{3,2,1,0:T(8,128)(2,1)S(1)} %bitcast.19), channel_id=1, source_target_pairs={{0,96},{8,40},{32,0},{40,72},{64,32},{72,104},{96,64},{104,8},{1,9... | collective-permute-start | bytes 3145736 | tf_op jit(solution)/shard_map/ppermute | solution.py:270
  68.8 40.8 %collective-permute-start.9 = (bf16[3,2,4,128,256]{4,3,2,1,0:T(8,128)(2,1)}, bf16[3,2,4,128,256]{4,3,2,1,0:T(8,128)(2,1)}, u32[]{:S(2)}, u32[]{:S(2)}) collective-permute-start(bf16[3,2,4,128,256]{4,3,2,1,0:T(8,128)(2,1)} %get-tuple-element.43), channel_id=1, source_target_pairs={{0,8},{8,0},{1,9},{9,1},{2,10},{10,2},{3,11},{11,3},{4,12},{12,4},... | collective-permute-start | bytes 4718600 | tf_op jit(solution)/shard_map/ppermute | solution.py:272
  79.8 25.8 %collective-permute-start.1 = (bf16[16,4,64,128]{3,2,1,0:T(8,128)(2,1)S(1)}, bf16[16,4,64,128]{3,2,1,0:T(8,128)(2,1)}, u32[]{:S(2)}, u32[]{:S(2)}) collective-permute-start(bf16[16,4,64,128]{3,2,1,0:T(8,128)(2,1)S(1)} %bitcast.20), channel_id=1, source_target_pairs={{0,16},{16,0},{1,17},{17,1},{2,18},{18,2},{3,19},{19,3},{4,20},{20... | collective-permute-start | bytes 3145736 | tf_op jit(solution)/shard_map/ppermute | solution.py:271
  84.5 21.1 %collective-permute-start.8 = (bf16[16,4,64,128]{3,2,1,0:T(8,128)(2,1)}, bf16[16,4,64,128]{3,2,1,0:T(8,128)(2,1)S(1)}, u32[]{:S(2)}, u32[]{:S(2)}) collective-permute-start(bf16[16,4,64,128]{3,2,1,0:T(8,128)(2,1)} %collective-permute-done.7.refs_2_), channel_id=1, source_target_pairs={{0,32},{8,104},{32,64},{40,8},{64,96},{72,40},{96,0},{104,72},{1,3... | collective-permute-start | bytes 3145736 | tf_op jit(solution)/shard_map/ppermute | solution.py:269
  93.4 1.0 copy-start
  94.4 24.6 %collective-permute-start.6 = (bf16[16,4,64,128]{3,2,1,0:T(8,128)(2,1)S(1)}, bf16[16,4,64,128]{3,2,1,0:T(8,128)(2,1)}, u32[]{:S(2)}, u32[]{:S(2)}) collective-permute-start(bf16[16,4,64,128]{3,2,1,0:T(8,128)(2,1)S(1)} %collective-permute-done.refs_3_), channel_id=1, source_target_pairs={{0,96},{8,40},{32,0},{40,72},{64,32},{72,104},{96,64},{104,8},{1,9... | collective-permute-start | bytes 3145736 | tf_op jit(solution)/shard_map/ppermute | solution.py:270
  103.2 50.7 %collective-permute-start.11 = (bf16[4,2,4,128,256]{4,3,2,1,0:T(8,128)(2,1)}, bf16[4,2,4,128,256]{4,3,2,1,0:T(8,128)(2,1)}, u32[]{:S(2)}, u32[]{:S(2)}) collective-permute-start(bf16[4,2,4,128,256]{4,3,2,1,0:T(8,128)(2,1)} %get-tuple-element.48), channel_id=1, source_target_pairs={{0,8},{8,0},{1,9},{9,1},{2,10},{10,2},{3,11},{11,3},{4,12},{12,4},... | collective-permute-start | bytes 6291464 | tf_op jit(solution)/shard_map/ppermute | solution.py:272
  105.6 24.9 %collective-permute-start.12 = (bf16[16,4,64,128]{3,2,1,0:T(8,128)(2,1)}, bf16[16,4,64,128]{3,2,1,0:T(8,128)(2,1)}, u32[]{:S(2)}, u32[]{:S(2)}) collective-permute-start(bf16[16,4,64,128]{3,2,1,0:T(8,128)(2,1)} %collective-permute-done.1.refs_2_), channel_id=1, source_target_pairs={{0,96},{8,40},{32,0},{40,72},{64,32},{72,104},{96,64},{104,8},{1,9... | collective-permute-start | bytes 3145736 | tf_op jit(solution)/shard_map/ppermute | solution.py:270
  106.8 23.7 %collective-permute-start.13 = (bf16[16,4,64,128]{3,2,1,0:T(8,128)(2,1)}, bf16[16,4,64,128]{3,2,1,0:T(8,128)(2,1)}, u32[]{:S(2)}, u32[]{:S(2)}) collective-permute-start(bf16[16,4,64,128]{3,2,1,0:T(8,128)(2,1)} %collective-permute-done.2.refs_1_), channel_id=1, source_target_pairs={{0,16},{16,0},{1,17},{17,1},{2,18},{18,2},{3,19},{19,3},{4,20},{20... | collective-permute-start | bytes 3145736 | tf_op jit(solution)/shard_map/ppermute | solution.py:271
  109.5 1.2 copy-start.1
  116.5 1.2 copy-start.2
  119.0 34.6 %collective-permute-start.10 = (bf16[16,4,64,128]{3,2,1,0:T(8,128)(2,1)}, bf16[16,4,64,128]{3,2,1,0:T(8,128)(2,1)}, u32[]{:S(2)}, u32[]{:S(2)}) collective-permute-start(bf16[16,4,64,128]{3,2,1,0:T(8,128)(2,1)} %collective-permute-done.1.refs_2_), channel_id=1, source_target_pairs={{0,32},{8,104},{32,64},{40,8},{64,96},{72,40},{96,0},{104,72},{1,3... | collective-permute-start | bytes 3145736 | tf_op jit(solution)/shard_map/ppermute | solution.py:269
  130.5 28.2 %collective-permute-start.15 = (bf16[16,4,64,128]{3,2,1,0:T(8,128)(2,1)}, bf16[16,4,64,128]{3,2,1,0:T(8,128)(2,1)S(1)}, u32[]{:S(2)}, u32[]{:S(2)}) collective-permute-start(bf16[16,4,64,128]{3,2,1,0:T(8,128)(2,1)} %collective-permute-done.13.refs_2_), channel_id=1, source_target_pairs={{0,32},{8,104},{32,64},{40,8},{64,96},{72,40},{96,0},{104,72},{1,3... | collective-permute-start | bytes 3145736 | tf_op jit(solution)/shard_map/ppermute | solution.py:269
  130.5 28.2 %collective-permute-start.16 = (bf16[16,4,64,128]{3,2,1,0:T(8,128)(2,1)S(1)}, bf16[16,4,64,128]{3,2,1,0:T(8,128)(2,1)S(1)}, u32[]{:S(2)}, u32[]{:S(2)}) collective-permute-start(bf16[16,4,64,128]{3,2,1,0:T(8,128)(2,1)S(1)} %collective-permute-done.8.refs_1_), channel_id=1, source_target_pairs={{0,16},{16,0},{1,17},{17,1},{2,18},{18,2},{3,19},{19,3},{4,20},{20... | collective-permute-start | bytes 3145736 | tf_op jit(solution)/shard_map/ppermute | solution.py:271
  133.2 31.4 %collective-permute-start.18 = (bf16[3,2,4,128,256]{4,3,2,1,0:T(8,128)(2,1)}, bf16[3,2,4,128,256]{4,3,2,1,0:T(8,128)(2,1)}, u32[]{:S(2)}, u32[]{:S(2)}) collective-permute-start(bf16[3,2,4,128,256]{4,3,2,1,0:T(8,128)(2,1)} %copy-done.2), channel_id=1, source_target_pairs={{0,8},{8,0},{1,9},{9,1},{2,10},{10,2},{3,11},{11,3},{4,12},{12,4},... | collective-permute-start | bytes 4718600 | tf_op jit(solution)/shard_map/ppermute | solution.py:272
  153.5 11.0 %collective-permute-start.19 = (bf16[3,2,4,128,256]{4,3,2,1,0:T(8,128)(2,1)}, bf16[3,2,4,128,256]{4,3,2,1,0:T(8,128)(2,1)}, u32[]{:S(2)}, u32[]{:S(2)}) collective-permute-start(bf16[3,2,4,128,256]{4,3,2,1,0:T(8,128)(2,1)} %get-tuple-element.58), channel_id=1, source_target_pairs={{0,8},{8,0},{1,9},{9,1},{2,10},{10,2},{3,11},{11,3},{4,12},{12,4},... | collective-permute-start | bytes 4718600 | tf_op jit(solution)/shard_map/ppermute | solution.py:272
  162.8 7.2 %collective-permute-start.17 = (bf16[2,2,4,128,256]{4,3,2,1,0:T(8,128)(2,1)}, bf16[2,2,4,128,256]{4,3,2,1,0:T(8,128)(2,1)S(1)}, u32[]{:S(2)}, u32[]{:S(2)}) collective-permute-start(bf16[2,2,4,128,256]{4,3,2,1,0:T(8,128)(2,1)} %gram.12), channel_id=1, source_target_pairs={{0,8},{8,0},{1,9},{9,1},{2,10},{10,2},{3,11},{11,3},{4,12},{12,4},... | collective-permute-start | bytes 3145736 | tf_op jit(solution)/shard_map/ppermute | solution.py:272
  164.3 5.7 %collective-permute-start.14 = (bf16[1,2,4,128,256]{4,3,2,1,0:T(8,128)(2,1)}, bf16[1,2,4,128,256]{4,3,2,1,0:T(8,128)(2,1)}, u32[]{:S(2)}, u32[]{:S(2)}) collective-permute-start(bf16[1,2,4,128,256]{4,3,2,1,0:T(8,128)(2,1)} %get-tuple-element.52), channel_id=1, source_target_pairs={{0,8},{8,0},{1,9},{9,1},{2,10},{10,2},{3,11},{11,3},{4,12},{12,4},... | collective-permute-start | bytes 1572872 | tf_op jit(solution)/shard_map/ppermute | solution.py:272

commit v15 on v14

--- a/solution.py
+++ b/solution.py
@@ -310,12 +310,12 @@
 
     sent4 = blocks4, swap(sent)
     blocks5 = [entry(1, 1, 1, nob)]
-    out, sent = gram(core, mine, blocks5, shape, out, sent2)
+    out, sent = gram(core, mine, blocks5, shape, out, sent2, sent3)
 
     sent5 = blocks5, swap(sent)
     blocks6 = [entry(0, 2, 1, after(foa, out)), entry(1, 2, 1, fob)]
     (sent,) = gram(core, mine, blocks6, shape, None, own=False)
-    (out,) = gram(core, mine, blocks6, shape, out, sent3, sent4, other=False)
+    (out,) = gram(core, mine, blocks6, shape, out, sent4, other=False)
     return place(core, out, sent5, (blocks6, swap(sent)))
 
 

time: 174 us -> 173 us (level)
  starting transfers between devices: 49.6 us -> 43.1 us
  waiting for transfers between devices: 41.9 us -> 46.9 us
    ppermute x6, starting transfers between devices: 22.5 us -> 15.6 us  [shards(): swap = lambda v: lax.ppermute(v, 'core', [(0, 1), (1, 0)])]
    ppermute x4, waiting for transfers between devices: 7.1 us -> 13.4 us  [shards(): over = lambda v: lax.ppermute(v, 'yh', [(0, 1), (1, 0)])]
    unnamed x6 -> x8, local copies, waits for them, and re-layouts: 3.41 us -> 4.46 us
where the time goes in v15:
time: 173 us
  Pallas kernels  54.3 us (31%)
  waiting for transfers between devices  46.9 us (27%)
  starting transfers between devices  43.1 us (25%)
  blocking collectives  23.3 us (13%)
  local copies, waits for them, and re-layouts  4.8 us (3%)
    pallas_call x7, Pallas kernels, gram(): pl.pallas_call(functools.partial(gram_kernel, 2.0 / depth, chunks, [[bloc...  38.7 us
    all_to_all x1, blocking collectives, owned(): lax.all_to_all(chunk, ('yl', 'z', 'core'), split_axis=0, concat_axis=0, t...  23.3 us
    ppermute x4, waiting for transfers between devices, shards(): bwd = lambda v: lax.ppermute(v, ('x', 'core'), mirrored(-1))  16.4 us
    ppermute x6, starting transfers between devices, shards(): swap = lambda v: lax.ppermute(v, 'core', [(0, 1), (1, 0)])  15.6 us
    all_to_all x1, waiting for transfers between devices, owned(): lax.all_to_all(chunk, ('yl', 'z', 'core'), split_axis=0, concat_axis=0, t...  14.7 us
    ppermute x4, waiting for transfers between devices, shards(): over = lambda v: lax.ppermute(v, 'yh', [(0, 1), (1, 0)])  13.4 us
    ppermute x4, starting transfers between devices, shards(): over = lambda v: lax.ppermute(v, 'yh', [(0, 1), (1, 0)])  10.1 us
    ppermute x6, starting transfers between devices, shards(): fwd = lambda v: lax.ppermute(v, ('x', 'core'), mirrored(1))  8.96 us
  transfers between devices with their start and end apart: 21, of which 7 were waited for; matrix products, arithmetic and copies ran while one was open for 0% of the time, Pallas kernels for 25%

profile of v15, /device:TPU:1, one launch (start us, length us, event | category | flops | bytes accessed | tf_op | source)
XLA Modules:
  0.0 173.0 jit_solution(7579509177244396719)
XLA Ops:
  0.0 7.8 %whiten.1 = (bf16[16,4,2,32,128]{4,3,2,1,0:T(8,128)(2,1)}, bf16[16,4,2,32,128]{4,3,2,1,0:T(8,128)(2,1)}) custom-call(bf16[128,32,512]{2,1,0:T(8,128)(2,1)} %records_ref.1, s32[32,128]{1,0:T(8,128)} %bitcast.28, bf16[512,256]{1,0:T(8,128)(2,1)} %constant.183.clone.high_ref, bf16[512,256]{1,0:T(8,128)(2,1)} %constant.184.clone.low_ref), custom_call_target="tpu_custom_call" | custom-call | tf_op jit(solution)/shard_map/whiten/pallas_call | solution.py:56
  7.8 23.3 %all_to_all.10 = bf16[16,4,2,32,128]{4,3,2,1,0:T(8,128)(2,1)S(1)} all-to-all(bf16[16,4,2,32,128]{4,3,2,1,0:T(8,128)(2,1)} %get-tuple-element.32), channel_id=1, replica_groups=mesh['x'=4,'yh'=2,'core'=2,'yl'=2,'z'=4] {'yl','z','core'}, dimensions={0} | all-to-all | bytes 2097152 | tf_op jit(solution)/shard_map/all_to_all | solution.py:276
  31.0 2.5 %collective-permute-start.2 = (bf16[16,4,64,128]{3,2,1,0:T(8,128)(2,1)S(1)}, bf16[16,4,64,128]{3,2,1,0:T(8,128)(2,1)}, u32[]{:S(2)}, u32[]{:S(2)}) collective-permute-start(bf16[16,4,64,128]{3,2,1,0:T(8,128)(2,1)S(1)} %bitcast.23), channel_id=1, source_target_pairs={{0,32},{8,104},{32,64},{40,8},{64,96},{72,40},{96,0},{104,72},{1,3... | collective-permute-start | bytes 3145736 | tf_op jit(solution)/shard_map/ppermute | solution.py:269
  33.5 3.6 %all-to-all-start.1 = ((bf16[16,4,2,32,128]{4,3,2,1,0:T(8,128)(2,1)}), bf16[16,4,2,32,128]{4,3,2,1,0:T(8,128)(2,1)S(1)}, u32[]{:S(2)}, u32[]{:S(2)}) async-start(bf16[16,4,2,32,128]{4,3,2,1,0:T(8,128)(2,1)} %get-tuple-element.34), calls=%async_computation.1 | async-start | bytes 2097152 | tf_op jit(solution)/shard_map/all_to_all | solution.py:276
  37.1 1.2 collective-permute-start.4
  38.3 14.7 %all-to-all-done.1 = bf16[16,4,2,32,128]{4,3,2,1,0:T(8,128)(2,1)S(1)} async-done(((bf16[16,4,2,32,128]{4,3,2,1,0:T(8,128)(2,1)}), bf16[16,4,2,32,128]{4,3,2,1,0:T(8,128)(2,1)S(1)}, u32[]{:S(2)}, u32[]{:S(2)}) %all-to-all-start.1) | async-done | bytes 1048608 | tf_op jit(solution)/shard_map/all_to_all | solution.py:276
  53.0 2.6 %collective-permute-start = (bf16[16,4,64,128]{3,2,1,0:T(8,128)(2,1)S(1)}, bf16[16,4,64,128]{3,2,1,0:T(8,128)(2,1)S(1)}, u32[]{:S(2)}, u32[]{:S(2)}) collective-permute-start(bf16[16,4,64,128]{3,2,1,0:T(8,128)(2,1)S(1)} %bitcast.25), channel_id=1, source_target_pairs={{0,16},{16,0},{1,17},{17,1},{2,18},{18,2},{3,19},{19,3},{4,20},{20... | collective-permute-start | bytes 3145736 | tf_op jit(solution)/shard_map/ppermute | solution.py:271
  55.7 0.0 collective-permute-done.2.refs_1_
  55.7 1.5 collective-permute-start.3
  57.1 1.3 collective-permute-start.7
  58.4 0.1 add_add_fusion.1.where
  58.5 2.3 %rows.2.mine0_ref.mine1_ref = bf16[4,512,512]{2,1,0:T(8,128)(2,1)} custom-call(bf16[16,4,64,128]{3,2,1,0:T(8,128)(2,1)S(1)} %bitcast.26), custom_call_target="tpu_custom_call" | custom-call | tf_op jit(solution)/shard_map/rows/pallas_call | solution.py:90
  60.7 0.0 collective-permute-done.4.refs_2_
  60.7 6.3 %gram.7 = (bf16[2,16,128,2048]{3,2,1,0:T(8,128)(2,1)}, bf16[3,2,4,128,256]{4,3,2,1,0:T(8,128)(2,1)}) custom-call(s32[4]{0:T(128)S(1)} %add_add_fusion.1.where, bf16[4,512,512]{2,1,0:T(8,128)(2,1)} %rows.2.mine0_ref.mine1_ref, bf16[4,512,512]{2,1,0:T(8,128)(2,1)} %rows.2.mine0_ref.mine1_ref, bf16[16,4,64,128]{3,2,1,0:T(8,128)(2,1)S(1)} %bitcast.27, ...), custom_call_target="tpu_custom_call" | custom-call | flops 1610612736 | bytes 10485760 | tf_op jit(solution)/shard_map/gram/pallas_call | solution.py:195
  67.1 1.2 collective-permute-start.9
  68.2 10.1 %collective-permute-done.refs_3_ = bf16[16,4,64,128]{3,2,1,0:T(8,128)(2,1)S(1)} collective-permute-done((bf16[16,4,64,128]{3,2,1,0:T(8,128)(2,1)S(1)}, bf16[16,4,64,128]{3,2,1,0:T(8,128)(2,1)S(1)}, u32[]{:S(2)}, u32[]{:S(2)}) %collective-permute-start) | collective-permute-done | bytes 1048608 | tf_op jit(solution)/shard_map/ppermute | solution.py:271
  78.3 0.0 collective-permute-done.3.refs_1_
  78.3 1.2 collective-permute-start.5
  79.6 2.6 %collective-permute-start.1 = (bf16[16,4,64,128]{3,2,1,0:T(8,128)(2,1)S(1)}, bf16[16,4,64,128]{3,2,1,0:T(8,128)(2,1)}, u32[]{:S(2)}, u32[]{:S(2)}) collective-permute-start(bf16[16,4,64,128]{3,2,1,0:T(8,128)(2,1)S(1)} %bitcast.20), channel_id=1, source_target_pairs={{0,16},{16,0},{1,17},{17,1},{2,18},{18,2},{3,19},{19,3},{4,20},{20... | collective-permute-start | bytes 3145736 | tf_op jit(solution)/shard_map/ppermute | solution.py:271
  82.2 0.0 collective-permute-done.7.refs_2_
  82.2 1.6 collective-permute-start.8
  83.8 0.1 stack.112.where
  83.8 0.1 stack.111.where
  83.9 2.3 %rows.3.mine1_ref = bf16[4,512,512]{2,1,0:T(8,128)(2,1)} custom-call(bf16[16,4,64,128]{3,2,1,0:T(8,128)(2,1)S(1)} %bitcast.21), custom_call_target="tpu_custom_call" | custom-call | tf_op jit(solution)/shard_map/rows/pallas_call | solution.py:90
  86.2 13.6 %collective-permute-done.5.refs_0_ = bf16[16,4,64,128]{3,2,1,0:T(8,128)(2,1)} collective-permute-done((bf16[16,4,64,128]{3,2,1,0:T(8,128)(2,1)S(1)}, bf16[16,4,64,128]{3,2,1,0:T(8,128)(2,1)}, u32[]{:S(2)}, u32[]{:S(2)}) %collective-permute-start.5) | collective-permute-done | bytes 1048608 | tf_op jit(solution)/shard_map/ppermute | solution.py:270
  99.8 1.2 collective-permute-start.6
  101.0 2.5 %collective-permute-done.1.refs_2_ = bf16[16,4,64,128]{3,2,1,0:T(8,128)(2,1)} collective-permute-done((bf16[16,4,64,128]{3,2,1,0:T(8,128)(2,1)S(1)}, bf16[16,4,64,128]{3,2,1,0:T(8,128)(2,1)}, u32[]{:S(2)}, u32[]{:S(2)}) %collective-permute-start.1) | collective-permute-done | bytes 1048608 | tf_op jit(solution)/shard_map/ppermute | solution.py:271
  103.5 2.4 %collective-permute-done.8.refs_1_ = bf16[16,4,64,128]{3,2,1,0:T(8,128)(2,1)S(1)} collective-permute-done((bf16[16,4,64,128]{3,2,1,0:T(8,128)(2,1)}, bf16[16,4,64,128]{3,2,1,0:T(8,128)(2,1)S(1)}, u32[]{:S(2)}, u32[]{:S(2)}) %collective-permute-start.8) | collective-permute-done | bytes 1048608 | tf_op jit(solution)/shard_map/ppermute | solution.py:269
  105.9 1.2 collective-permute-start.13
  107.1 1.2 collective-permute-start.14
  108.2 6.5 %gram.8 = (bf16[2,16,128,2048]{3,2,1,0:T(8,128)(2,1)}, bf16[4,2,4,128,256]{4,3,2,1,0:T(8,128)(2,1)}) custom-call(s32[5]{0:T(128)S(1)} %stack.112.where, bf16[4,512,512]{2,1,0:T(8,128)(2,1)} %rows.2.mine0_ref.mine1_ref, bf16[4,512,512]{2,1,0:T(8,128)(2,1)} %rows.3.mine1_ref, bf16[16,4,64,128]{3,2,1,0:T(8,128)(2,1)S(1)} %bitcast.22, ...), custom_call_target="tpu_custom_call", output_to_operand_aliasing={{0}: (7, {})} | custom-call | flops 2147483648 | bytes 12582912 | tf_op jit(solution)/shard_map/gram/pallas_call | solution.py:195
  114.7 3.8 %collective-permute-start.11 = (bf16[4,2,4,128,256]{4,3,2,1,0:T(8,128)(2,1)}, bf16[4,2,4,128,256]{4,3,2,1,0:T(8,128)(2,1)}, u32[]{:S(2)}, u32[]{:S(2)}) collective-permute-start(bf16[4,2,4,128,256]{4,3,2,1,0:T(8,128)(2,1)} %get-tuple-element.48), channel_id=1, source_target_pairs={{0,8},{8,0},{1,9},{9,1},{2,10},{10,2},{3,11},{11,3},{4,12},{12,4},... | collective-permute-start | bytes 6291464 | tf_op jit(solution)/shard_map/ppermute | solution.py:272
  118.5 0.0 collective-permute-done.9.refs_3_
  118.5 6.1 %gram.9 = (bf16[2,16,128,2048]{3,2,1,0:T(8,128)(2,1)}, bf16[3,2,4,128,256]{4,3,2,1,0:T(8,128)(2,1)}) custom-call(s32[7]{0:T(128)S(1)} %stack.111.where, bf16[4,512,512]{2,1,0:T(8,128)(2,1)} %rows.2.mine0_ref.mine1_ref, bf16[4,512,512]{2,1,0:T(8,128)(2,1)} %rows.3.mine1_ref, ...), custom_call_target="tpu_custom_call", output_to_operand_aliasing={{0}: (7, {})} | custom-call | flops 1610612736 | bytes 10485760 | tf_op jit(solution)/shard_map/gram/pallas_call | solution.py:195
  124.6 0.1 collective-permute-start.12
  124.8 0.0 collective-permute-done.6.refs_0_
  124.8 1.0 copy-done
  125.7 0.3 collective-permute-start.10
  126.0 2.9 %collective-permute-done.13.refs_1_ = bf16[16,4,64,128]{3,2,1,0:T(8,128)(2,1)S(1)} collective-permute-done((bf16[16,4,64,128]{3,2,1,0:T(8,128)(2,1)}, bf16[16,4,64,128]{3,2,1,0:T(8,128)(2,1)S(1)}, u32[]{:S(2)}, u32[]{:S(2)}) %collective-permute-start.13) | collective-permute-done | bytes 1048608 | tf_op jit(solution)/shard_map/ppermute | solution.py:270
  128.9 1.0 copy-done.2
  130.0 0.8 collective-permute-done.14.refs_2_
  130.7 1.9 %collective-permute-start.16 = (bf16[16,4,64,128]{3,2,1,0:T(8,128)(2,1)}, bf16[16,4,64,128]{3,2,1,0:T(8,128)(2,1)S(1)}, u32[]{:S(2)}, u32[]{:S(2)}) collective-permute-start(bf16[16,4,64,128]{3,2,1,0:T(8,128)(2,1)} %collective-permute-done.14.refs_2_), channel_id=1, source_target_pairs={{0,32},{8,104},{32,64},{40,8},{64,96},{72,40},{96,0},{104,72},{1,3... | collective-permute-start | bytes 3145736 | tf_op jit(solution)/shard_map/ppermute | solution.py:269
  132.6 3.7 %collective-permute-start.17 = (bf16[16,4,64,128]{3,2,1,0:T(8,128)(2,1)S(1)}, bf16[16,4,64,128]{3,2,1,0:T(8,128)(2,1)S(1)}, u32[]{:S(2)}, u32[]{:S(2)}) collective-permute-start(bf16[16,4,64,128]{3,2,1,0:T(8,128)(2,1)S(1)} %collective-permute-done.8.refs_1_), channel_id=1, source_target_pairs={{0,16},{16,0},{1,17},{17,1},{2,18},{18,2},{3,19},{19,3},{4,20},{20... | collective-permute-start | bytes 3145736 | tf_op jit(solution)/shard_map/ppermute | solution.py:271
  136.3 0.1 add_add_fusion.2.where
  136.4 1.2 copy-done.1
  137.6 1.2 copy-done.3
  138.8 5.5 %gram.10 = (bf16[2,16,128,2048]{3,2,1,0:T(8,128)(2,1)}, bf16[3,2,4,128,256]{4,3,2,1,0:T(8,128)(2,1)}) custom-call(s32[4]{0:T(128)S(1)} %add_add_fusion.2.where, bf16[4,512,512]{2,1,0:T(8,128)(2,1)} %rows.2.mine0_ref.mine1_ref, bf16[4,512,512]{2,1,0:T(8,128)(2,1)} %rows.3.mine1_ref, ...), custom_call_target="tpu_custom_call", output_to_operand_aliasing={{0}: (6, {})} | custom-call | flops 1610612736 | bytes 10485760 | tf_op jit(solution)/shard_map/gram/pallas_call | solution.py:195
  144.4 6.1 %collective-permute-start.19 = (bf16[3,2,4,128,256]{4,3,2,1,0:T(8,128)(2,1)}, bf16[3,2,4,128,256]{4,3,2,1,0:T(8,128)(2,1)}, u32[]{:S(2)}, u32[]{:S(2)}) collective-permute-start(bf16[3,2,4,128,256]{4,3,2,1,0:T(8,128)(2,1)} %get-tuple-element.58), channel_id=1, source_target_pairs={{0,8},{8,0},{1,9},{9,1},{2,10},{10,2},{3,11},{11,3},{4,12},{12,4},... | collective-permute-start | bytes 4718600 | tf_op jit(solution)/shard_map/ppermute | solution.py:272
  150.5 0.1 stack.106.where
  150.6 0.1 pad_add_fusion.where
  150.6 0.0 collective-permute-done.10.refs_0_
  150.6 0.0 collective-permute-done.11.refs_1_
  150.6 5.5 %gram.11 = (bf16[2,16,128,2048]{3,2,1,0:T(8,128)(2,1)}, bf16[1,2,4,128,256]{4,3,2,1,0:T(8,128)(2,1)}) custom-call(s32[9]{0:T(128)S(1)} %stack.106.where, bf16[4,512,512]{2,1,0:T(8,128)(2,1)} %rows.2.mine0_ref.mine1_ref, bf16[4,512,512]{2,1,0:T(8,128)(2,1)} %rows.3.mine1_ref, ...), custom_call_target="tpu_custom_call", output_to_operand_aliasing={{0}: (6, {})} | custom-call | flops 536870912 | bytes 6291456 | tf_op jit(solution)/shard_map/gram/pallas_call | solution.py:195
  156.1 0.0 collective-permute-done.17.refs_1_
  156.2 4.1 %gram.12 = bf16[2,2,4,128,256]{4,3,2,1,0:T(8,128)(2,1)} custom-call(s32[3]{0:T(128)S(1)} %pad_add_fusion.where, bf16[4,512,512]{2,1,0:T(8,128)(2,1)} %rows.2.mine0_ref.mine1_ref, bf16[4,512,512]{2,1,0:T(8,128)(2,1)} %rows.3.mine1_ref, bf16[16,4,64,128]{3,2,1,0:T(8,128)(2,1)S(1)} %collective-permute-done.16.refs_0_, ...), custom_call_target="tpu_custom_call" | custom-call | flops 1073741824 | bytes 8388608 | tf_op jit(solution)/shard_map/gram/pallas_call | solution.py:195
  160.3 4.3 %collective-permute-start.18 = (bf16[2,2,4,128,256]{4,3,2,1,0:T(8,128)(2,1)}, bf16[2,2,4,128,256]{4,3,2,1,0:T(8,128)(2,1)S(1)}, u32[]{:S(2)}, u32[]{:S(2)}) collective-permute-start(bf16[2,2,4,128,256]{4,3,2,1,0:T(8,128)(2,1)} %gram.12), channel_id=1, source_target_pairs={{0,8},{8,0},{1,9},{9,1},{2,10},{10,2},{3,11},{11,3},{4,12},{12,4},... | collective-permute-start | bytes 3145736 | tf_op jit(solution)/shard_map/ppermute | solution.py:272
  164.6 0.1 collective-permute-start.15
  164.7 0.1 stack.118.where
  164.8 0.1 add_add_fusion.where
  164.9 0.0 collective-permute-done.19.refs_2_
  164.9 4.7 %gram.13.refs_2_ = bf16[2,16,128,2048]{3,2,1,0:T(8,128)(2,1)} custom-call(s32[6]{0:T(128)S(1)} %stack.118.where, bf16[4,512,512]{2,1,0:T(8,128)(2,1)} %rows.2.mine0_ref.mine1_ref, bf16[4,512,512]{2,1,0:T(8,128)(2,1)} %rows.3.mine1_ref, bf16[16,4,64,128]{3,2,1,0:T(8,128)(2,1)S(1)} %collective-permute-done.16.refs_0_, ...), custom_call_target="tpu_custom_call", output_to_operand_aliasing={{}: (6, {})} | custom-call | flops 1073741824 | bytes 8388608 | tf_op jit(solution)/shard_map/gram/pallas_call | solution.py:195
  169.5 0.0 collective-permute-done.15.refs_0_
  169.5 0.0 collective-permute-done.18.refs_1_
  169.5 3.3 %place.1 = bf16[2,16,128,2048]{3,2,1,0:T(8,128)(2,1)} custom-call(s32[4]{0:T(128)S(1)} %add_add_fusion.where, bf16[1,2,4,128,256]{4,3,2,1,0:T(8,128)(2,1)} %collective-permute-done.15.refs_0_, bf16[2,2,4,128,256]{4,3,2,1,0:T(8,128)(2,1)S(1)} %collective-permute-done.18.refs_1_, bf16[2,16,128,2048]{3,2,1,0:T(8,128)(2,1)} %gram.13.refs_2_), custom_call_target="tpu_custom_call", output_to_operand_aliasing={{}: (3, {})} | custom-call | tf_op jit(solution)/shard_map/place/pallas_call | solution.py:244
  (6 shorter events, 0.0 us)
Async XLA Ops:
  31.0 24.6 %collective-permute-start.2 = (bf16[16,4,64,128]{3,2,1,0:T(8,128)(2,1)S(1)}, bf16[16,4,64,128]{3,2,1,0:T(8,128)(2,1)}, u32[]{:S(2)}, u32[]{:S(2)}) collective-permute-start(bf16[16,4,64,128]{3,2,1,0:T(8,128)(2,1)S(1)} %bitcast.23), channel_id=1, source_target_pairs={{0,32},{8,104},{32,64},{40,8},{64,96},{72,40},{96,0},{104,72},{1,3... | collective-permute-start | bytes 3145736 | tf_op jit(solution)/shard_map/ppermute | solution.py:269
  33.5 19.5 %all-to-all-start.1 = ((bf16[16,4,2,32,128]{4,3,2,1,0:T(8,128)(2,1)}), bf16[16,4,2,32,128]{4,3,2,1,0:T(8,128)(2,1)S(1)}, u32[]{:S(2)}, u32[]{:S(2)}) async-start(bf16[16,4,2,32,128]{4,3,2,1,0:T(8,128)(2,1)} %get-tuple-element.34), calls=%async_computation.1 | async-start | bytes 2097152 | tf_op jit(solution)/shard_map/all_to_all | solution.py:276
  37.1 23.6 %collective-permute-start.4 = (bf16[16,4,64,128]{3,2,1,0:T(8,128)(2,1)S(1)}, bf16[16,4,64,128]{3,2,1,0:T(8,128)(2,1)}, u32[]{:S(2)}, u32[]{:S(2)}) collective-permute-start(bf16[16,4,64,128]{3,2,1,0:T(8,128)(2,1)S(1)} %bitcast.24), channel_id=1, source_target_pairs={{0,96},{8,40},{32,0},{40,72},{64,32},{72,104},{96,64},{104,8},{1,9... | collective-permute-start | bytes 3145736 | tf_op jit(solution)/shard_map/ppermute | solution.py:270
  53.0 25.3 %collective-permute-start = (bf16[16,4,64,128]{3,2,1,0:T(8,128)(2,1)S(1)}, bf16[16,4,64,128]{3,2,1,0:T(8,128)(2,1)S(1)}, u32[]{:S(2)}, u32[]{:S(2)}) collective-permute-start(bf16[16,4,64,128]{3,2,1,0:T(8,128)(2,1)S(1)} %bitcast.25), channel_id=1, source_target_pairs={{0,16},{16,0},{1,17},{17,1},{2,18},{18,2},{3,19},{19,3},{4,20},{20... | collective-permute-start | bytes 3145736 | tf_op jit(solution)/shard_map/ppermute | solution.py:271
  55.7 22.7 %collective-permute-start.3 = (bf16[16,4,64,128]{3,2,1,0:T(8,128)(2,1)}, bf16[16,4,64,128]{3,2,1,0:T(8,128)(2,1)}, u32[]{:S(2)}, u32[]{:S(2)}) collective-permute-start(bf16[16,4,64,128]{3,2,1,0:T(8,128)(2,1)} %collective-permute-done.2.refs_1_), channel_id=1, source_target_pairs={{0,32},{8,104},{32,64},{40,8},{64,96},{72,40},{96,0},{104,72},{1,3... | collective-permute-start | bytes 3145736 | tf_op jit(solution)/shard_map/ppermute | solution.py:269
  57.1 25.1 %collective-permute-start.7 = (bf16[16,4,64,128]{3,2,1,0:T(8,128)(2,1)S(1)}, bf16[16,4,64,128]{3,2,1,0:T(8,128)(2,1)}, u32[]{:S(2)}, u32[]{:S(2)}) collective-permute-start(bf16[16,4,64,128]{3,2,1,0:T(8,128)(2,1)S(1)} %bitcast.18), channel_id=1, source_target_pairs={{0,32},{8,104},{32,64},{40,8},{64,96},{72,40},{96,0},{104,72},{1,3... | collective-permute-start | bytes 3145736 | tf_op jit(solution)/shard_map/ppermute | solution.py:269
  67.1 51.4 %collective-permute-start.9 = (bf16[3,2,4,128,256]{4,3,2,1,0:T(8,128)(2,1)}, bf16[3,2,4,128,256]{4,3,2,1,0:T(8,128)(2,1)}, u32[]{:S(2)}, u32[]{:S(2)}) collective-permute-start(bf16[3,2,4,128,256]{4,3,2,1,0:T(8,128)(2,1)} %get-tuple-element.43), channel_id=1, source_target_pairs={{0,8},{8,0},{1,9},{9,1},{2,10},{10,2},{3,11},{11,3},{4,12},{12,4},... | collective-permute-start | bytes 4718600 | tf_op jit(solution)/shard_map/ppermute | solution.py:272
  78.3 21.4 %collective-permute-start.5 = (bf16[16,4,64,128]{3,2,1,0:T(8,128)(2,1)S(1)}, bf16[16,4,64,128]{3,2,1,0:T(8,128)(2,1)}, u32[]{:S(2)}, u32[]{:S(2)}) collective-permute-start(bf16[16,4,64,128]{3,2,1,0:T(8,128)(2,1)S(1)} %bitcast.19), channel_id=1, source_target_pairs={{0,96},{8,40},{32,0},{40,72},{64,32},{72,104},{96,64},{104,8},{1,9... | collective-permute-start | bytes 3145736 | tf_op jit(solution)/shard_map/ppermute | solution.py:270
  79.6 24.0 %collective-permute-start.1 = (bf16[16,4,64,128]{3,2,1,0:T(8,128)(2,1)S(1)}, bf16[16,4,64,128]{3,2,1,0:T(8,128)(2,1)}, u32[]{:S(2)}, u32[]{:S(2)}) collective-permute-start(bf16[16,4,64,128]{3,2,1,0:T(8,128)(2,1)S(1)} %bitcast.20), channel_id=1, source_target_pairs={{0,16},{16,0},{1,17},{17,1},{2,18},{18,2},{3,19},{19,3},{4,20},{20... | collective-permute-start | bytes 3145736 | tf_op jit(solution)/shard_map/ppermute | solution.py:271
  82.2 23.7 %collective-permute-start.8 = (bf16[16,4,64,128]{3,2,1,0:T(8,128)(2,1)}, bf16[16,4,64,128]{3,2,1,0:T(8,128)(2,1)S(1)}, u32[]{:S(2)}, u32[]{:S(2)}) collective-permute-start(bf16[16,4,64,128]{3,2,1,0:T(8,128)(2,1)} %collective-permute-done.7.refs_2_), channel_id=1, source_target_pairs={{0,32},{8,104},{32,64},{40,8},{64,96},{72,40},{96,0},{104,72},{1,3... | collective-permute-start | bytes 3145736 | tf_op jit(solution)/shard_map/ppermute | solution.py:269
  99.8 25.0 %collective-permute-start.6 = (bf16[16,4,64,128]{3,2,1,0:T(8,128)(2,1)S(1)}, bf16[16,4,64,128]{3,2,1,0:T(8,128)(2,1)S(1)}, u32[]{:S(2)}, u32[]{:S(2)}) collective-permute-start(bf16[16,4,64,128]{3,2,1,0:T(8,128)(2,1)S(1)} %collective-permute-done.refs_3_), channel_id=1, source_target_pairs={{0,96},{8,40},{32,0},{40,72},{64,32},{72,104},{96,64},{104,8},{1,9... | collective-permute-start | bytes 3145736 | tf_op jit(solution)/shard_map/ppermute | solution.py:270
  105.9 23.1 %collective-permute-start.13 = (bf16[16,4,64,128]{3,2,1,0:T(8,128)(2,1)}, bf16[16,4,64,128]{3,2,1,0:T(8,128)(2,1)S(1)}, u32[]{:S(2)}, u32[]{:S(2)}) collective-permute-start(bf16[16,4,64,128]{3,2,1,0:T(8,128)(2,1)} %collective-permute-done.1.refs_2_), channel_id=1, source_target_pairs={{0,96},{8,40},{32,0},{40,72},{64,32},{72,104},{96,64},{104,8},{1,9... | collective-permute-start | bytes 3145736 | tf_op jit(solution)/shard_map/ppermute | solution.py:270
  107.1 23.7 %collective-permute-start.14 = (bf16[16,4,64,128]{3,2,1,0:T(8,128)(2,1)}, bf16[16,4,64,128]{3,2,1,0:T(8,128)(2,1)}, u32[]{:S(2)}, u32[]{:S(2)}) collective-permute-start(bf16[16,4,64,128]{3,2,1,0:T(8,128)(2,1)} %collective-permute-done.2.refs_1_), channel_id=1, source_target_pairs={{0,16},{16,0},{1,17},{17,1},{2,18},{18,2},{3,19},{19,3},{4,20},{20... | collective-permute-start | bytes 3145736 | tf_op jit(solution)/shard_map/ppermute | solution.py:271
  114.7 35.9 %collective-permute-start.11 = (bf16[4,2,4,128,256]{4,3,2,1,0:T(8,128)(2,1)}, bf16[4,2,4,128,256]{4,3,2,1,0:T(8,128)(2,1)}, u32[]{:S(2)}, u32[]{:S(2)}) collective-permute-start(bf16[4,2,4,128,256]{4,3,2,1,0:T(8,128)(2,1)} %get-tuple-element.48), channel_id=1, source_target_pairs={{0,8},{8,0},{1,9},{9,1},{2,10},{10,2},{3,11},{11,3},{4,12},{12,4},... | collective-permute-start | bytes 6291464 | tf_op jit(solution)/shard_map/ppermute | solution.py:272
  124.6 19.7 %collective-permute-start.12 = (bf16[3,2,4,128,256]{4,3,2,1,0:T(8,128)(2,1)}, bf16[3,2,4,128,256]{4,3,2,1,0:T(8,128)(2,1)}, u32[]{:S(2)}, u32[]{:S(2)}) collective-permute-start(bf16[3,2,4,128,256]{4,3,2,1,0:T(8,128)(2,1)} %get-tuple-element.49), channel_id=1, source_target_pairs={{0,8},{8,0},{1,9},{9,1},{2,10},{10,2},{3,11},{11,3},{4,12},{12,4},... | collective-permute-start | bytes 4718600 | tf_op jit(solution)/shard_map/ppermute | solution.py:272
  124.8 1.0 copy-start
  125.7 24.9 %collective-permute-start.10 = (bf16[16,4,64,128]{3,2,1,0:T(8,128)(2,1)}, bf16[16,4,64,128]{3,2,1,0:T(8,128)(2,1)}, u32[]{:S(2)}, u32[]{:S(2)}) collective-permute-start(bf16[16,4,64,128]{3,2,1,0:T(8,128)(2,1)} %collective-permute-done.1.refs_2_), channel_id=1, source_target_pairs={{0,32},{8,104},{32,64},{40,8},{64,96},{72,40},{96,0},{104,72},{1,3... | collective-permute-start | bytes 3145736 | tf_op jit(solution)/shard_map/ppermute | solution.py:269
  128.9 1.0 copy-start.2
  130.7 25.4 %collective-permute-start.16 = (bf16[16,4,64,128]{3,2,1,0:T(8,128)(2,1)}, bf16[16,4,64,128]{3,2,1,0:T(8,128)(2,1)S(1)}, u32[]{:S(2)}, u32[]{:S(2)}) collective-permute-start(bf16[16,4,64,128]{3,2,1,0:T(8,128)(2,1)} %collective-permute-done.14.refs_2_), channel_id=1, source_target_pairs={{0,32},{8,104},{32,64},{40,8},{64,96},{72,40},{96,0},{104,72},{1,3... | collective-permute-start | bytes 3145736 | tf_op jit(solution)/shard_map/ppermute | solution.py:269
  132.6 23.6 %collective-permute-start.17 = (bf16[16,4,64,128]{3,2,1,0:T(8,128)(2,1)S(1)}, bf16[16,4,64,128]{3,2,1,0:T(8,128)(2,1)S(1)}, u32[]{:S(2)}, u32[]{:S(2)}) collective-permute-start(bf16[16,4,64,128]{3,2,1,0:T(8,128)(2,1)S(1)} %collective-permute-done.8.refs_1_), channel_id=1, source_target_pairs={{0,16},{16,0},{1,17},{17,1},{2,18},{18,2},{3,19},{19,3},{4,20},{20... | collective-permute-start | bytes 3145736 | tf_op jit(solution)/shard_map/ppermute | solution.py:271
  136.4 1.2 copy-start.1
  137.6 1.2 copy-start.3
  144.4 20.5 %collective-permute-start.19 = (bf16[3,2,4,128,256]{4,3,2,1,0:T(8,128)(2,1)}, bf16[3,2,4,128,256]{4,3,2,1,0:T(8,128)(2,1)}, u32[]{:S(2)}, u32[]{:S(2)}) collective-permute-start(bf16[3,2,4,128,256]{4,3,2,1,0:T(8,128)(2,1)} %get-tuple-element.58), channel_id=1, source_target_pairs={{0,8},{8,0},{1,9},{9,1},{2,10},{10,2},{3,11},{11,3},{4,12},{12,4},... | collective-permute-start | bytes 4718600 | tf_op jit(solution)/shard_map/ppermute | solution.py:272
  160.3 9.3 %collective-permute-start.18 = (bf16[2,2,4,128,256]{4,3,2,1,0:T(8,128)(2,1)}, bf16[2,2,4,128,256]{4,3,2,1,0:T(8,128)(2,1)S(1)}, u32[]{:S(2)}, u32[]{:S(2)}) collective-permute-start(bf16[2,2,4,128,256]{4,3,2,1,0:T(8,128)(2,1)} %gram.12), channel_id=1, source_target_pairs={{0,8},{8,0},{1,9},{9,1},{2,10},{10,2},{3,11},{11,3},{4,12},{12,4},... | collective-permute-start | bytes 3145736 | tf_op jit(solution)/shard_map/ppermute | solution.py:272
  164.6 4.9 %collective-permute-start.15 = (bf16[1,2,4,128,256]{4,3,2,1,0:T(8,128)(2,1)}, bf16[1,2,4,128,256]{4,3,2,1,0:T(8,128)(2,1)}, u32[]{:S(2)}, u32[]{:S(2)}) collective-permute-start(bf16[1,2,4,128,256]{4,3,2,1,0:T(8,128)(2,1)} %get-tuple-element.53), channel_id=1, source_target_pairs={{0,8},{8,0},{1,9},{9,1},{2,10},{10,2},{3,11},{11,3},{4,12},{12,4},... | collective-permute-start | bytes 1572872 | tf_op jit(solution)/shard_map/ppermute | solution.py:272
